TPU v7x, 128 devices: a whole 4x4x4 slice. The times are simulated.
128 devices in a mesh: lat: 16 (over x, y), var: 8 (over z, core).
Axes of the slice: x: 4, y: 4, z: 4, core: 2. Of those that a mesh axis runs over, the one named last changes fastest.
Arguments:
- patches: bfloat16 [96, 192, 1024], P('lat', 'var'), may hold values from -6 to 6
- norm_gain: float32 [1024], replicated, may hold values from 0.25 to 1.75
- input_proj: bfloat16 [1024, 3072], replicated, may hold values from -7 to 7
- output_proj: bfloat16 [1024, 1024], replicated, may hold values from -0.1875 to 0.1875
- level_scale: float32 [40, 1024], P('var'), may hold values from 0.1 to 1.9
- level_shift: float32 [40, 1024], P('var'), may hold values from -3 to 3
- head_weight: bfloat16 [40, 1024, 320], P('var', 'lat'), may hold values from -0.1875 to 0.1875
- targets: bfloat16 [40, 96, 192, 320], P('var', 'lat'), may hold values from -6 to 6
- level_counts: int32 [4], replicated, may hold values from 13 to 37
- tile_dataset: int32 [16, 8], P('lat'), may hold values from 0 to 3
- slot_level: int32 [40], P('var'), may hold values from 0 to 39, as said below
Outputs:
- latent: bfloat16 [96, 192, 1024], P('lat', 'var')
- grad_latent: bfloat16 [96, 192, 1024], P('lat', 'var')
- grad_head: float32 [40, 1024, 320], P('var', 'lat')
Inputs may be any that keep to these rules, and one draw needn't show every extreme that they name: `slot_level`: for each j, slots j * 5 to (j + 1) * 5 - 1 hold the levels j * 5 to (j + 1) * 5 - 1 in some order.
All inputs are finite; a program needn't handle non-finite values.
Results may differ from a plain program's by a relative error of at most 0.012.
Values may be sent and summed in bfloat16 or wider, within the bound.
A program may use at most 128 MiB of HBM per device.

v0:
```python
import math

import jax
import jax.numpy as jnp
from jax import lax
from jax.sharding import PartitionSpec as P

HEADS = 16
WH = 6
WW = 12


EPS = 1e-05


def padded(array, sides, width, wrap):
    for axis, dim in sides:
        size, length = (lax.axis_size(axis), array.shape[dim])
        up = [(i, (i + 1) % size) for i in range(size if wrap else size - 1)]
        down = [(j, i) for i, j in up]
        last = lax.slice_in_dim(array, length - width, length, axis=dim)
        initial = lax.slice_in_dim(array, 0, width, axis=dim)
        before = lax.ppermute(last, axis, up)
        after = lax.ppermute(initial, axis, down)
        array = jnp.concatenate([before, array, after], axis=dim)
    return array


def layer_norm(values, gain):
    wide = values.astype(jnp.float32)
    average = jnp.mean(wide, axis=-1, keepdims=True)
    centred = wide - average
    variance = jnp.mean(centred * centred, axis=-1, keepdims=True)
    return (centred * lax.rsqrt(variance + EPS) * gain).astype(jnp.bfloat16)


def window_attention(query_ext, keyval, row_valid, heads):
    ext_rows, ext_cols, width = query_ext.shape
    head_size = width // heads
    win_rows = ext_rows // WH
    win_cols = ext_cols // WW

    def split(values, parts):
        shaped = values.reshape(win_rows, WH, win_cols, WW, parts, heads, head_size)
        return shaped.transpose(0, 2, 1, 3, 4, 5, 6).reshape(
            win_rows * win_cols, WH * WW, parts, heads, head_size
        )

    query_win = split(query_ext, 1)[:, :, 0]
    pairs = split(keyval, 2)
    key_win = pairs[:, :, 0]
    value_win = pairs[:, :, 1]
    key_mask = jnp.broadcast_to(
        row_valid.reshape(win_rows, 1, WH, 1), (win_rows, win_cols, WH, WW)
    ).reshape(win_rows * win_cols, WH * WW)
    scores = jnp.einsum(
        "wqhd,wkhd->whqk", query_win, key_win, preferred_element_type=jnp.float32
    ) / math.sqrt(head_size)
    scores = jnp.where(key_mask[:, None, None, :], scores, -jnp.inf)
    peak = jnp.max(scores, axis=-1, keepdims=True)
    weights = jnp.exp(scores - peak)
    probs = (weights / jnp.sum(weights, axis=-1, keepdims=True)).astype(jnp.bfloat16)
    mixed = jnp.einsum("whqk,wkhd->wqhd", probs, value_win, preferred_element_type=jnp.float32)
    return (
        mixed.reshape(win_rows, win_cols, WH, WW, width)
        .transpose(0, 2, 1, 3, 4)
        .reshape(ext_rows, ext_cols, width)
    )


def slot_terms(piece, target_rows, live_cols, level_scale, level_shift, heads_full):
    piece_wide = piece.astype(jnp.float32)
    rows = (
        piece_wide[None] * level_scale[:, None, None, :] + level_shift[:, None, None, :]
    ).astype(jnp.bfloat16)
    predicted = jnp.einsum("krnd,kdo->krno", rows, heads_full, preferred_element_type=jnp.float32)
    errors = ((predicted - target_rows.astype(jnp.float32)) * live_cols[:, None, :, None]).astype(
        jnp.bfloat16
    )
    back_grad = jnp.einsum("krno,kdo->krnd", errors, heads_full, preferred_element_type=jnp.float32)
    piece_grad = jnp.sum(back_grad * level_scale[:, None, None, :], axis=0)
    head_add = jnp.einsum("krnd,krno->dko", rows, errors, preferred_element_type=jnp.float32)
    return (piece_grad, head_add)


def local(
    patches,
    norm_gain,
    input_proj,
    output_proj,
    level_scale,
    level_shift,
    head_weight,
    targets,
    level_counts,
    tile_dataset,
    slot_level,
):
    band_rows, band_cols, width = patches.shape
    half_rows = WH // 2
    half_cols = WW // 2
    lat_count = lax.axis_size("lat")
    var_count = lax.axis_size("var")
    lat_place = lax.axis_index("lat")
    ext_rows = band_rows + WH
    ext_cols = band_cols + WW
    extended = padded(patches, (("lat", 0),), half_rows, False)
    extended = padded(extended, (("var", 1),), half_cols, True)
    normed_ext = layer_norm(extended, norm_gain)
    keyval = jnp.dot(
        normed_ext.reshape(-1, width), input_proj[:, width:], preferred_element_type=jnp.float32
    )
    keyval = keyval.astype(jnp.bfloat16).reshape(ext_rows, ext_cols, 2 * width)
    normed = normed_ext[half_rows : half_rows + band_rows, half_cols : half_cols + band_cols]
    queries = jnp.dot(
        normed.reshape(-1, width), input_proj[:, :width], preferred_element_type=jnp.float32
    )
    queries = queries.astype(jnp.bfloat16).reshape(band_rows, band_cols, width)
    query_ext = jnp.pad(queries, ((half_rows, WH - half_rows), (half_cols, WW - half_cols), (0, 0)))
    global_row = lat_place * band_rows - half_rows + jnp.arange(ext_rows, dtype=jnp.int32)
    row_valid = (global_row >= 0) & (global_row < lat_count * band_rows)
    mixed = window_attention(query_ext, keyval, row_valid, HEADS)
    attn = mixed[half_rows : half_rows + band_rows, half_cols : half_cols + band_cols].astype(
        jnp.bfloat16
    )
    update = jnp.dot(
        attn.reshape(-1, width), output_proj, preferred_element_type=jnp.float32
    ).reshape(band_rows, band_cols, width)
    latent = (patches.astype(jnp.float32) + update).astype(jnp.bfloat16)
    dataset_row = tile_dataset[0]
    dataset_ids = jnp.arange(level_counts.shape[0], dtype=jnp.int32)
    tile_levels = jnp.sum(
        jnp.where(dataset_row[:, None] == dataset_ids[None, :], level_counts[None, :], 0), axis=1
    )
    live_tiles = (slot_level[None, :] < tile_levels[:, None]).astype(jnp.float32)
    heads_full = lax.all_gather(head_weight, "lat", axis=1, tiled=True)
    tile_ids = jnp.arange(var_count, dtype=jnp.int32)
    piece = lax.all_gather(latent, "var", axis=1, tiled=True)
    piece_cols = piece.shape[1]
    column_tile = jnp.arange(piece_cols, dtype=jnp.int32) // band_cols
    onehot = (column_tile[:, None] == tile_ids[None, :]).astype(jnp.float32)
    column_live = jnp.dot(onehot, live_tiles)
    piece_grad, head_add = slot_terms(
        piece, targets, column_live.T, level_scale, level_shift, heads_full
    )
    latent_terms = piece_grad
    latent_terms, head_terms = (latent_terms, head_add)
    grad_latent = lax.psum_scatter(
        latent_terms.astype(jnp.bfloat16), "var", scatter_dimension=1, tiled=True
    )
    head_terms = head_terms * (1.0 / math.sqrt(lat_count * band_rows * var_count * band_cols))
    share_rows = width // lat_count
    summed = lax.psum(head_terms.astype(jnp.bfloat16), "lat").astype(jnp.float32)
    mine = lax.dynamic_slice_in_dim(summed, lat_place * share_rows, share_rows, 0)
    grad_head = jnp.transpose(mine, (1, 0, 2))
    return (latent, grad_latent, grad_head)


def solution(mesh):
    in_specs = (
        P("lat", "var", None),
        P(),
        P(),
        P(),
        P("var", None),
        P("var", None),
        P("var", "lat", None),
        P("var", "lat", None, None),
        P(),
        P("lat", None),
        P("var"),
    )
    out_specs = (P("lat", "var", None), P("lat", "var", None), P("var", "lat", None))
    return jax.shard_map(local, mesh=mesh, in_specs=in_specs, out_specs=out_specs, check_vma=False)
```

profile of v0, /device:TPU:0, one launch (start us, length us, event | category | flops | bytes accessed | tf_op | source)
XLA Modules:
  0.0 327.8 jit_solution(17000856274102400193)
XLA Ops:
  8.4 3.6 %collective-permute-start = (bf16[3,24,1024]{2,1,0:T(8,128)(2,1)S(1)}, bf16[3,24,1024]{2,1,0:T(8,128)(2,1)S(1)}, u32[]{:S(2)}, u32[]{:S(2)}) collective-permute-start(bf16[3,24,1024]{2,1,0:T(8,128)(2,1)S(1)} %get-tuple-element.25), channel_id=1, source_target_pairs={{0,8},{8,16},{16,24},{24,32},{32,40},{40,48},{48,56},{56,64},{64,7... | collective-permute-start | bytes 442376 | tf_op jit(solution)/shard_map/ppermute | solution.py:23
  13.3 1.8 collective-permute-done
  16.0 3.1 collective-permute-done.1
  19.3 2.9 collective-permute-start.3
  22.4 3.2 collective-permute-done.2
  26.1 1.9 multiply_reduce_fusion.1
  29.8 2.6 reshape.102
  33.7 2.1 fusion.40
  35.9 2.1 reshape.99
  38.0 3.2 copy.47
  41.2 5.5 %fusion.15 = bf16[432,2048]{1,0:T(8,128)(2,1)} fusion(bf16[1024,3072]{1,0:T(8,128)(2,1)} %param.13, f32[432,1024]{1,0:T(8,128)S(1)} %copy-done.3, f32[1024]{0:T(1024)S(1)} %copy-done.5, f32[432]{0:T(512)S(1)} %rsqrt.13, f32[432]{0:T(512)S(1)} %div.33), kind=kOutput, calls=%fused_computation.22 | convolution fusion | flops 1814593536 | bytes 7740800 | tf_op jit(solution)/shard_map/dot_general | solution.py:110
  46.8 6.4 %reshape_reshape.3 = bf16[2,6,3,12,2,16,64]{6,5,4,3,2,1,0:T(8,128)(2,1)} reshape(bf16[432,2048]{1,0:T(8,128)(2,1)} %fusion.15) | data formatting | bytes 3538944 | tf_op jit(solution)/shard_map/reshape;reshape | solution.py:44
  53.1 2.6 copy.45
  55.8 2.7 fusion.59
  58.4 4.0 %copy.59 = bf16[6,72,1,16,64]{1,4,3,0,2:T(8,128)(2,1)} copy(bf16[6,72,1,16,64]{4,3,2,1,0:T(8,128)(2,1)} %get-tuple-element.18) | data formatting | bytes 1769472
  62.5 4.0 %copy.60 = bf16[6,72,1,16,64]{1,4,3,0,2:T(8,128)(2,1)} copy(bf16[6,72,1,16,64]{4,3,2,1,0:T(8,128)(2,1)} %get-tuple-element.19) | data formatting | bytes 1769472
  66.5 3.1 fusion.25
  69.6 1.8 fusion.62
  71.4 1.9 fusion.34
  73.3 4.0 %copy.51 = bf16[6,72,16,64]{3,2,1,0:T(8,128)(2,1)} copy(bf16[6,72,16,64]{1,3,2,0:T(8,128)(2,1)} %fusion.34) | data formatting | bytes 1769472 | tf_op jit(solution)/shard_map/whqk,wkhd->wqhd/transpose | solution.py:63
  77.3 3.9 %reshape.100 = bf16[2,3,6,12,1024]{4,3,2,1,0:T(8,128)(2,1)} reshape(bf16[6,72,16,64]{3,2,1,0:T(8,128)(2,1)} %copy.51) | data formatting | bytes 1769472 | tf_op jit(solution)/shard_map/reshape | solution.py:65
  83.7 2.3 fusion.43
  87.1 28.4 %all-gather.3.cloned.1.call-done = bf16[6,192,1024]{2,1,0:T(8,128)(2,1)} async-done(((bf16[6,24,1024]{2,1,0:T(8,128)(2,1)}), bf16[6,192,1024]{2,1,0:T(8,128)(2,1)}) %all-gather.3.cloned.1.call-update) | async-done | bytes 2359312 | tf_op jit(solution)/shard_map/all_gather | solution.py:138
  115.6 4.4 %convert_element_type.69 = f32[6,192,1024]{2,1,0:T(8,128)} convert(bf16[6,192,1024]{2,1,0:T(8,128)(2,1)} %all-gather.3.cloned.1.call-done) | non-fusion elementwise | flops 1179648 | bytes 7077888 | tf_op jit(solution)/shard_map/convert_element_type | solution.py:72
  119.9 48.6 %all-gather.5.cloned.1.call-done = bf16[5,1024,320]{2,1,0:T(8,128)(2,1)} async-done(((bf16[5,64,320]{2,1,0:T(8,128)(2,1)}), bf16[5,1024,320]{2,1,0:T(8,128)(2,1)}) %all-gather.5.cloned.1.call-update) | async-done | bytes 3276816 | tf_op jit(solution)/shard_map/all_gather | solution.py:136
  168.5 10.1 %multiply_convert_fusion = bf16[5,6,192,320]{3,2,1,0:T(8,128)(2,1)S(1)} fusion(bf16[5,6,192,320]{3,2,1,0:T(8,128)(2,1)} %param.18, f32[5,192]{1,0:T(8,128)S(1)} %fusion.52, bf16[5,1024,320]{2,1,0:T(8,128)(2,1)} %all-gather.5.cloned.1.call-done, f32[5,1024]{1,0:T(8,128)S(1)} %copy-done.6, f32[5,1024]{1,0:T(8,128)S(1)} %copy-done.7, ...), kind=kOutput, calls=%fused_computation.11 | convolution fusion | flops 3799941120 | bytes 15412992 | tf_op jit(solution)/shard_map/krnd,kdo->krno/dot_general | solution.py:76
  178.6 2.1 copy-done.11
  180.8 6.6 %fusion.14 = bf16[1024,5,320]{0,2,1:T(8,128)(2,1)} fusion(bf16[5,6,192,320]{3,2,1,0:T(8,128)(2,1)S(1)} %multiply_convert_fusion, f32[5,1024]{1,0:T(8,128)S(1)} %copy-done.6, f32[5,1024]{1,0:T(8,128)S(1)} %copy-done.7, f32[6,192,1024]{2,1,0:T(8,128)S(1)} %copy-done.2), kind=kOutput, calls=%fused_computation.21 | convolution fusion | flops 3795845120 | bytes 11722752 | tf_op jit(solution)/shard_map/krnd,krno->dko/dot_general | solution.py:82
  187.5 9.9 %multiply_reduce_fusion = bf16[6,192,1024]{2,1,0:T(8,128)(2,1)S(1)} fusion(f32[5,1024]{1,0:T(8,128)S(1)} %copy-done.7, bf16[5,6,192,320]{3,2,1,0:T(8,128)(2,1)} %copy-done.11, bf16[5,1024,320]{2,1,0:T(8,128)(2,1)} %all-gather.5.cloned.1.call-done), kind=kOutput, calls=%fused_computation.1 | convolution fusion | flops 3785490432 | bytes 9342976 | tf_op jit(solution)/shard_map/krno,kdo->krnd/dot_general | solution.py:80
  197.4 1.7 copy.61
  199.1 84.3 %all-reduce.3.cloned.1.call-done = bf16[1024,5,320]{0,2,1:T(8,128)(2,1)} async-done(((bf16[1024,5,320]{0,2,1:T(8,128)(2,1)}), bf16[1024,5,320]{0,2,1:T(8,128)(2,1)}) %all-reduce.3.cloned.1.call-update) | async-done | bytes 3276816 | tf_op jit(solution)/shard_map/psum | solution.py:153
  285.6 33.4 %reduce-scatter.4.cloned.1.call-done = bf16[24,6144]{1,0:T(8,128)(2,1)} async-done(((bf16[192,6144]{1,0:T(8,128)(2,1)}), bf16[24,6144]{1,0:T(8,128)(2,1)}) %reduce-scatter.4.cloned.1.call-update) | async-done | bytes 294928
  (60 shorter events, 15.7 us)
Async XLA Ops:
  7.2 76.5 %copy-start = (bf16[1024,1024]{1,0:T(8,128)(2,1)S(1)}, bf16[1024,1024]{1,0:T(8,128)(2,1)}, u32[]{:S(2)}) copy-start(bf16[1024,1024]{1,0:T(8,128)(2,1)} %param.14) | copy-start | bytes 6291460
  7.2 108.4 %all-gather.3.cloned.1.call-start = ((), (), s32[]{:S(2)}) async-start(), calls=%async_computation.1 | async-start | bytes 2654208 | tf_op jit(solution)/shard_map/all_gather | solution.py:138
  8.4 6.7 %collective-permute-start = (bf16[3,24,1024]{2,1,0:T(8,128)(2,1)S(1)}, bf16[3,24,1024]{2,1,0:T(8,128)(2,1)S(1)}, u32[]{:S(2)}, u32[]{:S(2)}) collective-permute-start(bf16[3,24,1024]{2,1,0:T(8,128)(2,1)S(1)} %get-tuple-element.25), channel_id=1, source_target_pairs={{0,8},{8,16},{16,24},{24,32},{32,40},{40,48},{48,56},{56,64},{64,7... | collective-permute-start | bytes 442376 | tf_op jit(solution)/shard_map/ppermute | solution.py:23
  12.0 7.2 %collective-permute-start.1 = (bf16[3,24,1024]{2,1,0:T(8,128)(2,1)S(1)}, bf16[3,24,1024]{2,1,0:T(8,128)(2,1)S(1)}, u32[]{:S(2)}, u32[]{:S(2)}) collective-permute-start(bf16[3,24,1024]{2,1,0:T(8,128)(2,1)S(1)} %get-tuple-element.24), channel_id=1, source_target_pairs={{8,0},{16,8},{24,16},{32,24},{40,32},{48,40},{56,48},{64,56},{72,6... | collective-permute-start | bytes 442376 | tf_op jit(solution)/shard_map/ppermute | solution.py:24
  19.2 6.3 %collective-permute-start.2 = (bf16[12,6,1024]{2,1,0:T(8,128)(2,1)S(1)}, bf16[12,6,1024]{2,1,0:T(8,128)(2,1)S(1)}, u32[]{:S(2)}, u32[]{:S(2)}) collective-permute-start(bf16[12,6,1024]{2,1,0:T(8,128)(2,1)S(1)} %get-tuple-element.22), channel_id=1, source_target_pairs={{0,1},{1,2},{2,3},{3,4},{4,5},{5,6},{6,7},{7,0},{8,9},{9,10},{10,1... | collective-permute-start | bytes 442376 | tf_op jit(solution)/shard_map/ppermute | solution.py:23
  19.3 6.3 %collective-permute-start.3 = (bf16[12,6,1024]{2,1,0:T(8,128)(2,1)S(1)}, bf16[12,6,1024]{2,1,0:T(8,128)(2,1)S(1)}, u32[]{:S(2)}, u32[]{:S(2)}) collective-permute-start(bf16[12,6,1024]{2,1,0:T(8,128)(2,1)S(1)} %get-tuple-element.23), channel_id=1, source_target_pairs={{1,0},{2,1},{3,2},{4,3},{5,4},{6,5},{7,6},{0,7},{9,8},{10,9},{11,1... | collective-permute-start | bytes 442376 | tf_op jit(solution)/shard_map/ppermute | solution.py:24
  27.9 4.4 %copy-start.5 = (f32[1024]{0:T(1024)S(1)}, f32[1024]{0:T(1024)}, u32[]{:S(2)}) copy-start(f32[1024]{0:T(1024)} %param.12) | copy-start | bytes 12292
  38.0 3.2 copy-start.3
  69.6 1.8 copy-start.4
  82.6 4.2 %copy-start.8 = (s32[4]{0:T(128)S(1)}, s32[4]{0:T(128)}, u32[]{:S(2)}) copy-start(s32[4]{0:T(128)} %param.19) | copy-start | bytes 52
  82.6 4.2 %copy-start.9 = (s32[1,8]{1,0:T(1,128)S(1)}, s32[1,8]{1,0:T(1,128)}, u32[]{:S(2)}) copy-start(s32[1,8]{1,0:T(1,128)} %param.20) | copy-start | bytes 100
  82.6 4.3 %copy-start.10 = (s32[5]{0:T(128)S(1)}, s32[5]{0:T(128)}, u32[]{:S(2)}) copy-start(s32[5]{0:T(128)} %param.21) | copy-start | bytes 64
  86.0 82.5 %all-gather.5.cloned.1.call-start = ((), (), s32[]{:S(2)}) async-start(), calls=%async_computation.2 | async-start | bytes 4177920 | tf_op jit(solution)/shard_map/all_gather | solution.py:136
  86.7 196.6 %all-reduce.3.cloned.1.call-start = ((), (), s32[]{:S(2)}) async-start(), calls=%async_computation.3 | async-start | bytes 6553600 | tf_op jit(solution)/shard_map/psum | solution.py:153
  87.1 81.4 %copy-start.6 = (f32[5,1024]{1,0:T(8,128)S(1)}, f32[5,1024]{1,0:T(8,128)}, u32[]{:S(2)}) copy-start(f32[5,1024]{1,0:T(8,128)} %param.16) | copy-start | bytes 61444
  87.1 81.4 %copy-start.7 = (f32[5,1024]{1,0:T(8,128)S(1)}, f32[5,1024]{1,0:T(8,128)}, u32[]{:S(2)}) copy-start(f32[5,1024]{1,0:T(8,128)} %param.15) | copy-start | bytes 61444
  168.5 12.3 %copy-start.2 = (f32[6,192,1024]{2,1,0:T(8,128)S(1)}, f32[6,192,1024]{2,1,0:T(8,128)}, u32[]{:S(2)}) copy-start(f32[6,192,1024]{2,1,0:T(8,128)} %convert_element_type.69) | copy-start | bytes 14155780
  178.6 2.2 copy-start.11
  187.4 131.6 %reduce-scatter.4.cloned.1.call-start = ((), (), s32[]{:S(2)}) async-start(), calls=%async_computation.4 | async-start | bytes 2654208
  197.4 123.9 %copy-start.1 = (bf16[1024,1024]{1,0:T(8,128)(2,1)S(1)}, bf16[1024,1024]{1,0:T(8,128)(2,1)}, u32[]{:S(2)}) copy-start(bf16[1024,1024]{1,0:T(8,128)(2,1)} %param.14) | copy-start | bytes 6291460
Sparse Core Ops, SparseCore 0:
  86.1 29.4 all-gather.2
  117.7 50.7 all-gather.4
  187.6 95.7 all-reduce.2
  285.8 33.2 reduce-scatter.3
where the time goes:
time: 329 us; the launch traced here: 328 us
  waiting for transfers between devices  204 us (62%)
  local copies, waits for them, and re-layouts  48 us (15%)
  matrix products  41.6 us (13%)
  between operations  14 us (4%)
  other arithmetic  12.7 us (4%)
  starting transfers between devices  7.98 us (2%)
    psum x1, waiting for transfers between devices, local(): lax.psum(head_terms.astype(jnp.bfloat16), 'lat').astype(jnp.float32)  84.3 us
    all_gather x1, waiting for transfers between devices, local(): heads_full = lax.all_gather(head_weight, 'lat', axis=1, tiled=True)  48.6 us
    unnamed x5, waiting for transfers between devices  34.2 us
    all_gather x1, waiting for transfers between devices, local(): piece = lax.all_gather(latent, 'var', axis=1, tiled=True)  28.4 us
    unnamed x32, local copies, waits for them, and re-layouts  16.3 us
    dot_general x1, matrix products, slot_terms(): jnp.einsum('krnd,kdo->krno', rows, heads_full, preferred_element_type=jnp...  10.1 us
    dot_general x1, matrix products, slot_terms(): jnp.einsum('krno,kdo->krnd', errors, heads_full, preferred_element_type=j...  9.86 us
    another operation x2, local copies, waits for them, and re-layouts, split(): shaped = values.reshape(win_rows, WH, win_cols, WW, parts, heads, head_size)  8.98 us
  transfers between devices with their start and end apart: 8, of which 7 were waited for; matrix products, arithmetic and copies ran while one was open for 6% of the time, Pallas kernels for 0%

commit v1 on v0

--- a/solution.py
+++ b/solution.py
@@ -150,8 +150,9 @@
     )
     head_terms = head_terms * (1.0 / math.sqrt(lat_count * band_rows * var_count * band_cols))
     share_rows = width // lat_count
-    summed = lax.psum(head_terms.astype(jnp.bfloat16), "lat").astype(jnp.float32)
-    mine = lax.dynamic_slice_in_dim(summed, lat_place * share_rows, share_rows, 0)
+    mine = lax.psum_scatter(
+        head_terms.astype(jnp.bfloat16), "lat", scatter_dimension=0, tiled=True
+    ).astype(jnp.float32)
     grad_head = jnp.transpose(mine, (1, 0, 2))
     return (latent, grad_latent, grad_head)
 

time: 329 us -> 315 us (0.957)
  waiting for transfers between devices: 204 us -> 183 us
  local copies, waits for them, and re-layouts: 48 us -> 53.8 us
    psum x1 -> x0, waiting for transfers between devices: 84.3 us -> none  [local(): lax.psum(head_terms.astype(jnp.bfloat16), 'lat').astype(jnp.float32)]
    reduce_scatter x0 -> x1, waiting for transfers between devices: none -> 80.9 us  [local(): lax.psum_scatter(head_terms.astype(jnp.bfloat16), 'lat', scatter_dimensio...]
    unnamed x5, waiting for transfers between devices: 34.2 us -> 17.3 us
    convert_element_type x0 -> x1, local copies, waits for them, and re-layouts: none -> 8.2 us  [local(): head_terms.astype(jnp.bfloat16)]
  transfers between devices with their start and end apart: 8 -> 8, of which waited for: 7 -> 7; matrix products, arithmetic and copies ran while one was open for 6% -> 8% of each run, Pallas kernels for 0% -> 0%
where the time goes in v1:
time: 315 us; the launch traced here: 314 us
  waiting for transfers between devices  183 us (58%)
  local copies, waits for them, and re-layouts  53.8 us (17%)
  matrix products  42.2 us (13%)
  between operations  14 us (4%)
  other arithmetic  12.5 us (4%)
  starting transfers between devices  7.98 us (3%)
    reduce_scatter x1, waiting for transfers between devices, local(): lax.psum_scatter(head_terms.astype(jnp.bfloat16), 'lat', scatter_dimensio...  80.9 us
    all_gather x1, waiting for transfers between devices, local(): heads_full = lax.all_gather(head_weight, 'lat', axis=1, tiled=True)  48.6 us
    all_gather x1, waiting for transfers between devices, local(): piece = lax.all_gather(latent, 'var', axis=1, tiled=True)  28.5 us
    unnamed x5, waiting for transfers between devices  17.3 us
    unnamed x32, local copies, waits for them, and re-layouts  13.9 us
    dot_general x1, matrix products, slot_terms(): jnp.einsum('krnd,kdo->krno', rows, heads_full, preferred_element_type=jnp...  10.6 us
    dot_general x1, matrix products, slot_terms(): jnp.einsum('krnd,krno->dko', rows, errors, preferred_element_type=jnp.flo...  9.29 us
    another operation x2, local copies, waits for them, and re-layouts, split(): shaped = values.reshape(win_rows, WH, win_cols, WW, parts, heads, head_size)  8.98 us
  transfers between devices with their start and end apart: 8, of which 7 were waited for; matrix products, arithmetic and copies ran while one was open for 8% of the time, Pallas kernels for 0%

profile of v1, /device:TPU:0, one launch (start us, length us, event | category | flops | bytes accessed | tf_op | source)
XLA Modules:
  0.0 313.8 jit_solution(12802649083848093492)
XLA Ops:
  8.4 3.6 %collective-permute-start = (bf16[3,24,1024]{2,1,0:T(8,128)(2,1)S(1)}, bf16[3,24,1024]{2,1,0:T(8,128)(2,1)S(1)}, u32[]{:S(2)}, u32[]{:S(2)}) collective-permute-start(bf16[3,24,1024]{2,1,0:T(8,128)(2,1)S(1)} %get-tuple-element.25), channel_id=1, source_target_pairs={{0,8},{8,16},{16,24},{24,32},{32,40},{40,48},{48,56},{56,64},{64,7... | collective-permute-start | bytes 442376 | tf_op jit(solution)/shard_map/ppermute | solution.py:23
  13.3 1.8 collective-permute-done
  16.0 3.1 collective-permute-done.1
  19.3 2.9 collective-permute-start.3
  22.4 3.2 %collective-permute-done.2 = bf16[12,6,1024]{2,1,0:T(8,128)(2,1)S(1)} collective-permute-done((bf16[12,6,1024]{2,1,0:T(8,128)(2,1)S(1)}, bf16[12,6,1024]{2,1,0:T(8,128)(2,1)S(1)}, u32[]{:S(2)}, u32[]{:S(2)}) %collective-permute-start.2) | collective-permute-done | bytes 147488 | tf_op jit(solution)/shard_map/ppermute | solution.py:23
  26.1 1.8 multiply_reduce_fusion.1
  29.7 2.7 reshape.102
  33.7 2.1 fusion.40
  35.9 2.1 reshape.99
  38.0 3.2 %copy.48 = bf16[2,3,6,12,1,16,64]{6,5,3,2,1,0,4:T(8,128)(2,1)} copy(bf16[2,3,6,12,1,16,64]{6,5,3,1,2,0,4:T(8,128)(2,1)} %bitcast.58) | data formatting | bytes 1769472 | tf_op jit(solution)/shard_map/transpose | solution.py:45
  41.2 5.5 %fusion.15 = bf16[432,2048]{1,0:T(8,128)(2,1)} fusion(bf16[1024,3072]{1,0:T(8,128)(2,1)} %param.13, f32[432,1024]{1,0:T(8,128)S(1)} %copy-done.2, f32[1024]{0:T(1024)S(1)} %copy-done.4, f32[432]{0:T(512)S(1)} %rsqrt.13, f32[432]{0:T(512)S(1)} %div.33), kind=kOutput, calls=%fused_computation.22 | convolution fusion | flops 1814593536 | bytes 7740800 | tf_op jit(solution)/shard_map/dot_general | solution.py:110
  46.8 6.4 %reshape_reshape.3 = bf16[2,6,3,12,2,16,64]{6,5,4,3,2,1,0:T(8,128)(2,1)} reshape(bf16[432,2048]{1,0:T(8,128)(2,1)} %fusion.15) | data formatting | bytes 3538944 | tf_op jit(solution)/shard_map/reshape;reshape | solution.py:44
  53.1 2.6 copy.46
  55.7 2.6 fusion.59
  58.3 4.0 %copy.61 = bf16[6,72,1,16,64]{1,4,3,0,2:T(8,128)(2,1)} copy(bf16[6,72,1,16,64]{4,3,2,1,0:T(8,128)(2,1)} %get-tuple-element.18) | data formatting | bytes 1769472
  62.4 4.0 %copy.62 = bf16[6,72,1,16,64]{1,4,3,0,2:T(8,128)(2,1)} copy(bf16[6,72,1,16,64]{4,3,2,1,0:T(8,128)(2,1)} %get-tuple-element.19) | data formatting | bytes 1769472
  66.4 3.1 fusion.25
  69.5 1.8 fusion.62
  71.3 1.9 fusion.34
  73.2 4.0 %copy.52 = bf16[6,72,16,64]{3,2,1,0:T(8,128)(2,1)} copy(bf16[6,72,16,64]{1,3,2,0:T(8,128)(2,1)} %fusion.34) | data formatting | bytes 1769472 | tf_op jit(solution)/shard_map/whqk,wkhd->wqhd/transpose | solution.py:63
  77.2 3.9 %reshape.100 = bf16[2,3,6,12,1024]{4,3,2,1,0:T(8,128)(2,1)} reshape(bf16[6,72,16,64]{3,2,1,0:T(8,128)(2,1)} %copy.52) | data formatting | bytes 1769472 | tf_op jit(solution)/shard_map/reshape | solution.py:65
  83.6 2.3 fusion.43
  87.1 28.5 %all-gather.3.cloned.1.call-done = bf16[6,192,1024]{2,1,0:T(8,128)(2,1)} async-done(((bf16[6,24,1024]{2,1,0:T(8,128)(2,1)}), bf16[6,192,1024]{2,1,0:T(8,128)(2,1)}) %all-gather.3.cloned.1.call-update) | async-done | bytes 2359312 | tf_op jit(solution)/shard_map/all_gather | solution.py:138
  115.6 4.3 %convert_element_type.67 = f32[6,192,1024]{2,1,0:T(8,128)} convert(bf16[6,192,1024]{2,1,0:T(8,128)(2,1)} %all-gather.3.cloned.1.call-done) | non-fusion elementwise | flops 1179648 | bytes 7077888 | tf_op jit(solution)/shard_map/convert_element_type | solution.py:72
  119.9 48.6 %all-gather.5.cloned.1.call-done = bf16[5,1024,320]{2,1,0:T(8,128)(2,1)} async-done(((bf16[5,64,320]{2,1,0:T(8,128)(2,1)}), bf16[5,1024,320]{2,1,0:T(8,128)(2,1)}) %all-gather.5.cloned.1.call-update) | async-done | bytes 3276816 | tf_op jit(solution)/shard_map/all_gather | solution.py:136
  168.5 10.6 %multiply_convert_fusion = bf16[5,6,192,320]{3,2,1,0:T(8,128)(2,1)S(1)} fusion(bf16[5,6,192,320]{3,2,1,0:T(8,128)(2,1)} %param.18, f32[5,192]{1,0:T(8,128)S(1)} %fusion.52, bf16[5,1024,320]{2,1,0:T(8,128)(2,1)} %all-gather.5.cloned.1.call-done, f32[5,1024]{1,0:T(8,128)S(1)} %copy-done.7, f32[5,1024]{1,0:T(8,128)S(1)} %copy-done.6, ...), kind=kOutput, calls=%fused_computation.11 | convolution fusion | flops 3799941120 | bytes 15412992 | tf_op jit(solution)/shard_map/krnd,kdo->krno/dot_general | solution.py:76
  179.2 7.2 %multiply_reduce_fusion = bf16[6,192,1024]{2,1,0:T(8,128)(2,1)S(1)} fusion(f32[5,1024]{1,0:T(8,128)S(1)} %copy-done.6, bf16[5,6,192,320]{3,2,1,0:T(8,128)(2,1)S(1)} %multiply_convert_fusion, bf16[5,1024,320]{2,1,0:T(8,128)(2,1)S(1)} %copy-done.5), kind=kOutput, calls=%fused_computation.1 | convolution fusion | flops 3785490432 | bytes 9342976 | tf_op jit(solution)/shard_map/krno,kdo->krnd/dot_general | solution.py:80
  186.4 1.7 copy.63
  188.2 9.3 %fusion.14 = bf16[1024,5,320]{0,2,1:T(8,128)(2,1)} fusion(bf16[5,6,192,320]{3,2,1,0:T(8,128)(2,1)} %copy-done.11, f32[5,1024]{1,0:T(8,128)S(1)} %copy-done.7, f32[5,1024]{1,0:T(8,128)S(1)} %copy-done.6, f32[6,192,1024]{2,1,0:T(8,128)} %convert_element_type.67), kind=kOutput, calls=%fused_computation.21 | convolution fusion | flops 3795845120 | bytes 11722752 | tf_op jit(solution)/shard_map/krnd,krno->dko/dot_general | solution.py:82
  197.5 8.2 %copy.54 = bf16[1024,5,320]{2,1,0:T(8,128)(2,1)} copy(bf16[1024,5,320]{0,2,1:T(8,128)(2,1)} %fusion.14) | data formatting | bytes 6553600 | tf_op jit(solution)/shard_map/convert_element_type | solution.py:154
  205.7 16.5 %reduce-scatter.7.cloned.1.call-done = bf16[24,6144]{1,0:T(8,128)(2,1)} async-done(((bf16[192,6144]{1,0:T(8,128)(2,1)}), bf16[24,6144]{1,0:T(8,128)(2,1)}) %reduce-scatter.7.cloned.1.call-update) | async-done | bytes 294928
  224.4 80.9 %reduce-scatter.5.cloned.1.call-done = bf16[64,5,320]{2,1,0:T(8,128)(2,1)} async-done(((bf16[1024,5,320]{2,1,0:T(8,128)(2,1)}), bf16[64,5,320]{2,1,0:T(8,128)(2,1)}) %reduce-scatter.5.cloned.1.call-update) | async-done | bytes 204816 | tf_op jit(solution)/shard_map/reduce_scatter | solution.py:153
  (61 shorter events, 15.3 us)
Async XLA Ops:
  7.2 76.4 %copy-start = (bf16[1024,1024]{1,0:T(8,128)(2,1)S(1)}, bf16[1024,1024]{1,0:T(8,128)(2,1)}, u32[]{:S(2)}) copy-start(bf16[1024,1024]{1,0:T(8,128)(2,1)} %param.14) | copy-start | bytes 6291460
  7.2 108.4 %all-gather.3.cloned.1.call-start = ((), (), s32[]{:S(2)}) async-start(), calls=%async_computation.2 | async-start | bytes 2654208 | tf_op jit(solution)/shard_map/all_gather | solution.py:138
  8.4 6.7 %collective-permute-start = (bf16[3,24,1024]{2,1,0:T(8,128)(2,1)S(1)}, bf16[3,24,1024]{2,1,0:T(8,128)(2,1)S(1)}, u32[]{:S(2)}, u32[]{:S(2)}) collective-permute-start(bf16[3,24,1024]{2,1,0:T(8,128)(2,1)S(1)} %get-tuple-element.25), channel_id=1, source_target_pairs={{0,8},{8,16},{16,24},{24,32},{32,40},{40,48},{48,56},{56,64},{64,7... | collective-permute-start | bytes 442376 | tf_op jit(solution)/shard_map/ppermute | solution.py:23
  12.0 7.2 %collective-permute-start.1 = (bf16[3,24,1024]{2,1,0:T(8,128)(2,1)S(1)}, bf16[3,24,1024]{2,1,0:T(8,128)(2,1)S(1)}, u32[]{:S(2)}, u32[]{:S(2)}) collective-permute-start(bf16[3,24,1024]{2,1,0:T(8,128)(2,1)S(1)} %get-tuple-element.24), channel_id=1, source_target_pairs={{8,0},{16,8},{24,16},{32,24},{40,32},{48,40},{56,48},{64,56},{72,6... | collective-permute-start | bytes 442376 | tf_op jit(solution)/shard_map/ppermute | solution.py:24
  19.2 6.3 %collective-permute-start.2 = (bf16[12,6,1024]{2,1,0:T(8,128)(2,1)S(1)}, bf16[12,6,1024]{2,1,0:T(8,128)(2,1)S(1)}, u32[]{:S(2)}, u32[]{:S(2)}) collective-permute-start(bf16[12,6,1024]{2,1,0:T(8,128)(2,1)S(1)} %get-tuple-element.22), channel_id=1, source_target_pairs={{0,1},{1,2},{2,3},{3,4},{4,5},{5,6},{6,7},{7,0},{8,9},{9,10},{10,1... | collective-permute-start | bytes 442376 | tf_op jit(solution)/shard_map/ppermute | solution.py:23
  19.3 6.3 %collective-permute-start.3 = (bf16[12,6,1024]{2,1,0:T(8,128)(2,1)S(1)}, bf16[12,6,1024]{2,1,0:T(8,128)(2,1)S(1)}, u32[]{:S(2)}, u32[]{:S(2)}) collective-permute-start(bf16[12,6,1024]{2,1,0:T(8,128)(2,1)S(1)} %get-tuple-element.23), channel_id=1, source_target_pairs={{1,0},{2,1},{3,2},{4,3},{5,4},{6,5},{7,6},{0,7},{9,8},{10,9},{11,1... | collective-permute-start | bytes 442376 | tf_op jit(solution)/shard_map/ppermute | solution.py:24
  27.9 4.5 %copy-start.4 = (f32[1024]{0:T(1024)S(1)}, f32[1024]{0:T(1024)}, u32[]{:S(2)}) copy-start(f32[1024]{0:T(1024)} %param.12) | copy-start | bytes 12292
  38.0 3.2 %copy-start.2 = (f32[432,1024]{1,0:T(8,128)S(1)}, f32[432,1024]{1,0:T(8,128)}, u32[]{:S(2)}) copy-start(f32[432,1024]{1,0:T(8,128)} %reshape.102) | copy-start | bytes 5308420
  69.5 1.8 copy-start.3
  82.5 4.2 %copy-start.8 = (s32[4]{0:T(128)S(1)}, s32[4]{0:T(128)}, u32[]{:S(2)}) copy-start(s32[4]{0:T(128)} %param.19) | copy-start | bytes 52
  82.5 4.2 %copy-start.9 = (s32[1,8]{1,0:T(1,128)S(1)}, s32[1,8]{1,0:T(1,128)}, u32[]{:S(2)}) copy-start(s32[1,8]{1,0:T(1,128)} %param.20) | copy-start | bytes 100
  82.5 4.3 %copy-start.10 = (s32[5]{0:T(128)S(1)}, s32[5]{0:T(128)}, u32[]{:S(2)}) copy-start(s32[5]{0:T(128)} %param.21) | copy-start | bytes 64
  85.9 82.6 %all-gather.5.cloned.1.call-start = ((), (), s32[]{:S(2)}) async-start(), calls=%async_computation.3 | async-start | bytes 4177920 | tf_op jit(solution)/shard_map/all_gather | solution.py:136
  86.6 135.5 %reduce-scatter.7.cloned.1.call-start = ((), (), s32[]{:S(2)}) async-start(), calls=%async_computation.5 | async-start | bytes 2654208
  87.1 81.5 %copy-start.6 = (f32[5,1024]{1,0:T(8,128)S(1)}, f32[5,1024]{1,0:T(8,128)}, u32[]{:S(2)}) copy-start(f32[5,1024]{1,0:T(8,128)} %param.15) | copy-start | bytes 61444
  87.1 81.5 %copy-start.7 = (f32[5,1024]{1,0:T(8,128)S(1)}, f32[5,1024]{1,0:T(8,128)}, u32[]{:S(2)}) copy-start(f32[5,1024]{1,0:T(8,128)} %param.16) | copy-start | bytes 61444
  168.5 10.6 %copy-start.5 = (bf16[5,1024,320]{2,1,0:T(8,128)(2,1)S(1)}, bf16[5,1024,320]{2,1,0:T(8,128)(2,1)}, u32[]{:S(2)}) copy-start(bf16[5,1024,320]{2,1,0:T(8,128)(2,1)} %all-gather.5.cloned.1.call-done) | copy-start | bytes 9830404
  179.2 7.2 %copy-start.11 = (bf16[5,6,192,320]{3,2,1,0:T(8,128)(2,1)}, bf16[5,6,192,320]{3,2,1,0:T(8,128)(2,1)S(1)}, u32[]{:S(2)}) copy-start(bf16[5,6,192,320]{3,2,1,0:T(8,128)(2,1)S(1)} %multiply_convert_fusion) | copy-start | bytes 11059204
  188.1 117.2 %reduce-scatter.5.cloned.1.call-start = ((), (), s32[]{:S(2)}) async-start(), calls=%async_computation.4 | async-start | bytes 6684672 | tf_op jit(solution)/shard_map/reduce_scatter | solution.py:153
  205.7 101.6 %copy-start.1 = (bf16[1024,1024]{1,0:T(8,128)(2,1)S(1)}, bf16[1024,1024]{1,0:T(8,128)(2,1)}, u32[]{:S(2)}) copy-start(bf16[1024,1024]{1,0:T(8,128)(2,1)} %param.14) | copy-start | bytes 6291460
Sparse Core Ops, SparseCore 0:
  86.0 29.4 all-gather.2
  117.7 50.7 all-gather.4
  188.2 33.9 reduce-scatter.6
  225.5 79.7 reduce-scatter.4

commit v2 on v0

--- a/solution.py
+++ b/solution.py
@@ -3,7 +3,87 @@
 import jax
 import jax.numpy as jnp
 from jax import lax
+from jax.experimental import pallas as pl
+from jax.experimental.pallas import tpu as pltpu
 from jax.sharding import PartitionSpec as P
+
+MESH_ID = pl.DeviceIdType.MESH
+
+
+def _greet(axis, n, me):
+    barrier = pltpu.get_barrier_semaphore()
+    for k in range(1, n):
+        pl.semaphore_signal(barrier, inc=1, device_id={axis: lax.rem(me + k, n)},
+                            device_id_type=MESH_ID)
+    pl.semaphore_wait(barrier, n - 1)
+
+
+def peer_gather(block, axis, n, cid):
+    def kernel(x_ref, out_ref, send_sem, recv_sem):
+        me = lax.axis_index(axis)
+        _greet(axis, n, me)
+        sends = []
+        for k in range(1, n):
+            copy = pltpu.make_async_remote_copy(
+                src_ref=x_ref, dst_ref=out_ref.at[me], send_sem=send_sem.at[k],
+                recv_sem=recv_sem.at[me], device_id={axis: lax.rem(me + k, n)},
+                device_id_type=MESH_ID)
+            copy.start()
+            sends.append(copy)
+        out_ref[me] = x_ref[...]
+        for k in range(1, n):
+            src = lax.rem(me + n - k, n)
+            pltpu.make_async_remote_copy(
+                src_ref=x_ref, dst_ref=out_ref.at[src], send_sem=send_sem.at[k],
+                recv_sem=recv_sem.at[src], device_id={axis: src},
+                device_id_type=MESH_ID).wait_recv()
+        for copy in sends:
+            copy.wait_send()
+
+    return pl.pallas_call(
+        kernel,
+        out_shape=jax.ShapeDtypeStruct((n,) + block.shape, block.dtype),
+        in_specs=[pl.BlockSpec(memory_space=pltpu.VMEM)],
+        out_specs=pl.BlockSpec(memory_space=pltpu.VMEM),
+        scratch_shapes=[pltpu.SemaphoreType.DMA((n,)), pltpu.SemaphoreType.DMA((n,))],
+        compiler_params=pltpu.CompilerParams(collective_id=cid, has_side_effects=True),
+    )(block)
+
+
+def peer_reduce_scatter(parts, axis, n, cid, out_dtype):
+    def kernel(x_ref, out_ref, held, send_sem, recv_sem):
+        me = lax.axis_index(axis)
+        _greet(axis, n, me)
+        sends = []
+        for k in range(1, n):
+            dst = lax.rem(me + k, n)
+            copy = pltpu.make_async_remote_copy(
+                src_ref=x_ref.at[dst], dst_ref=held.at[me], send_sem=send_sem.at[k],
+                recv_sem=recv_sem.at[me], device_id={axis: dst},
+                device_id_type=MESH_ID)
+            copy.start()
+            sends.append(copy)
+        total = x_ref[me].astype(jnp.float32)
+        for k in range(1, n):
+            src = lax.rem(me + n - k, n)
+            pltpu.make_async_remote_copy(
+                src_ref=x_ref.at[src], dst_ref=held.at[src], send_sem=send_sem.at[k],
+                recv_sem=recv_sem.at[src], device_id={axis: src},
+                device_id_type=MESH_ID).wait_recv()
+            total = total + held[src].astype(jnp.float32)
+        out_ref[...] = total.astype(out_ref.dtype)
+        for copy in sends:
+            copy.wait_send()
+
+    return pl.pallas_call(
+        kernel,
+        out_shape=jax.ShapeDtypeStruct(parts.shape[1:], out_dtype),
+        in_specs=[pl.BlockSpec(memory_space=pltpu.VMEM)],
+        out_specs=pl.BlockSpec(memory_space=pltpu.VMEM),
+        scratch_shapes=[pltpu.VMEM(parts.shape, parts.dtype),
+                        pltpu.SemaphoreType.DMA((n,)), pltpu.SemaphoreType.DMA((n,))],
+        compiler_params=pltpu.CompilerParams(collective_id=cid, has_side_effects=True),
+    )(parts)
 
 HEADS = 16
 WH = 6
@@ -135,7 +215,12 @@
     live_tiles = (slot_level[None, :] < tile_levels[:, None]).astype(jnp.float32)
     heads_full = lax.all_gather(head_weight, "lat", axis=1, tiled=True)
     tile_ids = jnp.arange(var_count, dtype=jnp.int32)
-    piece = lax.all_gather(latent, "var", axis=1, tiled=True)
+    tiles = peer_gather(latent.reshape(band_rows * band_cols, width), "var", var_count, 1)
+    piece = (
+        tiles.reshape(var_count, band_rows, band_cols, width)
+        .transpose(1, 0, 2, 3)
+        .reshape(band_rows, var_count * band_cols, width)
+    )
     piece_cols = piece.shape[1]
     column_tile = jnp.arange(piece_cols, dtype=jnp.int32) // band_cols
     onehot = (column_tile[:, None] == tile_ids[None, :]).astype(jnp.float32)
@@ -145,14 +230,21 @@
     )
     latent_terms = piece_grad
     latent_terms, head_terms = (latent_terms, head_add)
-    grad_latent = lax.psum_scatter(
-        latent_terms.astype(jnp.bfloat16), "var", scatter_dimension=1, tiled=True
-    )
+    latent_parts = (
+        latent_terms.astype(jnp.bfloat16)
+        .reshape(band_rows, var_count, band_cols, width)
+        .transpose(1, 0, 2, 3)
+        .reshape(var_count, band_rows * band_cols, width)
+    )
+    grad_latent = peer_reduce_scatter(
+        latent_parts, "var", var_count, 2, jnp.bfloat16
+    ).reshape(band_rows, band_cols, width)
     head_terms = head_terms * (1.0 / math.sqrt(lat_count * band_rows * var_count * band_cols))
     share_rows = width // lat_count
-    summed = lax.psum(head_terms.astype(jnp.bfloat16), "lat").astype(jnp.float32)
-    mine = lax.dynamic_slice_in_dim(summed, lat_place * share_rows, share_rows, 0)
-    grad_head = jnp.transpose(mine, (1, 0, 2))
+    slots, outs = head_terms.shape[1], head_terms.shape[2]
+    head_parts = head_terms.astype(jnp.bfloat16).reshape(lat_count, share_rows * slots, outs)
+    mine = peer_reduce_scatter(head_parts, "lat", lat_count, 3, jnp.float32)
+    grad_head = jnp.transpose(mine.reshape(share_rows, slots, outs), (1, 0, 2))
     return (latent, grad_latent, grad_head)
 
 

time: 329 us -> 303 us (0.921)
  the two profiles are of different devices: /device:TPU:0 before, /device:TPU:29 now
where the time goes in v2:
time: 303 us; the launch traced here: 302 us
  Pallas kernels  156 us (51%)
  local copies, waits for them, and re-layouts  66.5 us (22%)
  matrix products  39.8 us (13%)
  between operations  14.3 us (5%)
  starting transfers between devices  10.9 us (4%)
  other arithmetic  7.76 us (3%)
  waiting for transfers between devices  6.39 us (2%)
    pallas_call x2, Pallas kernels, peer_reduce_scatter(): pl.pallas_call(kernel, out_shape=jax.ShapeDtypeStruct(parts.shape[1:], ou...  123 us
    pallas_call x1, Pallas kernels, peer_gather(): pl.pallas_call(kernel, out_shape=jax.ShapeDtypeStruct((n,) + block.shape,...  32.9 us
    unnamed x26, local copies, waits for them, and re-layouts  10.7 us
    dot_general x1, matrix products, slot_terms(): jnp.einsum('krnd,kdo->krno', rows, heads_full, preferred_element_type=jnp...  10.1 us
    another operation x2, local copies, waits for them, and re-layouts, split(): shaped = values.reshape(win_rows, WH, win_cols, WW, parts, heads, head_size)  9 us
    reshape x1, local copies, waits for them, and re-layouts, local(): head_terms.astype(jnp.bfloat16).reshape(lat_count, share_rows * slots, outs)  8.87 us
    ppermute x2, starting transfers between devices, padded(): before = lax.ppermute(last, axis, up)  8.52 us
    convert_element_type x1, local copies, waits for them, and re-layouts, local(): head_terms.astype(jnp.bfloat16).reshape(lat_count, share_rows * slots, outs)  8.18 us
  transfers between devices with their start and end apart: 5, of which 3 were waited for; matrix products, arithmetic and copies ran while one was open for 23% of the time, Pallas kernels for 11%

profile of v2, /device:TPU:29, one launch (start us, length us, event | category | flops | bytes accessed | tf_op | source)
XLA Modules:
  0.0 301.9 jit_solution(12315700445112973533)
XLA Ops:
  8.9 2.4 collective-permute-start.1
  11.3 5.0 %collective-permute-start = (bf16[3,24,1024]{2,1,0:T(8,128)(2,1)S(1)}, bf16[3,24,1024]{2,1,0:T(8,128)(2,1)S(1)}, u32[]{:S(2)}, u32[]{:S(2)}) collective-permute-start(bf16[3,24,1024]{2,1,0:T(8,128)(2,1)S(1)} %get-tuple-element.19), channel_id=1, source_target_pairs={{0,8},{8,16},{16,24},{24,32},{32,40},{40,48},{48,56},{56,64},{64,7... | collective-permute-start | bytes 442376 | tf_op jit(solution)/shard_map/ppermute | solution.py:103
  19.5 3.5 %collective-permute-start.2 = (bf16[12,6,1024]{2,1,0:T(8,128)(2,1)S(1)}, bf16[12,6,1024]{2,1,0:T(8,128)(2,1)S(1)}, u32[]{:S(2)}, u32[]{:S(2)}) collective-permute-start(bf16[12,6,1024]{2,1,0:T(8,128)(2,1)S(1)} %get-tuple-element.16), channel_id=1, source_target_pairs={{0,1},{1,2},{2,3},{3,4},{4,5},{5,6},{6,7},{7,0},{8,9},{9,10},{10,1... | collective-permute-start | bytes 442376 | tf_op jit(solution)/shard_map/ppermute | solution.py:103
  23.9 1.7 collective-permute-done.2
  25.6 2.9 collective-permute-done.3
  29.0 1.8 multiply_reduce_fusion.1
  32.6 2.7 reshape.135
  36.6 2.1 fusion.40
  38.8 2.1 reshape.127
  40.9 3.3 %copy.45 = bf16[2,3,6,12,1,16,64]{6,5,3,2,1,0,4:T(8,128)(2,1)} copy(bf16[2,3,6,12,1,16,64]{6,5,3,1,2,0,4:T(8,128)(2,1)} %bitcast.64) | data formatting | bytes 1769472 | tf_op jit(solution)/shard_map/transpose | solution.py:125
  44.2 5.5 %fusion.15 = bf16[432,2048]{1,0:T(8,128)(2,1)} fusion(bf16[1024,3072]{1,0:T(8,128)(2,1)} %param.13, f32[432,1024]{1,0:T(8,128)S(1)} %copy-done.3, f32[1024]{0:T(1024)S(1)} %copy-done.6, f32[432]{0:T(512)S(1)} %rsqrt.13, f32[432]{0:T(512)S(1)} %div.33), kind=kOutput, calls=%fused_computation.22 | convolution fusion | flops 1814593536 | bytes 7740800 | tf_op jit(solution)/shard_map/dot_general | solution.py:190
  49.7 6.4 %reshape_reshape.3 = bf16[2,6,3,12,2,16,64]{6,5,4,3,2,1,0:T(8,128)(2,1)} reshape(bf16[432,2048]{1,0:T(8,128)(2,1)} %fusion.15) | data formatting | bytes 3538944 | tf_op jit(solution)/shard_map/reshape;reshape | solution.py:124
  56.1 2.6 copy.43
  58.7 2.6 fusion.59
  61.3 4.0 %copy.58 = bf16[6,72,1,16,64]{1,4,3,0,2:T(8,128)(2,1)} copy(bf16[6,72,1,16,64]{4,3,2,1,0:T(8,128)(2,1)} %get-tuple-element.12) | data formatting | bytes 1769472
  65.4 4.1 %copy.59 = bf16[6,72,1,16,64]{1,4,3,0,2:T(8,128)(2,1)} copy(bf16[6,72,1,16,64]{4,3,2,1,0:T(8,128)(2,1)} %get-tuple-element.13) | data formatting | bytes 1769472
  69.4 3.1 %fusion.25 = f32[6,16,72,72]{2,3,1,0:T(8,128)S(1)} fusion(bf16[6,72,16,64]{3,2,1,0:T(8,128)(2,1)} %bitcast.65, bf16[6,72,1,16,64]{1,4,3,0,2:T(8,128)(2,1)} %copy.59), kind=kOutput, calls=%fused_computation.29 | convolution fusion | flops 63700992 | bytes 3760128 | tf_op jit(solution)/shard_map/wqhd,wkhd->whqk/dot_general | solution.py:136
  72.5 1.8 fusion.62
  74.3 1.9 fusion.34
  76.2 4.0 %copy.49 = bf16[6,72,16,64]{3,2,1,0:T(8,128)(2,1)} copy(bf16[6,72,16,64]{1,3,2,0:T(8,128)(2,1)} %fusion.34) | data formatting | bytes 1769472 | tf_op jit(solution)/shard_map/whqk,wkhd->wqhd/transpose | solution.py:143
  80.2 3.9 %reshape.128 = bf16[2,3,6,12,1024]{4,3,2,1,0:T(8,128)(2,1)} reshape(bf16[6,72,16,64]{3,2,1,0:T(8,128)(2,1)} %copy.49) | data formatting | bytes 1769472 | tf_op jit(solution)/shard_map/reshape | solution.py:145
  86.6 2.3 fusion.43
  88.9 32.9 %shard_map.130 = bf16[8,144,1024]{2,1,0:T(8,128)(2,1)} custom-call(bf16[144,1024]{1,0:T(8,128)(2,1)} %bitcast.73), custom_call_target="tpu_custom_call" | custom-call | tf_op jit(solution)/shard_map/pallas_call | solution.py:43
  121.8 4.3 %copy.51 = f32[8,6,24,1024]{3,2,0,1:T(8,128)} copy(bf16[8,6,24,1024]{3,2,1,0:T(8,128)(2,1)} %bitcast.62) | data formatting | bytes 7077888 | tf_op jit(solution)/shard_map/convert_element_type | solution.py:152
  126.2 10.1 %multiply_convert_fusion = bf16[5,6,192,320]{3,2,1,0:T(8,128)(2,1)S(1)} fusion(bf16[5,6,192,320]{3,2,1,0:T(8,128)(2,1)} %param.18, f32[5,192]{1,0:T(8,128)S(1)} %fusion.52, bf16[5,1024,320]{2,1,0:T(8,128)(2,1)} %all-gather.2.cloned.1.call-done, f32[5,1024]{1,0:T(8,128)S(1)} %copy-done.8, f32[5,1024]{1,0:T(8,128)S(1)} %copy-done.9, f32[6,192,1024]{2,1,0:T(8,128)} %bitcast.66), kind=kOutput, calls=%fused_computation.11 | convolution fusion | flops 3799941120 | bytes 15412992 | tf_op jit(solution)/shard_map/krnd,kdo->krno/dot_general | solution.py:156
  136.3 6.8 %fusion.14 = bf16[1024,5,320]{0,2,1:T(8,128)(2,1)} fusion(bf16[5,6,192,320]{3,2,1,0:T(8,128)(2,1)S(1)} %multiply_convert_fusion, f32[5,1024]{1,0:T(8,128)S(1)} %copy-done.8, f32[5,1024]{1,0:T(8,128)S(1)} %copy-done.9, f32[6,192,1024]{2,1,0:T(8,128)S(1)} %bitcast.67), kind=kOutput, calls=%fused_computation.21 | convolution fusion | flops 3795845120 | bytes 11722752 | tf_op jit(solution)/shard_map/krnd,krno->dko/dot_general | solution.py:162
  143.1 7.2 %multiply_reduce_fusion = bf16[6,192,1024]{2,1,0:T(8,128)(2,1)S(1)} fusion(f32[5,1024]{1,0:T(8,128)S(1)} %copy-done.9, bf16[5,6,192,320]{3,2,1,0:T(8,128)(2,1)S(1)} %multiply_convert_fusion, bf16[5,1024,320]{2,1,0:T(8,128)(2,1)S(1)} %copy-done.7), kind=kOutput, calls=%fused_computation.1 | convolution fusion | flops 3785490432 | bytes 9342976 | tf_op jit(solution)/shard_map/krno,kdo->krnd/dot_general | solution.py:160
  150.3 1.7 copy.52
  152.0 32.0 %shard_map.131 = bf16[144,1024]{1,0:T(8,128)(2,1)} custom-call(bf16[8,144,1024]{2,1,0:T(8,128)(2,1)} %bitcast.63), custom_call_target="tpu_custom_call" | custom-call | tf_op jit(solution)/shard_map/pallas_call | solution.py:78
  184.0 8.2 %copy.53 = bf16[1024,5,320]{2,1,0:T(8,128)(2,1)} copy(bf16[1024,5,320]{0,2,1:T(8,128)(2,1)} %fusion.14) | data formatting | bytes 6553600 | tf_op jit(solution)/shard_map/convert_element_type | solution.py:245
  192.1 8.9 %reshape.133.x_ref = bf16[16,320,320]{2,1,0:T(8,128)(2,1)} reshape(bf16[1024,5,320]{2,1,0:T(8,128)(2,1)} %copy.53) | data formatting | bytes 6553600 | tf_op jit(solution)/shard_map/reshape | solution.py:245
  201.0 91.3 %shard_map.132 = f32[320,320]{1,0:T(8,128)} custom-call(bf16[16,320,320]{2,1,0:T(8,128)(2,1)} %reshape.133.x_ref), custom_call_target="tpu_custom_call" | custom-call | tf_op jit(solution)/shard_map/pallas_call | solution.py:78
  (51 shorter events, 14.7 us)
Async XLA Ops:
  7.2 79.4 %copy-start = (bf16[1024,1024]{1,0:T(8,128)(2,1)S(1)}, bf16[1024,1024]{1,0:T(8,128)(2,1)}, u32[]{:S(2)}) copy-start(bf16[1024,1024]{1,0:T(8,128)(2,1)} %param.14) | copy-start | bytes 6291460
  7.2 119.0 %all-gather.2.cloned.1.call-start = ((), (), s32[]{:S(2)}) async-start(), calls=%async_computation | async-start | bytes 4177920 | tf_op jit(solution)/shard_map/all_gather | solution.py:216
  8.9 10.5 %collective-permute-start.1 = (bf16[3,24,1024]{2,1,0:T(8,128)(2,1)S(1)}, bf16[3,24,1024]{2,1,0:T(8,128)(2,1)S(1)}, u32[]{:S(2)}, u32[]{:S(2)}) collective-permute-start(bf16[3,24,1024]{2,1,0:T(8,128)(2,1)S(1)} %get-tuple-element.18), channel_id=1, source_target_pairs={{8,0},{16,8},{24,16},{32,24},{40,32},{48,40},{56,48},{64,56},{72,6... | collective-permute-start | bytes 442376 | tf_op jit(solution)/shard_map/ppermute | solution.py:104
  11.3 7.1 %collective-permute-start = (bf16[3,24,1024]{2,1,0:T(8,128)(2,1)S(1)}, bf16[3,24,1024]{2,1,0:T(8,128)(2,1)S(1)}, u32[]{:S(2)}, u32[]{:S(2)}) collective-permute-start(bf16[3,24,1024]{2,1,0:T(8,128)(2,1)S(1)} %get-tuple-element.19), channel_id=1, source_target_pairs={{0,8},{8,16},{16,24},{24,32},{32,40},{40,48},{48,56},{56,64},{64,7... | collective-permute-start | bytes 442376 | tf_op jit(solution)/shard_map/ppermute | solution.py:103
  19.5 6.1 %collective-permute-start.2 = (bf16[12,6,1024]{2,1,0:T(8,128)(2,1)S(1)}, bf16[12,6,1024]{2,1,0:T(8,128)(2,1)S(1)}, u32[]{:S(2)}, u32[]{:S(2)}) collective-permute-start(bf16[12,6,1024]{2,1,0:T(8,128)(2,1)S(1)} %get-tuple-element.16), channel_id=1, source_target_pairs={{0,1},{1,2},{2,3},{3,4},{4,5},{5,6},{6,7},{7,0},{8,9},{9,10},{10,1... | collective-permute-start | bytes 442376 | tf_op jit(solution)/shard_map/ppermute | solution.py:103
  23.0 5.5 %collective-permute-start.3 = (bf16[12,6,1024]{2,1,0:T(8,128)(2,1)S(1)}, bf16[12,6,1024]{2,1,0:T(8,128)(2,1)S(1)}, u32[]{:S(2)}, u32[]{:S(2)}) collective-permute-start(bf16[12,6,1024]{2,1,0:T(8,128)(2,1)S(1)} %get-tuple-element.17), channel_id=1, source_target_pairs={{1,0},{2,1},{3,2},{4,3},{5,4},{6,5},{7,6},{0,7},{9,8},{10,9},{11,1... | collective-permute-start | bytes 442376 | tf_op jit(solution)/shard_map/ppermute | solution.py:104
  30.9 4.4 %copy-start.6 = (f32[1024]{0:T(1024)S(1)}, f32[1024]{0:T(1024)}, u32[]{:S(2)}) copy-start(f32[1024]{0:T(1024)} %param.12) | copy-start | bytes 12292
  40.9 3.3 %copy-start.3 = (f32[432,1024]{1,0:T(8,128)S(1)}, f32[432,1024]{1,0:T(8,128)}, u32[]{:S(2)}) copy-start(f32[432,1024]{1,0:T(8,128)} %reshape.135) | copy-start | bytes 5308420
  72.5 1.8 copy-start.4
  121.8 4.4 %copy-start.8 = (f32[5,1024]{1,0:T(8,128)S(1)}, f32[5,1024]{1,0:T(8,128)}, u32[]{:S(2)}) copy-start(f32[5,1024]{1,0:T(8,128)} %param.16) | copy-start | bytes 61444
  121.8 4.3 %copy-start.9 = (f32[5,1024]{1,0:T(8,128)S(1)}, f32[5,1024]{1,0:T(8,128)}, u32[]{:S(2)}) copy-start(f32[5,1024]{1,0:T(8,128)} %param.15) | copy-start | bytes 61444
  126.1 10.1 %copy-start.2 = (f32[8,6,24,1024]{3,2,0,1:T(8,128)S(1)}, f32[8,6,24,1024]{3,2,0,1:T(8,128)}, u32[]{:S(2)}) copy-start(f32[8,6,24,1024]{3,2,0,1:T(8,128)} %copy.51) | copy-start | bytes 14155780
  136.3 6.8 %copy-start.7 = (bf16[5,1024,320]{2,1,0:T(8,128)(2,1)S(1)}, bf16[5,1024,320]{2,1,0:T(8,128)(2,1)}, u32[]{:S(2)}) copy-start(bf16[5,1024,320]{2,1,0:T(8,128)(2,1)} %all-gather.2.cloned.1.call-done) | copy-start | bytes 9830404
  192.1 102.9 %copy-start.1 = (bf16[1024,1024]{1,0:T(8,128)(2,1)S(1)}, bf16[1024,1024]{1,0:T(8,128)(2,1)}, u32[]{:S(2)}) copy-start(bf16[1024,1024]{1,0:T(8,128)(2,1)} %param.14) | copy-start | bytes 6291460
  201.0 93.3 %copy-start.5 = (bf16[144,1024]{1,0:T(8,128)(2,1)S(1)}, bf16[144,1024]{1,0:T(8,128)(2,1)}, u32[]{:S(2)}) copy-start(bf16[144,1024]{1,0:T(8,128)(2,1)} %shard_map.131) | copy-start | bytes 884740
Sparse Core Ops, SparseCore 0:
  10.2 50.7 all-gather.1

commit v3 on v2

--- a/solution.py
+++ b/solution.py
@@ -241,10 +241,10 @@
     ).reshape(band_rows, band_cols, width)
     head_terms = head_terms * (1.0 / math.sqrt(lat_count * band_rows * var_count * band_cols))
     share_rows = width // lat_count
-    slots, outs = head_terms.shape[1], head_terms.shape[2]
-    head_parts = head_terms.astype(jnp.bfloat16).reshape(lat_count, share_rows * slots, outs)
-    mine = peer_reduce_scatter(head_parts, "lat", lat_count, 3, jnp.float32)
-    grad_head = jnp.transpose(mine.reshape(share_rows, slots, outs), (1, 0, 2))
+    mine = lax.psum_scatter(
+        head_terms.astype(jnp.bfloat16), "lat", scatter_dimension=0, tiled=True
+    ).astype(jnp.float32)
+    grad_head = jnp.transpose(mine, (1, 0, 2))
     return (latent, grad_latent, grad_head)
 
 

time: 303 us -> 247 us (0.82)
  the two profiles are of different devices: /device:TPU:29 before, /device:TPU:0 now
where the time goes in v3:
time: 247 us; the launch traced here: 246 us
  Pallas kernels  65 us (26%)
  local copies, waits for them, and re-layouts  59.8 us (24%)
  waiting for transfers between devices  47.3 us (19%)
  matrix products  42.2 us (17%)
  between operations  14.3 us (6%)
  starting transfers between devices  8.88 us (4%)
  other arithmetic  8.82 us (4%)
    reduce_scatter x1, waiting for transfers between devices, local(): lax.psum_scatter(head_terms.astype(jnp.bfloat16), 'lat', scatter_dimensio...  42.4 us
    pallas_call x1, Pallas kernels, peer_gather(): pl.pallas_call(kernel, out_shape=jax.ShapeDtypeStruct((n,) + block.shape,...  33.2 us
    pallas_call x1, Pallas kernels, peer_reduce_scatter(): pl.pallas_call(kernel, out_shape=jax.ShapeDtypeStruct(parts.shape[1:], ou...  31.8 us
    unnamed x24, local copies, waits for them, and re-layouts  13.8 us
    dot_general x1, matrix products, slot_terms(): jnp.einsum('krnd,kdo->krno', rows, heads_full, preferred_element_type=jnp...  10.1 us
    dot_general x1, matrix products, slot_terms(): jnp.einsum('krno,kdo->krnd', errors, heads_full, preferred_element_type=j...  9.86 us
    another operation x2, local copies, waits for them, and re-layouts, split(): shaped = values.reshape(win_rows, WH, win_cols, WW, parts, heads, head_size)  9.06 us
    convert_element_type x1, local copies, waits for them, and re-layouts, local(): head_terms.astype(jnp.bfloat16)  8.16 us
  transfers between devices with their start and end apart: 6, of which 3 were waited for; matrix products, arithmetic and copies ran while one was open for 33% of the time, Pallas kernels for 26%

profile of v3, /device:TPU:0, one launch (start us, length us, event | category | flops | bytes accessed | tf_op | source)
XLA Modules:
  0.0 246.3 jit_solution(16435181875823251297)
XLA Ops:
  10.3 4.6 %collective-permute-start = (bf16[3,24,1024]{2,1,0:T(8,128)(2,1)S(1)}, bf16[3,24,1024]{2,1,0:T(8,128)(2,1)S(1)}, u32[]{:S(2)}, u32[]{:S(2)}) collective-permute-start(bf16[3,24,1024]{2,1,0:T(8,128)(2,1)S(1)} %get-tuple-element.25), channel_id=1, source_target_pairs={{0,8},{8,16},{16,24},{24,32},{32,40},{40,48},{48,56},{56,64},{64,7... | collective-permute-start | bytes 442376 | tf_op jit(solution)/shard_map/ppermute | solution.py:103
  15.8 1.8 collective-permute-done
  18.7 2.9 %collective-permute-start.3 = (bf16[12,6,1024]{2,1,0:T(8,128)(2,1)S(1)}, bf16[12,6,1024]{2,1,0:T(8,128)(2,1)S(1)}, u32[]{:S(2)}, u32[]{:S(2)}) collective-permute-start(bf16[12,6,1024]{2,1,0:T(8,128)(2,1)S(1)} %get-tuple-element.23), channel_id=1, source_target_pairs={{1,0},{2,1},{3,2},{4,3},{5,4},{6,5},{7,6},{0,7},{9,8},{10,9},{11,1... | collective-permute-start | bytes 442376 | tf_op jit(solution)/shard_map/ppermute | solution.py:104
  22.5 2.5 collective-permute-done.2
  25.5 1.8 multiply_reduce_fusion.1
  29.1 2.7 %reshape.127 = f32[432,1024]{1,0:T(8,128)} reshape(f32[12,36,1024]{2,1,0:T(8,128)} %maximum_convert_fusion) | data formatting | bytes 3538944 | tf_op jit(solution)/shard_map/convert_element_type | solution.py:110
  33.1 2.1 fusion.40
  35.4 2.1 reshape.121
  37.5 3.2 %copy.54 = bf16[2,3,6,12,1,16,64]{6,5,3,2,1,0,4:T(8,128)(2,1)} copy(bf16[2,3,6,12,1,16,64]{6,5,3,1,2,0,4:T(8,128)(2,1)} %bitcast.65) | data formatting | bytes 1769472 | tf_op jit(solution)/shard_map/transpose | solution.py:125
  40.7 5.5 %fusion.15 = bf16[432,2048]{1,0:T(8,128)(2,1)} fusion(bf16[1024,3072]{1,0:T(8,128)(2,1)} %param.13, f32[432,1024]{1,0:T(8,128)S(1)} %copy-done.3, f32[1024]{0:T(1024)S(1)} %copy-done.5, f32[432]{0:T(512)S(1)} %rsqrt.13, f32[432]{0:T(512)S(1)} %div.33), kind=kOutput, calls=%fused_computation.22 | convolution fusion | flops 1814593536 | bytes 7740800 | tf_op jit(solution)/shard_map/dot_general | solution.py:190
  46.2 6.4 %reshape_reshape.3 = bf16[2,6,3,12,2,16,64]{6,5,4,3,2,1,0:T(8,128)(2,1)} reshape(bf16[432,2048]{1,0:T(8,128)(2,1)} %fusion.15) | data formatting | bytes 3538944 | tf_op jit(solution)/shard_map/reshape;reshape | solution.py:124
  52.6 2.7 %copy.52 = bf16[2,6,3,12,2,16,64]{6,5,4,3,1,2,0:T(8,128)(2,1)S(1)} copy(bf16[2,6,3,12,2,16,64]{6,5,4,3,2,1,0:T(8,128)(2,1)} %reshape_reshape.3) | data formatting | bytes 3538944 | tf_op jit(solution)/shard_map/reshape;reshape | solution.py:124
  55.3 2.7 %fusion.59 = (bf16[6,72,1,16,64]{4,3,2,1,0:T(8,128)(2,1)}, bf16[6,72,1,16,64]{4,3,2,1,0:T(8,128)(2,1)}) fusion(bf16[6,72,2,16,64]{4,3,2,1,0:T(8,128)(2,1)S(1)} %bitcast.62), kind=kLoop, calls=%fused_computation.74 | loop fusion | bytes 3538944 | tf_op jit(solution)/shard_map/slice | solution.py:132
  58.0 4.1 %copy.67 = bf16[6,72,1,16,64]{1,4,3,0,2:T(8,128)(2,1)} copy(bf16[6,72,1,16,64]{4,3,2,1,0:T(8,128)(2,1)} %get-tuple-element.18) | data formatting | bytes 1769472
  62.0 4.1 %copy.68 = bf16[6,72,1,16,64]{1,4,3,0,2:T(8,128)(2,1)} copy(bf16[6,72,1,16,64]{4,3,2,1,0:T(8,128)(2,1)} %get-tuple-element.19) | data formatting | bytes 1769472
  66.1 3.1 %fusion.25 = f32[6,16,72,72]{2,3,1,0:T(8,128)S(1)} fusion(bf16[6,72,16,64]{3,2,1,0:T(8,128)(2,1)} %bitcast.66, bf16[6,72,1,16,64]{1,4,3,0,2:T(8,128)(2,1)} %copy.68), kind=kOutput, calls=%fused_computation.29 | convolution fusion | flops 63700992 | bytes 3760128 | tf_op jit(solution)/shard_map/wqhd,wkhd->whqk/dot_general | solution.py:136
  69.2 1.8 fusion.62
  71.0 1.9 fusion.34
  72.9 4.0 %copy.58 = bf16[6,72,16,64]{3,2,1,0:T(8,128)(2,1)} copy(bf16[6,72,16,64]{1,3,2,0:T(8,128)(2,1)} %fusion.34) | data formatting | bytes 1769472 | tf_op jit(solution)/shard_map/whqk,wkhd->wqhd/transpose | solution.py:143
  76.9 3.9 %reshape.122 = bf16[2,3,6,12,1024]{4,3,2,1,0:T(8,128)(2,1)} reshape(bf16[6,72,16,64]{3,2,1,0:T(8,128)(2,1)} %copy.58) | data formatting | bytes 1769472 | tf_op jit(solution)/shard_map/reshape | solution.py:145
  83.3 2.3 fusion.43
  85.5 33.2 %shard_map.130 = bf16[8,144,1024]{2,1,0:T(8,128)(2,1)} custom-call(bf16[144,1024]{1,0:T(8,128)(2,1)} %bitcast.73), custom_call_target="tpu_custom_call" | custom-call | tf_op jit(solution)/shard_map/pallas_call | solution.py:43
  118.8 4.3 %copy.60 = f32[8,6,24,1024]{3,2,0,1:T(8,128)} copy(bf16[8,6,24,1024]{3,2,1,0:T(8,128)(2,1)} %bitcast.63) | data formatting | bytes 7077888 | tf_op jit(solution)/shard_map/convert_element_type | solution.py:152
  123.2 10.1 %multiply_convert_fusion = bf16[5,6,192,320]{3,2,1,0:T(8,128)(2,1)S(1)} fusion(bf16[5,6,192,320]{3,2,1,0:T(8,128)(2,1)} %param.18, f32[5,192]{1,0:T(8,128)S(1)} %fusion.52, bf16[5,1024,320]{2,1,0:T(8,128)(2,1)} %all-gather.2.cloned.1.call-done, f32[5,1024]{1,0:T(8,128)S(1)} %copy-done.6, f32[5,1024]{1,0:T(8,128)S(1)} %copy-done.7, f32[6,192,1024]{2,1,0:T(8,128)} %bitcast.67), kind=kOutput, calls=%fused_computation.11 | convolution fusion | flops 3799941120 | bytes 15412992 | tf_op jit(solution)/shard_map/krnd,kdo->krno/dot_general | solution.py:156
  133.3 2.1 copy-done.8
  135.4 6.5 %fusion.14 = bf16[1024,5,320]{0,2,1:T(8,128)(2,1)} fusion(bf16[5,6,192,320]{3,2,1,0:T(8,128)(2,1)S(1)} %multiply_convert_fusion, f32[5,1024]{1,0:T(8,128)S(1)} %copy-done.6, f32[5,1024]{1,0:T(8,128)S(1)} %copy-done.7, f32[6,192,1024]{2,1,0:T(8,128)S(1)} %bitcast.68), kind=kOutput, calls=%fused_computation.21 | convolution fusion | flops 3795845120 | bytes 11722752 | tf_op jit(solution)/shard_map/krnd,krno->dko/dot_general | solution.py:162
  141.9 8.2 %copy.62 = bf16[1024,5,320]{2,1,0:T(8,128)(2,1)} copy(bf16[1024,5,320]{0,2,1:T(8,128)(2,1)} %fusion.14) | data formatting | bytes 6553600 | tf_op jit(solution)/shard_map/convert_element_type | solution.py:245
  150.1 9.9 %multiply_reduce_fusion = bf16[6,192,1024]{2,1,0:T(8,128)(2,1)S(1)} fusion(f32[5,1024]{1,0:T(8,128)S(1)} %copy-done.7, bf16[5,6,192,320]{3,2,1,0:T(8,128)(2,1)} %copy-done.8, bf16[5,1024,320]{2,1,0:T(8,128)(2,1)} %all-gather.2.cloned.1.call-done), kind=kOutput, calls=%fused_computation.1 | convolution fusion | flops 3785490432 | bytes 9342976 | tf_op jit(solution)/shard_map/krno,kdo->krnd/dot_general | solution.py:160
  160.0 1.7 copy.61
  161.7 31.8 %shard_map.131 = bf16[144,1024]{1,0:T(8,128)(2,1)} custom-call(bf16[8,144,1024]{2,1,0:T(8,128)(2,1)} %bitcast.64), custom_call_target="tpu_custom_call" | custom-call | tf_op jit(solution)/shard_map/pallas_call | solution.py:78
  193.4 42.4 %reduce-scatter.2.cloned.1.call-done = bf16[64,5,320]{2,1,0:T(8,128)(2,1)} async-done(((bf16[1024,5,320]{2,1,0:T(8,128)(2,1)}), bf16[64,5,320]{2,1,0:T(8,128)(2,1)}) %reduce-scatter.2.cloned.1.call-update) | async-done | bytes 204816 | tf_op jit(solution)/shard_map/reduce_scatter | solution.py:244
  237.7 1.7 copy.74
  (50 shorter events, 14.1 us)
Async XLA Ops:
  7.2 76.1 %copy-start = (bf16[1024,1024]{1,0:T(8,128)(2,1)S(1)}, bf16[1024,1024]{1,0:T(8,128)(2,1)}, u32[]{:S(2)}) copy-start(bf16[1024,1024]{1,0:T(8,128)(2,1)} %param.14) | copy-start | bytes 6291460
  7.2 116.0 %all-gather.2.cloned.1.call-start = ((), (), s32[]{:S(2)}) async-start(), calls=%async_computation.1 | async-start | bytes 4177920 | tf_op jit(solution)/shard_map/all_gather | solution.py:216
  7.9 227.9 %reduce-scatter.2.cloned.1.call-start = ((), (), s32[]{:S(2)}) async-start(), calls=%async_computation.2 | async-start | bytes 6684672 | tf_op jit(solution)/shard_map/reduce_scatter | solution.py:244
  9.0 9.6 %collective-permute-start.1 = (bf16[3,24,1024]{2,1,0:T(8,128)(2,1)S(1)}, bf16[3,24,1024]{2,1,0:T(8,128)(2,1)S(1)}, u32[]{:S(2)}, u32[]{:S(2)}) collective-permute-start(bf16[3,24,1024]{2,1,0:T(8,128)(2,1)S(1)} %get-tuple-element.24), channel_id=1, source_target_pairs={{8,0},{16,8},{24,16},{32,24},{40,32},{48,40},{56,48},{64,56},{72,6... | collective-permute-start | bytes 442376 | tf_op jit(solution)/shard_map/ppermute | solution.py:104
  10.3 7.3 %collective-permute-start = (bf16[3,24,1024]{2,1,0:T(8,128)(2,1)S(1)}, bf16[3,24,1024]{2,1,0:T(8,128)(2,1)S(1)}, u32[]{:S(2)}, u32[]{:S(2)}) collective-permute-start(bf16[3,24,1024]{2,1,0:T(8,128)(2,1)S(1)} %get-tuple-element.25), channel_id=1, source_target_pairs={{0,8},{8,16},{16,24},{24,32},{32,40},{40,48},{48,56},{56,64},{64,7... | collective-permute-start | bytes 442376 | tf_op jit(solution)/shard_map/ppermute | solution.py:103
  18.7 6.3 %collective-permute-start.2 = (bf16[12,6,1024]{2,1,0:T(8,128)(2,1)S(1)}, bf16[12,6,1024]{2,1,0:T(8,128)(2,1)S(1)}, u32[]{:S(2)}, u32[]{:S(2)}) collective-permute-start(bf16[12,6,1024]{2,1,0:T(8,128)(2,1)S(1)} %get-tuple-element.22), channel_id=1, source_target_pairs={{0,1},{1,2},{2,3},{3,4},{4,5},{5,6},{6,7},{7,0},{8,9},{9,10},{10,1... | collective-permute-start | bytes 442376 | tf_op jit(solution)/shard_map/ppermute | solution.py:103
  18.7 6.3 %collective-permute-start.3 = (bf16[12,6,1024]{2,1,0:T(8,128)(2,1)S(1)}, bf16[12,6,1024]{2,1,0:T(8,128)(2,1)S(1)}, u32[]{:S(2)}, u32[]{:S(2)}) collective-permute-start(bf16[12,6,1024]{2,1,0:T(8,128)(2,1)S(1)} %get-tuple-element.23), channel_id=1, source_target_pairs={{1,0},{2,1},{3,2},{4,3},{5,4},{6,5},{7,6},{0,7},{9,8},{10,9},{11,1... | collective-permute-start | bytes 442376 | tf_op jit(solution)/shard_map/ppermute | solution.py:104
  27.3 4.5 %copy-start.5 = (f32[1024]{0:T(1024)S(1)}, f32[1024]{0:T(1024)}, u32[]{:S(2)}) copy-start(f32[1024]{0:T(1024)} %param.12) | copy-start | bytes 12292
  37.5 3.2 %copy-start.3 = (f32[432,1024]{1,0:T(8,128)S(1)}, f32[432,1024]{1,0:T(8,128)}, u32[]{:S(2)}) copy-start(f32[432,1024]{1,0:T(8,128)} %reshape.127) | copy-start | bytes 5308420
  69.2 1.8 copy-start.4
  118.8 4.4 %copy-start.6 = (f32[5,1024]{1,0:T(8,128)S(1)}, f32[5,1024]{1,0:T(8,128)}, u32[]{:S(2)}) copy-start(f32[5,1024]{1,0:T(8,128)} %param.16) | copy-start | bytes 61444
  118.8 4.3 %copy-start.7 = (f32[5,1024]{1,0:T(8,128)S(1)}, f32[5,1024]{1,0:T(8,128)}, u32[]{:S(2)}) copy-start(f32[5,1024]{1,0:T(8,128)} %param.15) | copy-start | bytes 61444
  123.1 12.2 %copy-start.2 = (f32[8,6,24,1024]{3,2,0,1:T(8,128)S(1)}, f32[8,6,24,1024]{3,2,0,1:T(8,128)}, u32[]{:S(2)}) copy-start(f32[8,6,24,1024]{3,2,0,1:T(8,128)} %copy.60) | copy-start | bytes 14155780
  133.3 2.1 copy-start.8
  160.0 79.4 %copy-start.1 = (bf16[1024,1024]{1,0:T(8,128)(2,1)S(1)}, bf16[1024,1024]{1,0:T(8,128)(2,1)}, u32[]{:S(2)}) copy-start(bf16[1024,1024]{1,0:T(8,128)(2,1)} %param.14) | copy-start | bytes 6291460
Sparse Core Ops, SparseCore 0:
  10.2 52.8 all-gather.1
  150.2 85.5 reduce-scatter.1

commit v4 on v3

--- a/solution.py
+++ b/solution.py
@@ -5,9 +5,10 @@
 from jax import lax
 from jax.experimental import pallas as pl
 from jax.experimental.pallas import tpu as pltpu
-from jax.sharding import PartitionSpec as P
+from jax.sharding import Mesh, PartitionSpec as P
 
 MESH_ID = pl.DeviceIdType.MESH
+LAT = ("lat_hi", "lat_lo")
 
 
 def _greet(axis, n, me):
@@ -179,12 +180,12 @@
     band_rows, band_cols, width = patches.shape
     half_rows = WH // 2
     half_cols = WW // 2
-    lat_count = lax.axis_size("lat")
+    lat_count = lax.axis_size(LAT)
     var_count = lax.axis_size("var")
-    lat_place = lax.axis_index("lat")
+    lat_place = lax.axis_index(LAT)
     ext_rows = band_rows + WH
     ext_cols = band_cols + WW
-    extended = padded(patches, (("lat", 0),), half_rows, False)
+    extended = padded(patches, ((LAT, 0),), half_rows, False)
     extended = padded(extended, (("var", 1),), half_cols, True)
     normed_ext = layer_norm(extended, norm_gain)
     keyval = jnp.dot(
@@ -213,7 +214,7 @@
         jnp.where(dataset_row[:, None] == dataset_ids[None, :], level_counts[None, :], 0), axis=1
     )
     live_tiles = (slot_level[None, :] < tile_levels[:, None]).astype(jnp.float32)
-    heads_full = lax.all_gather(head_weight, "lat", axis=1, tiled=True)
+    heads_full = lax.all_gather(head_weight, LAT, axis=1, tiled=True)
     tile_ids = jnp.arange(var_count, dtype=jnp.int32)
     tiles = peer_gather(latent.reshape(band_rows * band_cols, width), "var", var_count, 1)
     piece = (
@@ -241,26 +242,39 @@
     ).reshape(band_rows, band_cols, width)
     head_terms = head_terms * (1.0 / math.sqrt(lat_count * band_rows * var_count * band_cols))
     share_rows = width // lat_count
-    mine = lax.psum_scatter(
-        head_terms.astype(jnp.bfloat16), "lat", scatter_dimension=0, tiled=True
-    ).astype(jnp.float32)
+    outer, inner = lax.axis_size(LAT[0]), lax.axis_size(LAT[1])
+    slots, outs = head_terms.shape[1], head_terms.shape[2]
+    head_grid = (
+        head_terms.astype(jnp.bfloat16)
+        .reshape(outer, inner, share_rows * slots, outs)
+        .transpose(1, 0, 2, 3)
+        .reshape(inner * outer * share_rows * slots, outs)
+    )
+    head_grid = lax.psum_scatter(head_grid, LAT[1], scatter_dimension=0, tiled=True)
+    head_grid = lax.psum_scatter(head_grid, LAT[0], scatter_dimension=0, tiled=True)
+    mine = head_grid.reshape(share_rows, slots, outs).astype(jnp.float32)
     grad_head = jnp.transpose(mine, (1, 0, 2))
     return (latent, grad_latent, grad_head)
 
 
 def solution(mesh):
     in_specs = (
-        P("lat", "var", None),
+        P(LAT, "var", None),
         P(),
         P(),
         P(),
         P("var", None),
         P("var", None),
-        P("var", "lat", None),
-        P("var", "lat", None, None),
-        P(),
-        P("lat", None),
+        P("var", LAT, None),
+        P("var", LAT, None, None),
+        P(),
+        P(LAT, None),
         P("var"),
     )
-    out_specs = (P("lat", "var", None), P("lat", "var", None), P("var", "lat", None))
-    return jax.shard_map(local, mesh=mesh, in_specs=in_specs, out_specs=out_specs, check_vma=False)
+    out_specs = (P(LAT, "var", None), P(LAT, "var", None), P("var", LAT, None))
+    lat_size = mesh.shape["lat"]
+    inner = 4 if lat_size % 4 == 0 else 1
+    grid = Mesh(
+        mesh.devices.reshape(lat_size // inner, inner, mesh.shape["var"]), LAT + ("var",)
+    )
+    return jax.shard_map(local, mesh=grid, in_specs=in_specs, out_specs=out_specs, check_vma=False)

time: 247 us -> 280 us (1.13); the launches traced: 246 us -> 275 us
  local copies, waits for them, and re-layouts: 59.8 us -> 88.9 us
    reshape x0 -> x2, local copies, waits for them, and re-layouts: none -> 17 us  [local(): head_grid = head_terms.astype(jnp.bfloat16).reshape(outer, inner, share_r...]
    transpose x0 -> x3, local copies, waits for them, and re-layouts: none -> 8.81 us  [the longest x1 8.58 us: local(): head_grid = head_terms.astype(jnp.bfloat16).reshape(outer, inner, share_r...]
    unnamed x24 -> x26, local copies, waits for them, and re-layouts: 13.8 us -> 17.2 us
  transfers between devices with their start and end apart: 6 -> 7, of which waited for: 3 -> 3; matrix products, arithmetic and copies ran while one was open for 33% -> 29% of each run, Pallas kernels for 26% -> 24%
where the time goes in v4:
time: 280 us; the launch traced here: 275 us
  local copies, waits for them, and re-layouts  88.9 us (32%)
  Pallas kernels  64.7 us (23%)
  waiting for transfers between devices  48.8 us (17%)
  matrix products  42.2 us (15%)
  between operations  14 us (5%)
  starting transfers between devices  8.93 us (3%)
  other arithmetic  7.77 us (3%)
    reduce_scatter x1, waiting for transfers between devices, local(): lax.psum_scatter(head_grid, LAT[1], scatter_dimension=0, tiled=True)  43.8 us
    pallas_call x1, Pallas kernels, peer_gather(): pl.pallas_call(kernel, out_shape=jax.ShapeDtypeStruct((n,) + block.shape,...  33.2 us
    pallas_call x1, Pallas kernels, peer_reduce_scatter(): pl.pallas_call(kernel, out_shape=jax.ShapeDtypeStruct(parts.shape[1:], ou...  31.5 us
    unnamed x26, local copies, waits for them, and re-layouts  17.2 us
    reshape x2, local copies, waits for them, and re-layouts, local(): head_grid = head_terms.astype(jnp.bfloat16).reshape(outer, inner, share_r...  17 us
    dot_general x1, matrix products, slot_terms(): jnp.einsum('krnd,kdo->krno', rows, heads_full, preferred_element_type=jnp...  10.1 us
    dot_general x1, matrix products, slot_terms(): jnp.einsum('krno,kdo->krnd', errors, heads_full, preferred_element_type=j...  9.86 us
    another operation x2, local copies, waits for them, and re-layouts, split(): shaped = values.reshape(win_rows, WH, win_cols, WW, parts, heads, head_size)  9.06 us
  transfers between devices with their start and end apart: 7, of which 3 were waited for; matrix products, arithmetic and copies ran while one was open for 29% of the time, Pallas kernels for 24%

profile of v4, /device:TPU:0, one launch (start us, length us, event | category | flops | bytes accessed | tf_op | source)
XLA Modules:
  0.0 275.3 jit_solution(8401713344185954222)
XLA Ops:
  10.3 4.6 %collective-permute-start = (bf16[3,24,1024]{2,1,0:T(8,128)(2,1)S(1)}, bf16[3,24,1024]{2,1,0:T(8,128)(2,1)S(1)}, u32[]{:S(2)}, u32[]{:S(2)}) collective-permute-start(bf16[3,24,1024]{2,1,0:T(8,128)(2,1)S(1)} %get-tuple-element.22), channel_id=1, source_target_pairs={{0,8},{8,16},{16,24},{24,32},{32,40},{40,48},{48,56},{56,64},{64,7... | collective-permute-start | bytes 442376 | tf_op jit(solution)/shard_map/ppermute | solution.py:104
  18.7 2.9 %collective-permute-start.3 = (bf16[12,6,1024]{2,1,0:T(8,128)(2,1)S(1)}, bf16[12,6,1024]{2,1,0:T(8,128)(2,1)S(1)}, u32[]{:S(2)}, u32[]{:S(2)}) collective-permute-start(bf16[12,6,1024]{2,1,0:T(8,128)(2,1)S(1)} %get-tuple-element.20), channel_id=1, source_target_pairs={{1,0},{2,1},{3,2},{4,3},{5,4},{6,5},{7,6},{0,7},{9,8},{10,9},{11,1... | collective-permute-start | bytes 442376 | tf_op jit(solution)/shard_map/ppermute | solution.py:105
  22.5 2.5 collective-permute-done.2
  25.5 1.8 multiply_reduce_fusion.1
  29.1 2.7 reshape.138
  33.1 2.1 fusion.40
  35.4 2.1 reshape.130
  37.5 3.2 %copy.61 = bf16[2,3,6,12,1,16,64]{6,5,3,2,1,0,4:T(8,128)(2,1)} copy(bf16[2,3,6,12,1,16,64]{6,5,3,1,2,0,4:T(8,128)(2,1)} %bitcast.69) | data formatting | bytes 1769472 | tf_op jit(solution)/shard_map/transpose | solution.py:126
  40.7 5.5 %fusion.15 = bf16[432,2048]{1,0:T(8,128)(2,1)} fusion(bf16[1024,3072]{1,0:T(8,128)(2,1)} %param.13, f32[432,1024]{1,0:T(8,128)S(1)} %copy-done.3, f32[1024]{0:T(1024)S(1)} %copy-done.5, f32[432]{0:T(512)S(1)} %rsqrt.13, f32[432]{0:T(512)S(1)} %div.33), kind=kOutput, calls=%fused_computation.22 | convolution fusion | flops 1814593536 | bytes 7740800 | tf_op jit(solution)/shard_map/dot_general | solution.py:191
  46.2 6.4 %reshape_reshape.3 = bf16[2,6,3,12,2,16,64]{6,5,4,3,2,1,0:T(8,128)(2,1)} reshape(bf16[432,2048]{1,0:T(8,128)(2,1)} %fusion.15) | data formatting | bytes 3538944 | tf_op jit(solution)/shard_map/reshape;reshape | solution.py:125
  52.6 2.7 copy.59
  55.3 2.7 fusion.59
  58.0 4.1 %copy.78 = bf16[6,72,1,16,64]{1,4,3,0,2:T(8,128)(2,1)} copy(bf16[6,72,1,16,64]{4,3,2,1,0:T(8,128)(2,1)} %get-tuple-element.15) | data formatting | bytes 1769472
  62.0 4.1 %copy.79 = bf16[6,72,1,16,64]{1,4,3,0,2:T(8,128)(2,1)} copy(bf16[6,72,1,16,64]{4,3,2,1,0:T(8,128)(2,1)} %get-tuple-element.16) | data formatting | bytes 1769472
  66.1 3.1 %fusion.25 = f32[6,16,72,72]{2,3,1,0:T(8,128)S(1)} fusion(bf16[6,72,16,64]{3,2,1,0:T(8,128)(2,1)} %bitcast.70, bf16[6,72,1,16,64]{1,4,3,0,2:T(8,128)(2,1)} %copy.79), kind=kOutput, calls=%fused_computation.29 | convolution fusion | flops 63700992 | bytes 3760128 | tf_op jit(solution)/shard_map/wqhd,wkhd->whqk/dot_general | solution.py:137
  71.0 1.9 fusion.34
  72.9 4.0 %copy.65 = bf16[6,72,16,64]{3,2,1,0:T(8,128)(2,1)} copy(bf16[6,72,16,64]{1,3,2,0:T(8,128)(2,1)} %fusion.34) | data formatting | bytes 1769472 | tf_op jit(solution)/shard_map/whqk,wkhd->wqhd/transpose | solution.py:144
  76.9 3.9 %reshape.131 = bf16[2,3,6,12,1024]{4,3,2,1,0:T(8,128)(2,1)} reshape(bf16[6,72,16,64]{3,2,1,0:T(8,128)(2,1)} %copy.65) | data formatting | bytes 1769472 | tf_op jit(solution)/shard_map/reshape | solution.py:146
  83.3 2.3 fusion.43
  85.5 33.2 %shard_map.130 = bf16[8,144,1024]{2,1,0:T(8,128)(2,1)} custom-call(bf16[144,1024]{1,0:T(8,128)(2,1)} %bitcast.78), custom_call_target="tpu_custom_call" | custom-call | tf_op jit(solution)/shard_map/pallas_call | solution.py:44
  118.8 4.3 %copy.67 = f32[8,6,24,1024]{3,2,0,1:T(8,128)} copy(bf16[8,6,24,1024]{3,2,1,0:T(8,128)(2,1)} %bitcast.67) | data formatting | bytes 7077888 | tf_op jit(solution)/shard_map/convert_element_type | solution.py:153
  123.2 10.1 %multiply_convert_fusion = bf16[5,6,192,320]{3,2,1,0:T(8,128)(2,1)S(1)} fusion(bf16[5,6,192,320]{3,2,1,0:T(8,128)(2,1)} %param.18, f32[5,192]{1,0:T(8,128)S(1)} %fusion.52, bf16[5,1024,320]{2,1,0:T(8,128)(2,1)} %all-gather.2.cloned.1.call-done, f32[5,1024]{1,0:T(8,128)S(1)} %copy-done.6, f32[5,1024]{1,0:T(8,128)S(1)} %copy-done.7, f32[6,192,1024]{2,1,0:T(8,128)} %bitcast.71), kind=kOutput, calls=%fused_computation.11 | convolution fusion | flops 3799941120 | bytes 15412992 | tf_op jit(solution)/shard_map/krnd,kdo->krno/dot_general | solution.py:157
  133.3 2.1 copy-done.8
  135.4 6.5 %fusion.14 = bf16[1024,5,320]{0,2,1:T(8,128)(2,1)} fusion(bf16[5,6,192,320]{3,2,1,0:T(8,128)(2,1)S(1)} %multiply_convert_fusion, f32[5,1024]{1,0:T(8,128)S(1)} %copy-done.6, f32[5,1024]{1,0:T(8,128)S(1)} %copy-done.7, f32[6,192,1024]{2,1,0:T(8,128)S(1)} %bitcast.72), kind=kOutput, calls=%fused_computation.21 | convolution fusion | flops 3795845120 | bytes 11722752 | tf_op jit(solution)/shard_map/krnd,krno->dko/dot_general | solution.py:163
  141.9 8.2 %copy.69 = bf16[1024,5,320]{2,1,0:T(8,128)(2,1)} copy(bf16[1024,5,320]{0,2,1:T(8,128)(2,1)} %fusion.14) | data formatting | bytes 6553600 | tf_op jit(solution)/shard_map/convert_element_type | solution.py:248
  150.1 8.7 %reshape.136 = bf16[4,4,320,320]{3,2,1,0:T(8,128)(2,1)} reshape(bf16[1024,5,320]{2,1,0:T(8,128)(2,1)} %copy.69) | data formatting | bytes 6553600 | tf_op jit(solution)/shard_map/reshape | solution.py:249
  158.8 8.6 %copy.70 = bf16[4,4,320,320]{2,1,0,3:T(4,128)(2,1)} copy(bf16[4,4,320,320]{3,2,0,1:T(8,128)(2,1)} %bitcast.65) | data formatting | bytes 6553600 | tf_op jit(solution)/shard_map/transpose | solution.py:250
  167.4 8.2 %reshape.137 = bf16[5120,320]{0,1:T(8,128)(2,1)} reshape(bf16[4,4,320,320]{2,1,0,3:T(4,128)(2,1)} %copy.70) | data formatting | bytes 6553600 | tf_op jit(solution)/shard_map/reshape | solution.py:251
  175.7 43.8 %reduce-scatter.5.cloned.1.call-done = bf16[1280,320]{0,1:T(8,128)(2,1)} async-done(((bf16[5120,320]{0,1:T(8,128)(2,1)}), bf16[1280,320]{0,1:T(8,128)(2,1)}) %reduce-scatter.5.cloned.1.call-update) | async-done | bytes 819216 | tf_op jit(solution)/shard_map/reduce_scatter | solution.py:253
  219.5 2.2 copy.76
  221.8 9.9 %multiply_reduce_fusion = bf16[6,192,1024]{2,1,0:T(8,128)(2,1)S(1)} fusion(f32[5,1024]{1,0:T(8,128)S(1)} %copy-done.7, bf16[5,6,192,320]{3,2,1,0:T(8,128)(2,1)} %copy-done.8, bf16[5,1024,320]{2,1,0:T(8,128)(2,1)} %all-gather.2.cloned.1.call-done), kind=kOutput, calls=%fused_computation.1 | convolution fusion | flops 3785490432 | bytes 9342976 | tf_op jit(solution)/shard_map/krno,kdo->krnd/dot_general | solution.py:161
  233.3 31.5 %shard_map.131 = bf16[144,1024]{1,0:T(8,128)(2,1)} custom-call(bf16[8,144,1024]{2,1,0:T(8,128)(2,1)} %bitcast.68), custom_call_target="tpu_custom_call" | custom-call | tf_op jit(solution)/shard_map/pallas_call | solution.py:79
  (59 shorter events, 21.4 us)
Async XLA Ops:
  7.2 76.1 %copy-start = (bf16[1024,1024]{1,0:T(8,128)(2,1)S(1)}, bf16[1024,1024]{1,0:T(8,128)(2,1)}, u32[]{:S(2)}) copy-start(bf16[1024,1024]{1,0:T(8,128)(2,1)} %param.14) | copy-start | bytes 6291460
  7.2 116.0 %all-gather.2.cloned.1.call-start = ((), (), s32[]{:S(2)}) async-start(), calls=%async_computation.2 | async-start | bytes 4177920 | tf_op jit(solution)/shard_map/all_gather | solution.py:217
  7.9 211.6 %reduce-scatter.5.cloned.1.call-start = ((), (), s32[]{:S(2)}) async-start(), calls=%async_computation.3 | async-start | bytes 4096000 | tf_op jit(solution)/shard_map/reduce_scatter | solution.py:253
  9.0 9.6 %collective-permute-start.1 = (bf16[3,24,1024]{2,1,0:T(8,128)(2,1)S(1)}, bf16[3,24,1024]{2,1,0:T(8,128)(2,1)S(1)}, u32[]{:S(2)}, u32[]{:S(2)}) collective-permute-start(bf16[3,24,1024]{2,1,0:T(8,128)(2,1)S(1)} %get-tuple-element.21), channel_id=1, source_target_pairs={{8,0},{16,8},{24,16},{32,24},{40,32},{48,40},{56,48},{64,56},{72,6... | collective-permute-start | bytes 442376 | tf_op jit(solution)/shard_map/ppermute | solution.py:105
  10.3 7.3 %collective-permute-start = (bf16[3,24,1024]{2,1,0:T(8,128)(2,1)S(1)}, bf16[3,24,1024]{2,1,0:T(8,128)(2,1)S(1)}, u32[]{:S(2)}, u32[]{:S(2)}) collective-permute-start(bf16[3,24,1024]{2,1,0:T(8,128)(2,1)S(1)} %get-tuple-element.22), channel_id=1, source_target_pairs={{0,8},{8,16},{16,24},{24,32},{32,40},{40,48},{48,56},{56,64},{64,7... | collective-permute-start | bytes 442376 | tf_op jit(solution)/shard_map/ppermute | solution.py:104
  18.7 6.3 %collective-permute-start.2 = (bf16[12,6,1024]{2,1,0:T(8,128)(2,1)S(1)}, bf16[12,6,1024]{2,1,0:T(8,128)(2,1)S(1)}, u32[]{:S(2)}, u32[]{:S(2)}) collective-permute-start(bf16[12,6,1024]{2,1,0:T(8,128)(2,1)S(1)} %get-tuple-element.19), channel_id=1, source_target_pairs={{0,1},{1,2},{2,3},{3,4},{4,5},{5,6},{6,7},{7,0},{8,9},{9,10},{10,1... | collective-permute-start | bytes 442376 | tf_op jit(solution)/shard_map/ppermute | solution.py:104
  18.7 6.3 %collective-permute-start.3 = (bf16[12,6,1024]{2,1,0:T(8,128)(2,1)S(1)}, bf16[12,6,1024]{2,1,0:T(8,128)(2,1)S(1)}, u32[]{:S(2)}, u32[]{:S(2)}) collective-permute-start(bf16[12,6,1024]{2,1,0:T(8,128)(2,1)S(1)} %get-tuple-element.20), channel_id=1, source_target_pairs={{1,0},{2,1},{3,2},{4,3},{5,4},{6,5},{7,6},{0,7},{9,8},{10,9},{11,1... | collective-permute-start | bytes 442376 | tf_op jit(solution)/shard_map/ppermute | solution.py:105
  27.3 4.5 %copy-start.5 = (f32[1024]{0:T(1024)S(1)}, f32[1024]{0:T(1024)}, u32[]{:S(2)}) copy-start(f32[1024]{0:T(1024)} %param.12) | copy-start | bytes 12292
  37.5 3.2 %copy-start.3 = (f32[432,1024]{1,0:T(8,128)S(1)}, f32[432,1024]{1,0:T(8,128)}, u32[]{:S(2)}) copy-start(f32[432,1024]{1,0:T(8,128)} %reshape.138) | copy-start | bytes 5308420
  69.2 1.8 copy-start.4
  118.8 4.4 %copy-start.6 = (f32[5,1024]{1,0:T(8,128)S(1)}, f32[5,1024]{1,0:T(8,128)}, u32[]{:S(2)}) copy-start(f32[5,1024]{1,0:T(8,128)} %param.16) | copy-start | bytes 61444
  118.8 4.3 %copy-start.7 = (f32[5,1024]{1,0:T(8,128)S(1)}, f32[5,1024]{1,0:T(8,128)}, u32[]{:S(2)}) copy-start(f32[5,1024]{1,0:T(8,128)} %param.15) | copy-start | bytes 61444
  123.1 12.2 %copy-start.2 = (f32[8,6,24,1024]{3,2,0,1:T(8,128)S(1)}, f32[8,6,24,1024]{3,2,0,1:T(8,128)}, u32[]{:S(2)}) copy-start(f32[8,6,24,1024]{3,2,0,1:T(8,128)} %copy.67) | copy-start | bytes 14155780
  133.3 2.1 copy-start.8
  175.6 89.2 %reduce-scatter.7.cloned.1.call-start = ((), (), s32[]{:S(2)}) async-start(), calls=%async_computation.4 | async-start | bytes 1228800
  231.6 37.1 %copy-start.1 = (bf16[1024,1024]{1,0:T(8,128)(2,1)S(1)}, bf16[1024,1024]{1,0:T(8,128)(2,1)}, u32[]{:S(2)}) copy-start(bf16[1024,1024]{1,0:T(8,128)(2,1)} %param.14) | copy-start | bytes 6291460
Sparse Core Ops, SparseCore 0:
  10.2 52.8 all-gather.1
  175.8 43.7 reduce-scatter.4
  222.0 22.8 reduce-scatter.6

commit v5 on v3

--- a/solution.py
+++ b/solution.py
@@ -84,6 +84,33 @@
                         pltpu.SemaphoreType.DMA((n,)), pltpu.SemaphoreType.DMA((n,))],
         compiler_params=pltpu.CompilerParams(collective_id=cid, has_side_effects=True),
     )(parts)
+
+
+def masked_window_attention(queries, keyval, query_win, key_win, heads):
+    nq, width = queries.shape
+    head_size = width // heads
+    scale = 1.0 / float(head_size) ** 0.5
+
+    def kernel(q_ref, kv_ref, qw_ref, kw_ref, out_ref):
+        mask = qw_ref[...] == kw_ref[...]
+        for h in range(heads):
+            cols = slice(h * head_size, (h + 1) * head_size)
+            q = q_ref[:, cols]
+            k = kv_ref[:, h * head_size:(h + 1) * head_size]
+            v = kv_ref[:, width + h * head_size:width + (h + 1) * head_size]
+            s = lax.dot_general(q, k, (((1,), (1,)), ((), ())),
+                                preferred_element_type=jnp.float32) * scale
+            s = jnp.where(mask, s, -jnp.inf)
+            w = jnp.exp(s - jnp.max(s, axis=1, keepdims=True))
+            p = (w / jnp.sum(w, axis=1, keepdims=True)).astype(jnp.bfloat16)
+            out_ref[:, cols] = jnp.dot(p, v, preferred_element_type=jnp.float32).astype(out_ref.dtype)
+
+    return pl.pallas_call(
+        kernel,
+        out_shape=jax.ShapeDtypeStruct((nq, width), jnp.bfloat16),
+        in_specs=[pl.BlockSpec(memory_space=pltpu.VMEM)] * 4,
+        out_specs=pl.BlockSpec(memory_space=pltpu.VMEM),
+    )(queries, keyval, query_win, key_win)
 
 HEADS = 16
 WH = 6
@@ -195,14 +222,23 @@
     queries = jnp.dot(
         normed.reshape(-1, width), input_proj[:, :width], preferred_element_type=jnp.float32
     )
-    queries = queries.astype(jnp.bfloat16).reshape(band_rows, band_cols, width)
-    query_ext = jnp.pad(queries, ((half_rows, WH - half_rows), (half_cols, WW - half_cols), (0, 0)))
+    queries = queries.astype(jnp.bfloat16)
     global_row = lat_place * band_rows - half_rows + jnp.arange(ext_rows, dtype=jnp.int32)
     row_valid = (global_row >= 0) & (global_row < lat_count * band_rows)
-    mixed = window_attention(query_ext, keyval, row_valid, HEADS)
-    attn = mixed[half_rows : half_rows + band_rows, half_cols : half_cols + band_cols].astype(
-        jnp.bfloat16
-    )
+    win_cols = ext_cols // WW
+    ext_r = jnp.arange(ext_rows, dtype=jnp.int32)[:, None]
+    ext_c = jnp.arange(ext_cols, dtype=jnp.int32)[None, :]
+    key_win = jnp.where(row_valid[:, None], (ext_r // WH) * win_cols + ext_c // WW, -1)
+    own_r = ext_r[half_rows : half_rows + band_rows]
+    own_c = ext_c[:, half_cols : half_cols + band_cols]
+    query_win = (own_r // WH) * win_cols + own_c // WW
+    attn = masked_window_attention(
+        queries,
+        keyval.reshape(ext_rows * ext_cols, 2 * width),
+        query_win.reshape(-1, 1),
+        key_win.reshape(1, -1),
+        HEADS,
+    ).reshape(band_rows, band_cols, width)
     update = jnp.dot(
         attn.reshape(-1, width), output_proj, preferred_element_type=jnp.float32
     ).reshape(band_rows, band_cols, width)

time: 247 us -> 214 us (0.87)
  local copies, waits for them, and re-layouts: 59.8 us -> 25.3 us
  Pallas kernels: 65 us -> 73.6 us
  matrix products: 42.2 us -> 37 us
    another operation x2 -> x0, local copies, waits for them, and re-layouts: 9.06 us -> none  [split(): shaped = values.reshape(win_rows, WH, win_cols, WW, parts, heads, head_size)]
    pallas_call x0 -> x1, Pallas kernels: none -> 8.8 us  [masked_window_attention(): pl.pallas_call(kernel, out_shape=jax.ShapeDtypeStruct((nq, width), jnp.bf...]
    transpose x3 -> x0, local copies, waits for them, and re-layouts: 8.62 us -> none  [the longest x1 4.04 us: window_attention(): jnp.einsum('whqk,wkhd->wqhd', probs, value_win, preferred_element_type=jn...]
    unnamed x24 -> x20, local copies, waits for them, and re-layouts: 13.8 us -> 5.7 us
    reshape x3 -> x0, local copies, waits for them, and re-layouts: 7.11 us -> none  [the longest x1 3.93 us: window_attention(): mixed.reshape(win_rows, win_cols, WH, WW, width).transpose(0, 2, 1, 3, 4)]
    dot_general x2 -> x0, matrix products: 4.92 us -> none  [the longest x1 3.06 us: window_attention(): jnp.einsum('wqhd,wkhd->whqk', query_win, key_win, preferred_element_type=...]
    slice x1 -> x0, local copies, waits for them, and re-layouts: 2.65 us -> none  [window_attention(): value_win = pairs[:, :, 1]]
  transfers between devices with their start and end apart: 6 -> 6, of which waited for: 3 -> 3; matrix products, arithmetic and copies ran while one was open for 33% -> 19% of each run, Pallas kernels for 26% -> 35%
where the time goes in v5:
time: 214 us; the launch traced here: 213 us
  Pallas kernels  73.6 us (34%)
  waiting for transfers between devices  46 us (21%)
  matrix products  37 us (17%)
  local copies, waits for them, and re-layouts  25.3 us (12%)
  between operations  14.2 us (7%)
  starting transfers between devices  8.88 us (4%)
  other arithmetic  8.27 us (4%)
    reduce_scatter x1, waiting for transfers between devices, local(): lax.psum_scatter(head_terms.astype(jnp.bfloat16), 'lat', scatter_dimensio...  42.6 us
    pallas_call x1, Pallas kernels, peer_gather(): pl.pallas_call(kernel, out_shape=jax.ShapeDtypeStruct((n,) + block.shape,...  33.1 us
    pallas_call x1, Pallas kernels, peer_reduce_scatter(): pl.pallas_call(kernel, out_shape=jax.ShapeDtypeStruct(parts.shape[1:], ou...  31.8 us
    dot_general x1, matrix products, slot_terms(): jnp.einsum('krnd,kdo->krno', rows, heads_full, preferred_element_type=jnp...  9.92 us
    dot_general x1, matrix products, slot_terms(): jnp.einsum('krno,kdo->krnd', errors, heads_full, preferred_element_type=j...  9.86 us
    pallas_call x1, Pallas kernels, masked_window_attention(): pl.pallas_call(kernel, out_shape=jax.ShapeDtypeStruct((nq, width), jnp.bf...  8.8 us
    convert_element_type x1, local copies, waits for them, and re-layouts, local(): head_terms.astype(jnp.bfloat16)  8.16 us
    dot_general x1, matrix products, slot_terms(): jnp.einsum('krnd,krno->dko', rows, errors, preferred_element_type=jnp.flo...  6.56 us
  transfers between devices with their start and end apart: 6, of which 3 were waited for; matrix products, arithmetic and copies ran while one was open for 19% of the time, Pallas kernels for 35%

profile of v5, /device:TPU:0, one launch (start us, length us, event | category | flops | bytes accessed | tf_op | source)
XLA Modules:
  0.0 213.3 jit_solution(8272329871972398882)
XLA Ops:
  7.2 0.7 all-gather.2.cloned.1.call-update
  8.0 1.0 fusion.37
  9.0 1.3 collective-permute-start.1
  10.3 4.6 %collective-permute-start = (bf16[3,24,1024]{2,1,0:T(8,128)(2,1)S(1)}, bf16[3,24,1024]{2,1,0:T(8,128)(2,1)S(1)}, u32[]{:S(2)}, u32[]{:S(2)}) collective-permute-start(bf16[3,24,1024]{2,1,0:T(8,128)(2,1)S(1)} %get-tuple-element.20), channel_id=1, source_target_pairs={{0,8},{8,16},{16,24},{24,32},{32,40},{40,48},{48,56},{56,64},{64,7... | collective-permute-start | bytes 442376 | tf_op jit(solution)/shard_map/ppermute | solution.py:130
  15.9 0.7 add.120.qw_ref
  16.6 0.8 select_reduce_fusion
  17.6 1.0 constant_dynamic-update-slice_fusion.1
  18.7 2.9 %collective-permute-start.3 = (bf16[12,6,1024]{2,1,0:T(8,128)(2,1)S(1)}, bf16[12,6,1024]{2,1,0:T(8,128)(2,1)S(1)}, u32[]{:S(2)}, u32[]{:S(2)}) collective-permute-start(bf16[12,6,1024]{2,1,0:T(8,128)(2,1)S(1)} %get-tuple-element.18), channel_id=1, source_target_pairs={{1,0},{2,1},{3,2},{4,3},{5,4},{6,5},{7,6},{0,7},{9,8},{10,9},{11,1... | collective-permute-start | bytes 442376 | tf_op jit(solution)/shard_map/ppermute | solution.py:131
  21.6 0.9 fusion.29
  22.5 2.5 %collective-permute-done.2 = bf16[12,6,1024]{2,1,0:T(8,128)(2,1)S(1)} collective-permute-done((bf16[12,6,1024]{2,1,0:T(8,128)(2,1)S(1)}, bf16[12,6,1024]{2,1,0:T(8,128)(2,1)S(1)}, u32[]{:S(2)}, u32[]{:S(2)}) %collective-permute-start.2) | collective-permute-done | bytes 147488 | tf_op jit(solution)/shard_map/ppermute | solution.py:130
  25.5 1.9 multiply_reduce_fusion.1
  27.5 1.6 maximum_convert_fusion
  29.1 2.7 %reshape.205 = f32[432,1024]{1,0:T(8,128)} reshape(f32[12,36,1024]{2,1,0:T(8,128)} %maximum_convert_fusion) | data formatting | bytes 3538944 | tf_op jit(solution)/shard_map/convert_element_type | solution.py:137
  31.8 1.4 fusion.28
  33.3 2.8 %fusion.21.q_ref = bf16[144,1024]{1,0:T(8,128)(2,1)} fusion(bf16[144,1024]{1,0:T(8,128)(2,1)S(1)} %bitcast.51, bf16[1024,3072]{1,0:T(8,128)(2,1)} %param.13), kind=kOutput, calls=%fused_computation.23 | convolution fusion | flops 302137344 | bytes 2686976 | tf_op jit(solution)/shard_map/dot_general | solution.py:222
  36.1 5.5 %fusion.14.kv_ref = bf16[432,2048]{1,0:T(8,128)(2,1)} fusion(bf16[1024,3072]{1,0:T(8,128)(2,1)} %param.13, f32[432,1024]{1,0:T(8,128)S(1)} %copy-done.3, f32[1024]{0:T(1024)S(1)} %copy-done.4, f32[432]{0:T(512)S(1)} %rsqrt.13, f32[432]{0:T(512)S(1)} %div.54), kind=kOutput, calls=%fused_computation.18 | convolution fusion | flops 1814593536 | bytes 7740800 | tf_op jit(solution)/shard_map/dot_general | solution.py:217
  41.6 8.8 %shard_map.130 = bf16[144,1024]{1,0:T(8,128)(2,1)} custom-call(bf16[144,1024]{1,0:T(8,128)(2,1)} %fusion.21.q_ref, bf16[432,2048]{1,0:T(8,128)(2,1)} %fusion.14.kv_ref, s32[144,1]{1,0:T(8,128)} %add.120.qw_ref, s32[1,432]{1,0:T(1,128)} %select_n.62.kw_ref), custom_call_target="tpu_custom_call" | custom-call | tf_op jit(solution)/shard_map/pallas_call | solution.py:108
  50.4 1.4 fusion.38
  51.9 0.8 add_convert_fusion.7
  52.6 33.1 %shard_map.131 = bf16[8,144,1024]{2,1,0:T(8,128)(2,1)} custom-call(bf16[144,1024]{1,0:T(8,128)(2,1)} %bitcast.50), custom_call_target="tpu_custom_call" | custom-call | tf_op jit(solution)/shard_map/pallas_call | solution.py:43
  85.7 4.3 %copy.25 = f32[8,6,24,1024]{3,2,0,1:T(8,128)} copy(bf16[8,6,24,1024]{3,2,1,0:T(8,128)(2,1)} %bitcast.43) | data formatting | bytes 7077888 | tf_op jit(solution)/shard_map/convert_element_type | solution.py:179
  90.1 9.9 %multiply_convert_fusion = bf16[5,6,192,320]{3,2,1,0:T(8,128)(2,1)S(1)} fusion(bf16[5,6,192,320]{3,2,1,0:T(8,128)(2,1)} %param.18, f32[5,192]{1,0:T(8,128)S(1)} %fusion.29, bf16[5,1024,320]{2,1,0:T(8,128)(2,1)} %all-gather.2.cloned.1.call-done, f32[5,1024]{1,0:T(8,128)S(1)} %copy-done.5, f32[5,1024]{1,0:T(8,128)S(1)} %copy-done.6, f32[6,192,1024]{2,1,0:T(8,128)} %bitcast.45), kind=kOutput, calls=%fused_computation.10 | convolution fusion | flops 3799941120 | bytes 15412992 | tf_op jit(solution)/shard_map/krnd,kdo->krno/dot_general | solution.py:183
  100.0 2.1 copy-done.7
  102.1 6.6 %fusion.13 = bf16[1024,5,320]{0,2,1:T(8,128)(2,1)} fusion(bf16[5,6,192,320]{3,2,1,0:T(8,128)(2,1)S(1)} %multiply_convert_fusion, f32[5,1024]{1,0:T(8,128)S(1)} %copy-done.5, f32[5,1024]{1,0:T(8,128)S(1)} %copy-done.6, f32[6,192,1024]{2,1,0:T(8,128)S(1)} %bitcast.46), kind=kOutput, calls=%fused_computation.17 | convolution fusion | flops 3795845120 | bytes 11722752 | tf_op jit(solution)/shard_map/krnd,krno->dko/dot_general | solution.py:189
  108.7 8.2 %copy.27 = bf16[1024,5,320]{2,1,0:T(8,128)(2,1)} copy(bf16[1024,5,320]{0,2,1:T(8,128)(2,1)} %fusion.13) | data formatting | bytes 6553600 | tf_op jit(solution)/shard_map/convert_element_type | solution.py:281
  116.9 9.9 %multiply_reduce_fusion = bf16[6,192,1024]{2,1,0:T(8,128)(2,1)S(1)} fusion(f32[5,1024]{1,0:T(8,128)S(1)} %copy-done.6, bf16[5,6,192,320]{3,2,1,0:T(8,128)(2,1)} %copy-done.7, bf16[5,1024,320]{2,1,0:T(8,128)(2,1)} %all-gather.2.cloned.1.call-done), kind=kOutput, calls=%fused_computation | convolution fusion | flops 3785490432 | bytes 9342976 | tf_op jit(solution)/shard_map/krno,kdo->krnd/dot_general | solution.py:187
  126.7 1.7 copy.26
  128.4 31.8 %shard_map.132 = bf16[144,1024]{1,0:T(8,128)(2,1)} custom-call(bf16[8,144,1024]{2,1,0:T(8,128)(2,1)} %bitcast.44), custom_call_target="tpu_custom_call" | custom-call | tf_op jit(solution)/shard_map/pallas_call | solution.py:78
  160.2 42.6 %reduce-scatter.2.cloned.1.call-done = bf16[64,5,320]{2,1,0:T(8,128)(2,1)} async-done(((bf16[1024,5,320]{2,1,0:T(8,128)(2,1)}), bf16[64,5,320]{2,1,0:T(8,128)(2,1)}) %reduce-scatter.2.cloned.1.call-update) | async-done | bytes 204816 | tf_op jit(solution)/shard_map/reduce_scatter | solution.py:280
  202.8 1.0 convert_bitcast_fusion
  203.9 0.9 copy.28
  204.8 1.7 copy.34
  (43 shorter events, 2.1 us)
Async XLA Ops:
  7.2 43.2 %copy-start = (bf16[1024,1024]{1,0:T(8,128)(2,1)S(1)}, bf16[1024,1024]{1,0:T(8,128)(2,1)}, u32[]{:S(2)}) copy-start(bf16[1024,1024]{1,0:T(8,128)(2,1)} %param.14) | copy-start | bytes 6291460
  7.2 82.9 %all-gather.2.cloned.1.call-start = ((), (), s32[]{:S(2)}) async-start(), calls=%async_computation.1 | async-start | bytes 4177920 | tf_op jit(solution)/shard_map/all_gather | solution.py:252
  7.9 194.9 %reduce-scatter.2.cloned.1.call-start = ((), (), s32[]{:S(2)}) async-start(), calls=%async_computation.2 | async-start | bytes 6684672 | tf_op jit(solution)/shard_map/reduce_scatter | solution.py:280
  9.0 9.6 %collective-permute-start.1 = (bf16[3,24,1024]{2,1,0:T(8,128)(2,1)S(1)}, bf16[3,24,1024]{2,1,0:T(8,128)(2,1)S(1)}, u32[]{:S(2)}, u32[]{:S(2)}) collective-permute-start(bf16[3,24,1024]{2,1,0:T(8,128)(2,1)S(1)} %get-tuple-element.19), channel_id=1, source_target_pairs={{8,0},{16,8},{24,16},{32,24},{40,32},{48,40},{56,48},{64,56},{72,6... | collective-permute-start | bytes 442376 | tf_op jit(solution)/shard_map/ppermute | solution.py:131
  10.3 7.3 %collective-permute-start = (bf16[3,24,1024]{2,1,0:T(8,128)(2,1)S(1)}, bf16[3,24,1024]{2,1,0:T(8,128)(2,1)S(1)}, u32[]{:S(2)}, u32[]{:S(2)}) collective-permute-start(bf16[3,24,1024]{2,1,0:T(8,128)(2,1)S(1)} %get-tuple-element.20), channel_id=1, source_target_pairs={{0,8},{8,16},{16,24},{24,32},{32,40},{40,48},{48,56},{56,64},{64,7... | collective-permute-start | bytes 442376 | tf_op jit(solution)/shard_map/ppermute | solution.py:130
  18.6 6.3 %collective-permute-start.2 = (bf16[12,6,1024]{2,1,0:T(8,128)(2,1)S(1)}, bf16[12,6,1024]{2,1,0:T(8,128)(2,1)S(1)}, u32[]{:S(2)}, u32[]{:S(2)}) collective-permute-start(bf16[12,6,1024]{2,1,0:T(8,128)(2,1)S(1)} %get-tuple-element.17), channel_id=1, source_target_pairs={{0,1},{1,2},{2,3},{3,4},{4,5},{5,6},{6,7},{7,0},{8,9},{9,10},{10,1... | collective-permute-start | bytes 442376 | tf_op jit(solution)/shard_map/ppermute | solution.py:130
  18.7 6.3 %collective-permute-start.3 = (bf16[12,6,1024]{2,1,0:T(8,128)(2,1)S(1)}, bf16[12,6,1024]{2,1,0:T(8,128)(2,1)S(1)}, u32[]{:S(2)}, u32[]{:S(2)}) collective-permute-start(bf16[12,6,1024]{2,1,0:T(8,128)(2,1)S(1)} %get-tuple-element.18), channel_id=1, source_target_pairs={{1,0},{2,1},{3,2},{4,3},{5,4},{6,5},{7,6},{0,7},{9,8},{10,9},{11,1... | collective-permute-start | bytes 442376 | tf_op jit(solution)/shard_map/ppermute | solution.py:131
  27.4 4.5 %copy-start.4 = (f32[1024]{0:T(1024)S(1)}, f32[1024]{0:T(1024)}, u32[]{:S(2)}) copy-start(f32[1024]{0:T(1024)} %param.12) | copy-start | bytes 12292
  31.8 4.2 %copy-start.3 = (f32[432,1024]{1,0:T(8,128)S(1)}, f32[432,1024]{1,0:T(8,128)}, u32[]{:S(2)}) copy-start(f32[432,1024]{1,0:T(8,128)} %reshape.205) | copy-start | bytes 5308420
  41.6 10.3 %copy-start.2 = (bf16[6,24,1024]{2,1,0:T(8,128)(2,1)S(1)}, bf16[6,24,1024]{2,1,0:T(8,128)(2,1)}, u32[]{:S(2)}) copy-start(bf16[6,24,1024]{2,1,0:T(8,128)(2,1)} %param.11) | copy-start | bytes 884740
  85.7 4.4 %copy-start.5 = (f32[5,1024]{1,0:T(8,128)S(1)}, f32[5,1024]{1,0:T(8,128)}, u32[]{:S(2)}) copy-start(f32[5,1024]{1,0:T(8,128)} %param.16) | copy-start | bytes 61444
  85.7 4.4 %copy-start.6 = (f32[5,1024]{1,0:T(8,128)S(1)}, f32[5,1024]{1,0:T(8,128)}, u32[]{:S(2)}) copy-start(f32[5,1024]{1,0:T(8,128)} %param.15) | copy-start | bytes 61444
  90.1 12.0 %copy-start.1 = (f32[8,6,24,1024]{3,2,0,1:T(8,128)S(1)}, f32[8,6,24,1024]{3,2,0,1:T(8,128)}, u32[]{:S(2)}) copy-start(f32[8,6,24,1024]{3,2,0,1:T(8,128)} %copy.25) | copy-start | bytes 14155780
  100.0 2.1 copy-start.7
Sparse Core Ops, SparseCore 0:
  10.2 52.8 all-gather.1
  117.0 85.8 reduce-scatter.1

commit v6 on v5

--- a/solution.py
+++ b/solution.py
@@ -111,6 +111,53 @@
         in_specs=[pl.BlockSpec(memory_space=pltpu.VMEM)] * 4,
         out_specs=pl.BlockSpec(memory_space=pltpu.VMEM),
     )(queries, keyval, query_win, key_win)
+
+
+def chip_pair_gather(block, axis, n, cid):
+    nz = n // 2
+
+    def kernel(x_ref, out_ref, send_sem, recv_sem):
+        me = lax.axis_index(axis)
+        partner = me + 1 - 2 * lax.rem(me, 2)
+        peers = [lax.rem(me + 2 * k, n) for k in range(1, nz)]
+        barrier = pltpu.get_barrier_semaphore()
+        for dev in peers + [partner]:
+            pl.semaphore_signal(barrier, inc=1, device_id={axis: dev}, device_id_type=MESH_ID)
+        pl.semaphore_wait(barrier, nz)
+
+        def send(src_ref, slot, dev, index):
+            copy = pltpu.make_async_remote_copy(
+                src_ref=src_ref, dst_ref=out_ref.at[slot], send_sem=send_sem.at[index],
+                recv_sem=recv_sem.at[slot], device_id={axis: dev}, device_id_type=MESH_ID)
+            copy.start()
+            return copy
+
+        def arrive(slot):
+            pltpu.make_async_remote_copy(
+                src_ref=x_ref, dst_ref=out_ref.at[slot], send_sem=send_sem.at[0],
+                recv_sem=recv_sem.at[slot], device_id={axis: slot},
+                device_id_type=MESH_ID).wait_recv()
+
+        sends = [send(x_ref, me, dev, i) for i, dev in enumerate(peers)]
+        sends.append(send(x_ref, me, partner, nz - 1))
+        out_ref[me] = x_ref[...]
+        for k in range(1, nz):
+            src = lax.rem(me + n - 2 * k, n)
+            arrive(src)
+            sends.append(send(out_ref.at[src], src, partner, nz - 1 + k))
+        for k in range(nz):
+            arrive(lax.rem(partner + 2 * k, n))
+        for copy in sends:
+            copy.wait_send()
+
+    return pl.pallas_call(
+        kernel,
+        out_shape=jax.ShapeDtypeStruct((n,) + block.shape, block.dtype),
+        in_specs=[pl.BlockSpec(memory_space=pltpu.VMEM)],
+        out_specs=pl.BlockSpec(memory_space=pltpu.VMEM),
+        scratch_shapes=[pltpu.SemaphoreType.DMA((n,)), pltpu.SemaphoreType.DMA((n,))],
+        compiler_params=pltpu.CompilerParams(collective_id=cid, has_side_effects=True),
+    )(block)
 
 HEADS = 16
 WH = 6
@@ -251,7 +298,7 @@
     live_tiles = (slot_level[None, :] < tile_levels[:, None]).astype(jnp.float32)
     heads_full = lax.all_gather(head_weight, "lat", axis=1, tiled=True)
     tile_ids = jnp.arange(var_count, dtype=jnp.int32)
-    tiles = peer_gather(latent.reshape(band_rows * band_cols, width), "var", var_count, 1)
+    tiles = chip_pair_gather(latent.reshape(band_rows * band_cols, width), "var", var_count, 1)
     piece = (
         tiles.reshape(var_count, band_rows, band_cols, width)
         .transpose(1, 0, 2, 3)

time: 214 us -> 203 us (0.949)
  Pallas kernels: 73.6 us -> 61.7 us
    pallas_call x1, Pallas kernels: 33.1 us -> 22.9 us  [chip_pair_gather(): pl.pallas_call(kernel, out_shape=jax.ShapeDtypeStruct((n,) + block.shape,...]
  transfers between devices with their start and end apart: 6 -> 6, of which waited for: 3 -> 3; matrix products, arithmetic and copies ran while one was open for 19% -> 20% of each run, Pallas kernels for 35% -> 31%
where the time goes in v6:
time: 203 us; the launch traced here: 202 us
  Pallas kernels  61.7 us (30%)
  waiting for transfers between devices  46.5 us (23%)
  matrix products  37 us (18%)
  local copies, waits for them, and re-layouts  25.3 us (12%)
  between operations  14.2 us (7%)
  starting transfers between devices  8.88 us (4%)
  other arithmetic  8.27 us (4%)
    reduce_scatter x1, waiting for transfers between devices, local(): lax.psum_scatter(head_terms.astype(jnp.bfloat16), 'lat', scatter_dimensio...  43.2 us
    pallas_call x1, Pallas kernels, peer_reduce_scatter(): pl.pallas_call(kernel, out_shape=jax.ShapeDtypeStruct(parts.shape[1:], ou...  30 us
    pallas_call x1, Pallas kernels, chip_pair_gather(): pl.pallas_call(kernel, out_shape=jax.ShapeDtypeStruct((n,) + block.shape,...  22.9 us
    dot_general x1, matrix products, slot_terms(): jnp.einsum('krnd,kdo->krno', rows, heads_full, preferred_element_type=jnp...  9.92 us
    dot_general x1, matrix products, slot_terms(): jnp.einsum('krno,kdo->krnd', errors, heads_full, preferred_element_type=j...  9.86 us
    pallas_call x1, Pallas kernels, masked_window_attention(): pl.pallas_call(kernel, out_shape=jax.ShapeDtypeStruct((nq, width), jnp.bf...  8.8 us
    convert_element_type x1, local copies, waits for them, and re-layouts, local(): head_terms.astype(jnp.bfloat16)  8.16 us
    dot_general x1, matrix products, slot_terms(): jnp.einsum('krnd,krno->dko', rows, errors, preferred_element_type=jnp.flo...  6.56 us
  transfers between devices with their start and end apart: 6, of which 3 were waited for; matrix products, arithmetic and copies ran while one was open for 20% of the time, Pallas kernels for 31%

profile of v6, /device:TPU:0, one launch (start us, length us, event | category | flops | bytes accessed | tf_op | source)
XLA Modules:
  0.0 201.9 jit_solution(8583518758268984388)
XLA Ops:
  7.2 0.7 all-gather.2.cloned.1.call-update
  8.0 1.0 fusion.37
  9.0 1.3 collective-permute-start.1
  10.3 4.6 %collective-permute-start = (bf16[3,24,1024]{2,1,0:T(8,128)(2,1)S(1)}, bf16[3,24,1024]{2,1,0:T(8,128)(2,1)S(1)}, u32[]{:S(2)}, u32[]{:S(2)}) collective-permute-start(bf16[3,24,1024]{2,1,0:T(8,128)(2,1)S(1)} %get-tuple-element.20), channel_id=1, source_target_pairs={{0,8},{8,16},{16,24},{24,32},{32,40},{40,48},{48,56},{56,64},{64,7... | collective-permute-start | bytes 442376 | tf_op jit(solution)/shard_map/ppermute | solution.py:177
  15.9 0.7 add.120.qw_ref
  16.6 0.8 select_reduce_fusion
  17.6 1.0 constant_dynamic-update-slice_fusion.1
  18.7 2.9 %collective-permute-start.3 = (bf16[12,6,1024]{2,1,0:T(8,128)(2,1)S(1)}, bf16[12,6,1024]{2,1,0:T(8,128)(2,1)S(1)}, u32[]{:S(2)}, u32[]{:S(2)}) collective-permute-start(bf16[12,6,1024]{2,1,0:T(8,128)(2,1)S(1)} %get-tuple-element.18), channel_id=1, source_target_pairs={{1,0},{2,1},{3,2},{4,3},{5,4},{6,5},{7,6},{0,7},{9,8},{10,9},{11,1... | collective-permute-start | bytes 442376 | tf_op jit(solution)/shard_map/ppermute | solution.py:178
  21.6 0.9 fusion.29
  22.5 2.5 %collective-permute-done.2 = bf16[12,6,1024]{2,1,0:T(8,128)(2,1)S(1)} collective-permute-done((bf16[12,6,1024]{2,1,0:T(8,128)(2,1)S(1)}, bf16[12,6,1024]{2,1,0:T(8,128)(2,1)S(1)}, u32[]{:S(2)}, u32[]{:S(2)}) %collective-permute-start.2) | collective-permute-done | bytes 147488 | tf_op jit(solution)/shard_map/ppermute | solution.py:177
  25.5 1.9 multiply_reduce_fusion.1
  27.5 1.6 maximum_convert_fusion
  29.1 2.7 %reshape.205 = f32[432,1024]{1,0:T(8,128)} reshape(f32[12,36,1024]{2,1,0:T(8,128)} %maximum_convert_fusion) | data formatting | bytes 3538944 | tf_op jit(solution)/shard_map/convert_element_type | solution.py:184
  31.8 1.4 fusion.28
  33.3 2.8 %fusion.21.q_ref = bf16[144,1024]{1,0:T(8,128)(2,1)} fusion(bf16[144,1024]{1,0:T(8,128)(2,1)S(1)} %bitcast.51, bf16[1024,3072]{1,0:T(8,128)(2,1)} %param.13), kind=kOutput, calls=%fused_computation.23 | convolution fusion | flops 302137344 | bytes 2686976 | tf_op jit(solution)/shard_map/dot_general | solution.py:269
  36.1 5.5 %fusion.14.kv_ref = bf16[432,2048]{1,0:T(8,128)(2,1)} fusion(bf16[1024,3072]{1,0:T(8,128)(2,1)} %param.13, f32[432,1024]{1,0:T(8,128)S(1)} %copy-done.3, f32[1024]{0:T(1024)S(1)} %copy-done.4, f32[432]{0:T(512)S(1)} %rsqrt.13, f32[432]{0:T(512)S(1)} %div.54), kind=kOutput, calls=%fused_computation.18 | convolution fusion | flops 1814593536 | bytes 7740800 | tf_op jit(solution)/shard_map/dot_general | solution.py:264
  41.6 8.8 %shard_map.130 = bf16[144,1024]{1,0:T(8,128)(2,1)} custom-call(bf16[144,1024]{1,0:T(8,128)(2,1)} %fusion.21.q_ref, bf16[432,2048]{1,0:T(8,128)(2,1)} %fusion.14.kv_ref, s32[144,1]{1,0:T(8,128)} %add.120.qw_ref, s32[1,432]{1,0:T(1,128)} %select_n.62.kw_ref), custom_call_target="tpu_custom_call" | custom-call | tf_op jit(solution)/shard_map/pallas_call | solution.py:108
  50.4 1.4 fusion.38
  51.9 0.8 add_convert_fusion.7
  52.6 22.9 %shard_map.131 = bf16[8,144,1024]{2,1,0:T(8,128)(2,1)} custom-call(bf16[144,1024]{1,0:T(8,128)(2,1)} %bitcast.50), custom_call_target="tpu_custom_call" | custom-call | tf_op jit(solution)/shard_map/pallas_call | solution.py:153
  75.6 4.3 %copy.25 = f32[8,6,24,1024]{3,2,0,1:T(8,128)} copy(bf16[8,6,24,1024]{3,2,1,0:T(8,128)(2,1)} %bitcast.43) | data formatting | bytes 7077888 | tf_op jit(solution)/shard_map/convert_element_type | solution.py:226
  79.9 9.9 %multiply_convert_fusion = bf16[5,6,192,320]{3,2,1,0:T(8,128)(2,1)S(1)} fusion(bf16[5,6,192,320]{3,2,1,0:T(8,128)(2,1)} %param.18, f32[5,192]{1,0:T(8,128)S(1)} %fusion.29, bf16[5,1024,320]{2,1,0:T(8,128)(2,1)} %all-gather.2.cloned.1.call-done, f32[5,1024]{1,0:T(8,128)S(1)} %copy-done.5, f32[5,1024]{1,0:T(8,128)S(1)} %copy-done.6, f32[6,192,1024]{2,1,0:T(8,128)} %bitcast.45), kind=kOutput, calls=%fused_computation.10 | convolution fusion | flops 3799941120 | bytes 15412992 | tf_op jit(solution)/shard_map/krnd,kdo->krno/dot_general | solution.py:230
  89.9 2.1 %copy-done.7 = bf16[5,6,192,320]{3,2,1,0:T(8,128)(2,1)} copy-done((bf16[5,6,192,320]{3,2,1,0:T(8,128)(2,1)}, bf16[5,6,192,320]{3,2,1,0:T(8,128)(2,1)S(1)}, u32[]{:S(2)}) %copy-start.7) | copy-done | bytes 3686424
  92.0 6.6 %fusion.13 = bf16[1024,5,320]{0,2,1:T(8,128)(2,1)} fusion(bf16[5,6,192,320]{3,2,1,0:T(8,128)(2,1)S(1)} %multiply_convert_fusion, f32[5,1024]{1,0:T(8,128)S(1)} %copy-done.5, f32[5,1024]{1,0:T(8,128)S(1)} %copy-done.6, f32[6,192,1024]{2,1,0:T(8,128)S(1)} %bitcast.46), kind=kOutput, calls=%fused_computation.17 | convolution fusion | flops 3795845120 | bytes 11722752 | tf_op jit(solution)/shard_map/krnd,krno->dko/dot_general | solution.py:236
  98.5 8.2 %copy.27 = bf16[1024,5,320]{2,1,0:T(8,128)(2,1)} copy(bf16[1024,5,320]{0,2,1:T(8,128)(2,1)} %fusion.13) | data formatting | bytes 6553600 | tf_op jit(solution)/shard_map/convert_element_type | solution.py:328
  106.7 9.9 %multiply_reduce_fusion = bf16[6,192,1024]{2,1,0:T(8,128)(2,1)S(1)} fusion(f32[5,1024]{1,0:T(8,128)S(1)} %copy-done.6, bf16[5,6,192,320]{3,2,1,0:T(8,128)(2,1)} %copy-done.7, bf16[5,1024,320]{2,1,0:T(8,128)(2,1)} %all-gather.2.cloned.1.call-done), kind=kOutput, calls=%fused_computation | convolution fusion | flops 3785490432 | bytes 9342976 | tf_op jit(solution)/shard_map/krno,kdo->krnd/dot_general | solution.py:234
  116.6 1.7 copy.26
  118.3 30.0 %shard_map.132 = bf16[144,1024]{1,0:T(8,128)(2,1)} custom-call(bf16[8,144,1024]{2,1,0:T(8,128)(2,1)} %bitcast.44), custom_call_target="tpu_custom_call" | custom-call | tf_op jit(solution)/shard_map/pallas_call | solution.py:78
  148.3 43.2 %reduce-scatter.2.cloned.1.call-done = bf16[64,5,320]{2,1,0:T(8,128)(2,1)} async-done(((bf16[1024,5,320]{2,1,0:T(8,128)(2,1)}), bf16[64,5,320]{2,1,0:T(8,128)(2,1)}) %reduce-scatter.2.cloned.1.call-update) | async-done | bytes 204816 | tf_op jit(solution)/shard_map/reduce_scatter | solution.py:327
  191.5 1.0 convert_bitcast_fusion
  192.5 0.9 copy.28
  193.4 1.7 copy.34
  (43 shorter events, 2.1 us)
Async XLA Ops:
  7.2 43.2 %copy-start = (bf16[1024,1024]{1,0:T(8,128)(2,1)S(1)}, bf16[1024,1024]{1,0:T(8,128)(2,1)}, u32[]{:S(2)}) copy-start(bf16[1024,1024]{1,0:T(8,128)(2,1)} %param.14) | copy-start | bytes 6291460
  7.2 72.7 %all-gather.2.cloned.1.call-start = ((), (), s32[]{:S(2)}) async-start(), calls=%async_computation.1 | async-start | bytes 4177920 | tf_op jit(solution)/shard_map/all_gather | solution.py:299
  7.9 183.5 %reduce-scatter.2.cloned.1.call-start = ((), (), s32[]{:S(2)}) async-start(), calls=%async_computation.2 | async-start | bytes 6684672 | tf_op jit(solution)/shard_map/reduce_scatter | solution.py:327
  9.0 9.6 %collective-permute-start.1 = (bf16[3,24,1024]{2,1,0:T(8,128)(2,1)S(1)}, bf16[3,24,1024]{2,1,0:T(8,128)(2,1)S(1)}, u32[]{:S(2)}, u32[]{:S(2)}) collective-permute-start(bf16[3,24,1024]{2,1,0:T(8,128)(2,1)S(1)} %get-tuple-element.19), channel_id=1, source_target_pairs={{8,0},{16,8},{24,16},{32,24},{40,32},{48,40},{56,48},{64,56},{72,6... | collective-permute-start | bytes 442376 | tf_op jit(solution)/shard_map/ppermute | solution.py:178
  10.3 7.3 %collective-permute-start = (bf16[3,24,1024]{2,1,0:T(8,128)(2,1)S(1)}, bf16[3,24,1024]{2,1,0:T(8,128)(2,1)S(1)}, u32[]{:S(2)}, u32[]{:S(2)}) collective-permute-start(bf16[3,24,1024]{2,1,0:T(8,128)(2,1)S(1)} %get-tuple-element.20), channel_id=1, source_target_pairs={{0,8},{8,16},{16,24},{24,32},{32,40},{40,48},{48,56},{56,64},{64,7... | collective-permute-start | bytes 442376 | tf_op jit(solution)/shard_map/ppermute | solution.py:177
  18.6 6.3 %collective-permute-start.2 = (bf16[12,6,1024]{2,1,0:T(8,128)(2,1)S(1)}, bf16[12,6,1024]{2,1,0:T(8,128)(2,1)S(1)}, u32[]{:S(2)}, u32[]{:S(2)}) collective-permute-start(bf16[12,6,1024]{2,1,0:T(8,128)(2,1)S(1)} %get-tuple-element.17), channel_id=1, source_target_pairs={{0,1},{1,2},{2,3},{3,4},{4,5},{5,6},{6,7},{7,0},{8,9},{9,10},{10,1... | collective-permute-start | bytes 442376 | tf_op jit(solution)/shard_map/ppermute | solution.py:177
  18.7 6.3 %collective-permute-start.3 = (bf16[12,6,1024]{2,1,0:T(8,128)(2,1)S(1)}, bf16[12,6,1024]{2,1,0:T(8,128)(2,1)S(1)}, u32[]{:S(2)}, u32[]{:S(2)}) collective-permute-start(bf16[12,6,1024]{2,1,0:T(8,128)(2,1)S(1)} %get-tuple-element.18), channel_id=1, source_target_pairs={{1,0},{2,1},{3,2},{4,3},{5,4},{6,5},{7,6},{0,7},{9,8},{10,9},{11,1... | collective-permute-start | bytes 442376 | tf_op jit(solution)/shard_map/ppermute | solution.py:178
  27.4 4.5 %copy-start.4 = (f32[1024]{0:T(1024)S(1)}, f32[1024]{0:T(1024)}, u32[]{:S(2)}) copy-start(f32[1024]{0:T(1024)} %param.12) | copy-start | bytes 12292
  31.8 4.2 %copy-start.3 = (f32[432,1024]{1,0:T(8,128)S(1)}, f32[432,1024]{1,0:T(8,128)}, u32[]{:S(2)}) copy-start(f32[432,1024]{1,0:T(8,128)} %reshape.205) | copy-start | bytes 5308420
  41.6 10.3 %copy-start.2 = (bf16[6,24,1024]{2,1,0:T(8,128)(2,1)S(1)}, bf16[6,24,1024]{2,1,0:T(8,128)(2,1)}, u32[]{:S(2)}) copy-start(bf16[6,24,1024]{2,1,0:T(8,128)(2,1)} %param.11) | copy-start | bytes 884740
  75.6 4.4 %copy-start.5 = (f32[5,1024]{1,0:T(8,128)S(1)}, f32[5,1024]{1,0:T(8,128)}, u32[]{:S(2)}) copy-start(f32[5,1024]{1,0:T(8,128)} %param.16) | copy-start | bytes 61444
  75.6 4.4 %copy-start.6 = (f32[5,1024]{1,0:T(8,128)S(1)}, f32[5,1024]{1,0:T(8,128)}, u32[]{:S(2)}) copy-start(f32[5,1024]{1,0:T(8,128)} %param.15) | copy-start | bytes 61444
  79.9 12.0 %copy-start.1 = (f32[8,6,24,1024]{3,2,0,1:T(8,128)S(1)}, f32[8,6,24,1024]{3,2,0,1:T(8,128)}, u32[]{:S(2)}) copy-start(f32[8,6,24,1024]{3,2,0,1:T(8,128)} %copy.25) | copy-start | bytes 14155780
  89.8 2.1 %copy-start.7 = (bf16[5,6,192,320]{3,2,1,0:T(8,128)(2,1)}, bf16[5,6,192,320]{3,2,1,0:T(8,128)(2,1)S(1)}, u32[]{:S(2)}) copy-start(bf16[5,6,192,320]{3,2,1,0:T(8,128)(2,1)S(1)} %multiply_convert_fusion) | copy-start | bytes 11059204
Sparse Core Ops, SparseCore 0:
  10.2 52.8 all-gather.1
  106.8 84.5 reduce-scatter.1

commit v7 on v6

--- a/solution.py
+++ b/solution.py
@@ -324,10 +324,11 @@
     ).reshape(band_rows, band_cols, width)
     head_terms = head_terms * (1.0 / math.sqrt(lat_count * band_rows * var_count * band_cols))
     share_rows = width // lat_count
-    mine = lax.psum_scatter(
-        head_terms.astype(jnp.bfloat16), "lat", scatter_dimension=0, tiled=True
-    ).astype(jnp.float32)
-    grad_head = jnp.transpose(mine, (1, 0, 2))
+    slots, outs = head_terms.shape[1], head_terms.shape[2]
+    lanes = 128
+    dense = head_terms.astype(jnp.bfloat16).reshape(width * slots * outs // lanes, lanes)
+    mine = lax.psum_scatter(dense, "lat", scatter_dimension=0, tiled=True).astype(jnp.float32)
+    grad_head = jnp.transpose(mine.reshape(share_rows, slots, outs), (1, 0, 2))
     return (latent, grad_latent, grad_head)
 
 

time: 203 us -> 207 us (1.020)
  local copies, waits for them, and re-layouts: 25.3 us -> 35.9 us
  waiting for transfers between devices: 46.5 us -> 41.1 us
    reshape x0 -> x1, local copies, waits for them, and re-layouts: none -> 9.38 us  [local(): head_terms.astype(jnp.bfloat16)]
    reduce_scatter x1, waiting for transfers between devices: 43.2 us -> 37.8 us  [local(): lax.psum_scatter(dense, 'lat', scatter_dimension=0, tiled=True)]
  transfers between devices with their start and end apart: 6 -> 6, of which waited for: 3 -> 3; matrix products, arithmetic and copies ran while one was open for 20% -> 19% of each run, Pallas kernels for 31% -> 30%
where the time goes in v7:
time: 207 us; the launch traced here: 206 us
  Pallas kernels  61.7 us (30%)
  waiting for transfers between devices  41.1 us (20%)
  matrix products  37 us (18%)
  local copies, waits for them, and re-layouts  35.9 us (17%)
  between operations  14.2 us (7%)
  starting transfers between devices  8.88 us (4%)
  other arithmetic  7.22 us (3%)
    reduce_scatter x1, waiting for transfers between devices, local(): lax.psum_scatter(dense, 'lat', scatter_dimension=0, tiled=True)  37.8 us
    pallas_call x1, Pallas kernels, peer_reduce_scatter(): pl.pallas_call(kernel, out_shape=jax.ShapeDtypeStruct(parts.shape[1:], ou...  30 us
    pallas_call x1, Pallas kernels, chip_pair_gather(): pl.pallas_call(kernel, out_shape=jax.ShapeDtypeStruct((n,) + block.shape,...  22.9 us
    dot_general x1, matrix products, slot_terms(): jnp.einsum('krnd,kdo->krno', rows, heads_full, preferred_element_type=jnp...  9.92 us
    dot_general x1, matrix products, slot_terms(): jnp.einsum('krno,kdo->krnd', errors, heads_full, preferred_element_type=j...  9.86 us
    reshape x1, local copies, waits for them, and re-layouts, local(): head_terms.astype(jnp.bfloat16)  9.38 us
    pallas_call x1, Pallas kernels, masked_window_attention(): pl.pallas_call(kernel, out_shape=jax.ShapeDtypeStruct((nq, width), jnp.bf...  8.8 us
    convert_element_type x1, local copies, waits for them, and re-layouts, local(): head_terms.astype(jnp.bfloat16)  8.16 us
  transfers between devices with their start and end apart: 6, of which 3 were waited for; matrix products, arithmetic and copies ran while one was open for 19% of the time, Pallas kernels for 30%

profile of v7, /device:TPU:0, one launch (start us, length us, event | category | flops | bytes accessed | tf_op | source)
XLA Modules:
  0.0 206.1 jit_solution(15922747427066459499)
XLA Ops:
  8.0 1.0 fusion.37
  9.0 1.3 collective-permute-start.1
  10.3 4.6 %collective-permute-start = (bf16[3,24,1024]{2,1,0:T(8,128)(2,1)S(1)}, bf16[3,24,1024]{2,1,0:T(8,128)(2,1)S(1)}, u32[]{:S(2)}, u32[]{:S(2)}) collective-permute-start(bf16[3,24,1024]{2,1,0:T(8,128)(2,1)S(1)} %get-tuple-element.14), channel_id=1, source_target_pairs={{0,8},{8,16},{16,24},{24,32},{32,40},{40,48},{48,56},{56,64},{64,7... | collective-permute-start | bytes 442376 | tf_op jit(solution)/shard_map/ppermute | solution.py:177
  15.9 0.7 add.120.qw_ref
  16.6 0.8 select_reduce_fusion
  17.6 1.0 constant_dynamic-update-slice_fusion.1
  18.7 2.9 %collective-permute-start.3 = (bf16[12,6,1024]{2,1,0:T(8,128)(2,1)S(1)}, bf16[12,6,1024]{2,1,0:T(8,128)(2,1)S(1)}, u32[]{:S(2)}, u32[]{:S(2)}) collective-permute-start(bf16[12,6,1024]{2,1,0:T(8,128)(2,1)S(1)} %get-tuple-element.12), channel_id=1, source_target_pairs={{1,0},{2,1},{3,2},{4,3},{5,4},{6,5},{7,6},{0,7},{9,8},{10,9},{11,1... | collective-permute-start | bytes 442376 | tf_op jit(solution)/shard_map/ppermute | solution.py:178
  21.6 0.9 fusion.29
  22.5 2.5 %collective-permute-done.2 = bf16[12,6,1024]{2,1,0:T(8,128)(2,1)S(1)} collective-permute-done((bf16[12,6,1024]{2,1,0:T(8,128)(2,1)S(1)}, bf16[12,6,1024]{2,1,0:T(8,128)(2,1)S(1)}, u32[]{:S(2)}, u32[]{:S(2)}) %collective-permute-start.2) | collective-permute-done | bytes 147488 | tf_op jit(solution)/shard_map/ppermute | solution.py:177
  25.5 1.9 multiply_reduce_fusion.1
  27.5 1.6 maximum_convert_fusion
  29.1 2.7 %reshape.214 = f32[432,1024]{1,0:T(8,128)} reshape(f32[12,36,1024]{2,1,0:T(8,128)} %maximum_convert_fusion) | data formatting | bytes 3538944 | tf_op jit(solution)/shard_map/convert_element_type | solution.py:184
  31.8 1.4 fusion.28
  33.3 2.8 %fusion.21.q_ref = bf16[144,1024]{1,0:T(8,128)(2,1)} fusion(bf16[144,1024]{1,0:T(8,128)(2,1)S(1)} %bitcast.51, bf16[1024,3072]{1,0:T(8,128)(2,1)} %param.13), kind=kOutput, calls=%fused_computation.23 | convolution fusion | flops 302137344 | bytes 2686976 | tf_op jit(solution)/shard_map/dot_general | solution.py:269
  36.1 5.5 %fusion.14.kv_ref = bf16[432,2048]{1,0:T(8,128)(2,1)} fusion(bf16[1024,3072]{1,0:T(8,128)(2,1)} %param.13, f32[432,1024]{1,0:T(8,128)S(1)} %copy-done.3, f32[1024]{0:T(1024)S(1)} %copy-done.4, f32[432]{0:T(512)S(1)} %rsqrt.13, f32[432]{0:T(512)S(1)} %div.54), kind=kOutput, calls=%fused_computation.18 | convolution fusion | flops 1814593536 | bytes 7740800 | tf_op jit(solution)/shard_map/dot_general | solution.py:264
  41.6 8.8 %shard_map.130 = bf16[144,1024]{1,0:T(8,128)(2,1)} custom-call(bf16[144,1024]{1,0:T(8,128)(2,1)} %fusion.21.q_ref, bf16[432,2048]{1,0:T(8,128)(2,1)} %fusion.14.kv_ref, s32[144,1]{1,0:T(8,128)} %add.120.qw_ref, s32[1,432]{1,0:T(1,128)} %select_n.62.kw_ref), custom_call_target="tpu_custom_call" | custom-call | tf_op jit(solution)/shard_map/pallas_call | solution.py:108
  50.4 1.4 fusion.38
  51.9 0.8 add_convert_fusion.7
  52.6 22.9 %shard_map.131 = bf16[8,144,1024]{2,1,0:T(8,128)(2,1)} custom-call(bf16[144,1024]{1,0:T(8,128)(2,1)} %bitcast.50), custom_call_target="tpu_custom_call" | custom-call | tf_op jit(solution)/shard_map/pallas_call | solution.py:153
  75.6 4.3 %copy.20 = f32[8,6,24,1024]{3,2,0,1:T(8,128)} copy(bf16[8,6,24,1024]{3,2,1,0:T(8,128)(2,1)} %bitcast.42) | data formatting | bytes 7077888 | tf_op jit(solution)/shard_map/convert_element_type | solution.py:226
  79.9 9.9 %multiply_convert_fusion = bf16[5,6,192,320]{3,2,1,0:T(8,128)(2,1)S(1)} fusion(bf16[5,6,192,320]{3,2,1,0:T(8,128)(2,1)} %param.18, f32[5,192]{1,0:T(8,128)S(1)} %fusion.29, bf16[5,1024,320]{2,1,0:T(8,128)(2,1)} %all-gather.2.cloned.1.call-done, f32[5,1024]{1,0:T(8,128)S(1)} %copy-done.5, f32[5,1024]{1,0:T(8,128)S(1)} %copy-done.6, f32[6,192,1024]{2,1,0:T(8,128)} %bitcast.44), kind=kOutput, calls=%fused_computation.10 | convolution fusion | flops 3799941120 | bytes 15412992 | tf_op jit(solution)/shard_map/krnd,kdo->krno/dot_general | solution.py:230
  89.9 2.1 %copy-done.7 = bf16[5,6,192,320]{3,2,1,0:T(8,128)(2,1)} copy-done((bf16[5,6,192,320]{3,2,1,0:T(8,128)(2,1)}, bf16[5,6,192,320]{3,2,1,0:T(8,128)(2,1)S(1)}, u32[]{:S(2)}) %copy-start.7) | copy-done | bytes 3686424
  92.0 6.6 %fusion.13 = bf16[1024,5,320]{0,2,1:T(8,128)(2,1)} fusion(bf16[5,6,192,320]{3,2,1,0:T(8,128)(2,1)S(1)} %multiply_convert_fusion, f32[5,1024]{1,0:T(8,128)S(1)} %copy-done.5, f32[5,1024]{1,0:T(8,128)S(1)} %copy-done.6, f32[6,192,1024]{2,1,0:T(8,128)S(1)} %bitcast.45), kind=kOutput, calls=%fused_computation.17 | convolution fusion | flops 3795845120 | bytes 11722752 | tf_op jit(solution)/shard_map/krnd,krno->dko/dot_general | solution.py:236
  98.5 8.2 %copy.22 = bf16[1024,5,320]{2,1,0:T(8,128)(2,1)} copy(bf16[1024,5,320]{0,2,1:T(8,128)(2,1)} %fusion.13) | data formatting | bytes 6553600 | tf_op jit(solution)/shard_map/convert_element_type | solution.py:329
  106.7 9.4 %reshape.212 = bf16[12800,128]{1,0:T(8,128)(2,1)} reshape(bf16[1024,5,320]{2,1,0:T(8,128)(2,1)} %copy.22) | data formatting | bytes 6553600 | tf_op jit(solution)/shard_map/reshape | solution.py:329
  116.1 9.9 %multiply_reduce_fusion = bf16[6,192,1024]{2,1,0:T(8,128)(2,1)S(1)} fusion(f32[5,1024]{1,0:T(8,128)S(1)} %copy-done.6, bf16[5,6,192,320]{3,2,1,0:T(8,128)(2,1)} %copy-done.7, bf16[5,1024,320]{2,1,0:T(8,128)(2,1)} %all-gather.2.cloned.1.call-done), kind=kOutput, calls=%fused_computation | convolution fusion | flops 3785490432 | bytes 9342976 | tf_op jit(solution)/shard_map/krno,kdo->krnd/dot_general | solution.py:234
  126.0 1.6 copy.21
  127.6 30.0 %shard_map.132 = bf16[144,1024]{1,0:T(8,128)(2,1)} custom-call(bf16[8,144,1024]{2,1,0:T(8,128)(2,1)} %bitcast.43), custom_call_target="tpu_custom_call" | custom-call | tf_op jit(solution)/shard_map/pallas_call | solution.py:78
  157.6 37.8 %reduce-scatter.2.cloned.1.call-done = bf16[800,128]{1,0:T(8,128)(2,1)} async-done(((bf16[12800,128]{1,0:T(8,128)(2,1)}), bf16[800,128]{1,0:T(8,128)(2,1)}) %reduce-scatter.2.cloned.1.call-update) | async-done | bytes 204816 | tf_op jit(solution)/shard_map/reduce_scatter | solution.py:330
  195.4 1.3 reshape.216
  196.7 0.9 copy.23
  197.5 1.7 copy.29
  (44 shorter events, 2.8 us)
Async XLA Ops:
  7.2 43.2 %copy-start = (bf16[1024,1024]{1,0:T(8,128)(2,1)S(1)}, bf16[1024,1024]{1,0:T(8,128)(2,1)}, u32[]{:S(2)}) copy-start(bf16[1024,1024]{1,0:T(8,128)(2,1)} %param.14) | copy-start | bytes 6291460
  7.2 72.7 %all-gather.2.cloned.1.call-start = ((), (), s32[]{:S(2)}) async-start(), calls=%async_computation.1 | async-start | bytes 4177920 | tf_op jit(solution)/shard_map/all_gather | solution.py:299
  7.9 187.5 %reduce-scatter.2.cloned.1.call-start = ((), (), s32[]{:S(2)}) async-start(), calls=%async_computation.2 | async-start | bytes 3481600 | tf_op jit(solution)/shard_map/reduce_scatter | solution.py:330
  9.0 9.6 %collective-permute-start.1 = (bf16[3,24,1024]{2,1,0:T(8,128)(2,1)S(1)}, bf16[3,24,1024]{2,1,0:T(8,128)(2,1)S(1)}, u32[]{:S(2)}, u32[]{:S(2)}) collective-permute-start(bf16[3,24,1024]{2,1,0:T(8,128)(2,1)S(1)} %get-tuple-element.13), channel_id=1, source_target_pairs={{8,0},{16,8},{24,16},{32,24},{40,32},{48,40},{56,48},{64,56},{72,6... | collective-permute-start | bytes 442376 | tf_op jit(solution)/shard_map/ppermute | solution.py:178
  10.3 7.3 %collective-permute-start = (bf16[3,24,1024]{2,1,0:T(8,128)(2,1)S(1)}, bf16[3,24,1024]{2,1,0:T(8,128)(2,1)S(1)}, u32[]{:S(2)}, u32[]{:S(2)}) collective-permute-start(bf16[3,24,1024]{2,1,0:T(8,128)(2,1)S(1)} %get-tuple-element.14), channel_id=1, source_target_pairs={{0,8},{8,16},{16,24},{24,32},{32,40},{40,48},{48,56},{56,64},{64,7... | collective-permute-start | bytes 442376 | tf_op jit(solution)/shard_map/ppermute | solution.py:177
  18.6 6.3 %collective-permute-start.2 = (bf16[12,6,1024]{2,1,0:T(8,128)(2,1)S(1)}, bf16[12,6,1024]{2,1,0:T(8,128)(2,1)S(1)}, u32[]{:S(2)}, u32[]{:S(2)}) collective-permute-start(bf16[12,6,1024]{2,1,0:T(8,128)(2,1)S(1)} %get-tuple-element.11), channel_id=1, source_target_pairs={{0,1},{1,2},{2,3},{3,4},{4,5},{5,6},{6,7},{7,0},{8,9},{9,10},{10,1... | collective-permute-start | bytes 442376 | tf_op jit(solution)/shard_map/ppermute | solution.py:177
  18.7 6.3 %collective-permute-start.3 = (bf16[12,6,1024]{2,1,0:T(8,128)(2,1)S(1)}, bf16[12,6,1024]{2,1,0:T(8,128)(2,1)S(1)}, u32[]{:S(2)}, u32[]{:S(2)}) collective-permute-start(bf16[12,6,1024]{2,1,0:T(8,128)(2,1)S(1)} %get-tuple-element.12), channel_id=1, source_target_pairs={{1,0},{2,1},{3,2},{4,3},{5,4},{6,5},{7,6},{0,7},{9,8},{10,9},{11,1... | collective-permute-start | bytes 442376 | tf_op jit(solution)/shard_map/ppermute | solution.py:178
  27.4 4.5 %copy-start.4 = (f32[1024]{0:T(1024)S(1)}, f32[1024]{0:T(1024)}, u32[]{:S(2)}) copy-start(f32[1024]{0:T(1024)} %param.12) | copy-start | bytes 12292
  31.8 4.2 %copy-start.3 = (f32[432,1024]{1,0:T(8,128)S(1)}, f32[432,1024]{1,0:T(8,128)}, u32[]{:S(2)}) copy-start(f32[432,1024]{1,0:T(8,128)} %reshape.214) | copy-start | bytes 5308420
  41.6 10.3 %copy-start.2 = (bf16[6,24,1024]{2,1,0:T(8,128)(2,1)S(1)}, bf16[6,24,1024]{2,1,0:T(8,128)(2,1)}, u32[]{:S(2)}) copy-start(bf16[6,24,1024]{2,1,0:T(8,128)(2,1)} %param.11) | copy-start | bytes 884740
  75.6 4.4 %copy-start.5 = (f32[5,1024]{1,0:T(8,128)S(1)}, f32[5,1024]{1,0:T(8,128)}, u32[]{:S(2)}) copy-start(f32[5,1024]{1,0:T(8,128)} %param.16) | copy-start | bytes 61444
  75.6 4.4 %copy-start.6 = (f32[5,1024]{1,0:T(8,128)S(1)}, f32[5,1024]{1,0:T(8,128)}, u32[]{:S(2)}) copy-start(f32[5,1024]{1,0:T(8,128)} %param.15) | copy-start | bytes 61444
  79.9 12.0 %copy-start.1 = (f32[8,6,24,1024]{3,2,0,1:T(8,128)S(1)}, f32[8,6,24,1024]{3,2,0,1:T(8,128)}, u32[]{:S(2)}) copy-start(f32[8,6,24,1024]{3,2,0,1:T(8,128)} %copy.20) | copy-start | bytes 14155780
  89.8 2.1 %copy-start.7 = (bf16[5,6,192,320]{3,2,1,0:T(8,128)(2,1)}, bf16[5,6,192,320]{3,2,1,0:T(8,128)(2,1)S(1)}, u32[]{:S(2)}) copy-start(bf16[5,6,192,320]{3,2,1,0:T(8,128)(2,1)S(1)} %multiply_convert_fusion) | copy-start | bytes 11059204
Sparse Core Ops, SparseCore 0:
  10.2 52.8 all-gather.1
  116.2 79.1 reduce-scatter.1

commit v8 on v6

--- a/solution.py
+++ b/solution.py
@@ -5,9 +5,10 @@
 from jax import lax
 from jax.experimental import pallas as pl
 from jax.experimental.pallas import tpu as pltpu
-from jax.sharding import PartitionSpec as P
+from jax.sharding import Mesh, PartitionSpec as P
 
 MESH_ID = pl.DeviceIdType.MESH
+LAT = ("lat_hi", "lat_lo")
 
 
 def _greet(axis, n, me):
@@ -159,6 +160,100 @@
         compiler_params=pltpu.CompilerParams(collective_id=cid, has_side_effects=True),
     )(block)
 
+
+def grid_reduce_scatter(parts, outer, inner, cid):
+    slots, n_hi, n_lo, rows, outs = parts.shape
+    half = rows // 2
+
+    def kernel(x_ref, out_ref, r1a, r1b, s1a, s1b, r2a, r2b, send_sem, recv_sem):
+        hi = lax.axis_index(outer)
+        lo = lax.axis_index(inner)
+        barrier = pltpu.get_barrier_semaphore()
+        for k in range(1, n_lo):
+            pl.semaphore_signal(barrier, inc=1, device_id={inner: lax.rem(lo + k, n_lo)},
+                                device_id_type=MESH_ID)
+        for k in range(1, n_hi):
+            pl.semaphore_signal(barrier, inc=1, device_id={outer: lax.rem(hi + k, n_hi)},
+                                device_id_type=MESH_ID)
+        pl.semaphore_wait(barrier, n_lo + n_hi - 2)
+
+        def send(src_ref, dst_ref, axis, dev, group, k, slot):
+            copy = pltpu.make_async_remote_copy(
+                src_ref=src_ref, dst_ref=dst_ref, send_sem=send_sem.at[group, k],
+                recv_sem=recv_sem.at[group, slot], device_id={axis: dev},
+                device_id_type=MESH_ID)
+            copy.start()
+            return copy
+
+        def arrive(dst_ref, group, slot):
+            pltpu.make_async_remote_copy(
+                src_ref=dst_ref, dst_ref=dst_ref, send_sem=send_sem.at[group, 0],
+                recv_sem=recv_sem.at[group, slot], device_id={inner: lo},
+                device_id_type=MESH_ID).wait_recv()
+
+        sends = []
+        for k in range(1, n_lo):
+            dev = lax.rem(lo + k, n_lo)
+            sends.append(send(x_ref.at[:, :, dev, pl.ds(0, half), :], r1a.at[lo], inner, dev, 0, k, lo))
+        for k in range(1, n_hi):
+            dev = lax.rem(hi + k, n_hi)
+            sends.append(send(x_ref.at[:, dev, :, pl.ds(half, half), :], r1b.at[hi], outer, dev, 1, k, hi))
+
+        sources_lo = [lax.rem(lo + n_lo - k, n_lo) for k in range(1, n_lo)]
+        sources_hi = [lax.rem(hi + n_hi - k, n_hi) for k in range(1, n_hi)]
+        for src in sources_lo:
+            arrive(r1a.at[src], 0, src)
+        for h in range(n_hi):
+            total = x_ref[:, h, lo, pl.ds(0, half), :].astype(jnp.float32)
+            for src in sources_lo:
+                total = total + r1a[src, :, h].astype(jnp.float32)
+            s1a[h] = total.astype(s1a.dtype)
+        for k in range(1, n_hi):
+            dev = lax.rem(hi + k, n_hi)
+            sends.append(send(s1a.at[dev], r2a.at[hi], outer, dev, 2, k, hi))
+        for src in sources_hi:
+            arrive(r1b.at[src], 1, src)
+        for l in range(n_lo):
+            total = x_ref[:, hi, l, pl.ds(half, half), :].astype(jnp.float32)
+            for src in sources_hi:
+                total = total + r1b[src, :, l].astype(jnp.float32)
+            s1b[l] = total.astype(s1b.dtype)
+        for k in range(1, n_lo):
+            dev = lax.rem(lo + k, n_lo)
+            sends.append(send(s1b.at[dev], r2b.at[lo], inner, dev, 3, k, lo))
+
+        total = s1a[hi].astype(jnp.float32)
+        for src in sources_hi:
+            arrive(r2a.at[src], 2, src)
+            total = total + r2a[src].astype(jnp.float32)
+        out_ref[:, pl.ds(0, half), :] = total
+        total = s1b[lo].astype(jnp.float32)
+        for src in sources_lo:
+            arrive(r2b.at[src], 3, src)
+            total = total + r2b[src].astype(jnp.float32)
+        out_ref[:, pl.ds(half, half), :] = total
+        for copy in sends:
+            copy.wait_send()
+
+    most = max(n_hi, n_lo)
+    return pl.pallas_call(
+        kernel,
+        out_shape=jax.ShapeDtypeStruct((slots, rows, outs), jnp.float32),
+        in_specs=[pl.BlockSpec(memory_space=pltpu.VMEM)],
+        out_specs=pl.BlockSpec(memory_space=pltpu.VMEM),
+        scratch_shapes=[
+            pltpu.VMEM((n_lo, slots, n_hi, half, outs), parts.dtype),
+            pltpu.VMEM((n_hi, slots, n_lo, half, outs), parts.dtype),
+            pltpu.VMEM((n_hi, slots, half, outs), parts.dtype),
+            pltpu.VMEM((n_lo, slots, half, outs), parts.dtype),
+            pltpu.VMEM((n_hi, slots, half, outs), parts.dtype),
+            pltpu.VMEM((n_lo, slots, half, outs), parts.dtype),
+            pltpu.SemaphoreType.DMA((4, most)),
+            pltpu.SemaphoreType.DMA((4, most)),
+        ],
+        compiler_params=pltpu.CompilerParams(collective_id=cid, has_side_effects=True),
+    )(parts)
+
 HEADS = 16
 WH = 6
 WW = 12
@@ -233,7 +328,7 @@
     )
     back_grad = jnp.einsum("krno,kdo->krnd", errors, heads_full, preferred_element_type=jnp.float32)
     piece_grad = jnp.sum(back_grad * level_scale[:, None, None, :], axis=0)
-    head_add = jnp.einsum("krnd,krno->dko", rows, errors, preferred_element_type=jnp.float32)
+    head_add = jnp.einsum("krnd,krno->kdo", rows, errors, preferred_element_type=jnp.float32)
     return (piece_grad, head_add)
 
 
@@ -253,12 +348,12 @@
     band_rows, band_cols, width = patches.shape
     half_rows = WH // 2
     half_cols = WW // 2
-    lat_count = lax.axis_size("lat")
+    lat_count = lax.axis_size(LAT)
     var_count = lax.axis_size("var")
-    lat_place = lax.axis_index("lat")
+    lat_place = lax.axis_index(LAT)
     ext_rows = band_rows + WH
     ext_cols = band_cols + WW
-    extended = padded(patches, (("lat", 0),), half_rows, False)
+    extended = padded(patches, ((LAT, 0),), half_rows, False)
     extended = padded(extended, (("var", 1),), half_cols, True)
     normed_ext = layer_norm(extended, norm_gain)
     keyval = jnp.dot(
@@ -296,7 +391,7 @@
         jnp.where(dataset_row[:, None] == dataset_ids[None, :], level_counts[None, :], 0), axis=1
     )
     live_tiles = (slot_level[None, :] < tile_levels[:, None]).astype(jnp.float32)
-    heads_full = lax.all_gather(head_weight, "lat", axis=1, tiled=True)
+    heads_full = lax.all_gather(head_weight, LAT, axis=1, tiled=True)
     tile_ids = jnp.arange(var_count, dtype=jnp.int32)
     tiles = chip_pair_gather(latent.reshape(band_rows * band_cols, width), "var", var_count, 1)
     piece = (
@@ -313,37 +408,36 @@
     )
     latent_terms = piece_grad
     latent_terms, head_terms = (latent_terms, head_add)
-    latent_parts = (
-        latent_terms.astype(jnp.bfloat16)
-        .reshape(band_rows, var_count, band_cols, width)
-        .transpose(1, 0, 2, 3)
-        .reshape(var_count, band_rows * band_cols, width)
-    )
-    grad_latent = peer_reduce_scatter(
-        latent_parts, "var", var_count, 2, jnp.bfloat16
-    ).reshape(band_rows, band_cols, width)
+    grad_latent = lax.psum_scatter(
+        latent_terms.astype(jnp.bfloat16), "var", scatter_dimension=1, tiled=True
+    )
     head_terms = head_terms * (1.0 / math.sqrt(lat_count * band_rows * var_count * band_cols))
+    outer, inner = lax.axis_size(LAT[0]), lax.axis_size(LAT[1])
+    slots, outs = head_terms.shape[0], head_terms.shape[2]
     share_rows = width // lat_count
-    mine = lax.psum_scatter(
-        head_terms.astype(jnp.bfloat16), "lat", scatter_dimension=0, tiled=True
-    ).astype(jnp.float32)
-    grad_head = jnp.transpose(mine, (1, 0, 2))
+    head_parts = head_terms.astype(jnp.bfloat16).reshape(slots, outer, inner, share_rows, outs)
+    grad_head = grid_reduce_scatter(head_parts, LAT[0], LAT[1], 3)
     return (latent, grad_latent, grad_head)
 
 
 def solution(mesh):
     in_specs = (
-        P("lat", "var", None),
+        P(LAT, "var", None),
         P(),
         P(),
         P(),
         P("var", None),
         P("var", None),
-        P("var", "lat", None),
-        P("var", "lat", None, None),
+        P("var", LAT, None),
+        P("var", LAT, None, None),
         P(),
-        P("lat", None),
+        P(LAT, None),
         P("var"),
     )
-    out_specs = (P("lat", "var", None), P("lat", "var", None), P("var", "lat", None))
-    return jax.shard_map(local, mesh=mesh, in_specs=in_specs, out_specs=out_specs, check_vma=False)
+    out_specs = (P(LAT, "var", None), P(LAT, "var", None), P("var", LAT, None))
+    lat_size = mesh.shape["lat"]
+    inner = 4 if lat_size % 4 == 0 else 1
+    grid = Mesh(
+        mesh.devices.reshape(lat_size // inner, inner, mesh.shape["var"]), LAT + ("var",)
+    )
+    return jax.shard_map(local, mesh=grid, in_specs=in_specs, out_specs=out_specs, check_vma=False)

time: 203 us -> 170 us (0.84)
  waiting for transfers between devices: 46.5 us -> 3.37 us
  Pallas kernels: 61.7 us -> 75.7 us
  local copies, waits for them, and re-layouts: 25.3 us -> 22.3 us
    reduce_scatter x1 -> x0, waiting for transfers between devices: 43.2 us -> none  [local(): lax.psum_scatter(head_terms.astype(jnp.bfloat16), 'lat', scatter_dimensio...]
    pallas_call x1, Pallas kernels: 30 us -> 43.9 us  [grid_reduce_scatter(): pl.pallas_call(kernel, out_shape=jax.ShapeDtypeStruct((slots, rows, outs)...]
    dot_general x1, matrix products: 6.56 us -> 9.27 us  [slot_terms(): jnp.einsum('krnd,krno->kdo', rows, errors, preferred_element_type=jnp.flo...]
    dot_general x1, matrix products: 9.86 us -> 7.4 us  [slot_terms(): jnp.einsum('krno,kdo->krnd', errors, heads_full, preferred_element_type=j...]
    convert_element_type x1, local copies, waits for them, and re-layouts: 8.16 us -> 5.77 us  [local(): head_terms.astype(jnp.bfloat16)]
    unnamed x20 -> x22, local copies, waits for them, and re-layouts: 5.7 us -> 6.75 us
  transfers between devices with their start and end apart: 6 -> 6, of which waited for: 3 -> 2; matrix products, arithmetic and copies ran while one was open for 20% -> 26% of each run, Pallas kernels for 31% -> 45%
where the time goes in v8:
time: 170 us; the launch traced here: 169 us
  Pallas kernels  75.7 us (45%)
  matrix products  37.2 us (22%)
  local copies, waits for them, and re-layouts  22.3 us (13%)
  between operations  14.3 us (8%)
  starting transfers between devices  8.88 us (5%)
  other arithmetic  7.22 us (4%)
  waiting for transfers between devices  3.37 us (2%)
    pallas_call x1, Pallas kernels, grid_reduce_scatter(): pl.pallas_call(kernel, out_shape=jax.ShapeDtypeStruct((slots, rows, outs)...  43.9 us
    pallas_call x1, Pallas kernels, chip_pair_gather(): pl.pallas_call(kernel, out_shape=jax.ShapeDtypeStruct((n,) + block.shape,...  23 us
    dot_general x1, matrix products, slot_terms(): jnp.einsum('krnd,kdo->krno', rows, heads_full, preferred_element_type=jnp...  9.92 us
    dot_general x1, matrix products, slot_terms(): jnp.einsum('krnd,krno->kdo', rows, errors, preferred_element_type=jnp.flo...  9.27 us
    pallas_call x1, Pallas kernels, masked_window_attention(): pl.pallas_call(kernel, out_shape=jax.ShapeDtypeStruct((nq, width), jnp.bf...  8.79 us
    dot_general x1, matrix products, slot_terms(): jnp.einsum('krno,kdo->krnd', errors, heads_full, preferred_element_type=j...  7.4 us
    unnamed x22, local copies, waits for them, and re-layouts  6.75 us
    convert_element_type x1, local copies, waits for them, and re-layouts, local(): head_terms.astype(jnp.bfloat16)  5.77 us
  transfers between devices with their start and end apart: 6, of which 2 were waited for; matrix products, arithmetic and copies ran while one was open for 26% of the time, Pallas kernels for 45%

profile of v8, /device:TPU:0, one launch (start us, length us, event | category | flops | bytes accessed | tf_op | source)
XLA Modules:
  0.0 168.9 jit_solution(8790061869334076016)
XLA Ops:
  7.2 0.7 all-gather.2.cloned.1.call-update
  8.0 1.0 fusion.36
  9.0 1.3 collective-permute-start.1
  10.3 4.6 %collective-permute-start = (bf16[3,24,1024]{2,1,0:T(8,128)(2,1)S(1)}, bf16[3,24,1024]{2,1,0:T(8,128)(2,1)S(1)}, u32[]{:S(2)}, u32[]{:S(2)}) collective-permute-start(bf16[3,24,1024]{2,1,0:T(8,128)(2,1)S(1)} %get-tuple-element.8), channel_id=1, source_target_pairs={{0,8},{8,16},{16,24},{24,32},{32,40},{40,48},{48,56},{56,64},{64,7... | collective-permute-start | bytes 442376 | tf_op jit(solution)/shard_map/ppermute | solution.py:272
  15.2 0.7 select_n.62.kw_ref
  15.9 0.7 add.124.qw_ref
  16.6 0.8 select_reduce_fusion
  17.6 1.0 constant_dynamic-update-slice_fusion.1
  18.7 2.9 %collective-permute-start.3 = (bf16[12,6,1024]{2,1,0:T(8,128)(2,1)S(1)}, bf16[12,6,1024]{2,1,0:T(8,128)(2,1)S(1)}, u32[]{:S(2)}, u32[]{:S(2)}) collective-permute-start(bf16[12,6,1024]{2,1,0:T(8,128)(2,1)S(1)} %get-tuple-element.6), channel_id=1, source_target_pairs={{1,0},{2,1},{3,2},{4,3},{5,4},{6,5},{7,6},{0,7},{9,8},{10,9},{11,1... | collective-permute-start | bytes 442376 | tf_op jit(solution)/shard_map/ppermute | solution.py:273
  21.6 0.9 fusion.28
  22.5 2.5 %collective-permute-done.2 = bf16[12,6,1024]{2,1,0:T(8,128)(2,1)S(1)} collective-permute-done((bf16[12,6,1024]{2,1,0:T(8,128)(2,1)S(1)}, bf16[12,6,1024]{2,1,0:T(8,128)(2,1)S(1)}, u32[]{:S(2)}, u32[]{:S(2)}) %collective-permute-start.2) | collective-permute-done | bytes 147488 | tf_op jit(solution)/shard_map/ppermute | solution.py:272
  25.0 0.4 fusion.34
  25.5 1.9 %multiply_reduce_fusion.1 = (f32[12,36]{1,0:T(8,128)S(1)}, f32[12,36,1024]{2,1,0:T(8,128)}) fusion(f32[12,36]{1,0:T(8,128)S(1)} %broadcast_multiply_fusion, bf16[12,6,1024]{2,1,0:T(8,128)(2,1)S(1)} %collective-permute-done.3, bf16[12,24,1024]{2,1,0:T(8,128)(2,1)S(1)} %constant_dynamic-update-slice_fusion, bf16[12,6,1024]{2,1,0:T(8,128)(2,1)S(1)} %collective-permute-done.2), kind=kLoop, calls=%fused_computation.20 | loop fusion | flops 3980880 | bytes 2657664 | tf_op jit(solution)/shard_map/reduce_sum | solution.py:282
  27.5 1.6 maximum_convert_fusion
  29.1 2.7 %reshape.198 = f32[432,1024]{1,0:T(8,128)} reshape(f32[12,36,1024]{2,1,0:T(8,128)} %maximum_convert_fusion) | data formatting | bytes 3538944 | tf_op jit(solution)/shard_map/convert_element_type | solution.py:279
  31.8 1.4 fusion.27
  33.3 2.8 %fusion.20.q_ref = bf16[144,1024]{1,0:T(8,128)(2,1)} fusion(bf16[144,1024]{1,0:T(8,128)(2,1)S(1)} %bitcast.47, bf16[1024,3072]{1,0:T(8,128)(2,1)} %param.13), kind=kOutput, calls=%fused_computation.22 | convolution fusion | flops 302137344 | bytes 2686976 | tf_op jit(solution)/shard_map/dot_general | solution.py:364
  36.1 5.5 %fusion.13.kv_ref = bf16[432,2048]{1,0:T(8,128)(2,1)} fusion(bf16[1024,3072]{1,0:T(8,128)(2,1)} %param.13, f32[432,1024]{1,0:T(8,128)S(1)} %copy-done.2, f32[1024]{0:T(1024)S(1)} %copy-done.3, f32[432]{0:T(512)S(1)} %rsqrt.13, f32[432]{0:T(512)S(1)} %div.54), kind=kOutput, calls=%fused_computation.17 | convolution fusion | flops 1814593536 | bytes 7740800 | tf_op jit(solution)/shard_map/dot_general | solution.py:359
  41.6 8.8 %shard_map.130 = bf16[144,1024]{1,0:T(8,128)(2,1)} custom-call(bf16[144,1024]{1,0:T(8,128)(2,1)} %fusion.20.q_ref, bf16[432,2048]{1,0:T(8,128)(2,1)} %fusion.13.kv_ref, s32[144,1]{1,0:T(8,128)} %add.124.qw_ref, s32[1,432]{1,0:T(1,128)} %select_n.62.kw_ref), custom_call_target="tpu_custom_call" | custom-call | tf_op jit(solution)/shard_map/pallas_call | solution.py:109
  50.4 1.4 fusion.37
  51.8 0.8 add_convert_fusion.7
  52.6 23.0 %shard_map.131 = bf16[8,144,1024]{2,1,0:T(8,128)(2,1)} custom-call(bf16[144,1024]{1,0:T(8,128)(2,1)} %bitcast.46), custom_call_target="tpu_custom_call" | custom-call | tf_op jit(solution)/shard_map/pallas_call | solution.py:154
  75.6 4.3 %copy.22 = f32[8,6,24,1024]{3,2,0,1:T(8,128)} copy(bf16[8,6,24,1024]{3,2,1,0:T(8,128)(2,1)} %bitcast.39) | data formatting | bytes 7077888 | tf_op jit(solution)/shard_map/convert_element_type | solution.py:321
  80.0 9.9 %multiply_convert_fusion = bf16[5,6,192,320]{3,2,1,0:T(8,128)(2,1)S(1)} fusion(bf16[5,6,192,320]{3,2,1,0:T(8,128)(2,1)} %param.18, f32[5,192]{1,0:T(8,128)S(1)} %fusion.28, bf16[5,1024,320]{2,1,0:T(8,128)(2,1)} %all-gather.2.cloned.1.call-done, f32[5,1024]{1,0:T(8,128)S(1)} %copy-done.6, f32[5,1024]{1,0:T(8,128)S(1)} %copy-done.5, f32[6,192,1024]{2,1,0:T(8,128)} %bitcast.41), kind=kOutput, calls=%fused_computation.10 | convolution fusion | flops 3799941120 | bytes 15412992 | tf_op jit(solution)/shard_map/krnd,kdo->krno/dot_general | solution.py:325
  89.9 7.4 %multiply_reduce_fusion = bf16[6,192,1024]{2,1,0:T(8,128)(2,1)S(1)} fusion(f32[5,1024]{1,0:T(8,128)S(1)} %copy-done.5, bf16[5,6,192,320]{3,2,1,0:T(8,128)(2,1)S(1)} %multiply_convert_fusion, bf16[5,1024,320]{2,1,0:T(8,128)(2,1)S(1)} %copy-done.4), kind=kOutput, calls=%fused_computation | convolution fusion | flops 3785490432 | bytes 9342976 | tf_op jit(solution)/shard_map/krno,kdo->krnd/dot_general | solution.py:329
  97.4 1.7 copy.28
  99.0 9.3 %fusion.8 = bf16[5,1024,320]{1,2,0:T(8,128)(2,1)} fusion(bf16[5,6,192,320]{3,2,1,0:T(8,128)(2,1)} %copy-done.7, f32[5,1024]{1,0:T(8,128)S(1)} %copy-done.6, f32[5,1024]{1,0:T(8,128)S(1)} %copy-done.5, f32[6,192,1024]{2,1,0:T(8,128)} %bitcast.42), kind=kOutput, calls=%fused_computation.12 | convolution fusion | flops 3795845120 | bytes 11722752 | tf_op jit(solution)/shard_map/krnd,krno->kdo/dot_general | solution.py:331
  108.3 5.8 %copy.23 = bf16[5,1024,320]{2,1,0:T(8,128)(2,1)} copy(bf16[5,1024,320]{1,2,0:T(8,128)(2,1)} %fusion.8) | data formatting | bytes 6553600 | tf_op jit(solution)/shard_map/convert_element_type | solution.py:418
  114.1 43.9 %shard_map.132 = f32[5,64,320]{2,1,0:T(8,128)} custom-call(bf16[5,4,4,64,320]{4,3,2,1,0:T(8,128)(2,1)} %bitcast.38), custom_call_target="tpu_custom_call" | custom-call | tf_op jit(solution)/shard_map/pallas_call | solution.py:239
  158.0 1.3 reshape.204
  159.4 0.9 copy.27
  160.2 1.8 %copy.33 = f32[5,64,320]{2,1,0:T(8,128)} copy(f32[5,64,320]{2,1,0:T(8,128)} %shard_map.132) | data formatting | bytes 819200
  (43 shorter events, 1.1 us)
Async XLA Ops:
  7.2 43.2 %copy-start = (bf16[1024,1024]{1,0:T(8,128)(2,1)S(1)}, bf16[1024,1024]{1,0:T(8,128)(2,1)}, u32[]{:S(2)}) copy-start(bf16[1024,1024]{1,0:T(8,128)(2,1)} %param.14) | copy-start | bytes 6291460
  7.2 72.8 %all-gather.2.cloned.1.call-start = ((), (), s32[]{:S(2)}) async-start(), calls=%async_computation.1 | async-start | bytes 4177920 | tf_op jit(solution)/shard_map/all_gather | solution.py:394
  7.9 150.1 %reduce-scatter.4.cloned.1.call-start = ((), (), s32[]{:S(2)}) async-start(), calls=%async_computation.2 | async-start | bytes 2654208
  9.0 9.6 %collective-permute-start.1 = (bf16[3,24,1024]{2,1,0:T(8,128)(2,1)S(1)}, bf16[3,24,1024]{2,1,0:T(8,128)(2,1)S(1)}, u32[]{:S(2)}, u32[]{:S(2)}) collective-permute-start(bf16[3,24,1024]{2,1,0:T(8,128)(2,1)S(1)} %get-tuple-element.7), channel_id=1, source_target_pairs={{8,0},{16,8},{24,16},{32,24},{40,32},{48,40},{56,48},{64,56},{72,6... | collective-permute-start | bytes 442376 | tf_op jit(solution)/shard_map/ppermute | solution.py:273
  10.3 7.3 %collective-permute-start = (bf16[3,24,1024]{2,1,0:T(8,128)(2,1)S(1)}, bf16[3,24,1024]{2,1,0:T(8,128)(2,1)S(1)}, u32[]{:S(2)}, u32[]{:S(2)}) collective-permute-start(bf16[3,24,1024]{2,1,0:T(8,128)(2,1)S(1)} %get-tuple-element.8), channel_id=1, source_target_pairs={{0,8},{8,16},{16,24},{24,32},{32,40},{40,48},{48,56},{56,64},{64,7... | collective-permute-start | bytes 442376 | tf_op jit(solution)/shard_map/ppermute | solution.py:272
  18.6 6.3 %collective-permute-start.2 = (bf16[12,6,1024]{2,1,0:T(8,128)(2,1)S(1)}, bf16[12,6,1024]{2,1,0:T(8,128)(2,1)S(1)}, u32[]{:S(2)}, u32[]{:S(2)}) collective-permute-start(bf16[12,6,1024]{2,1,0:T(8,128)(2,1)S(1)} %get-tuple-element.5), channel_id=1, source_target_pairs={{0,1},{1,2},{2,3},{3,4},{4,5},{5,6},{6,7},{7,0},{8,9},{9,10},{10,1... | collective-permute-start | bytes 442376 | tf_op jit(solution)/shard_map/ppermute | solution.py:272
  18.7 6.3 %collective-permute-start.3 = (bf16[12,6,1024]{2,1,0:T(8,128)(2,1)S(1)}, bf16[12,6,1024]{2,1,0:T(8,128)(2,1)S(1)}, u32[]{:S(2)}, u32[]{:S(2)}) collective-permute-start(bf16[12,6,1024]{2,1,0:T(8,128)(2,1)S(1)} %get-tuple-element.6), channel_id=1, source_target_pairs={{1,0},{2,1},{3,2},{4,3},{5,4},{6,5},{7,6},{0,7},{9,8},{10,9},{11,1... | collective-permute-start | bytes 442376 | tf_op jit(solution)/shard_map/ppermute | solution.py:273
  27.4 4.5 %copy-start.3 = (f32[1024]{0:T(1024)S(1)}, f32[1024]{0:T(1024)}, u32[]{:S(2)}) copy-start(f32[1024]{0:T(1024)} %param.12) | copy-start | bytes 12292
  31.8 4.2 %copy-start.2 = (f32[432,1024]{1,0:T(8,128)S(1)}, f32[432,1024]{1,0:T(8,128)}, u32[]{:S(2)}) copy-start(f32[432,1024]{1,0:T(8,128)} %reshape.198) | copy-start | bytes 5308420
  41.6 10.3 %copy-start.1 = (bf16[6,24,1024]{2,1,0:T(8,128)(2,1)S(1)}, bf16[6,24,1024]{2,1,0:T(8,128)(2,1)}, u32[]{:S(2)}) copy-start(bf16[6,24,1024]{2,1,0:T(8,128)(2,1)} %param.11) | copy-start | bytes 884740
  75.6 4.4 %copy-start.5 = (f32[5,1024]{1,0:T(8,128)S(1)}, f32[5,1024]{1,0:T(8,128)}, u32[]{:S(2)}) copy-start(f32[5,1024]{1,0:T(8,128)} %param.15) | copy-start | bytes 61444
  75.6 4.4 %copy-start.6 = (f32[5,1024]{1,0:T(8,128)S(1)}, f32[5,1024]{1,0:T(8,128)}, u32[]{:S(2)}) copy-start(f32[5,1024]{1,0:T(8,128)} %param.16) | copy-start | bytes 61444
  80.0 9.9 %copy-start.4 = (bf16[5,1024,320]{2,1,0:T(8,128)(2,1)S(1)}, bf16[5,1024,320]{2,1,0:T(8,128)(2,1)}, u32[]{:S(2)}) copy-start(bf16[5,1024,320]{2,1,0:T(8,128)(2,1)} %all-gather.2.cloned.1.call-done) | copy-start | bytes 9830404
  89.9 7.4 %copy-start.7 = (bf16[5,6,192,320]{3,2,1,0:T(8,128)(2,1)}, bf16[5,6,192,320]{3,2,1,0:T(8,128)(2,1)S(1)}, u32[]{:S(2)}) copy-start(bf16[5,6,192,320]{3,2,1,0:T(8,128)(2,1)S(1)} %multiply_convert_fusion) | copy-start | bytes 11059204
Sparse Core Ops, SparseCore 0:
  10.2 52.8 all-gather.1
  99.2 38.0 reduce-scatter.3

commit v9 on v8

--- a/solution.py
+++ b/solution.py
@@ -317,18 +317,25 @@
     )
 
 
-def slot_terms(piece, target_rows, live_cols, level_scale, level_shift, heads_full):
-    piece_wide = piece.astype(jnp.float32)
+def slot_terms(tiles, target_rows, live, level_scale, level_shift, heads_full):
+    n_tiles, per_tile, _ = tiles.shape
+    slots, band_rows, _, outs = target_rows.shape
+    targets_t = (
+        target_rows.reshape(slots, band_rows, n_tiles, per_tile // band_rows, outs)
+        .transpose(0, 2, 1, 3, 4)
+        .reshape(slots, n_tiles, per_tile, outs)
+    )
     rows = (
-        piece_wide[None] * level_scale[:, None, None, :] + level_shift[:, None, None, :]
+        tiles.astype(jnp.float32)[None] * level_scale[:, None, None, :]
+        + level_shift[:, None, None, :]
     ).astype(jnp.bfloat16)
-    predicted = jnp.einsum("krnd,kdo->krno", rows, heads_full, preferred_element_type=jnp.float32)
-    errors = ((predicted - target_rows.astype(jnp.float32)) * live_cols[:, None, :, None]).astype(
+    predicted = jnp.einsum("ktnd,kdo->ktno", rows, heads_full, preferred_element_type=jnp.float32)
+    errors = ((predicted - targets_t.astype(jnp.float32)) * live[:, :, None, None]).astype(
         jnp.bfloat16
     )
-    back_grad = jnp.einsum("krno,kdo->krnd", errors, heads_full, preferred_element_type=jnp.float32)
+    back_grad = jnp.einsum("ktno,kdo->ktnd", errors, heads_full, preferred_element_type=jnp.float32)
     piece_grad = jnp.sum(back_grad * level_scale[:, None, None, :], axis=0)
-    head_add = jnp.einsum("krnd,krno->kdo", rows, errors, preferred_element_type=jnp.float32)
+    head_add = jnp.einsum("ktnd,ktno->kdo", rows, errors, preferred_element_type=jnp.float32)
     return (piece_grad, head_add)
 
 
@@ -392,25 +399,14 @@
     )
     live_tiles = (slot_level[None, :] < tile_levels[:, None]).astype(jnp.float32)
     heads_full = lax.all_gather(head_weight, LAT, axis=1, tiled=True)
-    tile_ids = jnp.arange(var_count, dtype=jnp.int32)
     tiles = chip_pair_gather(latent.reshape(band_rows * band_cols, width), "var", var_count, 1)
-    piece = (
-        tiles.reshape(var_count, band_rows, band_cols, width)
-        .transpose(1, 0, 2, 3)
-        .reshape(band_rows, var_count * band_cols, width)
-    )
-    piece_cols = piece.shape[1]
-    column_tile = jnp.arange(piece_cols, dtype=jnp.int32) // band_cols
-    onehot = (column_tile[:, None] == tile_ids[None, :]).astype(jnp.float32)
-    column_live = jnp.dot(onehot, live_tiles)
     piece_grad, head_add = slot_terms(
-        piece, targets, column_live.T, level_scale, level_shift, heads_full
-    )
-    latent_terms = piece_grad
-    latent_terms, head_terms = (latent_terms, head_add)
+        tiles, targets, live_tiles.T, level_scale, level_shift, heads_full
+    )
     grad_latent = lax.psum_scatter(
-        latent_terms.astype(jnp.bfloat16), "var", scatter_dimension=1, tiled=True
-    )
+        piece_grad.astype(jnp.bfloat16), "var", scatter_dimension=0, tiled=True
+    ).reshape(band_rows, band_cols, width)
+    head_terms = head_add
     head_terms = head_terms * (1.0 / math.sqrt(lat_count * band_rows * var_count * band_cols))
     outer, inner = lax.axis_size(LAT[0]), lax.axis_size(LAT[1])
     slots, outs = head_terms.shape[0], head_terms.shape[2]

time: 170 us -> 172 us (1.012)
  other arithmetic: 7.22 us -> 11.1 us
  Pallas kernels: 75.7 us -> 72.5 us
    convert_element_type x0 -> x2, other arithmetic: none -> 4.49 us  [the longest x1 4.42 us: slot_terms(): tiles.astype(jnp.float32)[None] * level_scale[:, None, None, :]]
    pallas_call x1, Pallas kernels: 43.9 us -> 40.8 us  [grid_reduce_scatter(): pl.pallas_call(kernel, out_shape=jax.ShapeDtypeStruct((slots, rows, outs)...]
    unnamed x22 -> x25, local copies, waits for them, and re-layouts: 6.75 us -> 3.92 us
    convert_element_type x1, local copies, waits for them, and re-layouts: 4.33 us -> 6.49 us  [slot_terms(): targets_t.astype(jnp.float32)]
    dot_general x4 -> x3, matrix products: 27.5 us -> 28.9 us  [the longest x1 10.8 us: slot_terms(): jnp.einsum('ktnd,kdo->ktno', rows, heads_full, preferred_element_type=jnp...]
  transfers between devices with their start and end apart: 6 -> 6, of which waited for: 2 -> 1; matrix products, arithmetic and copies ran while one was open for 26% -> 28% of each run, Pallas kernels for 45% -> 42%
where the time goes in v9:
time: 172 us; the launch traced here: 171 us
  Pallas kernels  72.5 us (42%)
  matrix products  38.7 us (23%)
  local copies, waits for them, and re-layouts  21.7 us (13%)
  between operations  14.3 us (8%)
  other arithmetic  11.1 us (6%)
  starting transfers between devices  8.95 us (5%)
  waiting for transfers between devices  3.98 us (2%)
    pallas_call x1, Pallas kernels, grid_reduce_scatter(): pl.pallas_call(kernel, out_shape=jax.ShapeDtypeStruct((slots, rows, outs)...  40.8 us
    pallas_call x1, Pallas kernels, chip_pair_gather(): pl.pallas_call(kernel, out_shape=jax.ShapeDtypeStruct((n,) + block.shape,...  23 us
    dot_general x1, matrix products, slot_terms(): jnp.einsum('ktnd,kdo->ktno', rows, heads_full, preferred_element_type=jnp...  10.8 us
    dot_general x1, matrix products, slot_terms(): jnp.einsum('ktnd,ktno->kdo', rows, errors, preferred_element_type=jnp.flo...  9.32 us
    dot_general x1, matrix products, slot_terms(): jnp.einsum('ktno,kdo->ktnd', errors, heads_full, preferred_element_type=j...  8.85 us
    pallas_call x1, Pallas kernels, masked_window_attention(): pl.pallas_call(kernel, out_shape=jax.ShapeDtypeStruct((nq, width), jnp.bf...  8.75 us
    convert_element_type x1, local copies, waits for them, and re-layouts, slot_terms(): targets_t.astype(jnp.float32)  6.49 us
    convert_element_type x1, local copies, waits for them, and re-layouts, local(): head_terms.astype(jnp.bfloat16)  5.88 us
  transfers between devices with their start and end apart: 6, of which 1 were waited for; matrix products, arithmetic and copies ran while one was open for 28% of the time, Pallas kernels for 42%

profile of v9, /device:TPU:0, one launch (start us, length us, event | category | flops | bytes accessed | tf_op | source)
XLA Modules:
  0.0 171.1 jit_solution(2673641800565360314)
XLA Ops:
  7.2 0.7 all-gather.2.cloned.1.call-update
  8.0 1.0 fusion.34
  9.0 1.3 collective-permute-start.1
  10.3 4.6 %collective-permute-start = (bf16[3,24,1024]{2,1,0:T(8,128)(2,1)S(1)}, bf16[3,24,1024]{2,1,0:T(8,128)(2,1)S(1)}, u32[]{:S(2)}, u32[]{:S(2)}) collective-permute-start(bf16[3,24,1024]{2,1,0:T(8,128)(2,1)S(1)} %get-tuple-element.8), channel_id=1, source_target_pairs={{0,8},{8,16},{16,24},{24,32},{32,40},{40,48},{48,56},{56,64},{64,7... | collective-permute-start | bytes 442376 | tf_op jit(solution)/shard_map/ppermute | solution.py:272
  15.0 0.1 multiply_bitcast_fusion
  15.2 0.6 select_n.53.kw_ref
  15.8 0.7 add.119.qw_ref
  16.6 6.5 %copy.20 = f32[5,6,8,24,320]{4,3,1,2,0:T(8,128)} copy(bf16[5,6,8,24,320]{4,3,2,1,0:T(8,128)(2,1)} %bitcast.40) | data formatting | bytes 11059200 | tf_op jit(solution)/shard_map/convert_element_type | solution.py:333
  23.1 0.1 select_reduce_fusion
  23.3 3.0 %collective-permute-start.3 = (bf16[12,6,1024]{2,1,0:T(8,128)(2,1)S(1)}, bf16[12,6,1024]{2,1,0:T(8,128)(2,1)S(1)}, u32[]{:S(2)}, u32[]{:S(2)}) collective-permute-start(bf16[12,6,1024]{2,1,0:T(8,128)(2,1)S(1)} %get-tuple-element.6), channel_id=1, source_target_pairs={{1,0},{2,1},{3,2},{4,3},{5,4},{6,5},{7,6},{0,7},{9,8},{10,9},{11,1... | collective-permute-start | bytes 442376 | tf_op jit(solution)/shard_map/ppermute | solution.py:273
  26.4 3.3 %collective-permute-done.2 = bf16[12,6,1024]{2,1,0:T(8,128)(2,1)S(1)} collective-permute-done((bf16[12,6,1024]{2,1,0:T(8,128)(2,1)S(1)}, bf16[12,6,1024]{2,1,0:T(8,128)(2,1)S(1)}, u32[]{:S(2)}, u32[]{:S(2)}) %collective-permute-start.2) | collective-permute-done | bytes 147488 | tf_op jit(solution)/shard_map/ppermute | solution.py:272
  29.7 0.4 fusion.32
  30.1 0.1 div.44
  30.2 1.9 %multiply_reduce_fusion.1 = (f32[12,36]{1,0:T(8,128)S(1)}, f32[12,36,1024]{2,1,0:T(8,128)}) fusion(f32[12,36]{1,0:T(8,128)S(1)} %broadcast_multiply_fusion, bf16[12,6,1024]{2,1,0:T(8,128)(2,1)S(1)} %collective-permute-done.3, bf16[12,24,1024]{2,1,0:T(8,128)(2,1)S(1)} %constant_dynamic-update-slice_fusion, bf16[12,6,1024]{2,1,0:T(8,128)(2,1)S(1)} %collective-permute-done.2), kind=kLoop, calls=%fused_computation.22 | loop fusion | flops 3980880 | bytes 2657664 | tf_op jit(solution)/shard_map/reduce_sum | solution.py:282
  32.1 0.1 rsqrt.13
  32.2 1.6 maximum_convert_fusion
  33.9 2.7 %reshape.210 = f32[432,1024]{1,0:T(8,128)} reshape(f32[12,36,1024]{2,1,0:T(8,128)} %maximum_convert_fusion) | data formatting | bytes 3538944 | tf_op jit(solution)/shard_map/convert_element_type | solution.py:279
  36.6 1.4 fusion.29
  38.0 2.8 %fusion.22.q_ref = bf16[144,1024]{1,0:T(8,128)(2,1)} fusion(bf16[144,1024]{1,0:T(8,128)(2,1)S(1)} %bitcast.43, bf16[1024,3072]{1,0:T(8,128)(2,1)} %param.13), kind=kOutput, calls=%fused_computation.24 | convolution fusion | flops 302137344 | bytes 2686976 | tf_op jit(solution)/shard_map/dot_general | solution.py:371
  40.8 5.5 %fusion.15.kv_ref = bf16[432,2048]{1,0:T(8,128)(2,1)} fusion(bf16[1024,3072]{1,0:T(8,128)(2,1)} %param.13, f32[432,1024]{1,0:T(8,128)S(1)} %copy-done.2, f32[1024]{0:T(1024)S(1)} %copy-done.3, f32[432]{0:T(512)S(1)} %rsqrt.13, f32[432]{0:T(512)S(1)} %div.44), kind=kOutput, calls=%fused_computation.19 | convolution fusion | flops 1814593536 | bytes 7740800 | tf_op jit(solution)/shard_map/dot_general | solution.py:366
  46.3 8.8 %shard_map.130 = bf16[144,1024]{1,0:T(8,128)(2,1)} custom-call(bf16[144,1024]{1,0:T(8,128)(2,1)} %fusion.22.q_ref, bf16[432,2048]{1,0:T(8,128)(2,1)} %fusion.15.kv_ref, s32[144,1]{1,0:T(8,128)} %add.119.qw_ref, s32[1,432]{1,0:T(1,128)} %select_n.53.kw_ref), custom_call_target="tpu_custom_call" | custom-call | tf_op jit(solution)/shard_map/pallas_call | solution.py:109
  55.1 1.4 fusion.35
  56.5 0.8 add_convert_fusion.7
  57.3 23.0 %shard_map.131 = bf16[8,144,1024]{2,1,0:T(8,128)(2,1)} custom-call(bf16[144,1024]{1,0:T(8,128)(2,1)} %bitcast.42), custom_call_target="tpu_custom_call" | custom-call | tf_op jit(solution)/shard_map/pallas_call | solution.py:154
  80.3 4.4 %convert_element_type.71 = f32[8,144,1024]{2,1,0:T(8,128)} convert(bf16[8,144,1024]{2,1,0:T(8,128)(2,1)} %shard_map.131) | non-fusion elementwise | flops 1179648 | bytes 7077888 | tf_op jit(solution)/shard_map/convert_element_type | solution.py:329
  84.7 10.8 %fusion.9 = bf16[5,8,144,320]{3,2,1,0:T(8,128)(2,1)S(1)} fusion(f32[5,6,8,24,320]{4,3,1,2,0:T(8,128)} %copy.20, f32[5,8]{1,0:T(8,128)S(1)} %compare_convert_fusion, bf16[5,1024,320]{2,1,0:T(8,128)(2,1)} %all-gather.2.cloned.1.call-done, f32[5,1024]{1,0:T(8,128)S(1)} %copy-done.7, f32[5,1024]{1,0:T(8,128)S(1)} %copy-done.6, ...), kind=kOutput, calls=%fused_computation.12 | convolution fusion | flops 3798097920 | bytes 19095712 | tf_op jit(solution)/shard_map/ktnd,kdo->ktno/dot_general | solution.py:332
  95.5 2.0 %copy-done.10 = bf16[5,8,144,320]{3,2,1,0:T(8,128)(2,1)} copy-done((bf16[5,8,144,320]{3,2,1,0:T(8,128)(2,1)}, bf16[5,8,144,320]{3,2,1,0:T(8,128)(2,1)S(1)}, u32[]{:S(2)}) %copy-start.10) | copy-done | bytes 3686424
  97.5 8.8 %multiply_reduce_fusion = bf16[8,144,1024]{2,1,0:T(8,128)(2,1)} fusion(f32[5,1024]{1,0:T(8,128)S(1)} %copy-done.6, bf16[5,8,144,320]{3,2,1,0:T(8,128)(2,1)S(1)} %fusion.9, bf16[5,1024,320]{2,1,0:T(8,128)(2,1)S(1)} %copy-done.5), kind=kOutput, calls=%fused_computation | convolution fusion | flops 3785490432 | bytes 9342976 | tf_op jit(solution)/shard_map/ktno,kdo->ktnd/dot_general | solution.py:336
  106.4 9.3 %fusion.10 = bf16[5,1024,320]{1,2,0:T(8,128)(2,1)} fusion(bf16[5,8,144,320]{3,2,1,0:T(8,128)(2,1)} %copy-done.10, f32[5,1024]{1,0:T(8,128)S(1)} %copy-done.7, f32[5,1024]{1,0:T(8,128)S(1)} %copy-done.6, f32[8,144,1024]{2,1,0:T(8,128)} %convert_element_type.71), kind=kOutput, calls=%fused_computation.14 | convolution fusion | flops 3795845120 | bytes 11722752 | tf_op jit(solution)/shard_map/ktnd,ktno->kdo/dot_general | solution.py:338
  115.7 5.9 %copy.21 = bf16[5,1024,320]{2,1,0:T(8,128)(2,1)} copy(bf16[5,1024,320]{1,2,0:T(8,128)(2,1)} %fusion.10) | data formatting | bytes 6553600 | tf_op jit(solution)/shard_map/convert_element_type | solution.py:414
  121.6 40.8 %shard_map.132 = f32[5,64,320]{2,1,0:T(8,128)} custom-call(bf16[5,4,4,64,320]{4,3,2,1,0:T(8,128)(2,1)} %bitcast.39), custom_call_target="tpu_custom_call" | custom-call | tf_op jit(solution)/shard_map/pallas_call | solution.py:239
  162.4 1.8 %copy.27 = f32[5,64,320]{2,1,0:T(8,128)} copy(f32[5,64,320]{2,1,0:T(8,128)} %shard_map.132) | data formatting | bytes 819200
  (46 shorter events, 0.7 us)
Async XLA Ops:
  7.2 47.9 %copy-start = (bf16[1024,1024]{1,0:T(8,128)(2,1)S(1)}, bf16[1024,1024]{1,0:T(8,128)(2,1)}, u32[]{:S(2)}) copy-start(bf16[1024,1024]{1,0:T(8,128)(2,1)} %param.14) | copy-start | bytes 6291460
  7.2 77.6 %all-gather.2.cloned.1.call-start = ((), (), s32[]{:S(2)}) async-start(), calls=%async_computation.1 | async-start | bytes 4177920 | tf_op jit(solution)/shard_map/all_gather | solution.py:401
  7.9 154.5 %reduce-scatter.2.cloned.1.call-start = ((), (), s32[]{:S(2)}) async-start(), calls=%async_computation.2 | async-start | bytes 2654208 | tf_op jit(solution)/shard_map/reduce_scatter | solution.py:406
  9.0 14.3 %collective-permute-start.1 = (bf16[3,24,1024]{2,1,0:T(8,128)(2,1)S(1)}, bf16[3,24,1024]{2,1,0:T(8,128)(2,1)S(1)}, u32[]{:S(2)}, u32[]{:S(2)}) collective-permute-start(bf16[3,24,1024]{2,1,0:T(8,128)(2,1)S(1)} %get-tuple-element.7), channel_id=1, source_target_pairs={{8,0},{16,8},{24,16},{32,24},{40,32},{48,40},{56,48},{64,56},{72,6... | collective-permute-start | bytes 442376 | tf_op jit(solution)/shard_map/ppermute | solution.py:273
  10.3 12.9 %collective-permute-start = (bf16[3,24,1024]{2,1,0:T(8,128)(2,1)S(1)}, bf16[3,24,1024]{2,1,0:T(8,128)(2,1)S(1)}, u32[]{:S(2)}, u32[]{:S(2)}) collective-permute-start(bf16[3,24,1024]{2,1,0:T(8,128)(2,1)S(1)} %get-tuple-element.8), channel_id=1, source_target_pairs={{0,8},{8,16},{16,24},{24,32},{32,40},{40,48},{48,56},{56,64},{64,7... | collective-permute-start | bytes 442376 | tf_op jit(solution)/shard_map/ppermute | solution.py:272
  16.6 6.5 %copy-start.8 = (s32[4]{0:T(128)S(1)}, s32[4]{0:T(128)}, u32[]{:S(2)}) copy-start(s32[4]{0:T(128)} %param.19) | copy-start | bytes 52
  16.6 6.5 %copy-start.9 = (s32[1,8]{1,0:T(1,128)S(1)}, s32[1,8]{1,0:T(1,128)}, u32[]{:S(2)}) copy-start(s32[1,8]{1,0:T(1,128)} %param.20) | copy-start | bytes 100
  16.6 6.6 %copy-start.1 = (bf16[6,24,1024]{2,1,0:T(8,128)(2,1)S(1)}, bf16[6,24,1024]{2,1,0:T(8,128)(2,1)}, u32[]{:S(2)}) copy-start(bf16[6,24,1024]{2,1,0:T(8,128)(2,1)} %param.11) | copy-start | bytes 884740
  16.6 9.8 %copy-start.4 = (s32[5]{0:T(128)S(1)}, s32[5]{0:T(128)}, u32[]{:S(2)}) copy-start(s32[5]{0:T(128)} %param.21) | copy-start | bytes 64
  23.3 6.4 %collective-permute-start.2 = (bf16[12,6,1024]{2,1,0:T(8,128)(2,1)S(1)}, bf16[12,6,1024]{2,1,0:T(8,128)(2,1)S(1)}, u32[]{:S(2)}, u32[]{:S(2)}) collective-permute-start(bf16[12,6,1024]{2,1,0:T(8,128)(2,1)S(1)} %get-tuple-element.5), channel_id=1, source_target_pairs={{0,1},{1,2},{2,3},{3,4},{4,5},{5,6},{6,7},{7,0},{8,9},{9,10},{10,1... | collective-permute-start | bytes 442376 | tf_op jit(solution)/shard_map/ppermute | solution.py:272
  23.3 6.3 %collective-permute-start.3 = (bf16[12,6,1024]{2,1,0:T(8,128)(2,1)S(1)}, bf16[12,6,1024]{2,1,0:T(8,128)(2,1)S(1)}, u32[]{:S(2)}, u32[]{:S(2)}) collective-permute-start(bf16[12,6,1024]{2,1,0:T(8,128)(2,1)S(1)} %get-tuple-element.6), channel_id=1, source_target_pairs={{1,0},{2,1},{3,2},{4,3},{5,4},{6,5},{7,6},{0,7},{9,8},{10,9},{11,1... | collective-permute-start | bytes 442376 | tf_op jit(solution)/shard_map/ppermute | solution.py:273
  32.1 4.5 %copy-start.3 = (f32[1024]{0:T(1024)S(1)}, f32[1024]{0:T(1024)}, u32[]{:S(2)}) copy-start(f32[1024]{0:T(1024)} %param.12) | copy-start | bytes 12292
  36.6 4.2 %copy-start.2 = (f32[432,1024]{1,0:T(8,128)S(1)}, f32[432,1024]{1,0:T(8,128)}, u32[]{:S(2)}) copy-start(f32[432,1024]{1,0:T(8,128)} %reshape.210) | copy-start | bytes 5308420
  80.3 4.5 %copy-start.6 = (f32[5,1024]{1,0:T(8,128)S(1)}, f32[5,1024]{1,0:T(8,128)}, u32[]{:S(2)}) copy-start(f32[5,1024]{1,0:T(8,128)} %param.15) | copy-start | bytes 61444
  80.3 4.4 %copy-start.7 = (f32[5,1024]{1,0:T(8,128)S(1)}, f32[5,1024]{1,0:T(8,128)}, u32[]{:S(2)}) copy-start(f32[5,1024]{1,0:T(8,128)} %param.16) | copy-start | bytes 61444
  84.7 12.8 %copy-start.5 = (bf16[5,1024,320]{2,1,0:T(8,128)(2,1)S(1)}, bf16[5,1024,320]{2,1,0:T(8,128)(2,1)}, u32[]{:S(2)}) copy-start(bf16[5,1024,320]{2,1,0:T(8,128)(2,1)} %all-gather.2.cloned.1.call-done) | copy-start | bytes 9830404
  95.5 2.0 %copy-start.10 = (bf16[5,8,144,320]{3,2,1,0:T(8,128)(2,1)}, bf16[5,8,144,320]{3,2,1,0:T(8,128)(2,1)S(1)}, u32[]{:S(2)}) copy-start(bf16[5,8,144,320]{3,2,1,0:T(8,128)(2,1)S(1)} %fusion.9) | copy-start | bytes 11059204
Sparse Core Ops, SparseCore 0:
  10.2 52.8 all-gather.1
  106.5 36.7 reduce-scatter.1

commit v10 on v8

--- a/solution.py
+++ b/solution.py
@@ -353,30 +353,35 @@
     lat_place = lax.axis_index(LAT)
     ext_rows = band_rows + WH
     ext_cols = band_cols + WW
+    own_normed = layer_norm(patches, norm_gain).reshape(-1, width)
+    queries = jnp.dot(own_normed, input_proj[:, :width], preferred_element_type=jnp.float32)
+    queries = queries.astype(jnp.bfloat16)
+    own_keyval = jnp.dot(own_normed, input_proj[:, width:], preferred_element_type=jnp.float32)
     extended = padded(patches, ((LAT, 0),), half_rows, False)
     extended = padded(extended, (("var", 1),), half_cols, True)
-    normed_ext = layer_norm(extended, norm_gain)
-    keyval = jnp.dot(
-        normed_ext.reshape(-1, width), input_proj[:, width:], preferred_element_type=jnp.float32
-    )
-    keyval = keyval.astype(jnp.bfloat16).reshape(ext_rows, ext_cols, 2 * width)
-    normed = normed_ext[half_rows : half_rows + band_rows, half_cols : half_cols + band_cols]
-    queries = jnp.dot(
-        normed.reshape(-1, width), input_proj[:, :width], preferred_element_type=jnp.float32
-    )
-    queries = queries.astype(jnp.bfloat16)
+
+    def ring(grid):
+        top, bottom = grid[:half_rows], grid[half_rows + band_rows :]
+        middle = grid[half_rows : half_rows + band_rows]
+        left, right = middle[:, :half_cols], middle[:, half_cols + band_cols :]
+        return jnp.concatenate(
+            [part.reshape((-1,) + grid.shape[2:]) for part in (top, bottom, left, right)]
+        )
+
+    halo_normed = layer_norm(ring(extended), norm_gain)
+    halo_keyval = jnp.dot(halo_normed, input_proj[:, width:], preferred_element_type=jnp.float32)
+    keyval = jnp.concatenate([own_keyval, halo_keyval]).astype(jnp.bfloat16)
     global_row = lat_place * band_rows - half_rows + jnp.arange(ext_rows, dtype=jnp.int32)
     row_valid = (global_row >= 0) & (global_row < lat_count * band_rows)
     win_cols = ext_cols // WW
     ext_r = jnp.arange(ext_rows, dtype=jnp.int32)[:, None]
     ext_c = jnp.arange(ext_cols, dtype=jnp.int32)[None, :]
-    key_win = jnp.where(row_valid[:, None], (ext_r // WH) * win_cols + ext_c // WW, -1)
-    own_r = ext_r[half_rows : half_rows + band_rows]
-    own_c = ext_c[:, half_cols : half_cols + band_cols]
-    query_win = (own_r // WH) * win_cols + own_c // WW
+    key_grid = jnp.where(row_valid[:, None], (ext_r // WH) * win_cols + ext_c // WW, -1)
+    query_win = key_grid[half_rows : half_rows + band_rows, half_cols : half_cols + band_cols]
+    key_win = jnp.concatenate([query_win.reshape(-1), ring(key_grid)])
     attn = masked_window_attention(
         queries,
-        keyval.reshape(ext_rows * ext_cols, 2 * width),
+        keyval,
         query_win.reshape(-1, 1),
         key_win.reshape(1, -1),
         HEADS,

time: 170 us -> 170 us (level)
  Pallas kernels: 75.7 us -> 71.9 us
  matrix products: 37.2 us -> 40 us
  other arithmetic: 7.22 us -> 9.27 us
    convert_element_type x1 -> x0, local copies, waits for them, and re-layouts: 2.71 us -> none  [layer_norm(): wide = values.astype(jnp.float32)]
    pallas_call x1, Pallas kernels: 43.9 us -> 41.2 us  [grid_reduce_scatter(): pl.pallas_call(kernel, out_shape=jax.ShapeDtypeStruct((slots, rows, outs)...]
    dot_general x2 -> x3, matrix products: 8.31 us -> 10.6 us  [the longest x1 3.97 us: local(): jnp.dot(own_normed, input_proj[:, width:], preferred_element_type=jnp.flo...]
    reshape x0 -> x10, local copies, waits for them, and re-layouts: none -> 1.88 us  [the longest x8 1.07 us: ring(): part.reshape((-1,) + grid.shape[2:])]
    reduce_sum x1 -> x2, other arithmetic: 0.44 us -> 2.19 us  [layer_norm(): average = jnp.mean(wide, axis=-1, keepdims=True)]
    unnamed x22 -> x32, local copies, waits for them, and re-layouts: 6.75 us -> 7.15 us
  transfers between devices with their start and end apart: 6 -> 6, of which waited for: 2 -> 1; matrix products, arithmetic and copies ran while one was open for 26% -> 27% of each run, Pallas kernels for 45% -> 43%
where the time goes in v10:
time: 170 us; the launch traced here: 169 us
  Pallas kernels  71.9 us (42%)
  matrix products  40 us (24%)
  local copies, waits for them, and re-layouts  21.1 us (12%)
  between operations  14.4 us (8%)
  other arithmetic  9.27 us (5%)
  starting transfers between devices  8.97 us (5%)
  waiting for transfers between devices  3.2 us (2%)
    pallas_call x1, Pallas kernels, grid_reduce_scatter(): pl.pallas_call(kernel, out_shape=jax.ShapeDtypeStruct((slots, rows, outs)...  41.2 us
    pallas_call x1, Pallas kernels, chip_pair_gather(): pl.pallas_call(kernel, out_shape=jax.ShapeDtypeStruct((n,) + block.shape,...  21.9 us
    dot_general x1, matrix products, slot_terms(): jnp.einsum('krnd,kdo->krno', rows, heads_full, preferred_element_type=jnp...  10.6 us
    dot_general x1, matrix products, slot_terms(): jnp.einsum('krnd,krno->kdo', rows, errors, preferred_element_type=jnp.flo...  9.26 us
    pallas_call x1, Pallas kernels, masked_window_attention(): pl.pallas_call(kernel, out_shape=jax.ShapeDtypeStruct((nq, width), jnp.bf...  8.75 us
    dot_general x1, matrix products, slot_terms(): jnp.einsum('krno,kdo->krnd', errors, heads_full, preferred_element_type=j...  7.22 us
    unnamed x32, local copies, waits for them, and re-layouts  7.15 us
    convert_element_type x1, local copies, waits for them, and re-layouts, local(): head_terms.astype(jnp.bfloat16)  5.79 us
  transfers between devices with their start and end apart: 6, of which 1 were waited for; matrix products, arithmetic and copies ran while one was open for 27% of the time, Pallas kernels for 43%

profile of v10, /device:TPU:0, one launch (start us, length us, event | category | flops | bytes accessed | tf_op | source)
XLA Modules:
  0.0 168.8 jit_solution(9334387449701420266)
XLA Ops:
  8.0 1.0 fusion.49
  9.0 1.3 collective-permute-start.1
  10.3 4.6 %collective-permute-start = (bf16[3,24,1024]{2,1,0:T(8,128)(2,1)S(1)}, bf16[3,24,1024]{2,1,0:T(8,128)(2,1)S(1)}, u32[]{:S(2)}, u32[]{:S(2)}) collective-permute-start(bf16[3,24,1024]{2,1,0:T(8,128)(2,1)S(1)} %get-tuple-element.8), channel_id=1, source_target_pairs={{0,8},{8,16},{16,24},{24,32},{32,40},{40,48},{48,56},{56,64},{64,7... | collective-permute-start | bytes 442376 | tf_op jit(solution)/shard_map/ppermute | solution.py:272
  14.9 1.1 convert_reduce_fusion.1
  16.0 1.2 fusion.35
  17.3 1.2 fusion.37
  18.5 2.8 %fusion.27.q_ref = bf16[144,1024]{1,0:T(8,128)(2,1)} fusion(bf16[144,1024]{1,0:T(8,128)(2,1)S(1)} %bitcast.45, bf16[1024,3072]{1,0:T(8,128)(2,1)} %param.13), kind=kOutput, calls=%fused_computation.28 | convolution fusion | flops 302137344 | bytes 2686976 | tf_op jit(solution)/shard_map/dot_general | solution.py:357
  21.3 4.0 %fusion.18 = bf16[144,2048]{1,0:T(8,128)(2,1)} fusion(bf16[144,1024]{1,0:T(8,128)(2,1)S(1)} %bitcast.46, bf16[1024,3072]{1,0:T(8,128)(2,1)} %param.13), kind=kOutput, calls=%fused_computation.20 | convolution fusion | flops 604274688 | bytes 5079040 | tf_op jit(solution)/shard_map/dot_general | solution.py:359
  25.5 0.7 reshape.182.qw_ref
  26.5 0.7 concatenate.20
  27.5 3.0 %collective-permute-start.3 = (bf16[12,6,1024]{2,1,0:T(8,128)(2,1)S(1)}, bf16[12,6,1024]{2,1,0:T(8,128)(2,1)S(1)}, u32[]{:S(2)}, u32[]{:S(2)}) collective-permute-start(bf16[12,6,1024]{2,1,0:T(8,128)(2,1)S(1)} %get-tuple-element.6), channel_id=1, source_target_pairs={{1,0},{2,1},{3,2},{4,3},{5,4},{6,5},{7,6},{0,7},{9,8},{10,9},{11,1... | collective-permute-start | bytes 442376 | tf_op jit(solution)/shard_map/ppermute | solution.py:273
  30.5 0.9 fusion.43
  31.4 2.5 %collective-permute-done.2 = bf16[12,6,1024]{2,1,0:T(8,128)(2,1)S(1)} collective-permute-done((bf16[12,6,1024]{2,1,0:T(8,128)(2,1)S(1)}, bf16[12,6,1024]{2,1,0:T(8,128)(2,1)S(1)}, u32[]{:S(2)}, u32[]{:S(2)}) %collective-permute-start.2) | collective-permute-done | bytes 147488 | tf_op jit(solution)/shard_map/ppermute | solution.py:272
  35.9 1.0 pad_maximum_fusion.4
  37.0 1.1 convert_reduce_fusion
  38.1 1.2 fusion.30
  39.4 3.8 %fusion.15 = bf16[288,2048]{1,0:T(8,128)(2,1)S(1)} fusion(bf16[1024,3072]{1,0:T(8,128)(2,1)} %param.13, f32[1024]{0:T(1024)} %param.12, f32[288]{0:T(512)S(1)} %add_rsqrt_fusion.1, f32[288]{0:T(512)S(1)} %broadcast_multiply_fusion.1, bf16[36,1024]{1,0:T(8,128)(2,1)} %reshape.167, bf16[36,1024]{1,0:T(8,128)(2,1)S(1)} %reshape.166, ...), kind=kOutput, calls=%fused_computation.19 | convolution fusion | flops 1212088320 | bytes 5978368 | tf_op jit(solution)/shard_map/dot_general | solution.py:372
  43.2 1.4 pad_maximum_fusion.kv_ref
  44.7 8.7 %shard_map.130 = bf16[144,1024]{1,0:T(8,128)(2,1)} custom-call(bf16[144,1024]{1,0:T(8,128)(2,1)} %fusion.27.q_ref, bf16[432,2048]{1,0:T(8,128)(2,1)} %pad_maximum_fusion.kv_ref, s32[144,1]{1,0:T(8,128)} %reshape.182.qw_ref, s32[1,432]{1,0:T(1,128)} %bitcast.47), custom_call_target="tpu_custom_call" | custom-call | tf_op jit(solution)/shard_map/pallas_call | solution.py:109
  53.4 1.4 fusion.52
  54.9 0.8 fusion.38
  55.6 21.9 %shard_map.131 = bf16[8,144,1024]{2,1,0:T(8,128)(2,1)} custom-call(bf16[144,1024]{1,0:T(8,128)(2,1)} %bitcast.44), custom_call_target="tpu_custom_call" | custom-call | tf_op jit(solution)/shard_map/pallas_call | solution.py:154
  77.6 4.4 %copy.22 = f32[8,6,24,1024]{3,2,0,1:T(8,128)} copy(bf16[8,6,24,1024]{3,2,1,0:T(8,128)(2,1)} %bitcast.37) | data formatting | bytes 7077888 | tf_op jit(solution)/shard_map/convert_element_type | solution.py:321
  82.0 10.6 %multiply_convert_fusion = bf16[5,6,192,320]{3,2,1,0:T(8,128)(2,1)S(1)} fusion(bf16[5,6,192,320]{3,2,1,0:T(8,128)(2,1)} %param.18, f32[5,192]{1,0:T(8,128)S(1)} %copy-done.11, bf16[5,1024,320]{2,1,0:T(8,128)(2,1)} %all-gather.2.cloned.1.call-done, f32[5,1024]{1,0:T(8,128)S(1)} %copy-done.7, f32[5,1024]{1,0:T(8,128)S(1)} %copy-done.6, ...), kind=kOutput, calls=%fused_computation.10 | convolution fusion | flops 3799941120 | bytes 15412992 | tf_op jit(solution)/shard_map/krnd,kdo->krno/dot_general | solution.py:325
  92.6 7.2 %multiply_reduce_fusion = bf16[6,192,1024]{2,1,0:T(8,128)(2,1)S(1)} fusion(f32[5,1024]{1,0:T(8,128)S(1)} %copy-done.6, bf16[5,6,192,320]{3,2,1,0:T(8,128)(2,1)S(1)} %multiply_convert_fusion, bf16[5,1024,320]{2,1,0:T(8,128)(2,1)S(1)} %copy-done.5), kind=kOutput, calls=%fused_computation | convolution fusion | flops 3785490432 | bytes 9342976 | tf_op jit(solution)/shard_map/krno,kdo->krnd/dot_general | solution.py:329
  99.9 1.7 copy.28
  101.6 9.3 %fusion.8 = bf16[5,1024,320]{1,2,0:T(8,128)(2,1)} fusion(bf16[5,6,192,320]{3,2,1,0:T(8,128)(2,1)} %copy-done.12, f32[5,1024]{1,0:T(8,128)S(1)} %copy-done.7, f32[5,1024]{1,0:T(8,128)S(1)} %copy-done.6, f32[6,192,1024]{2,1,0:T(8,128)} %bitcast.40), kind=kOutput, calls=%fused_computation.12 | convolution fusion | flops 3795845120 | bytes 11722752 | tf_op jit(solution)/shard_map/krnd,krno->kdo/dot_general | solution.py:331
  110.8 5.8 %copy.23 = bf16[5,1024,320]{2,1,0:T(8,128)(2,1)} copy(bf16[5,1024,320]{1,2,0:T(8,128)(2,1)} %fusion.8) | data formatting | bytes 6553600 | tf_op jit(solution)/shard_map/convert_element_type | solution.py:423
  116.6 41.2 %shard_map.132 = f32[5,64,320]{2,1,0:T(8,128)} custom-call(bf16[5,4,4,64,320]{4,3,2,1,0:T(8,128)(2,1)} %bitcast.36), custom_call_target="tpu_custom_call" | custom-call | tf_op jit(solution)/shard_map/pallas_call | solution.py:239
  157.8 1.3 reshape.184
  159.2 0.9 copy.27
  160.1 1.8 %copy.33 = f32[5,64,320]{2,1,0:T(8,128)} copy(f32[5,64,320]{2,1,0:T(8,128)} %shard_map.132) | data formatting | bytes 819200
  (64 shorter events, 3.9 us)
Async XLA Ops:
  7.2 46.2 %copy-start = (bf16[1024,1024]{1,0:T(8,128)(2,1)S(1)}, bf16[1024,1024]{1,0:T(8,128)(2,1)}, u32[]{:S(2)}) copy-start(bf16[1024,1024]{1,0:T(8,128)(2,1)} %param.14) | copy-start | bytes 6291460
  7.2 74.8 %all-gather.2.cloned.1.call-start = ((), (), s32[]{:S(2)}) async-start(), calls=%async_computation.1 | async-start | bytes 4177920 | tf_op jit(solution)/shard_map/all_gather | solution.py:399
  7.9 149.9 %reduce-scatter.4.cloned.1.call-start = ((), (), s32[]{:S(2)}) async-start(), calls=%async_computation.2 | async-start | bytes 2654208
  9.0 18.4 %collective-permute-start.1 = (bf16[3,24,1024]{2,1,0:T(8,128)(2,1)S(1)}, bf16[3,24,1024]{2,1,0:T(8,128)(2,1)S(1)}, u32[]{:S(2)}, u32[]{:S(2)}) collective-permute-start(bf16[3,24,1024]{2,1,0:T(8,128)(2,1)S(1)} %get-tuple-element.7), channel_id=1, source_target_pairs={{8,0},{16,8},{24,16},{32,24},{40,32},{48,40},{56,48},{64,56},{72,6... | collective-permute-start | bytes 442376 | tf_op jit(solution)/shard_map/ppermute | solution.py:273
  10.3 17.0 %collective-permute-start = (bf16[3,24,1024]{2,1,0:T(8,128)(2,1)S(1)}, bf16[3,24,1024]{2,1,0:T(8,128)(2,1)S(1)}, u32[]{:S(2)}, u32[]{:S(2)}) collective-permute-start(bf16[3,24,1024]{2,1,0:T(8,128)(2,1)S(1)} %get-tuple-element.8), channel_id=1, source_target_pairs={{0,8},{8,16},{16,24},{24,32},{32,40},{40,48},{48,56},{56,64},{64,7... | collective-permute-start | bytes 442376 | tf_op jit(solution)/shard_map/ppermute | solution.py:272
  21.3 5.9 %copy-start.8 = (s32[4]{0:T(128)S(1)}, s32[4]{0:T(128)}, u32[]{:S(2)}) copy-start(s32[4]{0:T(128)} %param.19) | copy-start | bytes 52
  21.3 5.9 %copy-start.9 = (s32[1,8]{1,0:T(1,128)S(1)}, s32[1,8]{1,0:T(1,128)}, u32[]{:S(2)}) copy-start(s32[1,8]{1,0:T(1,128)} %param.20) | copy-start | bytes 100
  21.3 6.0 %copy-start.1 = (bf16[6,24,1024]{2,1,0:T(8,128)(2,1)S(1)}, bf16[6,24,1024]{2,1,0:T(8,128)(2,1)}, u32[]{:S(2)}) copy-start(bf16[6,24,1024]{2,1,0:T(8,128)(2,1)} %param.11) | copy-start | bytes 884740
  21.3 9.2 %copy-start.10 = (s32[5]{0:T(128)S(1)}, s32[5]{0:T(128)}, u32[]{:S(2)}) copy-start(s32[5]{0:T(128)} %param.21) | copy-start | bytes 64
  27.4 6.4 %collective-permute-start.2 = (bf16[12,6,1024]{2,1,0:T(8,128)(2,1)S(1)}, bf16[12,6,1024]{2,1,0:T(8,128)(2,1)S(1)}, u32[]{:S(2)}, u32[]{:S(2)}) collective-permute-start(bf16[12,6,1024]{2,1,0:T(8,128)(2,1)S(1)} %get-tuple-element.5), channel_id=1, source_target_pairs={{0,1},{1,2},{2,3},{3,4},{4,5},{5,6},{6,7},{7,0},{8,9},{9,10},{10,1... | collective-permute-start | bytes 442376 | tf_op jit(solution)/shard_map/ppermute | solution.py:272
  27.5 7.1 %collective-permute-start.3 = (bf16[12,6,1024]{2,1,0:T(8,128)(2,1)S(1)}, bf16[12,6,1024]{2,1,0:T(8,128)(2,1)S(1)}, u32[]{:S(2)}, u32[]{:S(2)}) collective-permute-start(bf16[12,6,1024]{2,1,0:T(8,128)(2,1)S(1)} %get-tuple-element.6), channel_id=1, source_target_pairs={{1,0},{2,1},{3,2},{4,3},{5,4},{6,5},{7,6},{0,7},{9,8},{10,9},{11,1... | collective-permute-start | bytes 442376 | tf_op jit(solution)/shard_map/ppermute | solution.py:273
  33.8 0.7 copy-start.3
  34.6 0.7 copy-start.4
  39.4 3.9 %copy-start.2 = (bf16[144,2048]{1,0:T(8,128)(2,1)S(1)}, bf16[144,2048]{1,0:T(8,128)(2,1)}, u32[]{:S(2)}) copy-start(bf16[144,2048]{1,0:T(8,128)(2,1)} %fusion.18) | copy-start | bytes 1769476
  77.6 4.4 %copy-start.6 = (f32[5,1024]{1,0:T(8,128)S(1)}, f32[5,1024]{1,0:T(8,128)}, u32[]{:S(2)}) copy-start(f32[5,1024]{1,0:T(8,128)} %param.15) | copy-start | bytes 61444
  77.6 4.4 %copy-start.7 = (f32[5,1024]{1,0:T(8,128)S(1)}, f32[5,1024]{1,0:T(8,128)}, u32[]{:S(2)}) copy-start(f32[5,1024]{1,0:T(8,128)} %param.16) | copy-start | bytes 61444
  77.6 4.4 %copy-start.11 = (f32[5,192]{1,0:T(8,128)S(1)}, f32[5,192]{1,0:T(8,128)}, u32[]{:S(2)}) copy-start(f32[5,192]{1,0:T(8,128)} %fusion.43) | copy-start | bytes 11524
  82.0 10.6 %copy-start.5 = (bf16[5,1024,320]{2,1,0:T(8,128)(2,1)S(1)}, bf16[5,1024,320]{2,1,0:T(8,128)(2,1)}, u32[]{:S(2)}) copy-start(bf16[5,1024,320]{2,1,0:T(8,128)(2,1)} %all-gather.2.cloned.1.call-done) | copy-start | bytes 9830404
  92.6 7.2 %copy-start.12 = (bf16[5,6,192,320]{3,2,1,0:T(8,128)(2,1)}, bf16[5,6,192,320]{3,2,1,0:T(8,128)(2,1)S(1)}, u32[]{:S(2)}) copy-start(bf16[5,6,192,320]{3,2,1,0:T(8,128)(2,1)S(1)} %multiply_convert_fusion) | copy-start | bytes 11059204
Sparse Core Ops, SparseCore 0:
  10.2 52.8 all-gather.1
  101.7 38.0 reduce-scatter.3

commit v11 on v10

--- a/solution.py
+++ b/solution.py
@@ -357,8 +357,29 @@
     queries = jnp.dot(own_normed, input_proj[:, :width], preferred_element_type=jnp.float32)
     queries = queries.astype(jnp.bfloat16)
     own_keyval = jnp.dot(own_normed, input_proj[:, width:], preferred_element_type=jnp.float32)
-    extended = padded(patches, ((LAT, 0),), half_rows, False)
-    extended = padded(extended, (("var", 1),), half_cols, True)
+    every = LAT + ("var",)
+
+    def shifted(piece, rows_from, cols_from):
+        pairs = []
+        for lat in range(lat_count):
+            for var in range(var_count):
+                source = lat + rows_from
+                if 0 <= source < lat_count:
+                    pairs.append((source * var_count + (var + cols_from) % var_count, lat * var_count + var))
+        return lax.ppermute(piece, every, pairs)
+
+    low, high = patches[band_rows - half_rows :], patches[:half_rows]
+    top = jnp.concatenate(
+        [shifted(low[:, band_cols - half_cols :], -1, -1), shifted(low, -1, 0),
+         shifted(low[:, :half_cols], -1, 1)], axis=1)
+    bottom = jnp.concatenate(
+        [shifted(high[:, band_cols - half_cols :], 1, -1), shifted(high, 1, 0),
+         shifted(high[:, :half_cols], 1, 1)], axis=1)
+    left = shifted(patches[:, band_cols - half_cols :], 0, -1)
+    right = shifted(patches[:, :half_cols], 0, 1)
+    halo = jnp.concatenate(
+        [part.reshape(-1, width) for part in (top, bottom, left, right)]
+    )
 
     def ring(grid):
         top, bottom = grid[:half_rows], grid[half_rows + band_rows :]
@@ -368,7 +389,7 @@
             [part.reshape((-1,) + grid.shape[2:]) for part in (top, bottom, left, right)]
         )
 
-    halo_normed = layer_norm(ring(extended), norm_gain)
+    halo_normed = layer_norm(halo, norm_gain)
     halo_keyval = jnp.dot(halo_normed, input_proj[:, width:], preferred_element_type=jnp.float32)
     keyval = jnp.concatenate([own_keyval, halo_keyval]).astype(jnp.bfloat16)
     global_row = lat_place * band_rows - half_rows + jnp.arange(ext_rows, dtype=jnp.int32)

time: 170 us -> 184 us (1.082)
  starting transfers between devices: 8.97 us -> 19 us
  waiting for transfers between devices: 3.2 us -> 7.53 us
  local copies, waits for them, and re-layouts: 21.1 us -> 23.5 us
    ppermute x4 -> x8, starting transfers between devices: 8.89 us -> 18.9 us  [shifted(): return lax.ppermute(piece, every, pairs)]
    ppermute x4 -> x8, waiting for transfers between devices: 2.48 us -> 6.81 us  [shifted(): return lax.ppermute(piece, every, pairs)]
    slice x2 -> x3, local copies, waits for them, and re-layouts: 1.05 us -> 3.55 us  [the longest x1 1.53 us: local(): low[:, band_cols - half_cols:]]
    concatenate x0 -> x2, other arithmetic: none -> 1.93 us  [the longest x1 1.02 us: local(): jnp.concatenate([shifted(high[:, band_cols - half_cols:], 1, -1), shifted...]
    reshape x0 -> x4, local copies, waits for them, and re-layouts: none -> 1.92 us  [local(): part.reshape(-1, width)]
    unnamed x32 -> x24, local copies, waits for them, and re-layouts: 7.15 us -> 5.79 us
  transfers between devices with their start and end apart: 6 -> 10, of which waited for: 1 -> 2; matrix products, arithmetic and copies ran while one was open for 27% -> 26% of each run, Pallas kernels for 43% -> 39%
where the time goes in v11:
time: 184 us; the launch traced here: 183 us
  Pallas kernels  71 us (39%)
  matrix products  39 us (21%)
  local copies, waits for them, and re-layouts  23.5 us (13%)
  starting transfers between devices  19 us (10%)
  between operations  14.4 us (8%)
  other arithmetic  9.07 us (5%)
  waiting for transfers between devices  7.53 us (4%)
    pallas_call x1, Pallas kernels, grid_reduce_scatter(): pl.pallas_call(kernel, out_shape=jax.ShapeDtypeStruct((slots, rows, outs)...  41.5 us
    pallas_call x1, Pallas kernels, chip_pair_gather(): pl.pallas_call(kernel, out_shape=jax.ShapeDtypeStruct((n,) + block.shape,...  20.7 us
    ppermute x8, starting transfers between devices, shifted(): return lax.ppermute(piece, every, pairs)  18.9 us
    dot_general x1, matrix products, slot_terms(): jnp.einsum('krnd,kdo->krno', rows, heads_full, preferred_element_type=jnp...  10.6 us
    dot_general x1, matrix products, slot_terms(): jnp.einsum('krnd,krno->kdo', rows, errors, preferred_element_type=jnp.flo...  9.26 us
    pallas_call x1, Pallas kernels, masked_window_attention(): pl.pallas_call(kernel, out_shape=jax.ShapeDtypeStruct((nq, width), jnp.bf...  8.81 us
    dot_general x1, matrix products, slot_terms(): jnp.einsum('krno,kdo->krnd', errors, heads_full, preferred_element_type=j...  7.22 us
    ppermute x8, waiting for transfers between devices, shifted(): return lax.ppermute(piece, every, pairs)  6.81 us
  transfers between devices with their start and end apart: 10, of which 2 were waited for; matrix products, arithmetic and copies ran while one was open for 26% of the time, Pallas kernels for 39%

profile of v11, /device:TPU:0, one launch (start us, length us, event | category | flops | bytes accessed | tf_op | source)
XLA Modules:
  0.0 183.4 jit_solution(14564431615428783488)
XLA Ops:
  8.0 1.5 fusion.48
  9.5 3.6 %collective-permute-start = (bf16[3,6,1024]{2,1,0:T(8,128)(2,1)}, bf16[3,6,1024]{2,1,0:T(8,128)(2,1)}, u32[]{:S(2)}, u32[]{:S(2)}) collective-permute-start(bf16[3,6,1024]{2,1,0:T(8,128)(2,1)} %get-tuple-element.3), channel_id=1, source_target_pairs={{7,8},{0,9},{1,10},{2,11},{3,12},{4,13},{5,14},{6,15},{15,16},{8,1... | collective-permute-start | bytes 110600 | tf_op jit(solution)/shard_map/ppermute | solution.py:369
  13.1 5.9 %collective-permute-start.2 = (bf16[3,6,1024]{2,1,0:T(8,128)(2,1)S(1)}, bf16[3,6,1024]{2,1,0:T(8,128)(2,1)}, u32[]{:S(2)}, u32[]{:S(2)}) collective-permute-start(bf16[3,6,1024]{2,1,0:T(8,128)(2,1)S(1)} %get-tuple-element.6), channel_id=1, source_target_pairs={{1,8},{2,9},{3,10},{4,11},{5,12},{6,13},{7,14},{0,15},{9,16},{10,1... | collective-permute-start | bytes 110600 | tf_op jit(solution)/shard_map/ppermute | solution.py:369
  19.0 1.0 fusion.50
  20.0 2.9 %collective-permute-start.7 = (bf16[6,6,1024]{2,1,0:T(8,128)(2,1)S(1)}, bf16[6,6,1024]{2,1,0:T(8,128)(2,1)}, u32[]{:S(2)}, u32[]{:S(2)}) collective-permute-start(bf16[6,6,1024]{2,1,0:T(8,128)(2,1)S(1)} %get-tuple-element.10), channel_id=1, source_target_pairs={{1,0},{2,1},{3,2},{4,3},{5,4},{6,5},{7,6},{0,7},{9,8},{10,9},{11,1... | collective-permute-start | bytes 221192 | tf_op jit(solution)/shard_map/ppermute | solution.py:369
  22.9 1.1 fusion.49
  24.0 2.6 %collective-permute-start.1 = (bf16[3,24,1024]{2,1,0:T(8,128)(2,1)S(1)}, bf16[3,24,1024]{2,1,0:T(8,128)(2,1)S(1)}, u32[]{:S(2)}, u32[]{:S(2)}) collective-permute-start(bf16[3,24,1024]{2,1,0:T(8,128)(2,1)S(1)} %get-tuple-element.7), channel_id=1, source_target_pairs={{0,8},{1,9},{2,10},{3,11},{4,12},{5,13},{6,14},{7,15},{8,16},{9,17... | collective-permute-start | bytes 442376 | tf_op jit(solution)/shard_map/ppermute | solution.py:369
  27.4 1.1 convert_reduce_fusion.1
  28.5 1.2 fusion.35
  29.8 1.2 fusion.37
  31.0 2.8 %fusion.27.q_ref = bf16[144,1024]{1,0:T(8,128)(2,1)} fusion(bf16[144,1024]{1,0:T(8,128)(2,1)S(1)} %bitcast.45, bf16[1024,3072]{1,0:T(8,128)(2,1)} %param.13), kind=kOutput, calls=%fused_computation.28 | convolution fusion | flops 302137344 | bytes 2686976 | tf_op jit(solution)/shard_map/dot_general | solution.py:357
  33.8 3.0 %fusion.18 = bf16[144,2048]{1,0:T(8,128)(2,1)S(1)} fusion(bf16[144,1024]{1,0:T(8,128)(2,1)S(1)} %bitcast.46, bf16[1024,3072]{1,0:T(8,128)(2,1)} %param.13), kind=kOutput, calls=%fused_computation.20 | convolution fusion | flops 604274688 | bytes 5079040 | tf_op jit(solution)/shard_map/dot_general | solution.py:359
  37.7 1.3 collective-permute-start.4
  41.8 1.3 collective-permute-start.5
  44.1 1.3 collective-permute-start.3
  46.3 2.2 %collective-permute-done.5 = bf16[3,6,1024]{2,1,0:T(8,128)(2,1)S(1)} collective-permute-done((bf16[3,6,1024]{2,1,0:T(8,128)(2,1)}, bf16[3,6,1024]{2,1,0:T(8,128)(2,1)S(1)}, u32[]{:S(2)}, u32[]{:S(2)}) %collective-permute-start.5) | collective-permute-done | bytes 36896 | tf_op jit(solution)/shard_map/ppermute | solution.py:369
  48.6 4.6 %collective-permute-done.3 = bf16[3,6,1024]{2,1,0:T(8,128)(2,1)} collective-permute-done((bf16[3,6,1024]{2,1,0:T(8,128)(2,1)}, bf16[3,6,1024]{2,1,0:T(8,128)(2,1)}, u32[]{:S(2)}, u32[]{:S(2)}) %collective-permute-start.3) | collective-permute-done | bytes 36896 | tf_op jit(solution)/shard_map/ppermute | solution.py:369
  53.1 1.0 pad_maximum_fusion.3
  54.8 3.8 %fusion.15 = bf16[288,2048]{1,0:T(8,128)(2,1)S(1)} fusion(bf16[1024,3072]{1,0:T(8,128)(2,1)} %param.13, f32[1024]{0:T(1024)} %param.12, f32[288]{0:T(512)S(1)} %add_rsqrt_fusion.1, f32[288]{0:T(512)S(1)} %broadcast_multiply_fusion.1, bf16[36,1024]{1,0:T(8,128)(2,1)S(1)} %reshape.167, bf16[36,1024]{1,0:T(8,128)(2,1)S(1)} %reshape.166, ...), kind=kOutput, calls=%fused_computation.19 | convolution fusion | flops 1212088320 | bytes 5970176 | tf_op jit(solution)/shard_map/dot_general | solution.py:393
  58.7 1.4 pad_maximum_fusion.kv_ref
  60.1 8.8 %shard_map.130 = bf16[144,1024]{1,0:T(8,128)(2,1)} custom-call(bf16[144,1024]{1,0:T(8,128)(2,1)} %fusion.27.q_ref, bf16[432,2048]{1,0:T(8,128)(2,1)} %pad_maximum_fusion.kv_ref, s32[144,1]{1,0:T(8,128)} %reshape.182.qw_ref, s32[1,432]{1,0:T(1,128)} %bitcast.47), custom_call_target="tpu_custom_call" | custom-call | tf_op jit(solution)/shard_map/pallas_call | solution.py:109
  68.9 1.4 fusion.53
  71.1 20.7 %shard_map.131 = bf16[8,144,1024]{2,1,0:T(8,128)(2,1)} custom-call(bf16[144,1024]{1,0:T(8,128)(2,1)} %bitcast.44), custom_call_target="tpu_custom_call" | custom-call | tf_op jit(solution)/shard_map/pallas_call | solution.py:154
  91.9 4.3 %copy.22 = f32[8,6,24,1024]{3,2,0,1:T(8,128)} copy(bf16[8,6,24,1024]{3,2,1,0:T(8,128)(2,1)} %bitcast.37) | data formatting | bytes 7077888 | tf_op jit(solution)/shard_map/convert_element_type | solution.py:321
  96.3 10.6 %multiply_convert_fusion = bf16[5,6,192,320]{3,2,1,0:T(8,128)(2,1)S(1)} fusion(bf16[5,6,192,320]{3,2,1,0:T(8,128)(2,1)} %param.18, f32[5,192]{1,0:T(8,128)S(1)} %copy-done.8, bf16[5,1024,320]{2,1,0:T(8,128)(2,1)} %all-gather.2.cloned.1.call-done, f32[5,1024]{1,0:T(8,128)S(1)} %copy-done.6, f32[5,1024]{1,0:T(8,128)S(1)} %copy-done.5, ...), kind=kOutput, calls=%fused_computation.10 | convolution fusion | flops 3799941120 | bytes 15412992 | tf_op jit(solution)/shard_map/krnd,kdo->krno/dot_general | solution.py:325
  106.9 7.2 %multiply_reduce_fusion = bf16[6,192,1024]{2,1,0:T(8,128)(2,1)S(1)} fusion(f32[5,1024]{1,0:T(8,128)S(1)} %copy-done.5, bf16[5,6,192,320]{3,2,1,0:T(8,128)(2,1)S(1)} %multiply_convert_fusion, bf16[5,1024,320]{2,1,0:T(8,128)(2,1)S(1)} %copy-done.4), kind=kOutput, calls=%fused_computation | convolution fusion | flops 3785490432 | bytes 9342976 | tf_op jit(solution)/shard_map/krno,kdo->krnd/dot_general | solution.py:329
  114.2 1.7 copy.28
  115.8 9.3 %fusion.8 = bf16[5,1024,320]{1,2,0:T(8,128)(2,1)} fusion(bf16[5,6,192,320]{3,2,1,0:T(8,128)(2,1)} %copy-done.9, f32[5,1024]{1,0:T(8,128)S(1)} %copy-done.6, f32[5,1024]{1,0:T(8,128)S(1)} %copy-done.5, f32[6,192,1024]{2,1,0:T(8,128)} %bitcast.40), kind=kOutput, calls=%fused_computation.12 | convolution fusion | flops 3795845120 | bytes 11722752 | tf_op jit(solution)/shard_map/krnd,krno->kdo/dot_general | solution.py:331
  125.1 5.9 %copy.23 = bf16[5,1024,320]{2,1,0:T(8,128)(2,1)} copy(bf16[5,1024,320]{1,2,0:T(8,128)(2,1)} %fusion.8) | data formatting | bytes 6553600 | tf_op jit(solution)/shard_map/convert_element_type | solution.py:444
  131.0 41.5 %shard_map.132 = f32[5,64,320]{2,1,0:T(8,128)} custom-call(bf16[5,4,4,64,320]{4,3,2,1,0:T(8,128)(2,1)} %bitcast.36), custom_call_target="tpu_custom_call" | custom-call | tf_op jit(solution)/shard_map/pallas_call | solution.py:239
  172.5 1.3 reshape.184
  174.8 1.8 %copy.31 = f32[5,64,320]{2,1,0:T(8,128)} copy(f32[5,64,320]{2,1,0:T(8,128)} %shard_map.132) | data formatting | bytes 819200
  (63 shorter events, 9.6 us)
Async XLA Ops:
  7.2 61.7 %copy-start = (bf16[1024,1024]{1,0:T(8,128)(2,1)S(1)}, bf16[1024,1024]{1,0:T(8,128)(2,1)}, u32[]{:S(2)}) copy-start(bf16[1024,1024]{1,0:T(8,128)(2,1)} %param.14) | copy-start | bytes 6291460
  7.2 89.1 %all-gather.2.cloned.1.call-start = ((), (), s32[]{:S(2)}) async-start(), calls=%async_computation.1 | async-start | bytes 4177920 | tf_op jit(solution)/shard_map/all_gather | solution.py:420
  7.9 164.6 %reduce-scatter.4.cloned.1.call-start = ((), (), s32[]{:S(2)}) async-start(), calls=%async_computation.2 | async-start | bytes 2654208
  9.5 34.6 %collective-permute-start = (bf16[3,6,1024]{2,1,0:T(8,128)(2,1)}, bf16[3,6,1024]{2,1,0:T(8,128)(2,1)}, u32[]{:S(2)}, u32[]{:S(2)}) collective-permute-start(bf16[3,6,1024]{2,1,0:T(8,128)(2,1)} %get-tuple-element.3), channel_id=1, source_target_pairs={{7,8},{0,9},{1,10},{2,11},{3,12},{4,13},{5,14},{6,15},{15,16},{8,1... | collective-permute-start | bytes 110600 | tf_op jit(solution)/shard_map/ppermute | solution.py:369
  13.1 32.3 %collective-permute-start.2 = (bf16[3,6,1024]{2,1,0:T(8,128)(2,1)S(1)}, bf16[3,6,1024]{2,1,0:T(8,128)(2,1)}, u32[]{:S(2)}, u32[]{:S(2)}) collective-permute-start(bf16[3,6,1024]{2,1,0:T(8,128)(2,1)S(1)} %get-tuple-element.6), channel_id=1, source_target_pairs={{1,8},{2,9},{3,10},{4,11},{5,12},{6,13},{7,14},{0,15},{9,16},{10,1... | collective-permute-start | bytes 110600 | tf_op jit(solution)/shard_map/ppermute | solution.py:369
  20.0 17.7 %collective-permute-start.6 = (bf16[6,6,1024]{2,1,0:T(8,128)(2,1)S(1)}, bf16[6,6,1024]{2,1,0:T(8,128)(2,1)S(1)}, u32[]{:S(2)}, u32[]{:S(2)}) collective-permute-start(bf16[6,6,1024]{2,1,0:T(8,128)(2,1)S(1)} %get-tuple-element.9), channel_id=1, source_target_pairs={{7,0},{0,1},{1,2},{2,3},{3,4},{4,5},{5,6},{6,7},{15,8},{8,9},{9,10... | collective-permute-start | bytes 221192 | tf_op jit(solution)/shard_map/ppermute | solution.py:369
  20.0 21.8 %collective-permute-start.7 = (bf16[6,6,1024]{2,1,0:T(8,128)(2,1)S(1)}, bf16[6,6,1024]{2,1,0:T(8,128)(2,1)}, u32[]{:S(2)}, u32[]{:S(2)}) collective-permute-start(bf16[6,6,1024]{2,1,0:T(8,128)(2,1)S(1)} %get-tuple-element.10), channel_id=1, source_target_pairs={{1,0},{2,1},{3,2},{4,3},{5,4},{6,5},{7,6},{0,7},{9,8},{10,9},{11,1... | collective-permute-start | bytes 221192 | tf_op jit(solution)/shard_map/ppermute | solution.py:369
  24.0 21.4 %collective-permute-start.1 = (bf16[3,24,1024]{2,1,0:T(8,128)(2,1)S(1)}, bf16[3,24,1024]{2,1,0:T(8,128)(2,1)S(1)}, u32[]{:S(2)}, u32[]{:S(2)}) collective-permute-start(bf16[3,24,1024]{2,1,0:T(8,128)(2,1)S(1)} %get-tuple-element.7), channel_id=1, source_target_pairs={{0,8},{1,9},{2,10},{3,11},{4,12},{5,13},{6,14},{7,15},{8,16},{9,17... | collective-permute-start | bytes 442376 | tf_op jit(solution)/shard_map/ppermute | solution.py:369
  33.8 3.0 %copy-start.7 = (s32[5]{0:T(128)S(1)}, s32[5]{0:T(128)}, u32[]{:S(2)}) copy-start(s32[5]{0:T(128)} %param.21) | copy-start | bytes 64
  37.7 2.5 %copy-start.2 = (bf16[6,6,1024]{2,1,0:T(8,128)(2,1)}, bf16[6,6,1024]{2,1,0:T(8,128)(2,1)S(1)}, u32[]{:S(2)}) copy-start(bf16[6,6,1024]{2,1,0:T(8,128)(2,1)S(1)} %collective-permute-done.6) | copy-start | bytes 221188
  37.7 15.4 %collective-permute-start.4 = (bf16[3,24,1024]{2,1,0:T(8,128)(2,1)S(1)}, bf16[3,24,1024]{2,1,0:T(8,128)(2,1)}, u32[]{:S(2)}, u32[]{:S(2)}) collective-permute-start(bf16[3,24,1024]{2,1,0:T(8,128)(2,1)S(1)} %get-tuple-element.8), channel_id=1, source_target_pairs={{8,0},{9,1},{10,2},{11,3},{12,4},{13,5},{14,6},{15,7},{16,8},{17,9... | collective-permute-start | bytes 442376 | tf_op jit(solution)/shard_map/ppermute | solution.py:369
  41.8 6.8 %collective-permute-start.5 = (bf16[3,6,1024]{2,1,0:T(8,128)(2,1)}, bf16[3,6,1024]{2,1,0:T(8,128)(2,1)S(1)}, u32[]{:S(2)}, u32[]{:S(2)}) collective-permute-start(bf16[3,6,1024]{2,1,0:T(8,128)(2,1)} %get-tuple-element.4), channel_id=1, source_target_pairs={{9,0},{10,1},{11,2},{12,3},{13,4},{14,5},{15,6},{8,7},{17,8},{18,9... | collective-permute-start | bytes 110600 | tf_op jit(solution)/shard_map/ppermute | solution.py:369
  44.1 9.1 %collective-permute-start.3 = (bf16[3,6,1024]{2,1,0:T(8,128)(2,1)}, bf16[3,6,1024]{2,1,0:T(8,128)(2,1)}, u32[]{:S(2)}, u32[]{:S(2)}) collective-permute-start(bf16[3,6,1024]{2,1,0:T(8,128)(2,1)} %get-tuple-element.5), channel_id=1, source_target_pairs={{15,0},{8,1},{9,2},{10,3},{11,4},{12,5},{13,6},{14,7},{23,8},{16,9... | collective-permute-start | bytes 110600 | tf_op jit(solution)/shard_map/ppermute | solution.py:369
  48.6 4.6 %copy-start.3 = (bf16[3,6,1024]{2,1,0:T(8,128)(2,1)}, bf16[3,6,1024]{2,1,0:T(8,128)(2,1)S(1)}, u32[]{:S(2)}) copy-start(bf16[3,6,1024]{2,1,0:T(8,128)(2,1)S(1)} %collective-permute-done.5) | copy-start | bytes 110596
  58.7 11.7 %copy-start.1 = (bf16[6,24,1024]{2,1,0:T(8,128)(2,1)S(1)}, bf16[6,24,1024]{2,1,0:T(8,128)(2,1)}, u32[]{:S(2)}) copy-start(bf16[6,24,1024]{2,1,0:T(8,128)(2,1)} %param.11) | copy-start | bytes 884740
  91.9 4.4 %copy-start.5 = (f32[5,1024]{1,0:T(8,128)S(1)}, f32[5,1024]{1,0:T(8,128)}, u32[]{:S(2)}) copy-start(f32[5,1024]{1,0:T(8,128)} %param.15) | copy-start | bytes 61444
  91.9 4.4 %copy-start.6 = (f32[5,1024]{1,0:T(8,128)S(1)}, f32[5,1024]{1,0:T(8,128)}, u32[]{:S(2)}) copy-start(f32[5,1024]{1,0:T(8,128)} %param.16) | copy-start | bytes 61444
  91.9 4.4 %copy-start.8 = (f32[5,192]{1,0:T(8,128)S(1)}, f32[5,192]{1,0:T(8,128)}, u32[]{:S(2)}) copy-start(f32[5,192]{1,0:T(8,128)} %fusion.43) | copy-start | bytes 11524
  96.3 10.6 %copy-start.4 = (bf16[5,1024,320]{2,1,0:T(8,128)(2,1)S(1)}, bf16[5,1024,320]{2,1,0:T(8,128)(2,1)}, u32[]{:S(2)}) copy-start(bf16[5,1024,320]{2,1,0:T(8,128)(2,1)} %all-gather.2.cloned.1.call-done) | copy-start | bytes 9830404
  106.9 7.2 %copy-start.9 = (bf16[5,6,192,320]{3,2,1,0:T(8,128)(2,1)}, bf16[5,6,192,320]{3,2,1,0:T(8,128)(2,1)S(1)}, u32[]{:S(2)}) copy-start(bf16[5,6,192,320]{3,2,1,0:T(8,128)(2,1)S(1)} %multiply_convert_fusion) | copy-start | bytes 11059204
Sparse Core Ops, SparseCore 0:
  10.2 55.3 all-gather.1
  116.0 37.5 reduce-scatter.3

commit v12 on v8

--- a/solution.py
+++ b/solution.py
@@ -253,6 +253,62 @@
         ],
         compiler_params=pltpu.CompilerParams(collective_id=cid, has_side_effects=True),
     )(parts)
+
+
+def chip_ring_gather(block, axis, n, cid):
+    rows = block.shape[0]
+    cut = rows // 32 * 16
+
+    def kernel(x_ref, out_ref, send_sem, recv_sem):
+        me = lax.axis_index(axis)
+        partner = me + 1 - 2 * lax.rem(me, 2)
+        up, down, far = lax.rem(me + 2, n), lax.rem(me + n - 2, n), lax.rem(me + 4, n)
+        barrier = pltpu.get_barrier_semaphore()
+        for dev in (up, down, partner):
+            pl.semaphore_signal(barrier, inc=1, device_id={axis: dev}, device_id_type=MESH_ID)
+        pl.semaphore_wait(barrier, 3)
+        head, tail = pl.ds(0, cut), pl.ds(cut, rows - cut)
+
+        def send(src_ref, slot, part, dev, index, sem_col):
+            copy = pltpu.make_async_remote_copy(
+                src_ref=src_ref, dst_ref=out_ref.at[slot, part], send_sem=send_sem.at[index],
+                recv_sem=recv_sem.at[slot, sem_col], device_id={axis: dev},
+                device_id_type=MESH_ID)
+            copy.start()
+            return copy
+
+        def arrive(slot, part, sem_col):
+            pltpu.make_async_remote_copy(
+                src_ref=out_ref.at[slot, part], dst_ref=out_ref.at[slot, part],
+                send_sem=send_sem.at[0], recv_sem=recv_sem.at[slot, sem_col],
+                device_id={axis: slot}, device_id_type=MESH_ID).wait_recv()
+
+        whole = pl.ds(0, rows)
+        sends = [send(x_ref, me, whole, up, 0, 0), send(x_ref, me, whole, down, 1, 0),
+                 send(x_ref, me, whole, partner, 2, 0)]
+        out_ref[me] = x_ref[...]
+        arrive(down, whole, 0)
+        sends.append(send(out_ref.at[down, head], down, head, up, 3, 0))
+        sends.append(send(out_ref.at[down], down, whole, partner, 4, 0))
+        arrive(up, whole, 0)
+        sends.append(send(out_ref.at[up, tail], up, tail, down, 5, 1))
+        sends.append(send(out_ref.at[up], up, whole, partner, 6, 0))
+        arrive(far, head, 0)
+        arrive(far, tail, 1)
+        sends.append(send(out_ref.at[far], far, whole, partner, 7, 0))
+        for k in range(4):
+            arrive(lax.rem(partner + 2 * k, n), whole, 0)
+        for copy in sends:
+            copy.wait_send()
+
+    return pl.pallas_call(
+        kernel,
+        out_shape=jax.ShapeDtypeStruct((n,) + block.shape, block.dtype),
+        in_specs=[pl.BlockSpec(memory_space=pltpu.VMEM)],
+        out_specs=pl.BlockSpec(memory_space=pltpu.VMEM),
+        scratch_shapes=[pltpu.SemaphoreType.DMA((8,)), pltpu.SemaphoreType.DMA((n, 2))],
+        compiler_params=pltpu.CompilerParams(collective_id=cid, has_side_effects=True),
+    )(block)
 
 HEADS = 16
 WH = 6
@@ -393,7 +449,8 @@
     live_tiles = (slot_level[None, :] < tile_levels[:, None]).astype(jnp.float32)
     heads_full = lax.all_gather(head_weight, LAT, axis=1, tiled=True)
     tile_ids = jnp.arange(var_count, dtype=jnp.int32)
-    tiles = chip_pair_gather(latent.reshape(band_rows * band_cols, width), "var", var_count, 1)
+    gather = chip_ring_gather if var_count == 8 else chip_pair_gather
+    tiles = gather(latent.reshape(band_rows * band_cols, width), "var", var_count, 1)
     piece = (
         tiles.reshape(var_count, band_rows, band_cols, width)
         .transpose(1, 0, 2, 3)

time: 170 us -> 168 us (0.988)
  Pallas kernels: 75.7 us -> 73.7 us
    pallas_call x1, Pallas kernels: 23 us -> 20.3 us  [chip_ring_gather(): pl.pallas_call(kernel, out_shape=jax.ShapeDtypeStruct((n,) + block.shape,...]
  transfers between devices with their start and end apart: 6 -> 6, of which waited for: 2 -> 2; matrix products, arithmetic and copies ran while one was open for 26% -> 26% of each run, Pallas kernels for 45% -> 44%
where the time goes in v12:
time: 168 us; the launch traced here: 167 us
  Pallas kernels  73.7 us (44%)
  matrix products  37.2 us (22%)
  local copies, waits for them, and re-layouts  22.4 us (13%)
  between operations  14.3 us (9%)
  starting transfers between devices  8.88 us (5%)
  other arithmetic  7.22 us (4%)
  waiting for transfers between devices  3.37 us (2%)
    pallas_call x1, Pallas kernels, grid_reduce_scatter(): pl.pallas_call(kernel, out_shape=jax.ShapeDtypeStruct((slots, rows, outs)...  44.6 us
    pallas_call x1, Pallas kernels, chip_ring_gather(): pl.pallas_call(kernel, out_shape=jax.ShapeDtypeStruct((n,) + block.shape,...  20.3 us
    dot_general x1, matrix products, slot_terms(): jnp.einsum('krnd,kdo->krno', rows, heads_full, preferred_element_type=jnp...  9.92 us
    dot_general x1, matrix products, slot_terms(): jnp.einsum('krnd,krno->kdo', rows, errors, preferred_element_type=jnp.flo...  9.27 us
    pallas_call x1, Pallas kernels, masked_window_attention(): pl.pallas_call(kernel, out_shape=jax.ShapeDtypeStruct((nq, width), jnp.bf...  8.79 us
    dot_general x1, matrix products, slot_terms(): jnp.einsum('krno,kdo->krnd', errors, heads_full, preferred_element_type=j...  7.4 us
    unnamed x22, local copies, waits for them, and re-layouts  6.75 us
    convert_element_type x1, local copies, waits for them, and re-layouts, local(): head_terms.astype(jnp.bfloat16)  5.87 us
  transfers between devices with their start and end apart: 6, of which 2 were waited for; matrix products, arithmetic and copies ran while one was open for 26% of the time, Pallas kernels for 44%

profile of v12, /device:TPU:0, one launch (start us, length us, event | category | flops | bytes accessed | tf_op | source)
XLA Modules:
  0.0 167.1 jit_solution(9899573341845756287)
XLA Ops:
  7.2 0.7 all-gather.2.cloned.1.call-update
  8.0 1.0 fusion.36
  9.0 1.3 collective-permute-start.1
  10.3 4.6 %collective-permute-start = (bf16[3,24,1024]{2,1,0:T(8,128)(2,1)S(1)}, bf16[3,24,1024]{2,1,0:T(8,128)(2,1)S(1)}, u32[]{:S(2)}, u32[]{:S(2)}) collective-permute-start(bf16[3,24,1024]{2,1,0:T(8,128)(2,1)S(1)} %get-tuple-element.8), channel_id=1, source_target_pairs={{0,8},{8,16},{16,24},{24,32},{32,40},{40,48},{48,56},{56,64},{64,7... | collective-permute-start | bytes 442376 | tf_op jit(solution)/shard_map/ppermute | solution.py:328
  15.2 0.7 select_n.62.kw_ref
  15.9 0.7 add.124.qw_ref
  16.6 0.8 select_reduce_fusion
  17.6 1.0 constant_dynamic-update-slice_fusion.1
  18.7 2.9 %collective-permute-start.3 = (bf16[12,6,1024]{2,1,0:T(8,128)(2,1)S(1)}, bf16[12,6,1024]{2,1,0:T(8,128)(2,1)S(1)}, u32[]{:S(2)}, u32[]{:S(2)}) collective-permute-start(bf16[12,6,1024]{2,1,0:T(8,128)(2,1)S(1)} %get-tuple-element.6), channel_id=1, source_target_pairs={{1,0},{2,1},{3,2},{4,3},{5,4},{6,5},{7,6},{0,7},{9,8},{10,9},{11,1... | collective-permute-start | bytes 442376 | tf_op jit(solution)/shard_map/ppermute | solution.py:329
  21.6 0.9 fusion.28
  22.5 2.5 %collective-permute-done.2 = bf16[12,6,1024]{2,1,0:T(8,128)(2,1)S(1)} collective-permute-done((bf16[12,6,1024]{2,1,0:T(8,128)(2,1)S(1)}, bf16[12,6,1024]{2,1,0:T(8,128)(2,1)S(1)}, u32[]{:S(2)}, u32[]{:S(2)}) %collective-permute-start.2) | collective-permute-done | bytes 147488 | tf_op jit(solution)/shard_map/ppermute | solution.py:328
  25.0 0.4 fusion.34
  25.5 1.9 %multiply_reduce_fusion.1 = (f32[12,36]{1,0:T(8,128)S(1)}, f32[12,36,1024]{2,1,0:T(8,128)}) fusion(f32[12,36]{1,0:T(8,128)S(1)} %broadcast_multiply_fusion, bf16[12,6,1024]{2,1,0:T(8,128)(2,1)S(1)} %collective-permute-done.3, bf16[12,24,1024]{2,1,0:T(8,128)(2,1)S(1)} %constant_dynamic-update-slice_fusion, bf16[12,6,1024]{2,1,0:T(8,128)(2,1)S(1)} %collective-permute-done.2), kind=kLoop, calls=%fused_computation.20 | loop fusion | flops 3980880 | bytes 2657664 | tf_op jit(solution)/shard_map/reduce_sum | solution.py:338
  27.5 1.6 maximum_convert_fusion
  29.1 2.7 %reshape.198 = f32[432,1024]{1,0:T(8,128)} reshape(f32[12,36,1024]{2,1,0:T(8,128)} %maximum_convert_fusion) | data formatting | bytes 3538944 | tf_op jit(solution)/shard_map/convert_element_type | solution.py:335
  31.8 1.4 fusion.27
  33.3 2.8 %fusion.20.q_ref = bf16[144,1024]{1,0:T(8,128)(2,1)} fusion(bf16[144,1024]{1,0:T(8,128)(2,1)S(1)} %bitcast.47, bf16[1024,3072]{1,0:T(8,128)(2,1)} %param.13), kind=kOutput, calls=%fused_computation.22 | convolution fusion | flops 302137344 | bytes 2686976 | tf_op jit(solution)/shard_map/dot_general | solution.py:420
  36.1 5.5 %fusion.13.kv_ref = bf16[432,2048]{1,0:T(8,128)(2,1)} fusion(bf16[1024,3072]{1,0:T(8,128)(2,1)} %param.13, f32[432,1024]{1,0:T(8,128)S(1)} %copy-done.2, f32[1024]{0:T(1024)S(1)} %copy-done.3, f32[432]{0:T(512)S(1)} %rsqrt.13, f32[432]{0:T(512)S(1)} %div.54), kind=kOutput, calls=%fused_computation.17 | convolution fusion | flops 1814593536 | bytes 7740800 | tf_op jit(solution)/shard_map/dot_general | solution.py:415
  41.6 8.8 %shard_map.130 = bf16[144,1024]{1,0:T(8,128)(2,1)} custom-call(bf16[144,1024]{1,0:T(8,128)(2,1)} %fusion.20.q_ref, bf16[432,2048]{1,0:T(8,128)(2,1)} %fusion.13.kv_ref, s32[144,1]{1,0:T(8,128)} %add.124.qw_ref, s32[1,432]{1,0:T(1,128)} %select_n.62.kw_ref), custom_call_target="tpu_custom_call" | custom-call | tf_op jit(solution)/shard_map/pallas_call | solution.py:109
  50.4 1.4 fusion.37
  51.8 0.8 add_convert_fusion.7
  52.6 20.3 %shard_map.131 = bf16[8,144,1024]{2,1,0:T(8,128)(2,1)} custom-call(bf16[144,1024]{1,0:T(8,128)(2,1)} %bitcast.46), custom_call_target="tpu_custom_call" | custom-call | tf_op jit(solution)/shard_map/pallas_call | solution.py:304
  73.0 4.3 %copy.22 = f32[8,6,24,1024]{3,2,0,1:T(8,128)} copy(bf16[8,6,24,1024]{3,2,1,0:T(8,128)(2,1)} %bitcast.39) | data formatting | bytes 7077888 | tf_op jit(solution)/shard_map/convert_element_type | solution.py:377
  77.3 9.9 %multiply_convert_fusion = bf16[5,6,192,320]{3,2,1,0:T(8,128)(2,1)S(1)} fusion(bf16[5,6,192,320]{3,2,1,0:T(8,128)(2,1)} %param.18, f32[5,192]{1,0:T(8,128)S(1)} %fusion.28, bf16[5,1024,320]{2,1,0:T(8,128)(2,1)} %all-gather.2.cloned.1.call-done, f32[5,1024]{1,0:T(8,128)S(1)} %copy-done.6, f32[5,1024]{1,0:T(8,128)S(1)} %copy-done.5, f32[6,192,1024]{2,1,0:T(8,128)} %bitcast.41), kind=kOutput, calls=%fused_computation.10 | convolution fusion | flops 3799941120 | bytes 15412992 | tf_op jit(solution)/shard_map/krnd,kdo->krno/dot_general | solution.py:381
  87.3 7.4 %multiply_reduce_fusion = bf16[6,192,1024]{2,1,0:T(8,128)(2,1)S(1)} fusion(f32[5,1024]{1,0:T(8,128)S(1)} %copy-done.5, bf16[5,6,192,320]{3,2,1,0:T(8,128)(2,1)S(1)} %multiply_convert_fusion, bf16[5,1024,320]{2,1,0:T(8,128)(2,1)S(1)} %copy-done.4), kind=kOutput, calls=%fused_computation | convolution fusion | flops 3785490432 | bytes 9342976 | tf_op jit(solution)/shard_map/krno,kdo->krnd/dot_general | solution.py:385
  94.7 1.7 copy.28
  96.4 9.3 %fusion.8 = bf16[5,1024,320]{1,2,0:T(8,128)(2,1)} fusion(bf16[5,6,192,320]{3,2,1,0:T(8,128)(2,1)} %copy-done.7, f32[5,1024]{1,0:T(8,128)S(1)} %copy-done.6, f32[5,1024]{1,0:T(8,128)S(1)} %copy-done.5, f32[6,192,1024]{2,1,0:T(8,128)} %bitcast.42), kind=kOutput, calls=%fused_computation.12 | convolution fusion | flops 3795845120 | bytes 11722752 | tf_op jit(solution)/shard_map/krnd,krno->kdo/dot_general | solution.py:387
  105.6 5.9 %copy.23 = bf16[5,1024,320]{2,1,0:T(8,128)(2,1)} copy(bf16[5,1024,320]{1,2,0:T(8,128)(2,1)} %fusion.8) | data formatting | bytes 6553600 | tf_op jit(solution)/shard_map/convert_element_type | solution.py:475
  111.5 44.6 %shard_map.132 = f32[5,64,320]{2,1,0:T(8,128)} custom-call(bf16[5,4,4,64,320]{4,3,2,1,0:T(8,128)(2,1)} %bitcast.38), custom_call_target="tpu_custom_call" | custom-call | tf_op jit(solution)/shard_map/pallas_call | solution.py:239
  156.1 1.3 reshape.204
  157.5 0.9 copy.27
  158.4 1.8 %copy.33 = f32[5,64,320]{2,1,0:T(8,128)} copy(f32[5,64,320]{2,1,0:T(8,128)} %shard_map.132) | data formatting | bytes 819200
  (43 shorter events, 1.1 us)
Async XLA Ops:
  7.2 43.2 %copy-start = (bf16[1024,1024]{1,0:T(8,128)(2,1)S(1)}, bf16[1024,1024]{1,0:T(8,128)(2,1)}, u32[]{:S(2)}) copy-start(bf16[1024,1024]{1,0:T(8,128)(2,1)} %param.14) | copy-start | bytes 6291460
  7.2 70.1 %all-gather.2.cloned.1.call-start = ((), (), s32[]{:S(2)}) async-start(), calls=%async_computation.1 | async-start | bytes 4177920 | tf_op jit(solution)/shard_map/all_gather | solution.py:450
  7.9 148.2 %reduce-scatter.4.cloned.1.call-start = ((), (), s32[]{:S(2)}) async-start(), calls=%async_computation.2 | async-start | bytes 2654208
  9.0 9.6 %collective-permute-start.1 = (bf16[3,24,1024]{2,1,0:T(8,128)(2,1)S(1)}, bf16[3,24,1024]{2,1,0:T(8,128)(2,1)S(1)}, u32[]{:S(2)}, u32[]{:S(2)}) collective-permute-start(bf16[3,24,1024]{2,1,0:T(8,128)(2,1)S(1)} %get-tuple-element.7), channel_id=1, source_target_pairs={{8,0},{16,8},{24,16},{32,24},{40,32},{48,40},{56,48},{64,56},{72,6... | collective-permute-start | bytes 442376 | tf_op jit(solution)/shard_map/ppermute | solution.py:329
  10.3 7.3 %collective-permute-start = (bf16[3,24,1024]{2,1,0:T(8,128)(2,1)S(1)}, bf16[3,24,1024]{2,1,0:T(8,128)(2,1)S(1)}, u32[]{:S(2)}, u32[]{:S(2)}) collective-permute-start(bf16[3,24,1024]{2,1,0:T(8,128)(2,1)S(1)} %get-tuple-element.8), channel_id=1, source_target_pairs={{0,8},{8,16},{16,24},{24,32},{32,40},{40,48},{48,56},{56,64},{64,7... | collective-permute-start | bytes 442376 | tf_op jit(solution)/shard_map/ppermute | solution.py:328
  18.6 6.3 %collective-permute-start.2 = (bf16[12,6,1024]{2,1,0:T(8,128)(2,1)S(1)}, bf16[12,6,1024]{2,1,0:T(8,128)(2,1)S(1)}, u32[]{:S(2)}, u32[]{:S(2)}) collective-permute-start(bf16[12,6,1024]{2,1,0:T(8,128)(2,1)S(1)} %get-tuple-element.5), channel_id=1, source_target_pairs={{0,1},{1,2},{2,3},{3,4},{4,5},{5,6},{6,7},{7,0},{8,9},{9,10},{10,1... | collective-permute-start | bytes 442376 | tf_op jit(solution)/shard_map/ppermute | solution.py:328
  18.7 6.3 %collective-permute-start.3 = (bf16[12,6,1024]{2,1,0:T(8,128)(2,1)S(1)}, bf16[12,6,1024]{2,1,0:T(8,128)(2,1)S(1)}, u32[]{:S(2)}, u32[]{:S(2)}) collective-permute-start(bf16[12,6,1024]{2,1,0:T(8,128)(2,1)S(1)} %get-tuple-element.6), channel_id=1, source_target_pairs={{1,0},{2,1},{3,2},{4,3},{5,4},{6,5},{7,6},{0,7},{9,8},{10,9},{11,1... | collective-permute-start | bytes 442376 | tf_op jit(solution)/shard_map/ppermute | solution.py:329
  27.4 4.5 %copy-start.3 = (f32[1024]{0:T(1024)S(1)}, f32[1024]{0:T(1024)}, u32[]{:S(2)}) copy-start(f32[1024]{0:T(1024)} %param.12) | copy-start | bytes 12292
  31.8 4.2 %copy-start.2 = (f32[432,1024]{1,0:T(8,128)S(1)}, f32[432,1024]{1,0:T(8,128)}, u32[]{:S(2)}) copy-start(f32[432,1024]{1,0:T(8,128)} %reshape.198) | copy-start | bytes 5308420
  41.6 10.3 %copy-start.1 = (bf16[6,24,1024]{2,1,0:T(8,128)(2,1)S(1)}, bf16[6,24,1024]{2,1,0:T(8,128)(2,1)}, u32[]{:S(2)}) copy-start(bf16[6,24,1024]{2,1,0:T(8,128)(2,1)} %param.11) | copy-start | bytes 884740
  72.9 4.4 %copy-start.5 = (f32[5,1024]{1,0:T(8,128)S(1)}, f32[5,1024]{1,0:T(8,128)}, u32[]{:S(2)}) copy-start(f32[5,1024]{1,0:T(8,128)} %param.15) | copy-start | bytes 61444
  73.0 4.4 %copy-start.6 = (f32[5,1024]{1,0:T(8,128)S(1)}, f32[5,1024]{1,0:T(8,128)}, u32[]{:S(2)}) copy-start(f32[5,1024]{1,0:T(8,128)} %param.16) | copy-start | bytes 61444
  77.3 9.9 %copy-start.4 = (bf16[5,1024,320]{2,1,0:T(8,128)(2,1)S(1)}, bf16[5,1024,320]{2,1,0:T(8,128)(2,1)}, u32[]{:S(2)}) copy-start(bf16[5,1024,320]{2,1,0:T(8,128)(2,1)} %all-gather.2.cloned.1.call-done) | copy-start | bytes 9830404
  87.3 7.4 %copy-start.7 = (bf16[5,6,192,320]{3,2,1,0:T(8,128)(2,1)}, bf16[5,6,192,320]{3,2,1,0:T(8,128)(2,1)S(1)}, u32[]{:S(2)}) copy-start(bf16[5,6,192,320]{3,2,1,0:T(8,128)(2,1)S(1)} %multiply_convert_fusion) | copy-start | bytes 11059204
Sparse Core Ops, SparseCore 0:
  10.2 52.8 all-gather.1
  96.5 39.5 reduce-scatter.3

commit v13 on v12

--- a/solution.py
+++ b/solution.py
@@ -309,6 +309,115 @@
         scratch_shapes=[pltpu.SemaphoreType.DMA((8,)), pltpu.SemaphoreType.DMA((n, 2))],
         compiler_params=pltpu.CompilerParams(collective_id=cid, has_side_effects=True),
     )(block)
+
+
+def grid_ring_reduce_scatter(parts, outer, inner, cid):
+    slots, n_hi, n_lo, rows, outs = parts.shape
+    half = rows // 2
+    quarter = half // 2
+    ring = 4
+
+    def kernel(x_ref, out_ref, r1a, r1b, s1a, s1b, r2a, r2b, ta, tb, send_sem, recv_sem):
+        hi = lax.axis_index(outer)
+        lo = lax.axis_index(inner)
+        barrier = pltpu.get_barrier_semaphore()
+        for k in range(1, ring):
+            pl.semaphore_signal(barrier, inc=1, device_id={inner: lax.rem(lo + k, ring)},
+                                device_id_type=MESH_ID)
+            pl.semaphore_signal(barrier, inc=1, device_id={outer: lax.rem(hi + k, ring)},
+                                device_id_type=MESH_ID)
+        pl.semaphore_wait(barrier, 2 * ring - 2)
+        sends = []
+
+        def send(src_ref, dst_ref, axis, dev, sem):
+            copy = pltpu.make_async_remote_copy(
+                src_ref=src_ref, dst_ref=dst_ref, send_sem=send_sem.at[len(sends)],
+                recv_sem=recv_sem.at[sem], device_id={axis: dev}, device_id_type=MESH_ID)
+            copy.start()
+            sends.append(copy)
+
+        def arrive(dst_ref, sem):
+            pltpu.make_async_remote_copy(
+                src_ref=dst_ref, dst_ref=dst_ref, send_sem=send_sem.at[0],
+                recv_sem=recv_sem.at[sem], device_id={inner: lo},
+                device_id_type=MESH_ID).wait_recv()
+
+        def first_stage(axis, pos, piece, recv, transit, group):
+            up, down, far = lax.rem(pos + 1, ring), lax.rem(pos + 3, ring), lax.rem(pos + 2, ring)
+            send(piece(up, 0, half), recv.at[pos], axis, up, (group, pos, 0))
+            send(piece(down, 0, half), recv.at[pos], axis, down, (group, pos, 0))
+            send(piece(far, 0, quarter), transit.at[0], axis, up, (group + 4, 0, 0))
+            send(piece(far, quarter, quarter), transit.at[1], axis, down, (group + 4, 1, 0))
+            arrive(transit.at[0], (group + 4, 0, 0))
+            send(transit.at[0], recv.at[down, :, :, pl.ds(0, quarter)], axis, up, (group, down, 0))
+            arrive(transit.at[1], (group + 4, 1, 0))
+            send(transit.at[1], recv.at[up, :, :, pl.ds(quarter, quarter)], axis, down, (group, up, 1))
+            return up, down, far
+
+        ends_a = first_stage(inner, lo, lambda d, s, z: x_ref.at[:, :, d, pl.ds(s, z), :], r1a, ta, 0)
+        ends_b = first_stage(outer, hi, lambda d, s, z: x_ref.at[:, d, :, pl.ds(half + s, z), :], r1b, tb, 1)
+
+        def settle(recv, ends, group):
+            up, down, far = ends
+            arrive(recv.at[up], (group, up, 0))
+            arrive(recv.at[down], (group, down, 0))
+            arrive(recv.at[far, :, :, pl.ds(0, quarter)], (group, far, 0))
+            arrive(recv.at[far, :, :, pl.ds(quarter, quarter)], (group, far, 1))
+            return ends
+
+        sources_lo = settle(r1a, ends_a, 0)
+        for h in range(n_hi):
+            total = x_ref[:, h, lo, pl.ds(0, half), :].astype(jnp.float32)
+            for src in sources_lo:
+                total = total + r1a[src, :, h].astype(jnp.float32)
+            s1a[h] = total.astype(s1a.dtype)
+        for k in range(1, ring):
+            dev = lax.rem(hi + k, ring)
+            send(s1a.at[dev], r2a.at[hi], outer, dev, (2, hi, 0))
+        sources_hi = settle(r1b, ends_b, 1)
+        for l in range(n_lo):
+            total = x_ref[:, hi, l, pl.ds(half, half), :].astype(jnp.float32)
+            for src in sources_hi:
+                total = total + r1b[src, :, l].astype(jnp.float32)
+            s1b[l] = total.astype(s1b.dtype)
+        for k in range(1, ring):
+            dev = lax.rem(lo + k, ring)
+            send(s1b.at[dev], r2b.at[lo], inner, dev, (3, lo, 0))
+
+        total = s1a[hi].astype(jnp.float32)
+        for k in range(1, ring):
+            src = lax.rem(hi + ring - k, ring)
+            arrive(r2a.at[src], (2, src, 0))
+            total = total + r2a[src].astype(jnp.float32)
+        out_ref[:, pl.ds(0, half), :] = total
+        total = s1b[lo].astype(jnp.float32)
+        for k in range(1, ring):
+            src = lax.rem(lo + ring - k, ring)
+            arrive(r2b.at[src], (3, src, 0))
+            total = total + r2b[src].astype(jnp.float32)
+        out_ref[:, pl.ds(half, half), :] = total
+        for copy in sends:
+            copy.wait_send()
+
+    return pl.pallas_call(
+        kernel,
+        out_shape=jax.ShapeDtypeStruct((slots, rows, outs), jnp.float32),
+        in_specs=[pl.BlockSpec(memory_space=pltpu.VMEM)],
+        out_specs=pl.BlockSpec(memory_space=pltpu.VMEM),
+        scratch_shapes=[
+            pltpu.VMEM((ring, slots, n_hi, half, outs), parts.dtype),
+            pltpu.VMEM((ring, slots, n_lo, half, outs), parts.dtype),
+            pltpu.VMEM((n_hi, slots, half, outs), parts.dtype),
+            pltpu.VMEM((n_lo, slots, half, outs), parts.dtype),
+            pltpu.VMEM((ring, slots, half, outs), parts.dtype),
+            pltpu.VMEM((ring, slots, half, outs), parts.dtype),
+            pltpu.VMEM((2, slots, n_hi, quarter, outs), parts.dtype),
+            pltpu.VMEM((2, slots, n_lo, quarter, outs), parts.dtype),
+            pltpu.SemaphoreType.DMA((24,)),
+            pltpu.SemaphoreType.DMA((6, ring, 2)),
+        ],
+        compiler_params=pltpu.CompilerParams(collective_id=cid, has_side_effects=True),
+    )(parts)
 
 HEADS = 16
 WH = 6
@@ -473,7 +582,8 @@
     slots, outs = head_terms.shape[0], head_terms.shape[2]
     share_rows = width // lat_count
     head_parts = head_terms.astype(jnp.bfloat16).reshape(slots, outer, inner, share_rows, outs)
-    grad_head = grid_reduce_scatter(head_parts, LAT[0], LAT[1], 3)
+    reduce = grid_ring_reduce_scatter if outer == inner == 4 else grid_reduce_scatter
+    grad_head = reduce(head_parts, LAT[0], LAT[1], 3)
     return (latent, grad_latent, grad_head)
 
 

time: 168 us -> 188 us (1.12)
  Pallas kernels: 73.7 us -> 92.8 us
    pallas_call x1, Pallas kernels: 44.6 us -> 63.7 us  [grid_ring_reduce_scatter(): pl.pallas_call(kernel, out_shape=jax.ShapeDtypeStruct((slots, rows, outs)...]
  transfers between devices with their start and end apart: 6 -> 6, of which waited for: 2 -> 2; matrix products, arithmetic and copies ran while one was open for 26% -> 23% of each run, Pallas kernels for 44% -> 50%
where the time goes in v13:
time: 188 us; the launch traced here: 186 us
  Pallas kernels  92.8 us (49%)
  matrix products  37.2 us (20%)
  local copies, waits for them, and re-layouts  22.4 us (12%)
  between operations  14.3 us (8%)
  starting transfers between devices  8.88 us (5%)
  other arithmetic  7.22 us (4%)
  waiting for transfers between devices  3.37 us (2%)
    pallas_call x1, Pallas kernels, grid_ring_reduce_scatter(): pl.pallas_call(kernel, out_shape=jax.ShapeDtypeStruct((slots, rows, outs)...  63.7 us
    pallas_call x1, Pallas kernels, chip_ring_gather(): pl.pallas_call(kernel, out_shape=jax.ShapeDtypeStruct((n,) + block.shape,...  20.3 us
    dot_general x1, matrix products, slot_terms(): jnp.einsum('krnd,kdo->krno', rows, heads_full, preferred_element_type=jnp...  9.92 us
    dot_general x1, matrix products, slot_terms(): jnp.einsum('krnd,krno->kdo', rows, errors, preferred_element_type=jnp.flo...  9.27 us
    pallas_call x1, Pallas kernels, masked_window_attention(): pl.pallas_call(kernel, out_shape=jax.ShapeDtypeStruct((nq, width), jnp.bf...  8.79 us
    dot_general x1, matrix products, slot_terms(): jnp.einsum('krno,kdo->krnd', errors, heads_full, preferred_element_type=j...  7.4 us
    unnamed x22, local copies, waits for them, and re-layouts  6.75 us
    convert_element_type x1, local copies, waits for them, and re-layouts, local(): head_terms.astype(jnp.bfloat16)  5.87 us
  transfers between devices with their start and end apart: 6, of which 2 were waited for; matrix products, arithmetic and copies ran while one was open for 23% of the time, Pallas kernels for 50%

profile of v13, /device:TPU:0, one launch (start us, length us, event | category | flops | bytes accessed | tf_op | source)
XLA Modules:
  0.0 186.2 jit_solution(11074774644773433327)
XLA Ops:
  7.2 0.7 all-gather.2.cloned.1.call-update
  8.0 1.0 fusion.36
  9.0 1.3 collective-permute-start.1
  10.3 4.6 %collective-permute-start = (bf16[3,24,1024]{2,1,0:T(8,128)(2,1)S(1)}, bf16[3,24,1024]{2,1,0:T(8,128)(2,1)S(1)}, u32[]{:S(2)}, u32[]{:S(2)}) collective-permute-start(bf16[3,24,1024]{2,1,0:T(8,128)(2,1)S(1)} %get-tuple-element.8), channel_id=1, source_target_pairs={{0,8},{8,16},{16,24},{24,32},{32,40},{40,48},{48,56},{56,64},{64,7... | collective-permute-start | bytes 442376 | tf_op jit(solution)/shard_map/ppermute | solution.py:437
  15.2 0.7 select_n.62.kw_ref
  15.9 0.7 add.124.qw_ref
  16.6 0.8 select_reduce_fusion
  17.6 1.0 constant_dynamic-update-slice_fusion.1
  18.7 2.9 %collective-permute-start.3 = (bf16[12,6,1024]{2,1,0:T(8,128)(2,1)S(1)}, bf16[12,6,1024]{2,1,0:T(8,128)(2,1)S(1)}, u32[]{:S(2)}, u32[]{:S(2)}) collective-permute-start(bf16[12,6,1024]{2,1,0:T(8,128)(2,1)S(1)} %get-tuple-element.6), channel_id=1, source_target_pairs={{1,0},{2,1},{3,2},{4,3},{5,4},{6,5},{7,6},{0,7},{9,8},{10,9},{11,1... | collective-permute-start | bytes 442376 | tf_op jit(solution)/shard_map/ppermute | solution.py:438
  21.6 0.9 fusion.28
  22.5 2.5 %collective-permute-done.2 = bf16[12,6,1024]{2,1,0:T(8,128)(2,1)S(1)} collective-permute-done((bf16[12,6,1024]{2,1,0:T(8,128)(2,1)S(1)}, bf16[12,6,1024]{2,1,0:T(8,128)(2,1)S(1)}, u32[]{:S(2)}, u32[]{:S(2)}) %collective-permute-start.2) | collective-permute-done | bytes 147488 | tf_op jit(solution)/shard_map/ppermute | solution.py:437
  25.0 0.4 fusion.34
  25.5 1.9 multiply_reduce_fusion.1
  27.5 1.6 maximum_convert_fusion
  29.1 2.7 %reshape.198 = f32[432,1024]{1,0:T(8,128)} reshape(f32[12,36,1024]{2,1,0:T(8,128)} %maximum_convert_fusion) | data formatting | bytes 3538944 | tf_op jit(solution)/shard_map/convert_element_type | solution.py:444
  31.8 1.4 fusion.27
  33.3 2.8 %fusion.20.q_ref = bf16[144,1024]{1,0:T(8,128)(2,1)} fusion(bf16[144,1024]{1,0:T(8,128)(2,1)S(1)} %bitcast.47, bf16[1024,3072]{1,0:T(8,128)(2,1)} %param.13), kind=kOutput, calls=%fused_computation.22 | convolution fusion | flops 302137344 | bytes 2686976 | tf_op jit(solution)/shard_map/dot_general | solution.py:529
  36.1 5.5 %fusion.13.kv_ref = bf16[432,2048]{1,0:T(8,128)(2,1)} fusion(bf16[1024,3072]{1,0:T(8,128)(2,1)} %param.13, f32[432,1024]{1,0:T(8,128)S(1)} %copy-done.2, f32[1024]{0:T(1024)S(1)} %copy-done.3, f32[432]{0:T(512)S(1)} %rsqrt.13, f32[432]{0:T(512)S(1)} %div.54), kind=kOutput, calls=%fused_computation.17 | convolution fusion | flops 1814593536 | bytes 7740800 | tf_op jit(solution)/shard_map/dot_general | solution.py:524
  41.6 8.8 %shard_map.130 = bf16[144,1024]{1,0:T(8,128)(2,1)} custom-call(bf16[144,1024]{1,0:T(8,128)(2,1)} %fusion.20.q_ref, bf16[432,2048]{1,0:T(8,128)(2,1)} %fusion.13.kv_ref, s32[144,1]{1,0:T(8,128)} %add.124.qw_ref, s32[1,432]{1,0:T(1,128)} %select_n.62.kw_ref), custom_call_target="tpu_custom_call" | custom-call | tf_op jit(solution)/shard_map/pallas_call | solution.py:109
  50.4 1.4 fusion.37
  51.8 0.8 add_convert_fusion.7
  52.6 20.3 %shard_map.131 = bf16[8,144,1024]{2,1,0:T(8,128)(2,1)} custom-call(bf16[144,1024]{1,0:T(8,128)(2,1)} %bitcast.46), custom_call_target="tpu_custom_call" | custom-call | tf_op jit(solution)/shard_map/pallas_call | solution.py:304
  73.0 4.3 %copy.22 = f32[8,6,24,1024]{3,2,0,1:T(8,128)} copy(bf16[8,6,24,1024]{3,2,1,0:T(8,128)(2,1)} %bitcast.39) | data formatting | bytes 7077888 | tf_op jit(solution)/shard_map/convert_element_type | solution.py:486
  77.3 9.9 %multiply_convert_fusion = bf16[5,6,192,320]{3,2,1,0:T(8,128)(2,1)S(1)} fusion(bf16[5,6,192,320]{3,2,1,0:T(8,128)(2,1)} %param.18, f32[5,192]{1,0:T(8,128)S(1)} %fusion.28, bf16[5,1024,320]{2,1,0:T(8,128)(2,1)} %all-gather.2.cloned.1.call-done, f32[5,1024]{1,0:T(8,128)S(1)} %copy-done.6, f32[5,1024]{1,0:T(8,128)S(1)} %copy-done.5, f32[6,192,1024]{2,1,0:T(8,128)} %bitcast.41), kind=kOutput, calls=%fused_computation.10 | convolution fusion | flops 3799941120 | bytes 15412992 | tf_op jit(solution)/shard_map/krnd,kdo->krno/dot_general | solution.py:490
  87.3 7.4 %multiply_reduce_fusion = bf16[6,192,1024]{2,1,0:T(8,128)(2,1)S(1)} fusion(f32[5,1024]{1,0:T(8,128)S(1)} %copy-done.5, bf16[5,6,192,320]{3,2,1,0:T(8,128)(2,1)S(1)} %multiply_convert_fusion, bf16[5,1024,320]{2,1,0:T(8,128)(2,1)S(1)} %copy-done.4), kind=kOutput, calls=%fused_computation | convolution fusion | flops 3785490432 | bytes 9342976 | tf_op jit(solution)/shard_map/krno,kdo->krnd/dot_general | solution.py:494
  94.7 1.7 copy.28
  96.4 9.3 %fusion.8 = bf16[5,1024,320]{1,2,0:T(8,128)(2,1)} fusion(bf16[5,6,192,320]{3,2,1,0:T(8,128)(2,1)} %copy-done.7, f32[5,1024]{1,0:T(8,128)S(1)} %copy-done.6, f32[5,1024]{1,0:T(8,128)S(1)} %copy-done.5, f32[6,192,1024]{2,1,0:T(8,128)} %bitcast.42), kind=kOutput, calls=%fused_computation.12 | convolution fusion | flops 3795845120 | bytes 11722752 | tf_op jit(solution)/shard_map/krnd,krno->kdo/dot_general | solution.py:496
  105.6 5.9 %copy.23 = bf16[5,1024,320]{2,1,0:T(8,128)(2,1)} copy(bf16[5,1024,320]{1,2,0:T(8,128)(2,1)} %fusion.8) | data formatting | bytes 6553600 | tf_op jit(solution)/shard_map/convert_element_type | solution.py:584
  111.5 63.7 %shard_map.132 = f32[5,64,320]{2,1,0:T(8,128)} custom-call(bf16[5,4,4,64,320]{4,3,2,1,0:T(8,128)(2,1)} %bitcast.38), custom_call_target="tpu_custom_call" | custom-call | tf_op jit(solution)/shard_map/pallas_call | solution.py:402
  175.3 1.3 reshape.204
  176.6 0.9 copy.27
  177.5 1.8 copy.33
  (43 shorter events, 1.1 us)
Async XLA Ops:
  7.2 43.2 %copy-start = (bf16[1024,1024]{1,0:T(8,128)(2,1)S(1)}, bf16[1024,1024]{1,0:T(8,128)(2,1)}, u32[]{:S(2)}) copy-start(bf16[1024,1024]{1,0:T(8,128)(2,1)} %param.14) | copy-start | bytes 6291460
  7.2 70.1 %all-gather.2.cloned.1.call-start = ((), (), s32[]{:S(2)}) async-start(), calls=%async_computation.1 | async-start | bytes 4177920 | tf_op jit(solution)/shard_map/all_gather | solution.py:559
  7.9 167.3 %reduce-scatter.4.cloned.1.call-start = ((), (), s32[]{:S(2)}) async-start(), calls=%async_computation.2 | async-start | bytes 2654208
  9.0 9.6 %collective-permute-start.1 = (bf16[3,24,1024]{2,1,0:T(8,128)(2,1)S(1)}, bf16[3,24,1024]{2,1,0:T(8,128)(2,1)S(1)}, u32[]{:S(2)}, u32[]{:S(2)}) collective-permute-start(bf16[3,24,1024]{2,1,0:T(8,128)(2,1)S(1)} %get-tuple-element.7), channel_id=1, source_target_pairs={{8,0},{16,8},{24,16},{32,24},{40,32},{48,40},{56,48},{64,56},{72,6... | collective-permute-start | bytes 442376 | tf_op jit(solution)/shard_map/ppermute | solution.py:438
  10.3 7.3 %collective-permute-start = (bf16[3,24,1024]{2,1,0:T(8,128)(2,1)S(1)}, bf16[3,24,1024]{2,1,0:T(8,128)(2,1)S(1)}, u32[]{:S(2)}, u32[]{:S(2)}) collective-permute-start(bf16[3,24,1024]{2,1,0:T(8,128)(2,1)S(1)} %get-tuple-element.8), channel_id=1, source_target_pairs={{0,8},{8,16},{16,24},{24,32},{32,40},{40,48},{48,56},{56,64},{64,7... | collective-permute-start | bytes 442376 | tf_op jit(solution)/shard_map/ppermute | solution.py:437
  18.6 6.3 %collective-permute-start.2 = (bf16[12,6,1024]{2,1,0:T(8,128)(2,1)S(1)}, bf16[12,6,1024]{2,1,0:T(8,128)(2,1)S(1)}, u32[]{:S(2)}, u32[]{:S(2)}) collective-permute-start(bf16[12,6,1024]{2,1,0:T(8,128)(2,1)S(1)} %get-tuple-element.5), channel_id=1, source_target_pairs={{0,1},{1,2},{2,3},{3,4},{4,5},{5,6},{6,7},{7,0},{8,9},{9,10},{10,1... | collective-permute-start | bytes 442376 | tf_op jit(solution)/shard_map/ppermute | solution.py:437
  18.7 6.3 %collective-permute-start.3 = (bf16[12,6,1024]{2,1,0:T(8,128)(2,1)S(1)}, bf16[12,6,1024]{2,1,0:T(8,128)(2,1)S(1)}, u32[]{:S(2)}, u32[]{:S(2)}) collective-permute-start(bf16[12,6,1024]{2,1,0:T(8,128)(2,1)S(1)} %get-tuple-element.6), channel_id=1, source_target_pairs={{1,0},{2,1},{3,2},{4,3},{5,4},{6,5},{7,6},{0,7},{9,8},{10,9},{11,1... | collective-permute-start | bytes 442376 | tf_op jit(solution)/shard_map/ppermute | solution.py:438
  27.4 4.5 %copy-start.3 = (f32[1024]{0:T(1024)S(1)}, f32[1024]{0:T(1024)}, u32[]{:S(2)}) copy-start(f32[1024]{0:T(1024)} %param.12) | copy-start | bytes 12292
  31.8 4.2 %copy-start.2 = (f32[432,1024]{1,0:T(8,128)S(1)}, f32[432,1024]{1,0:T(8,128)}, u32[]{:S(2)}) copy-start(f32[432,1024]{1,0:T(8,128)} %reshape.198) | copy-start | bytes 5308420
  41.6 10.3 %copy-start.1 = (bf16[6,24,1024]{2,1,0:T(8,128)(2,1)S(1)}, bf16[6,24,1024]{2,1,0:T(8,128)(2,1)}, u32[]{:S(2)}) copy-start(bf16[6,24,1024]{2,1,0:T(8,128)(2,1)} %param.11) | copy-start | bytes 884740
  72.9 4.4 %copy-start.5 = (f32[5,1024]{1,0:T(8,128)S(1)}, f32[5,1024]{1,0:T(8,128)}, u32[]{:S(2)}) copy-start(f32[5,1024]{1,0:T(8,128)} %param.15) | copy-start | bytes 61444
  73.0 4.4 %copy-start.6 = (f32[5,1024]{1,0:T(8,128)S(1)}, f32[5,1024]{1,0:T(8,128)}, u32[]{:S(2)}) copy-start(f32[5,1024]{1,0:T(8,128)} %param.16) | copy-start | bytes 61444
  77.3 9.9 %copy-start.4 = (bf16[5,1024,320]{2,1,0:T(8,128)(2,1)S(1)}, bf16[5,1024,320]{2,1,0:T(8,128)(2,1)}, u32[]{:S(2)}) copy-start(bf16[5,1024,320]{2,1,0:T(8,128)(2,1)} %all-gather.2.cloned.1.call-done) | copy-start | bytes 9830404
  87.3 7.4 %copy-start.7 = (bf16[5,6,192,320]{3,2,1,0:T(8,128)(2,1)}, bf16[5,6,192,320]{3,2,1,0:T(8,128)(2,1)S(1)}, u32[]{:S(2)}) copy-start(bf16[5,6,192,320]{3,2,1,0:T(8,128)(2,1)S(1)} %multiply_convert_fusion) | copy-start | bytes 11059204
Sparse Core Ops, SparseCore 0:
  10.2 52.8 all-gather.1
  96.5 39.5 reduce-scatter.3

commit v14 on v13

--- a/solution.py
+++ b/solution.py
@@ -342,20 +342,25 @@
                 recv_sem=recv_sem.at[sem], device_id={inner: lo},
                 device_id_type=MESH_ID).wait_recv()
 
-        def first_stage(axis, pos, piece, recv, transit, group):
+        def launch(axis, pos, piece, recv, transit, group):
             up, down, far = lax.rem(pos + 1, ring), lax.rem(pos + 3, ring), lax.rem(pos + 2, ring)
+            send(piece(far, 0, quarter), transit.at[0], axis, up, (group + 4, 0, 0))
+            send(piece(far, quarter, quarter), transit.at[1], axis, down, (group + 4, 1, 0))
             send(piece(up, 0, half), recv.at[pos], axis, up, (group, pos, 0))
             send(piece(down, 0, half), recv.at[pos], axis, down, (group, pos, 0))
-            send(piece(far, 0, quarter), transit.at[0], axis, up, (group + 4, 0, 0))
-            send(piece(far, quarter, quarter), transit.at[1], axis, down, (group + 4, 1, 0))
+            return up, down, far
+
+        def relay(axis, ends, recv, transit, group):
+            up, down, far = ends
             arrive(transit.at[0], (group + 4, 0, 0))
             send(transit.at[0], recv.at[down, :, :, pl.ds(0, quarter)], axis, up, (group, down, 0))
             arrive(transit.at[1], (group + 4, 1, 0))
             send(transit.at[1], recv.at[up, :, :, pl.ds(quarter, quarter)], axis, down, (group, up, 1))
-            return up, down, far
-
-        ends_a = first_stage(inner, lo, lambda d, s, z: x_ref.at[:, :, d, pl.ds(s, z), :], r1a, ta, 0)
-        ends_b = first_stage(outer, hi, lambda d, s, z: x_ref.at[:, d, :, pl.ds(half + s, z), :], r1b, tb, 1)
+
+        ends_a = launch(inner, lo, lambda d, s, z: x_ref.at[:, :, d, pl.ds(s, z), :], r1a, ta, 0)
+        ends_b = launch(outer, hi, lambda d, s, z: x_ref.at[:, d, :, pl.ds(half + s, z), :], r1b, tb, 1)
+        relay(inner, ends_a, r1a, ta, 0)
+        relay(outer, ends_b, r1b, tb, 1)
 
         def settle(recv, ends, group):
             up, down, far = ends

time: 188 us -> 168 us (0.89)
  Pallas kernels: 92.8 us -> 73.8 us
    pallas_call x1, Pallas kernels: 63.7 us -> 44.7 us  [grid_ring_reduce_scatter(): pl.pallas_call(kernel, out_shape=jax.ShapeDtypeStruct((slots, rows, outs)...]
  transfers between devices with their start and end apart: 6 -> 6, of which waited for: 2 -> 2; matrix products, arithmetic and copies ran while one was open for 23% -> 26% of each run, Pallas kernels for 50% -> 44%
where the time goes in v14:
time: 168 us; the launch traced here: 167 us
  Pallas kernels  73.8 us (44%)
  matrix products  37.2 us (22%)
  local copies, waits for them, and re-layouts  22.4 us (13%)
  between operations  14.3 us (9%)
  starting transfers between devices  8.88 us (5%)
  other arithmetic  7.22 us (4%)
  waiting for transfers between devices  3.37 us (2%)
    pallas_call x1, Pallas kernels, grid_ring_reduce_scatter(): pl.pallas_call(kernel, out_shape=jax.ShapeDtypeStruct((slots, rows, outs)...  44.7 us
    pallas_call x1, Pallas kernels, chip_ring_gather(): pl.pallas_call(kernel, out_shape=jax.ShapeDtypeStruct((n,) + block.shape,...  20.3 us
    dot_general x1, matrix products, slot_terms(): jnp.einsum('krnd,kdo->krno', rows, heads_full, preferred_element_type=jnp...  9.92 us
    dot_general x1, matrix products, slot_terms(): jnp.einsum('krnd,krno->kdo', rows, errors, preferred_element_type=jnp.flo...  9.27 us
    pallas_call x1, Pallas kernels, masked_window_attention(): pl.pallas_call(kernel, out_shape=jax.ShapeDtypeStruct((nq, width), jnp.bf...  8.79 us
    dot_general x1, matrix products, slot_terms(): jnp.einsum('krno,kdo->krnd', errors, heads_full, preferred_element_type=j...  7.4 us
    unnamed x22, local copies, waits for them, and re-layouts  6.75 us
    convert_element_type x1, local copies, waits for them, and re-layouts, local(): head_terms.astype(jnp.bfloat16)  5.87 us
  transfers between devices with their start and end apart: 6, of which 2 were waited for; matrix products, arithmetic and copies ran while one was open for 26% of the time, Pallas kernels for 44%

profile of v14, /device:TPU:0, one launch (start us, length us, event | category | flops | bytes accessed | tf_op | source)
XLA Modules:
  0.0 167.2 jit_solution(5162031092787227684)
XLA Ops:
  7.2 0.7 all-gather.2.cloned.1.call-update
  8.0 1.0 fusion.36
  9.0 1.3 collective-permute-start.1
  10.3 4.6 %collective-permute-start = (bf16[3,24,1024]{2,1,0:T(8,128)(2,1)S(1)}, bf16[3,24,1024]{2,1,0:T(8,128)(2,1)S(1)}, u32[]{:S(2)}, u32[]{:S(2)}) collective-permute-start(bf16[3,24,1024]{2,1,0:T(8,128)(2,1)S(1)} %get-tuple-element.8), channel_id=1, source_target_pairs={{0,8},{8,16},{16,24},{24,32},{32,40},{40,48},{48,56},{56,64},{64,7... | collective-permute-start | bytes 442376 | tf_op jit(solution)/shard_map/ppermute | solution.py:442
  15.2 0.7 select_n.62.kw_ref
  15.9 0.7 add.124.qw_ref
  16.6 0.8 select_reduce_fusion
  17.6 1.0 constant_dynamic-update-slice_fusion.1
  18.7 2.9 %collective-permute-start.3 = (bf16[12,6,1024]{2,1,0:T(8,128)(2,1)S(1)}, bf16[12,6,1024]{2,1,0:T(8,128)(2,1)S(1)}, u32[]{:S(2)}, u32[]{:S(2)}) collective-permute-start(bf16[12,6,1024]{2,1,0:T(8,128)(2,1)S(1)} %get-tuple-element.6), channel_id=1, source_target_pairs={{1,0},{2,1},{3,2},{4,3},{5,4},{6,5},{7,6},{0,7},{9,8},{10,9},{11,1... | collective-permute-start | bytes 442376 | tf_op jit(solution)/shard_map/ppermute | solution.py:443
  21.6 0.9 fusion.28
  22.5 2.5 %collective-permute-done.2 = bf16[12,6,1024]{2,1,0:T(8,128)(2,1)S(1)} collective-permute-done((bf16[12,6,1024]{2,1,0:T(8,128)(2,1)S(1)}, bf16[12,6,1024]{2,1,0:T(8,128)(2,1)S(1)}, u32[]{:S(2)}, u32[]{:S(2)}) %collective-permute-start.2) | collective-permute-done | bytes 147488 | tf_op jit(solution)/shard_map/ppermute | solution.py:442
  25.0 0.4 fusion.34
  25.5 1.9 %multiply_reduce_fusion.1 = (f32[12,36]{1,0:T(8,128)S(1)}, f32[12,36,1024]{2,1,0:T(8,128)}) fusion(f32[12,36]{1,0:T(8,128)S(1)} %broadcast_multiply_fusion, bf16[12,6,1024]{2,1,0:T(8,128)(2,1)S(1)} %collective-permute-done.3, bf16[12,24,1024]{2,1,0:T(8,128)(2,1)S(1)} %constant_dynamic-update-slice_fusion, bf16[12,6,1024]{2,1,0:T(8,128)(2,1)S(1)} %collective-permute-done.2), kind=kLoop, calls=%fused_computation.20 | loop fusion | flops 3980880 | bytes 2657664 | tf_op jit(solution)/shard_map/reduce_sum | solution.py:452
  27.5 1.6 maximum_convert_fusion
  29.1 2.7 %reshape.198 = f32[432,1024]{1,0:T(8,128)} reshape(f32[12,36,1024]{2,1,0:T(8,128)} %maximum_convert_fusion) | data formatting | bytes 3538944 | tf_op jit(solution)/shard_map/convert_element_type | solution.py:449
  31.8 1.4 fusion.27
  33.3 2.8 %fusion.20.q_ref = bf16[144,1024]{1,0:T(8,128)(2,1)} fusion(bf16[144,1024]{1,0:T(8,128)(2,1)S(1)} %bitcast.47, bf16[1024,3072]{1,0:T(8,128)(2,1)} %param.13), kind=kOutput, calls=%fused_computation.22 | convolution fusion | flops 302137344 | bytes 2686976 | tf_op jit(solution)/shard_map/dot_general | solution.py:534
  36.1 5.5 %fusion.13.kv_ref = bf16[432,2048]{1,0:T(8,128)(2,1)} fusion(bf16[1024,3072]{1,0:T(8,128)(2,1)} %param.13, f32[432,1024]{1,0:T(8,128)S(1)} %copy-done.2, f32[1024]{0:T(1024)S(1)} %copy-done.3, f32[432]{0:T(512)S(1)} %rsqrt.13, f32[432]{0:T(512)S(1)} %div.54), kind=kOutput, calls=%fused_computation.17 | convolution fusion | flops 1814593536 | bytes 7740800 | tf_op jit(solution)/shard_map/dot_general | solution.py:529
  41.6 8.8 %shard_map.130 = bf16[144,1024]{1,0:T(8,128)(2,1)} custom-call(bf16[144,1024]{1,0:T(8,128)(2,1)} %fusion.20.q_ref, bf16[432,2048]{1,0:T(8,128)(2,1)} %fusion.13.kv_ref, s32[144,1]{1,0:T(8,128)} %add.124.qw_ref, s32[1,432]{1,0:T(1,128)} %select_n.62.kw_ref), custom_call_target="tpu_custom_call" | custom-call | tf_op jit(solution)/shard_map/pallas_call | solution.py:109
  50.4 1.4 fusion.37
  51.8 0.8 add_convert_fusion.7
  52.6 20.3 %shard_map.131 = bf16[8,144,1024]{2,1,0:T(8,128)(2,1)} custom-call(bf16[144,1024]{1,0:T(8,128)(2,1)} %bitcast.46), custom_call_target="tpu_custom_call" | custom-call | tf_op jit(solution)/shard_map/pallas_call | solution.py:304
  73.0 4.3 %copy.22 = f32[8,6,24,1024]{3,2,0,1:T(8,128)} copy(bf16[8,6,24,1024]{3,2,1,0:T(8,128)(2,1)} %bitcast.39) | data formatting | bytes 7077888 | tf_op jit(solution)/shard_map/convert_element_type | solution.py:491
  77.3 9.9 %multiply_convert_fusion = bf16[5,6,192,320]{3,2,1,0:T(8,128)(2,1)S(1)} fusion(bf16[5,6,192,320]{3,2,1,0:T(8,128)(2,1)} %param.18, f32[5,192]{1,0:T(8,128)S(1)} %fusion.28, bf16[5,1024,320]{2,1,0:T(8,128)(2,1)} %all-gather.2.cloned.1.call-done, f32[5,1024]{1,0:T(8,128)S(1)} %copy-done.6, f32[5,1024]{1,0:T(8,128)S(1)} %copy-done.5, f32[6,192,1024]{2,1,0:T(8,128)} %bitcast.41), kind=kOutput, calls=%fused_computation.10 | convolution fusion | flops 3799941120 | bytes 15412992 | tf_op jit(solution)/shard_map/krnd,kdo->krno/dot_general | solution.py:495
  87.3 7.4 %multiply_reduce_fusion = bf16[6,192,1024]{2,1,0:T(8,128)(2,1)S(1)} fusion(f32[5,1024]{1,0:T(8,128)S(1)} %copy-done.5, bf16[5,6,192,320]{3,2,1,0:T(8,128)(2,1)S(1)} %multiply_convert_fusion, bf16[5,1024,320]{2,1,0:T(8,128)(2,1)S(1)} %copy-done.4), kind=kOutput, calls=%fused_computation | convolution fusion | flops 3785490432 | bytes 9342976 | tf_op jit(solution)/shard_map/krno,kdo->krnd/dot_general | solution.py:499
  94.7 1.7 copy.28
  96.4 9.3 %fusion.8 = bf16[5,1024,320]{1,2,0:T(8,128)(2,1)} fusion(bf16[5,6,192,320]{3,2,1,0:T(8,128)(2,1)} %copy-done.7, f32[5,1024]{1,0:T(8,128)S(1)} %copy-done.6, f32[5,1024]{1,0:T(8,128)S(1)} %copy-done.5, f32[6,192,1024]{2,1,0:T(8,128)} %bitcast.42), kind=kOutput, calls=%fused_computation.12 | convolution fusion | flops 3795845120 | bytes 11722752 | tf_op jit(solution)/shard_map/krnd,krno->kdo/dot_general | solution.py:501
  105.6 5.9 %copy.23 = bf16[5,1024,320]{2,1,0:T(8,128)(2,1)} copy(bf16[5,1024,320]{1,2,0:T(8,128)(2,1)} %fusion.8) | data formatting | bytes 6553600 | tf_op jit(solution)/shard_map/convert_element_type | solution.py:589
  111.5 44.7 %shard_map.132 = f32[5,64,320]{2,1,0:T(8,128)} custom-call(bf16[5,4,4,64,320]{4,3,2,1,0:T(8,128)(2,1)} %bitcast.38), custom_call_target="tpu_custom_call" | custom-call | tf_op jit(solution)/shard_map/pallas_call | solution.py:407
  156.2 1.3 reshape.204
  157.6 0.9 copy.27
  158.5 1.8 %copy.33 = f32[5,64,320]{2,1,0:T(8,128)} copy(f32[5,64,320]{2,1,0:T(8,128)} %shard_map.132) | data formatting | bytes 819200
  (43 shorter events, 1.1 us)
Async XLA Ops:
  7.2 43.2 %copy-start = (bf16[1024,1024]{1,0:T(8,128)(2,1)S(1)}, bf16[1024,1024]{1,0:T(8,128)(2,1)}, u32[]{:S(2)}) copy-start(bf16[1024,1024]{1,0:T(8,128)(2,1)} %param.14) | copy-start | bytes 6291460
  7.2 70.1 %all-gather.2.cloned.1.call-start = ((), (), s32[]{:S(2)}) async-start(), calls=%async_computation.1 | async-start | bytes 4177920 | tf_op jit(solution)/shard_map/all_gather | solution.py:564
  7.9 148.3 %reduce-scatter.4.cloned.1.call-start = ((), (), s32[]{:S(2)}) async-start(), calls=%async_computation.2 | async-start | bytes 2654208
  9.0 9.6 %collective-permute-start.1 = (bf16[3,24,1024]{2,1,0:T(8,128)(2,1)S(1)}, bf16[3,24,1024]{2,1,0:T(8,128)(2,1)S(1)}, u32[]{:S(2)}, u32[]{:S(2)}) collective-permute-start(bf16[3,24,1024]{2,1,0:T(8,128)(2,1)S(1)} %get-tuple-element.7), channel_id=1, source_target_pairs={{8,0},{16,8},{24,16},{32,24},{40,32},{48,40},{56,48},{64,56},{72,6... | collective-permute-start | bytes 442376 | tf_op jit(solution)/shard_map/ppermute | solution.py:443
  10.3 7.3 %collective-permute-start = (bf16[3,24,1024]{2,1,0:T(8,128)(2,1)S(1)}, bf16[3,24,1024]{2,1,0:T(8,128)(2,1)S(1)}, u32[]{:S(2)}, u32[]{:S(2)}) collective-permute-start(bf16[3,24,1024]{2,1,0:T(8,128)(2,1)S(1)} %get-tuple-element.8), channel_id=1, source_target_pairs={{0,8},{8,16},{16,24},{24,32},{32,40},{40,48},{48,56},{56,64},{64,7... | collective-permute-start | bytes 442376 | tf_op jit(solution)/shard_map/ppermute | solution.py:442
  18.6 6.3 %collective-permute-start.2 = (bf16[12,6,1024]{2,1,0:T(8,128)(2,1)S(1)}, bf16[12,6,1024]{2,1,0:T(8,128)(2,1)S(1)}, u32[]{:S(2)}, u32[]{:S(2)}) collective-permute-start(bf16[12,6,1024]{2,1,0:T(8,128)(2,1)S(1)} %get-tuple-element.5), channel_id=1, source_target_pairs={{0,1},{1,2},{2,3},{3,4},{4,5},{5,6},{6,7},{7,0},{8,9},{9,10},{10,1... | collective-permute-start | bytes 442376 | tf_op jit(solution)/shard_map/ppermute | solution.py:442
  18.7 6.3 %collective-permute-start.3 = (bf16[12,6,1024]{2,1,0:T(8,128)(2,1)S(1)}, bf16[12,6,1024]{2,1,0:T(8,128)(2,1)S(1)}, u32[]{:S(2)}, u32[]{:S(2)}) collective-permute-start(bf16[12,6,1024]{2,1,0:T(8,128)(2,1)S(1)} %get-tuple-element.6), channel_id=1, source_target_pairs={{1,0},{2,1},{3,2},{4,3},{5,4},{6,5},{7,6},{0,7},{9,8},{10,9},{11,1... | collective-permute-start | bytes 442376 | tf_op jit(solution)/shard_map/ppermute | solution.py:443
  27.4 4.5 %copy-start.3 = (f32[1024]{0:T(1024)S(1)}, f32[1024]{0:T(1024)}, u32[]{:S(2)}) copy-start(f32[1024]{0:T(1024)} %param.12) | copy-start | bytes 12292
  31.8 4.2 %copy-start.2 = (f32[432,1024]{1,0:T(8,128)S(1)}, f32[432,1024]{1,0:T(8,128)}, u32[]{:S(2)}) copy-start(f32[432,1024]{1,0:T(8,128)} %reshape.198) | copy-start | bytes 5308420
  41.6 10.3 %copy-start.1 = (bf16[6,24,1024]{2,1,0:T(8,128)(2,1)S(1)}, bf16[6,24,1024]{2,1,0:T(8,128)(2,1)}, u32[]{:S(2)}) copy-start(bf16[6,24,1024]{2,1,0:T(8,128)(2,1)} %param.11) | copy-start | bytes 884740
  72.9 4.4 %copy-start.5 = (f32[5,1024]{1,0:T(8,128)S(1)}, f32[5,1024]{1,0:T(8,128)}, u32[]{:S(2)}) copy-start(f32[5,1024]{1,0:T(8,128)} %param.15) | copy-start | bytes 61444
  73.0 4.4 %copy-start.6 = (f32[5,1024]{1,0:T(8,128)S(1)}, f32[5,1024]{1,0:T(8,128)}, u32[]{:S(2)}) copy-start(f32[5,1024]{1,0:T(8,128)} %param.16) | copy-start | bytes 61444
  77.3 9.9 %copy-start.4 = (bf16[5,1024,320]{2,1,0:T(8,128)(2,1)S(1)}, bf16[5,1024,320]{2,1,0:T(8,128)(2,1)}, u32[]{:S(2)}) copy-start(bf16[5,1024,320]{2,1,0:T(8,128)(2,1)} %all-gather.2.cloned.1.call-done) | copy-start | bytes 9830404
  87.3 7.4 %copy-start.7 = (bf16[5,6,192,320]{3,2,1,0:T(8,128)(2,1)}, bf16[5,6,192,320]{3,2,1,0:T(8,128)(2,1)S(1)}, u32[]{:S(2)}) copy-start(bf16[5,6,192,320]{3,2,1,0:T(8,128)(2,1)S(1)} %multiply_convert_fusion) | copy-start | bytes 11059204
Sparse Core Ops, SparseCore 0:
  10.2 52.8 all-gather.1
  96.5 39.5 reduce-scatter.3

commit v15 on v12

--- a/solution.py
+++ b/solution.py
@@ -410,29 +410,35 @@
     ext_rows = band_rows + WH
     ext_cols = band_cols + WW
     extended = padded(patches, ((LAT, 0),), half_rows, False)
+    extended, own = lax.optimization_barrier((extended, patches))
+    own_normed = layer_norm(own, norm_gain).reshape(-1, width)
+    queries = jnp.dot(own_normed, input_proj[:, :width], preferred_element_type=jnp.float32)
+    queries = queries.astype(jnp.bfloat16)
+    own_keyval = jnp.dot(own_normed, input_proj[:, width:], preferred_element_type=jnp.float32)
     extended = padded(extended, (("var", 1),), half_cols, True)
-    normed_ext = layer_norm(extended, norm_gain)
-    keyval = jnp.dot(
-        normed_ext.reshape(-1, width), input_proj[:, width:], preferred_element_type=jnp.float32
-    )
-    keyval = keyval.astype(jnp.bfloat16).reshape(ext_rows, ext_cols, 2 * width)
-    normed = normed_ext[half_rows : half_rows + band_rows, half_cols : half_cols + band_cols]
-    queries = jnp.dot(
-        normed.reshape(-1, width), input_proj[:, :width], preferred_element_type=jnp.float32
-    )
-    queries = queries.astype(jnp.bfloat16)
+
+    def ring(grid):
+        top, bottom = grid[:half_rows], grid[half_rows + band_rows :]
+        middle = grid[half_rows : half_rows + band_rows]
+        left, right = middle[:, :half_cols], middle[:, half_cols + band_cols :]
+        return jnp.concatenate(
+            [part.reshape((-1,) + grid.shape[2:]) for part in (top, bottom, left, right)]
+        )
+
+    halo_normed = layer_norm(ring(extended), norm_gain)
+    halo_keyval = jnp.dot(halo_normed, input_proj[:, width:], preferred_element_type=jnp.float32)
+    keyval = jnp.concatenate([own_keyval, halo_keyval]).astype(jnp.bfloat16)
     global_row = lat_place * band_rows - half_rows + jnp.arange(ext_rows, dtype=jnp.int32)
     row_valid = (global_row >= 0) & (global_row < lat_count * band_rows)
     win_cols = ext_cols // WW
     ext_r = jnp.arange(ext_rows, dtype=jnp.int32)[:, None]
     ext_c = jnp.arange(ext_cols, dtype=jnp.int32)[None, :]
-    key_win = jnp.where(row_valid[:, None], (ext_r // WH) * win_cols + ext_c // WW, -1)
-    own_r = ext_r[half_rows : half_rows + band_rows]
-    own_c = ext_c[:, half_cols : half_cols + band_cols]
-    query_win = (own_r // WH) * win_cols + own_c // WW
+    key_grid = jnp.where(row_valid[:, None], (ext_r // WH) * win_cols + ext_c // WW, -1)
+    query_win = key_grid[half_rows : half_rows + band_rows, half_cols : half_cols + band_cols]
+    key_win = jnp.concatenate([query_win.reshape(-1), ring(key_grid)])
     attn = masked_window_attention(
         queries,
-        keyval.reshape(ext_rows * ext_cols, 2 * width),
+        keyval,
         query_win.reshape(-1, 1),
         key_win.reshape(1, -1),
         HEADS,

time: 168 us -> 165 us (0.982)
  Pallas kernels: 73.7 us -> 66.9 us
  other arithmetic: 7.22 us -> 10.7 us
  matrix products: 37.2 us -> 40.6 us
    pallas_call x1, Pallas kernels: 44.6 us -> 40.3 us  [grid_reduce_scatter(): pl.pallas_call(kernel, out_shape=jax.ShapeDtypeStruct((slots, rows, outs)...]
    convert_element_type x1 -> x0, local copies, waits for them, and re-layouts: 2.71 us -> none  [layer_norm(): wide = values.astype(jnp.float32)]
    ppermute x2, waiting for transfers between devices: 2.64 us -> 0.01 us  [padded(): before = lax.ppermute(last, axis, up)]
    concatenate x0 -> x2, other arithmetic: none -> 2.46 us  [the longest x1 1.43 us: local(): keyval = jnp.concatenate([own_keyval, halo_keyval]).astype(jnp.bfloat16)]
    pallas_call x1, Pallas kernels: 20.3 us -> 17.9 us  [chip_ring_gather(): pl.pallas_call(kernel, out_shape=jax.ShapeDtypeStruct((n,) + block.shape,...]
    dot_general x2 -> x3, matrix products: 8.31 us -> 10.5 us  [the longest x1 3.89 us: local(): jnp.dot(own_normed, input_proj[:, width:], preferred_element_type=jnp.flo...]
    reshape x0 -> x10, local copies, waits for them, and re-layouts: none -> 1.89 us  [the longest x8 1.1 us: ring(): part.reshape((-1,) + grid.shape[2:])]
    reduce_sum x1 -> x2, other arithmetic: 0.44 us -> 2.19 us  [layer_norm(): average = jnp.mean(wide, axis=-1, keepdims=True)]
  transfers between devices with their start and end apart: 6 -> 6, of which waited for: 2 -> 1; matrix products, arithmetic and copies ran while one was open for 26% -> 29% of each run, Pallas kernels for 44% -> 41%
where the time goes in v15:
time: 165 us; the launch traced here: 164 us
  Pallas kernels  66.9 us (41%)
  matrix products  40.6 us (25%)
  local copies, waits for them, and re-layouts  21 us (13%)
  between operations  14.3 us (9%)
  other arithmetic  10.7 us (6%)
  starting transfers between devices  7.9 us (5%)
  waiting for transfers between devices  2.28 us (1%)
    pallas_call x1, Pallas kernels, grid_reduce_scatter(): pl.pallas_call(kernel, out_shape=jax.ShapeDtypeStruct((slots, rows, outs)...  40.3 us
    pallas_call x1, Pallas kernels, chip_ring_gather(): pl.pallas_call(kernel, out_shape=jax.ShapeDtypeStruct((n,) + block.shape,...  17.9 us
    dot_general x1, matrix products, slot_terms(): jnp.einsum('krnd,kdo->krno', rows, heads_full, preferred_element_type=jnp...  10.6 us
    dot_general x1, matrix products, slot_terms(): jnp.einsum('krnd,krno->kdo', rows, errors, preferred_element_type=jnp.flo...  9.27 us
    pallas_call x1, Pallas kernels, masked_window_attention(): pl.pallas_call(kernel, out_shape=jax.ShapeDtypeStruct((nq, width), jnp.bf...  8.75 us
    dot_general x1, matrix products, slot_terms(): jnp.einsum('krno,kdo->krnd', errors, heads_full, preferred_element_type=j...  7.22 us
    unnamed x24, local copies, waits for them, and re-layouts  7.12 us
    convert_element_type x1, local copies, waits for them, and re-layouts, local(): head_terms.astype(jnp.bfloat16)  5.78 us
  transfers between devices with their start and end apart: 6, of which 1 were waited for; matrix products, arithmetic and copies ran while one was open for 29% of the time, Pallas kernels for 41%

profile of v15, /device:TPU:0, one launch (start us, length us, event | category | flops | bytes accessed | tf_op | source)
XLA Modules:
  0.0 163.7 jit_solution(4012130569100910099)
XLA Ops:
  8.0 1.0 fusion.48
  9.0 3.6 %collective-permute-start = (bf16[3,24,1024]{2,1,0:T(8,128)(2,1)S(1)}, bf16[3,24,1024]{2,1,0:T(8,128)(2,1)S(1)}, u32[]{:S(2)}, u32[]{:S(2)}) collective-permute-start(bf16[3,24,1024]{2,1,0:T(8,128)(2,1)S(1)} %get-tuple-element.11), channel_id=1, source_target_pairs={{0,8},{8,16},{16,24},{24,32},{32,40},{40,48},{48,56},{56,64},{64,7... | collective-permute-start | bytes 442376 | tf_op jit(solution)/shard_map/ppermute | solution.py:328
  12.6 1.3 collective-permute-start.1
  15.9 0.8 select_reduce_fusion
  16.7 1.5 fusion.42
  18.2 1.6 collective-permute-done.1
  19.8 1.0 pad_maximum_fusion.1
  20.9 2.9 %collective-permute-start.3 = (bf16[12,6,1024]{2,1,0:T(8,128)(2,1)S(1)}, bf16[12,6,1024]{2,1,0:T(8,128)(2,1)S(1)}, u32[]{:S(2)}, u32[]{:S(2)}) collective-permute-start(bf16[12,6,1024]{2,1,0:T(8,128)(2,1)S(1)} %get-tuple-element.10), channel_id=1, source_target_pairs={{1,0},{2,1},{3,2},{4,3},{5,4},{6,5},{7,6},{0,7},{9,8},{10,9},{11,1... | collective-permute-start | bytes 442376 | tf_op jit(solution)/shard_map/ppermute | solution.py:329
  23.8 1.1 convert_reduce_fusion.1
  24.9 1.2 fusion.35
  26.1 0.9 fusion.37
  27.1 3.9 %fusion.18 = bf16[144,2048]{1,0:T(8,128)(2,1)} fusion(bf16[144,1024]{1,0:T(8,128)(2,1)S(1)} %bitcast.45, bf16[1024,3072]{1,0:T(8,128)(2,1)} %param.13), kind=kOutput, calls=%fused_computation.20 | convolution fusion | flops 604274688 | bytes 5079040 | tf_op jit(solution)/shard_map/dot_general | solution.py:417
  30.9 2.8 %fusion.27.q_ref = bf16[144,1024]{1,0:T(8,128)(2,1)} fusion(bf16[144,1024]{1,0:T(8,128)(2,1)S(1)} %bitcast.46, bf16[1024,3072]{1,0:T(8,128)(2,1)} %param.13), kind=kOutput, calls=%fused_computation.28 | convolution fusion | flops 302137344 | bytes 2686976 | tf_op jit(solution)/shard_map/dot_general | solution.py:415
  35.8 1.0 pad_maximum_fusion.5
  36.9 1.1 convert_reduce_fusion
  38.1 1.2 fusion.30
  39.3 3.8 %fusion.15 = bf16[288,2048]{1,0:T(8,128)(2,1)S(1)} fusion(bf16[1024,3072]{1,0:T(8,128)(2,1)} %param.13, f32[1024]{0:T(1024)} %param.12, f32[288]{0:T(512)S(1)} %add_rsqrt_fusion.1, f32[288]{0:T(512)S(1)} %broadcast_multiply_fusion.1, bf16[36,1024]{1,0:T(8,128)(2,1)} %reshape.167, bf16[36,1024]{1,0:T(8,128)(2,1)S(1)} %reshape.166, ...), kind=kOutput, calls=%fused_computation.19 | convolution fusion | flops 1212088320 | bytes 5978368 | tf_op jit(solution)/shard_map/dot_general | solution.py:429
  43.2 1.4 pad_maximum_fusion.kv_ref
  44.6 8.7 %shard_map.130 = bf16[144,1024]{1,0:T(8,128)(2,1)} custom-call(bf16[144,1024]{1,0:T(8,128)(2,1)} %fusion.27.q_ref, bf16[432,2048]{1,0:T(8,128)(2,1)} %pad_maximum_fusion.kv_ref, s32[144,1]{1,0:T(8,128)} %reshape.182.qw_ref, s32[1,432]{1,0:T(1,128)} %bitcast.47), custom_call_target="tpu_custom_call" | custom-call | tf_op jit(solution)/shard_map/pallas_call | solution.py:109
  53.3 1.4 fusion.51
  54.8 0.8 add_convert_fusion.7
  55.6 17.9 %shard_map.131 = bf16[8,144,1024]{2,1,0:T(8,128)(2,1)} custom-call(bf16[144,1024]{1,0:T(8,128)(2,1)} %bitcast.44), custom_call_target="tpu_custom_call" | custom-call | tf_op jit(solution)/shard_map/pallas_call | solution.py:304
  73.5 4.3 %copy.22 = f32[8,6,24,1024]{3,2,0,1:T(8,128)} copy(bf16[8,6,24,1024]{3,2,1,0:T(8,128)(2,1)} %bitcast.37) | data formatting | bytes 7077888 | tf_op jit(solution)/shard_map/convert_element_type | solution.py:377
  77.9 10.6 %multiply_convert_fusion = bf16[5,6,192,320]{3,2,1,0:T(8,128)(2,1)S(1)} fusion(bf16[5,6,192,320]{3,2,1,0:T(8,128)(2,1)} %param.18, f32[5,192]{1,0:T(8,128)S(1)} %copy-done.8, bf16[5,1024,320]{2,1,0:T(8,128)(2,1)} %all-gather.2.cloned.1.call-done, f32[5,1024]{1,0:T(8,128)S(1)} %copy-done.7, f32[5,1024]{1,0:T(8,128)S(1)} %copy-done.6, ...), kind=kOutput, calls=%fused_computation.10 | convolution fusion | flops 3799941120 | bytes 15412992 | tf_op jit(solution)/shard_map/krnd,kdo->krno/dot_general | solution.py:381
  88.5 7.2 %multiply_reduce_fusion = bf16[6,192,1024]{2,1,0:T(8,128)(2,1)S(1)} fusion(f32[5,1024]{1,0:T(8,128)S(1)} %copy-done.6, bf16[5,6,192,320]{3,2,1,0:T(8,128)(2,1)S(1)} %multiply_convert_fusion, bf16[5,1024,320]{2,1,0:T(8,128)(2,1)S(1)} %copy-done.5), kind=kOutput, calls=%fused_computation | convolution fusion | flops 3785490432 | bytes 9342976 | tf_op jit(solution)/shard_map/krno,kdo->krnd/dot_general | solution.py:385
  95.7 1.7 %copy.28 = bf16[24,8,6,1024]{3,1,2,0:T(8,128)(2,1)} copy(bf16[24,8,6,1024]{3,1,0,2:T(8,128)(2,1)S(1)} %bitcast.41) | data formatting | bytes 4718592
  97.4 9.3 %fusion.8 = bf16[5,1024,320]{1,2,0:T(8,128)(2,1)} fusion(bf16[5,6,192,320]{3,2,1,0:T(8,128)(2,1)} %copy-done.9, f32[5,1024]{1,0:T(8,128)S(1)} %copy-done.7, f32[5,1024]{1,0:T(8,128)S(1)} %copy-done.6, f32[6,192,1024]{2,1,0:T(8,128)} %bitcast.40), kind=kOutput, calls=%fused_computation.12 | convolution fusion | flops 3795845120 | bytes 11722752 | tf_op jit(solution)/shard_map/krnd,krno->kdo/dot_general | solution.py:387
  106.7 5.8 %copy.23 = bf16[5,1024,320]{2,1,0:T(8,128)(2,1)} copy(bf16[5,1024,320]{1,2,0:T(8,128)(2,1)} %fusion.8) | data formatting | bytes 6553600 | tf_op jit(solution)/shard_map/convert_element_type | solution.py:481
  112.5 40.3 %shard_map.132 = f32[5,64,320]{2,1,0:T(8,128)} custom-call(bf16[5,4,4,64,320]{4,3,2,1,0:T(8,128)(2,1)} %bitcast.36), custom_call_target="tpu_custom_call" | custom-call | tf_op jit(solution)/shard_map/pallas_call | solution.py:239
  152.8 1.3 reshape.184
  154.2 0.9 copy.27
  155.1 1.8 %copy.31 = f32[5,64,320]{2,1,0:T(8,128)} copy(f32[5,64,320]{2,1,0:T(8,128)} %shard_map.132) | data formatting | bytes 819200
  (56 shorter events, 5.1 us)
Async XLA Ops:
  7.2 46.2 %copy-start = (bf16[1024,1024]{1,0:T(8,128)(2,1)S(1)}, bf16[1024,1024]{1,0:T(8,128)(2,1)}, u32[]{:S(2)}) copy-start(bf16[1024,1024]{1,0:T(8,128)(2,1)} %param.14) | copy-start | bytes 6291460
  7.2 18.9 %copy-start.1 = (bf16[6,24,1024]{2,1,0:T(8,128)(2,1)S(1)}, bf16[6,24,1024]{2,1,0:T(8,128)(2,1)}, u32[]{:S(2)}) copy-start(bf16[6,24,1024]{2,1,0:T(8,128)(2,1)} %param.11) | copy-start | bytes 884740
  7.2 70.7 %all-gather.2.cloned.1.call-start = ((), (), s32[]{:S(2)}) async-start(), calls=%async_computation.1 | async-start | bytes 4177920 | tf_op jit(solution)/shard_map/all_gather | solution.py:456
  7.9 144.9 %reduce-scatter.4.cloned.1.call-start = ((), (), s32[]{:S(2)}) async-start(), calls=%async_computation.2 | async-start | bytes 2654208
  9.0 9.2 %collective-permute-start = (bf16[3,24,1024]{2,1,0:T(8,128)(2,1)S(1)}, bf16[3,24,1024]{2,1,0:T(8,128)(2,1)S(1)}, u32[]{:S(2)}, u32[]{:S(2)}) collective-permute-start(bf16[3,24,1024]{2,1,0:T(8,128)(2,1)S(1)} %get-tuple-element.11), channel_id=1, source_target_pairs={{0,8},{8,16},{16,24},{24,32},{32,40},{40,48},{48,56},{56,64},{64,7... | collective-permute-start | bytes 442376 | tf_op jit(solution)/shard_map/ppermute | solution.py:328
  12.6 7.2 %collective-permute-start.1 = (bf16[3,24,1024]{2,1,0:T(8,128)(2,1)S(1)}, bf16[3,24,1024]{2,1,0:T(8,128)(2,1)S(1)}, u32[]{:S(2)}, u32[]{:S(2)}) collective-permute-start(bf16[3,24,1024]{2,1,0:T(8,128)(2,1)S(1)} %get-tuple-element.12), channel_id=1, source_target_pairs={{8,0},{16,8},{24,16},{32,24},{40,32},{48,40},{56,48},{64,56},{72,6... | collective-permute-start | bytes 442376 | tf_op jit(solution)/shard_map/ppermute | solution.py:329
  20.9 12.9 %collective-permute-start.2 = (bf16[12,6,1024]{2,1,0:T(8,128)(2,1)S(1)}, bf16[12,6,1024]{2,1,0:T(8,128)(2,1)S(1)}, u32[]{:S(2)}, u32[]{:S(2)}) collective-permute-start(bf16[12,6,1024]{2,1,0:T(8,128)(2,1)S(1)} %get-tuple-element.9), channel_id=1, source_target_pairs={{0,1},{1,2},{2,3},{3,4},{4,5},{5,6},{6,7},{7,0},{8,9},{9,10},{10,1... | collective-permute-start | bytes 442376 | tf_op jit(solution)/shard_map/ppermute | solution.py:328
  20.9 13.6 %collective-permute-start.3 = (bf16[12,6,1024]{2,1,0:T(8,128)(2,1)S(1)}, bf16[12,6,1024]{2,1,0:T(8,128)(2,1)S(1)}, u32[]{:S(2)}, u32[]{:S(2)}) collective-permute-start(bf16[12,6,1024]{2,1,0:T(8,128)(2,1)S(1)} %get-tuple-element.10), channel_id=1, source_target_pairs={{1,0},{2,1},{3,2},{4,3},{5,4},{6,5},{7,6},{0,7},{9,8},{10,9},{11,1... | collective-permute-start | bytes 442376 | tf_op jit(solution)/shard_map/ppermute | solution.py:329
  33.7 0.7 copy-start.3
  34.5 0.7 copy-start.4
  39.3 3.9 %copy-start.2 = (bf16[144,2048]{1,0:T(8,128)(2,1)S(1)}, bf16[144,2048]{1,0:T(8,128)(2,1)}, u32[]{:S(2)}) copy-start(bf16[144,2048]{1,0:T(8,128)(2,1)} %fusion.18) | copy-start | bytes 1769476
  73.5 4.4 %copy-start.6 = (f32[5,1024]{1,0:T(8,128)S(1)}, f32[5,1024]{1,0:T(8,128)}, u32[]{:S(2)}) copy-start(f32[5,1024]{1,0:T(8,128)} %param.15) | copy-start | bytes 61444
  73.5 4.4 %copy-start.7 = (f32[5,1024]{1,0:T(8,128)S(1)}, f32[5,1024]{1,0:T(8,128)}, u32[]{:S(2)}) copy-start(f32[5,1024]{1,0:T(8,128)} %param.16) | copy-start | bytes 61444
  73.5 4.3 %copy-start.8 = (f32[5,192]{1,0:T(8,128)S(1)}, f32[5,192]{1,0:T(8,128)}, u32[]{:S(2)}) copy-start(f32[5,192]{1,0:T(8,128)} %fusion.42) | copy-start | bytes 11524
  77.9 10.6 %copy-start.5 = (bf16[5,1024,320]{2,1,0:T(8,128)(2,1)S(1)}, bf16[5,1024,320]{2,1,0:T(8,128)(2,1)}, u32[]{:S(2)}) copy-start(bf16[5,1024,320]{2,1,0:T(8,128)(2,1)} %all-gather.2.cloned.1.call-done) | copy-start | bytes 9830404
  88.5 7.2 %copy-start.9 = (bf16[5,6,192,320]{3,2,1,0:T(8,128)(2,1)}, bf16[5,6,192,320]{3,2,1,0:T(8,128)(2,1)S(1)}, u32[]{:S(2)}) copy-start(bf16[5,6,192,320]{3,2,1,0:T(8,128)(2,1)S(1)} %multiply_convert_fusion) | copy-start | bytes 11059204
Sparse Core Ops, SparseCore 0:
  10.2 52.8 all-gather.1
  97.6 37.9 reduce-scatter.3

commit v16 on v15

--- a/solution.py
+++ b/solution.py
@@ -471,9 +471,13 @@
     )
     latent_terms = piece_grad
     latent_terms, head_terms = (latent_terms, head_add)
-    grad_latent = lax.psum_scatter(
-        latent_terms.astype(jnp.bfloat16), "var", scatter_dimension=1, tiled=True
-    )
+    latent_parts = (
+        latent_terms.astype(jnp.bfloat16)
+        .reshape(band_rows, var_count, band_cols, width)
+        .transpose(1, 0, 2, 3)
+    )
+    grad_latent = lax.psum_scatter(latent_parts, "var", scatter_dimension=0, tiled=True)
+    grad_latent = grad_latent.reshape(band_rows, band_cols, width)
     head_terms = head_terms * (1.0 / math.sqrt(lat_count * band_rows * var_count * band_cols))
     outer, inner = lax.axis_size(LAT[0]), lax.axis_size(LAT[1])
     slots, outs = head_terms.shape[0], head_terms.shape[2]

time: 165 us -> 181 us (1.097)
  waiting for transfers between devices: 2.28 us -> 14.3 us
  Pallas kernels: 66.9 us -> 69.5 us
    unnamed x3, waiting for transfers between devices: 0.72 us -> 14.3 us
    unnamed x24 -> x22, local copies, waits for them, and re-layouts: 7.12 us -> 4.53 us
    reshape x0 -> x1, local copies, waits for them, and re-layouts: none -> 2.39 us  [local(): grad_latent = grad_latent.reshape(band_rows, band_cols, width)]
  transfers between devices with their start and end apart: 6 -> 6, of which waited for: 1 -> 1; matrix products, arithmetic and copies ran while one was open for 29% -> 27% of each run, Pallas kernels for 41% -> 39%
where the time goes in v16:
time: 181 us
  Pallas kernels  69.5 us (38%)
  matrix products  42 us (23%)
  local copies, waits for them, and re-layouts  20.9 us (12%)
  waiting for transfers between devices  14.3 us (8%)
  between operations  14.3 us (8%)
  other arithmetic  10.7 us (6%)
  starting transfers between devices  8.94 us (5%)
    pallas_call x1, Pallas kernels, grid_reduce_scatter(): pl.pallas_call(kernel, out_shape=jax.ShapeDtypeStruct((slots, rows, outs)...  41.2 us
    pallas_call x1, Pallas kernels, chip_ring_gather(): pl.pallas_call(kernel, out_shape=jax.ShapeDtypeStruct((n,) + block.shape,...  19.6 us
    unnamed x3, waiting for transfers between devices  14.3 us
    dot_general x1, matrix products, slot_terms(): jnp.einsum('krnd,kdo->krno', rows, heads_full, preferred_element_type=jnp...  10.6 us
    dot_general x1, matrix products, slot_terms(): jnp.einsum('krnd,krno->kdo', rows, errors, preferred_element_type=jnp.flo...  9.27 us
    pallas_call x1, Pallas kernels, masked_window_attention(): pl.pallas_call(kernel, out_shape=jax.ShapeDtypeStruct((nq, width), jnp.bf...  8.75 us
    dot_general x1, matrix products, slot_terms(): jnp.einsum('krno,kdo->krnd', errors, heads_full, preferred_element_type=j...  8.61 us
    convert_element_type x1, local copies, waits for them, and re-layouts, local(): head_terms.astype(jnp.bfloat16)  5.85 us
  transfers between devices with their start and end apart: 6, of which 1 were waited for; matrix products, arithmetic and copies ran while one was open for 27% of the time, Pallas kernels for 39%

profile of v16, /device:TPU:0, one launch (start us, length us, event | category | flops | bytes accessed | tf_op | source)
XLA Modules:
  0.0 180.5 jit_solution(12944670130160567383)
XLA Ops:
  8.0 1.0 fusion.48
  9.0 1.3 collective-permute-start.1
  10.3 4.6 %collective-permute-start = (bf16[3,24,1024]{2,1,0:T(8,128)(2,1)S(1)}, bf16[3,24,1024]{2,1,0:T(8,128)(2,1)S(1)}, u32[]{:S(2)}, u32[]{:S(2)}) collective-permute-start(bf16[3,24,1024]{2,1,0:T(8,128)(2,1)S(1)} %get-tuple-element.11), channel_id=1, source_target_pairs={{0,8},{8,16},{16,24},{24,32},{32,40},{40,48},{48,56},{56,64},{64,7... | collective-permute-start | bytes 442376 | tf_op jit(solution)/shard_map/ppermute | solution.py:328
  15.0 0.7 reshape.189.qw_ref
  16.2 1.3 dynamic-slice
  18.2 0.8 select_reduce_fusion
  19.0 1.5 fusion.42
  20.5 1.0 pad_maximum_fusion.1
  21.6 3.0 %collective-permute-start.3 = (bf16[12,6,1024]{2,1,0:T(8,128)(2,1)S(1)}, bf16[12,6,1024]{2,1,0:T(8,128)(2,1)S(1)}, u32[]{:S(2)}, u32[]{:S(2)}) collective-permute-start(bf16[12,6,1024]{2,1,0:T(8,128)(2,1)S(1)} %get-tuple-element.10), channel_id=1, source_target_pairs={{1,0},{2,1},{3,2},{4,3},{5,4},{6,5},{7,6},{0,7},{9,8},{10,9},{11,1... | collective-permute-start | bytes 442376 | tf_op jit(solution)/shard_map/ppermute | solution.py:329
  24.6 1.1 convert_reduce_fusion.1
  25.7 1.2 fusion.35
  26.9 0.9 fusion.37
  27.8 3.9 %fusion.18 = bf16[144,2048]{1,0:T(8,128)(2,1)} fusion(bf16[144,1024]{1,0:T(8,128)(2,1)S(1)} %bitcast.46, bf16[1024,3072]{1,0:T(8,128)(2,1)} %param.13), kind=kOutput, calls=%fused_computation.20 | convolution fusion | flops 604274688 | bytes 5079040 | tf_op jit(solution)/shard_map/dot_general | solution.py:417
  31.7 2.8 %fusion.27.q_ref = bf16[144,1024]{1,0:T(8,128)(2,1)} fusion(bf16[144,1024]{1,0:T(8,128)(2,1)S(1)} %bitcast.47, bf16[1024,3072]{1,0:T(8,128)(2,1)} %param.13), kind=kOutput, calls=%fused_computation.28 | convolution fusion | flops 302137344 | bytes 2686976 | tf_op jit(solution)/shard_map/dot_general | solution.py:415
  36.6 1.0 pad_maximum_fusion.5
  37.7 1.1 convert_reduce_fusion
  38.8 1.2 fusion.30
  40.1 3.9 %fusion.15 = bf16[288,2048]{1,0:T(8,128)(2,1)S(1)} fusion(bf16[1024,3072]{1,0:T(8,128)(2,1)} %param.13, f32[1024]{0:T(1024)} %param.12, f32[288]{0:T(512)S(1)} %add_rsqrt_fusion.1, f32[288]{0:T(512)S(1)} %broadcast_multiply_fusion.1, bf16[36,1024]{1,0:T(8,128)(2,1)S(1)} %reshape.173, bf16[36,1024]{1,0:T(8,128)(2,1)} %reshape.172, ...), kind=kOutput, calls=%fused_computation.19 | convolution fusion | flops 1212088320 | bytes 5978368 | tf_op jit(solution)/shard_map/dot_general | solution.py:429
  43.9 1.4 pad_maximum_fusion.kv_ref
  45.4 8.7 %shard_map.130 = bf16[144,1024]{1,0:T(8,128)(2,1)} custom-call(bf16[144,1024]{1,0:T(8,128)(2,1)} %fusion.27.q_ref, bf16[432,2048]{1,0:T(8,128)(2,1)} %pad_maximum_fusion.kv_ref, s32[144,1]{1,0:T(8,128)} %reshape.189.qw_ref, s32[1,432]{1,0:T(1,128)} %bitcast.48), custom_call_target="tpu_custom_call" | custom-call | tf_op jit(solution)/shard_map/pallas_call | solution.py:109
  54.1 1.4 fusion.51
  55.6 0.8 add_convert_fusion.7
  56.4 19.6 %shard_map.131 = bf16[8,144,1024]{2,1,0:T(8,128)(2,1)} custom-call(bf16[144,1024]{1,0:T(8,128)(2,1)} %bitcast.45), custom_call_target="tpu_custom_call" | custom-call | tf_op jit(solution)/shard_map/pallas_call | solution.py:304
  76.0 4.3 %copy.22 = f32[8,6,24,1024]{3,2,0,1:T(8,128)} copy(bf16[8,6,24,1024]{3,2,1,0:T(8,128)(2,1)} %bitcast.40) | data formatting | bytes 7077888 | tf_op jit(solution)/shard_map/convert_element_type | solution.py:377
  80.3 10.6 %multiply_convert_fusion = bf16[5,6,192,320]{3,2,1,0:T(8,128)(2,1)S(1)} fusion(bf16[5,6,192,320]{3,2,1,0:T(8,128)(2,1)} %param.18, f32[5,192]{1,0:T(8,128)S(1)} %copy-done.8, bf16[5,1024,320]{2,1,0:T(8,128)(2,1)} %all-gather.2.cloned.1.call-done, f32[5,1024]{1,0:T(8,128)S(1)} %copy-done.7, f32[5,1024]{1,0:T(8,128)S(1)} %copy-done.6, ...), kind=kOutput, calls=%fused_computation.10 | convolution fusion | flops 3799941120 | bytes 15412992 | tf_op jit(solution)/shard_map/krnd,kdo->krno/dot_general | solution.py:381
  91.0 8.6 %multiply_reduce_fusion = bf16[6,192,1024]{2,1,0:T(8,128)(2,1)} fusion(f32[5,1024]{1,0:T(8,128)S(1)} %copy-done.6, bf16[5,6,192,320]{3,2,1,0:T(8,128)(2,1)S(1)} %multiply_convert_fusion, bf16[5,1024,320]{2,1,0:T(8,128)(2,1)S(1)} %copy-done.5), kind=kOutput, calls=%fused_computation | convolution fusion | flops 3785490432 | bytes 9342976 | tf_op jit(solution)/shard_map/krno,kdo->krnd/dot_general | solution.py:385
  99.6 9.3 %fusion.8 = bf16[5,1024,320]{1,2,0:T(8,128)(2,1)} fusion(bf16[5,6,192,320]{3,2,1,0:T(8,128)(2,1)} %copy-done.9, f32[5,1024]{1,0:T(8,128)S(1)} %copy-done.7, f32[5,1024]{1,0:T(8,128)S(1)} %copy-done.6, f32[6,192,1024]{2,1,0:T(8,128)} %bitcast.42), kind=kOutput, calls=%fused_computation.12 | convolution fusion | flops 3795845120 | bytes 11722752 | tf_op jit(solution)/shard_map/krnd,krno->kdo/dot_general | solution.py:387
  108.9 5.9 %copy.23 = bf16[5,1024,320]{2,1,0:T(8,128)(2,1)} copy(bf16[5,1024,320]{1,2,0:T(8,128)(2,1)} %fusion.8) | data formatting | bytes 6553600 | tf_op jit(solution)/shard_map/convert_element_type | solution.py:485
  114.7 41.2 %shard_map.132 = f32[5,64,320]{2,1,0:T(8,128)} custom-call(bf16[5,4,4,64,320]{4,3,2,1,0:T(8,128)(2,1)} %bitcast.39), custom_call_target="tpu_custom_call" | custom-call | tf_op jit(solution)/shard_map/pallas_call | solution.py:239
  155.9 13.6 %all-reduce.3.cloned.1.call-done = bf16[8,6,24,1024]{3,2,0,1:T(8,128)(2,1)} async-done(((bf16[8,6,24,1024]{3,2,0,1:T(8,128)(2,1)}), bf16[8,6,24,1024]{3,2,0,1:T(8,128)(2,1)}) %all-reduce.3.cloned.1.call-update) | async-done | bytes 2359312
  169.5 2.4 %dynamic-slice_bitcast_fusion = bf16[6,24,1024]{2,1,0:T(8,128)(2,1)} fusion(bf16[8,6,24,1024]{3,2,0,1:T(8,128)(2,1)} %all-reduce.3.cloned.1.call-done, u32[]{:T(128)} %bitcast.22), kind=kLoop, calls=%fused_computation.45 | loop fusion | bytes 589828 | tf_op jit(solution)/shard_map/reshape | solution.py:480
  171.9 1.8 %copy.30 = f32[5,64,320]{2,1,0:T(8,128)} copy(f32[5,64,320]{2,1,0:T(8,128)} %shard_map.132) | data formatting | bytes 819200
  (55 shorter events, 4.3 us)
Async XLA Ops:
  7.2 47.0 %copy-start = (bf16[1024,1024]{1,0:T(8,128)(2,1)S(1)}, bf16[1024,1024]{1,0:T(8,128)(2,1)}, u32[]{:S(2)}) copy-start(bf16[1024,1024]{1,0:T(8,128)(2,1)} %param.14) | copy-start | bytes 6291460
  7.2 19.7 %copy-start.1 = (bf16[6,24,1024]{2,1,0:T(8,128)(2,1)S(1)}, bf16[6,24,1024]{2,1,0:T(8,128)(2,1)}, u32[]{:S(2)}) copy-start(bf16[6,24,1024]{2,1,0:T(8,128)(2,1)} %param.11) | copy-start | bytes 884740
  7.2 73.1 %all-gather.2.cloned.1.call-start = ((), (), s32[]{:S(2)}) async-start(), calls=%async_computation | async-start | bytes 4177920 | tf_op jit(solution)/shard_map/all_gather | solution.py:456
  7.9 161.5 %all-reduce.3.cloned.1.call-start = ((), (), s32[]{:S(2)}) async-start(), calls=%async_computation.1 | async-start | bytes 4718592
  9.0 11.5 %collective-permute-start.1 = (bf16[3,24,1024]{2,1,0:T(8,128)(2,1)S(1)}, bf16[3,24,1024]{2,1,0:T(8,128)(2,1)S(1)}, u32[]{:S(2)}, u32[]{:S(2)}) collective-permute-start(bf16[3,24,1024]{2,1,0:T(8,128)(2,1)S(1)} %get-tuple-element.12), channel_id=1, source_target_pairs={{8,0},{16,8},{24,16},{32,24},{40,32},{48,40},{56,48},{64,56},{72,6... | collective-permute-start | bytes 442376 | tf_op jit(solution)/shard_map/ppermute | solution.py:329
  10.3 10.2 %collective-permute-start = (bf16[3,24,1024]{2,1,0:T(8,128)(2,1)S(1)}, bf16[3,24,1024]{2,1,0:T(8,128)(2,1)S(1)}, u32[]{:S(2)}, u32[]{:S(2)}) collective-permute-start(bf16[3,24,1024]{2,1,0:T(8,128)(2,1)S(1)} %get-tuple-element.11), channel_id=1, source_target_pairs={{0,8},{8,16},{16,24},{24,32},{32,40},{40,48},{48,56},{56,64},{64,7... | collective-permute-start | bytes 442376 | tf_op jit(solution)/shard_map/ppermute | solution.py:328
  21.6 12.9 %collective-permute-start.3 = (bf16[12,6,1024]{2,1,0:T(8,128)(2,1)S(1)}, bf16[12,6,1024]{2,1,0:T(8,128)(2,1)S(1)}, u32[]{:S(2)}, u32[]{:S(2)}) collective-permute-start(bf16[12,6,1024]{2,1,0:T(8,128)(2,1)S(1)} %get-tuple-element.10), channel_id=1, source_target_pairs={{1,0},{2,1},{3,2},{4,3},{5,4},{6,5},{7,6},{0,7},{9,8},{10,9},{11,1... | collective-permute-start | bytes 442376 | tf_op jit(solution)/shard_map/ppermute | solution.py:329
  24.6 10.6 %collective-permute-start.2 = (bf16[12,6,1024]{2,1,0:T(8,128)(2,1)S(1)}, bf16[12,6,1024]{2,1,0:T(8,128)(2,1)S(1)}, u32[]{:S(2)}, u32[]{:S(2)}) collective-permute-start(bf16[12,6,1024]{2,1,0:T(8,128)(2,1)S(1)} %get-tuple-element.9), channel_id=1, source_target_pairs={{0,1},{1,2},{2,3},{3,4},{4,5},{5,6},{6,7},{7,0},{8,9},{9,10},{10,1... | collective-permute-start | bytes 442376 | tf_op jit(solution)/shard_map/ppermute | solution.py:328
  34.5 0.7 copy-start.3
  35.2 0.7 copy-start.4
  40.1 3.9 %copy-start.2 = (bf16[144,2048]{1,0:T(8,128)(2,1)S(1)}, bf16[144,2048]{1,0:T(8,128)(2,1)}, u32[]{:S(2)}) copy-start(bf16[144,2048]{1,0:T(8,128)(2,1)} %fusion.18) | copy-start | bytes 1769476
  75.9 4.4 %copy-start.6 = (f32[5,1024]{1,0:T(8,128)S(1)}, f32[5,1024]{1,0:T(8,128)}, u32[]{:S(2)}) copy-start(f32[5,1024]{1,0:T(8,128)} %param.15) | copy-start | bytes 61444
  76.0 4.4 %copy-start.7 = (f32[5,1024]{1,0:T(8,128)S(1)}, f32[5,1024]{1,0:T(8,128)}, u32[]{:S(2)}) copy-start(f32[5,1024]{1,0:T(8,128)} %param.16) | copy-start | bytes 61444
  76.0 4.3 %copy-start.8 = (f32[5,192]{1,0:T(8,128)S(1)}, f32[5,192]{1,0:T(8,128)}, u32[]{:S(2)}) copy-start(f32[5,192]{1,0:T(8,128)} %fusion.42) | copy-start | bytes 11524
  80.3 10.6 %copy-start.5 = (bf16[5,1024,320]{2,1,0:T(8,128)(2,1)S(1)}, bf16[5,1024,320]{2,1,0:T(8,128)(2,1)}, u32[]{:S(2)}) copy-start(bf16[5,1024,320]{2,1,0:T(8,128)(2,1)} %all-gather.2.cloned.1.call-done) | copy-start | bytes 9830404
  91.0 8.6 %copy-start.9 = (bf16[5,6,192,320]{3,2,1,0:T(8,128)(2,1)}, bf16[5,6,192,320]{3,2,1,0:T(8,128)(2,1)S(1)}, u32[]{:S(2)}) copy-start(bf16[5,6,192,320]{3,2,1,0:T(8,128)(2,1)S(1)} %multiply_convert_fusion) | copy-start | bytes 11059204
Sparse Core Ops, SparseCore 0:
  10.2 52.9 all-gather.1
  99.7 69.6 all-reduce.2

commit v17 on v15

--- a/solution.py
+++ b/solution.py
@@ -409,9 +409,9 @@
     lat_place = lax.axis_index(LAT)
     ext_rows = band_rows + WH
     ext_cols = band_cols + WW
+    own_normed = layer_norm(patches, norm_gain).reshape(-1, width)
     extended = padded(patches, ((LAT, 0),), half_rows, False)
-    extended, own = lax.optimization_barrier((extended, patches))
-    own_normed = layer_norm(own, norm_gain).reshape(-1, width)
+    extended, own_normed = lax.optimization_barrier((extended, own_normed))
     queries = jnp.dot(own_normed, input_proj[:, :width], preferred_element_type=jnp.float32)
     queries = queries.astype(jnp.bfloat16)
     own_keyval = jnp.dot(own_normed, input_proj[:, width:], preferred_element_type=jnp.float32)

time: 165 us -> 161 us (0.976)
    unnamed x24 -> x22, local copies, waits for them, and re-layouts: 7.12 us -> 6.44 us
  transfers between devices with their start and end apart: 6 -> 6, of which waited for: 1 -> 0; matrix products, arithmetic and copies ran while one was open for 29% -> 28% of each run, Pallas kernels for 41% -> 42%
where the time goes in v17:
time: 161 us; the launch traced here: 160 us
  Pallas kernels  67.8 us (42%)
  matrix products  39.8 us (25%)
  local copies, waits for them, and re-layouts  20.4 us (13%)
  between operations  14.3 us (9%)
  other arithmetic  9.17 us (6%)
  starting transfers between devices  8.14 us (5%)
    pallas_call x1, Pallas kernels, grid_reduce_scatter(): pl.pallas_call(kernel, out_shape=jax.ShapeDtypeStruct((slots, rows, outs)...  41.5 us
    pallas_call x1, Pallas kernels, chip_ring_gather(): pl.pallas_call(kernel, out_shape=jax.ShapeDtypeStruct((n,) + block.shape,...  17.4 us
    dot_general x1, matrix products, slot_terms(): jnp.einsum('krnd,kdo->krno', rows, heads_full, preferred_element_type=jnp...  10.6 us
    dot_general x1, matrix products, slot_terms(): jnp.einsum('krnd,krno->kdo', rows, errors, preferred_element_type=jnp.flo...  9.26 us
    pallas_call x1, Pallas kernels, masked_window_attention(): pl.pallas_call(kernel, out_shape=jax.ShapeDtypeStruct((nq, width), jnp.bf...  8.75 us
    dot_general x1, matrix products, slot_terms(): jnp.einsum('krno,kdo->krnd', errors, heads_full, preferred_element_type=j...  7.22 us
    unnamed x22, local copies, waits for them, and re-layouts  6.44 us
    convert_element_type x1, local copies, waits for them, and re-layouts, local(): head_terms.astype(jnp.bfloat16)  5.79 us
  transfers between devices with their start and end apart: 6, of which 0 were waited for; matrix products, arithmetic and copies ran while one was open for 28% of the time, Pallas kernels for 42%

profile of v17, /device:TPU:0, one launch (start us, length us, event | category | flops | bytes accessed | tf_op | source)
XLA Modules:
  0.0 160.3 jit_solution(16837725813910068742)
XLA Ops:
  7.2 0.7 all-gather.2.cloned.1.call-update
  8.0 1.0 fusion.49
  9.0 3.6 %collective-permute-start = (bf16[3,24,1024]{2,1,0:T(8,128)(2,1)S(1)}, bf16[3,24,1024]{2,1,0:T(8,128)(2,1)S(1)}, u32[]{:S(2)}, u32[]{:S(2)}) collective-permute-start(bf16[3,24,1024]{2,1,0:T(8,128)(2,1)S(1)} %get-tuple-element.11), channel_id=1, source_target_pairs={{0,8},{8,16},{16,24},{24,32},{32,40},{40,48},{48,56},{56,64},{64,7... | collective-permute-start | bytes 442376 | tf_op jit(solution)/shard_map/ppermute | solution.py:328
  12.5 1.3 collective-permute-start.1
  14.1 0.7 reshape.182.qw_ref
  16.0 0.8 select_reduce_fusion
  16.7 1.1 convert_reduce_fusion.1
  17.8 1.2 fusion.35
  19.0 1.2 fusion.37
  20.2 0.9 fusion.43
  21.1 1.1 pad_maximum_fusion.1
  22.2 0.7 fusion.48
  22.9 3.2 %collective-permute-start.3 = (bf16[12,6,1024]{2,1,0:T(8,128)(2,1)}, bf16[12,6,1024]{2,1,0:T(8,128)(2,1)S(1)}, u32[]{:S(2)}, u32[]{:S(2)}) collective-permute-start(bf16[12,6,1024]{2,1,0:T(8,128)(2,1)} %get-tuple-element.10), channel_id=1, source_target_pairs={{1,0},{2,1},{3,2},{4,3},{5,4},{6,5},{7,6},{0,7},{9,8},{10,9},{11,1... | collective-permute-start | bytes 442376 | tf_op jit(solution)/shard_map/ppermute | solution.py:329
  26.1 3.8 %fusion.18 = bf16[144,2048]{1,0:T(8,128)(2,1)} fusion(bf16[144,1024]{1,0:T(8,128)(2,1)S(1)} %bitcast.45, bf16[1024,3072]{1,0:T(8,128)(2,1)} %param.13), kind=kOutput, calls=%fused_computation.20 | convolution fusion | flops 604274688 | bytes 5079040 | tf_op jit(solution)/shard_map/dot_general | solution.py:417
  29.9 2.8 %fusion.27.q_ref = bf16[144,1024]{1,0:T(8,128)(2,1)} fusion(bf16[144,1024]{1,0:T(8,128)(2,1)S(1)} %bitcast.46, bf16[1024,3072]{1,0:T(8,128)(2,1)} %param.13), kind=kOutput, calls=%fused_computation.28 | convolution fusion | flops 302137344 | bytes 2686976 | tf_op jit(solution)/shard_map/dot_general | solution.py:415
  33.5 1.0 pad_maximum_fusion.5
  35.2 3.8 %fusion.15 = bf16[288,2048]{1,0:T(8,128)(2,1)S(1)} fusion(bf16[1024,3072]{1,0:T(8,128)(2,1)} %param.13, f32[1024]{0:T(1024)S(1)} %copy-done.4, f32[288]{0:T(512)S(1)} %add_rsqrt_fusion.1, f32[288]{0:T(512)S(1)} %broadcast_multiply_fusion.1, bf16[36,1024]{1,0:T(8,128)(2,1)S(1)} %reshape.167, bf16[36,1024]{1,0:T(8,128)(2,1)S(1)} %reshape.166, ...), kind=kOutput, calls=%fused_computation.19 | convolution fusion | flops 1212088320 | bytes 5970176 | tf_op jit(solution)/shard_map/dot_general | solution.py:429
  39.0 1.4 pad_maximum_fusion.kv_ref
  40.4 8.8 %shard_map.130 = bf16[144,1024]{1,0:T(8,128)(2,1)} custom-call(bf16[144,1024]{1,0:T(8,128)(2,1)} %fusion.27.q_ref, bf16[432,2048]{1,0:T(8,128)(2,1)} %pad_maximum_fusion.kv_ref, s32[144,1]{1,0:T(8,128)} %reshape.182.qw_ref, s32[1,432]{1,0:T(1,128)} %bitcast.47), custom_call_target="tpu_custom_call" | custom-call | tf_op jit(solution)/shard_map/pallas_call | solution.py:109
  49.2 1.4 fusion.52
  50.6 0.8 fusion.38
  51.4 17.4 %shard_map.131 = bf16[8,144,1024]{2,1,0:T(8,128)(2,1)} custom-call(bf16[144,1024]{1,0:T(8,128)(2,1)} %bitcast.44), custom_call_target="tpu_custom_call" | custom-call | tf_op jit(solution)/shard_map/pallas_call | solution.py:304
  68.9 4.3 %copy.22 = f32[8,6,24,1024]{3,2,0,1:T(8,128)} copy(bf16[8,6,24,1024]{3,2,1,0:T(8,128)(2,1)} %bitcast.37) | data formatting | bytes 7077888 | tf_op jit(solution)/shard_map/convert_element_type | solution.py:377
  73.2 10.6 %multiply_convert_fusion = bf16[5,6,192,320]{3,2,1,0:T(8,128)(2,1)S(1)} fusion(bf16[5,6,192,320]{3,2,1,0:T(8,128)(2,1)} %param.18, f32[5,192]{1,0:T(8,128)S(1)} %fusion.43, bf16[5,1024,320]{2,1,0:T(8,128)(2,1)} %all-gather.2.cloned.1.call-done, f32[5,1024]{1,0:T(8,128)S(1)} %copy-done.7, f32[5,1024]{1,0:T(8,128)S(1)} %copy-done.6, f32[6,192,1024]{2,1,0:T(8,128)} %bitcast.39), kind=kOutput, calls=%fused_computation.10 | convolution fusion | flops 3799941120 | bytes 15412992 | tf_op jit(solution)/shard_map/krnd,kdo->krno/dot_general | solution.py:381
  83.8 7.2 %multiply_reduce_fusion = bf16[6,192,1024]{2,1,0:T(8,128)(2,1)S(1)} fusion(f32[5,1024]{1,0:T(8,128)S(1)} %copy-done.6, bf16[5,6,192,320]{3,2,1,0:T(8,128)(2,1)S(1)} %multiply_convert_fusion, bf16[5,1024,320]{2,1,0:T(8,128)(2,1)S(1)} %copy-done.5), kind=kOutput, calls=%fused_computation | convolution fusion | flops 3785490432 | bytes 9342976 | tf_op jit(solution)/shard_map/krno,kdo->krnd/dot_general | solution.py:385
  91.1 1.7 %copy.28 = bf16[24,8,6,1024]{3,1,2,0:T(8,128)(2,1)} copy(bf16[24,8,6,1024]{3,1,0,2:T(8,128)(2,1)S(1)} %bitcast.41) | data formatting | bytes 4718592
  92.8 9.3 %fusion.8 = bf16[5,1024,320]{1,2,0:T(8,128)(2,1)} fusion(bf16[5,6,192,320]{3,2,1,0:T(8,128)(2,1)} %copy-done.8, f32[5,1024]{1,0:T(8,128)S(1)} %copy-done.7, f32[5,1024]{1,0:T(8,128)S(1)} %copy-done.6, f32[6,192,1024]{2,1,0:T(8,128)} %bitcast.40), kind=kOutput, calls=%fused_computation.12 | convolution fusion | flops 3795845120 | bytes 11722752 | tf_op jit(solution)/shard_map/krnd,krno->kdo/dot_general | solution.py:387
  102.0 5.8 %copy.23 = bf16[5,1024,320]{2,1,0:T(8,128)(2,1)} copy(bf16[5,1024,320]{1,2,0:T(8,128)(2,1)} %fusion.8) | data formatting | bytes 6553600 | tf_op jit(solution)/shard_map/convert_element_type | solution.py:481
  107.8 41.5 %shard_map.132 = f32[5,64,320]{2,1,0:T(8,128)} custom-call(bf16[5,4,4,64,320]{4,3,2,1,0:T(8,128)(2,1)} %bitcast.36), custom_call_target="tpu_custom_call" | custom-call | tf_op jit(solution)/shard_map/pallas_call | solution.py:239
  149.4 1.3 reshape.184
  150.8 0.9 copy.27
  151.6 1.8 %copy.31 = f32[5,64,320]{2,1,0:T(8,128)} copy(f32[5,64,320]{2,1,0:T(8,128)} %shard_map.132) | data formatting | bytes 819200
  (54 shorter events, 2.9 us)
Async XLA Ops:
  7.2 42.0 %copy-start = (bf16[1024,1024]{1,0:T(8,128)(2,1)S(1)}, bf16[1024,1024]{1,0:T(8,128)(2,1)}, u32[]{:S(2)}) copy-start(bf16[1024,1024]{1,0:T(8,128)(2,1)} %param.14) | copy-start | bytes 6291460
  7.2 66.0 %all-gather.2.cloned.1.call-start = ((), (), s32[]{:S(2)}) async-start(), calls=%async_computation.1 | async-start | bytes 4177920 | tf_op jit(solution)/shard_map/all_gather | solution.py:456
  7.9 141.5 %reduce-scatter.4.cloned.1.call-start = ((), (), s32[]{:S(2)}) async-start(), calls=%async_computation.2 | async-start | bytes 2654208
  9.0 12.1 %collective-permute-start = (bf16[3,24,1024]{2,1,0:T(8,128)(2,1)S(1)}, bf16[3,24,1024]{2,1,0:T(8,128)(2,1)S(1)}, u32[]{:S(2)}, u32[]{:S(2)}) collective-permute-start(bf16[3,24,1024]{2,1,0:T(8,128)(2,1)S(1)} %get-tuple-element.11), channel_id=1, source_target_pairs={{0,8},{8,16},{16,24},{24,32},{32,40},{40,48},{48,56},{56,64},{64,7... | collective-permute-start | bytes 442376 | tf_op jit(solution)/shard_map/ppermute | solution.py:328
  12.5 8.6 %collective-permute-start.1 = (bf16[3,24,1024]{2,1,0:T(8,128)(2,1)S(1)}, bf16[3,24,1024]{2,1,0:T(8,128)(2,1)S(1)}, u32[]{:S(2)}, u32[]{:S(2)}) collective-permute-start(bf16[3,24,1024]{2,1,0:T(8,128)(2,1)S(1)} %get-tuple-element.12), channel_id=1, source_target_pairs={{8,0},{16,8},{24,16},{32,24},{40,32},{48,40},{56,48},{64,56},{72,6... | collective-permute-start | bytes 442376 | tf_op jit(solution)/shard_map/ppermute | solution.py:329
  22.9 9.8 %collective-permute-start.2 = (bf16[12,6,1024]{2,1,0:T(8,128)(2,1)S(1)}, bf16[12,6,1024]{2,1,0:T(8,128)(2,1)S(1)}, u32[]{:S(2)}, u32[]{:S(2)}) collective-permute-start(bf16[12,6,1024]{2,1,0:T(8,128)(2,1)S(1)} %get-tuple-element.9), channel_id=1, source_target_pairs={{0,1},{1,2},{2,3},{3,4},{4,5},{5,6},{6,7},{7,0},{8,9},{9,10},{10,1... | collective-permute-start | bytes 442376 | tf_op jit(solution)/shard_map/ppermute | solution.py:328
  22.9 9.9 %collective-permute-start.3 = (bf16[12,6,1024]{2,1,0:T(8,128)(2,1)}, bf16[12,6,1024]{2,1,0:T(8,128)(2,1)S(1)}, u32[]{:S(2)}, u32[]{:S(2)}) collective-permute-start(bf16[12,6,1024]{2,1,0:T(8,128)(2,1)} %get-tuple-element.10), channel_id=1, source_target_pairs={{1,0},{2,1},{3,2},{4,3},{5,4},{6,5},{7,6},{0,7},{9,8},{10,9},{11,1... | collective-permute-start | bytes 442376 | tf_op jit(solution)/shard_map/ppermute | solution.py:329
  29.9 5.2 %copy-start.4 = (f32[1024]{0:T(1024)S(1)}, f32[1024]{0:T(1024)}, u32[]{:S(2)}) copy-start(f32[1024]{0:T(1024)} %param.12) | copy-start | bytes 12292
  32.8 0.7 copy-start.3
  35.2 3.8 %copy-start.2 = (bf16[144,2048]{1,0:T(8,128)(2,1)S(1)}, bf16[144,2048]{1,0:T(8,128)(2,1)}, u32[]{:S(2)}) copy-start(bf16[144,2048]{1,0:T(8,128)(2,1)} %fusion.18) | copy-start | bytes 1769476
  39.0 11.6 %copy-start.1 = (bf16[6,24,1024]{2,1,0:T(8,128)(2,1)S(1)}, bf16[6,24,1024]{2,1,0:T(8,128)(2,1)}, u32[]{:S(2)}) copy-start(bf16[6,24,1024]{2,1,0:T(8,128)(2,1)} %param.11) | copy-start | bytes 884740
  68.9 4.4 %copy-start.6 = (f32[5,1024]{1,0:T(8,128)S(1)}, f32[5,1024]{1,0:T(8,128)}, u32[]{:S(2)}) copy-start(f32[5,1024]{1,0:T(8,128)} %param.15) | copy-start | bytes 61444
  68.9 4.3 %copy-start.7 = (f32[5,1024]{1,0:T(8,128)S(1)}, f32[5,1024]{1,0:T(8,128)}, u32[]{:S(2)}) copy-start(f32[5,1024]{1,0:T(8,128)} %param.16) | copy-start | bytes 61444
  73.2 10.6 %copy-start.5 = (bf16[5,1024,320]{2,1,0:T(8,128)(2,1)S(1)}, bf16[5,1024,320]{2,1,0:T(8,128)(2,1)}, u32[]{:S(2)}) copy-start(bf16[5,1024,320]{2,1,0:T(8,128)(2,1)} %all-gather.2.cloned.1.call-done) | copy-start | bytes 9830404
  83.8 7.2 %copy-start.8 = (bf16[5,6,192,320]{3,2,1,0:T(8,128)(2,1)}, bf16[5,6,192,320]{3,2,1,0:T(8,128)(2,1)S(1)}, u32[]{:S(2)}) copy-start(bf16[5,6,192,320]{3,2,1,0:T(8,128)(2,1)S(1)} %multiply_convert_fusion) | copy-start | bytes 11059204
Sparse Core Ops, SparseCore 0:
  10.2 52.8 all-gather.1
  92.9 37.8 reduce-scatter.3

commit v18 on v17

--- a/solution.py
+++ b/solution.py
@@ -87,12 +87,12 @@
     )(parts)
 
 
-def masked_window_attention(queries, keyval, query_win, key_win, heads):
+def masked_window_attention(queries, keyval, query_win, key_win, heads, patches, output_proj):
     nq, width = queries.shape
     head_size = width // heads
     scale = 1.0 / float(head_size) ** 0.5
 
-    def kernel(q_ref, kv_ref, qw_ref, kw_ref, out_ref):
+    def kernel(q_ref, kv_ref, qw_ref, kw_ref, p_ref, w_ref, out_ref, attn_ref):
         mask = qw_ref[...] == kw_ref[...]
         for h in range(heads):
             cols = slice(h * head_size, (h + 1) * head_size)
@@ -104,14 +104,17 @@
             s = jnp.where(mask, s, -jnp.inf)
             w = jnp.exp(s - jnp.max(s, axis=1, keepdims=True))
             p = (w / jnp.sum(w, axis=1, keepdims=True)).astype(jnp.bfloat16)
-            out_ref[:, cols] = jnp.dot(p, v, preferred_element_type=jnp.float32).astype(out_ref.dtype)
+            attn_ref[:, cols] = jnp.dot(p, v, preferred_element_type=jnp.float32).astype(attn_ref.dtype)
+        update = jnp.dot(attn_ref[...], w_ref[...], preferred_element_type=jnp.float32)
+        out_ref[...] = (p_ref[...].astype(jnp.float32) + update).astype(out_ref.dtype)
 
     return pl.pallas_call(
         kernel,
-        out_shape=jax.ShapeDtypeStruct((nq, width), jnp.bfloat16),
-        in_specs=[pl.BlockSpec(memory_space=pltpu.VMEM)] * 4,
+        out_shape=jax.ShapeDtypeStruct((nq, width), patches.dtype),
+        in_specs=[pl.BlockSpec(memory_space=pltpu.VMEM)] * 6,
         out_specs=pl.BlockSpec(memory_space=pltpu.VMEM),
-    )(queries, keyval, query_win, key_win)
+        scratch_shapes=[pltpu.VMEM((nq, width), jnp.bfloat16)],
+    )(queries, keyval, query_win, key_win, patches, output_proj)
 
 
 def chip_pair_gather(block, axis, n, cid):
@@ -436,17 +439,15 @@
     key_grid = jnp.where(row_valid[:, None], (ext_r // WH) * win_cols + ext_c // WW, -1)
     query_win = key_grid[half_rows : half_rows + band_rows, half_cols : half_cols + band_cols]
     key_win = jnp.concatenate([query_win.reshape(-1), ring(key_grid)])
-    attn = masked_window_attention(
+    latent = masked_window_attention(
         queries,
         keyval,
         query_win.reshape(-1, 1),
         key_win.reshape(1, -1),
         HEADS,
+        patches.reshape(-1, width),
+        output_proj,
     ).reshape(band_rows, band_cols, width)
-    update = jnp.dot(
-        attn.reshape(-1, width), output_proj, preferred_element_type=jnp.float32
-    ).reshape(band_rows, band_cols, width)
-    latent = (patches.astype(jnp.float32) + update).astype(jnp.bfloat16)
     dataset_row = tile_dataset[0]
     dataset_ids = jnp.arange(level_counts.shape[0], dtype=jnp.int32)
     tile_levels = jnp.sum(

time: 161 us -> 153 us (0.950)
  matrix products: 39.8 us -> 36.3 us
  local copies, waits for them, and re-layouts: 20.4 us -> 16.9 us
  other arithmetic: 9.17 us -> 7.54 us
    convert_element_type x1, local copies, waits for them, and re-layouts: 5.79 us -> 3.62 us  [local(): head_terms.astype(jnp.bfloat16)]
    unnamed x22 -> x14, local copies, waits for them, and re-layouts: 6.44 us -> 5.76 us
  transfers between devices with their start and end apart: 6 -> 6, of which waited for: 0 -> 0; matrix products, arithmetic and copies ran while one was open for 28% -> 24% of each run, Pallas kernels for 42% -> 45%
where the time goes in v18:
time: 153 us
  Pallas kernels  68.8 us (45%)
  matrix products  36.3 us (24%)
  local copies, waits for them, and re-layouts  16.9 us (11%)
  between operations  14.3 us (9%)
  starting transfers between devices  8.17 us (5%)
  other arithmetic  7.54 us (5%)
    pallas_call x1, Pallas kernels, grid_reduce_scatter(): pl.pallas_call(kernel, out_shape=jax.ShapeDtypeStruct((slots, rows, outs)...  41.4 us
    pallas_call x1, Pallas kernels, chip_ring_gather(): pl.pallas_call(kernel, out_shape=jax.ShapeDtypeStruct((n,) + block.shape,...  17.5 us
    dot_general x1, matrix products, slot_terms(): jnp.einsum('krnd,kdo->krno', rows, heads_full, preferred_element_type=jnp...  10.6 us
    pallas_call x1, Pallas kernels, masked_window_attention(): pl.pallas_call(kernel, out_shape=jax.ShapeDtypeStruct((nq, width), patche...  9.96 us
    dot_general x1, matrix products, slot_terms(): jnp.einsum('krnd,krno->kdo', rows, errors, preferred_element_type=jnp.flo...  8.03 us
    dot_general x1, matrix products, slot_terms(): jnp.einsum('krno,kdo->krnd', errors, heads_full, preferred_element_type=j...  7.22 us
    unnamed x14, local copies, waits for them, and re-layouts  5.76 us
    ppermute x2, starting transfers between devices, padded(): after = lax.ppermute(initial, axis, down)  4.5 us
  transfers between devices with their start and end apart: 6, of which 0 were waited for; matrix products, arithmetic and copies ran while one was open for 24% of the time, Pallas kernels for 45%

profile of v18, /device:TPU:0, one launch (start us, length us, event | category | flops | bytes accessed | tf_op | source)
XLA Modules:
  0.0 152.8 jit_solution(3005880868404059222)
XLA Ops:
  7.2 0.7 all-gather.2.cloned.1.call-update
  7.9 1.0 fusion.48
  9.0 3.6 %collective-permute-start = (bf16[3,24,1024]{2,1,0:T(8,128)(2,1)S(1)}, bf16[3,24,1024]{2,1,0:T(8,128)(2,1)S(1)}, u32[]{:S(2)}, u32[]{:S(2)}) collective-permute-start(bf16[3,24,1024]{2,1,0:T(8,128)(2,1)S(1)} %get-tuple-element.11), channel_id=1, source_target_pairs={{0,8},{8,16},{16,24},{24,32},{32,40},{40,48},{48,56},{56,64},{64,7... | collective-permute-start | bytes 442376 | tf_op jit(solution)/shard_map/ppermute | solution.py:331
  12.5 1.3 collective-permute-start.1
  14.1 0.7 reshape.182.qw_ref
  15.3 0.7 concatenate.20
  15.9 0.8 select_reduce_fusion
  16.7 1.1 convert_reduce_fusion.1
  17.8 1.2 fusion.35
  19.0 1.2 fusion.37
  20.2 0.9 fusion.42
  21.1 1.1 pad_maximum_fusion.1
  22.2 3.2 %collective-permute-start.3 = (bf16[12,6,1024]{2,1,0:T(8,128)(2,1)S(1)}, bf16[12,6,1024]{2,1,0:T(8,128)(2,1)S(1)}, u32[]{:S(2)}, u32[]{:S(2)}) collective-permute-start(bf16[12,6,1024]{2,1,0:T(8,128)(2,1)S(1)} %get-tuple-element.10), channel_id=1, source_target_pairs={{1,0},{2,1},{3,2},{4,3},{5,4},{6,5},{7,6},{0,7},{9,8},{10,9},{11,1... | collective-permute-start | bytes 442376 | tf_op jit(solution)/shard_map/ppermute | solution.py:332
  25.5 3.0 %fusion.18 = bf16[144,2048]{1,0:T(8,128)(2,1)S(1)} fusion(bf16[144,1024]{1,0:T(8,128)(2,1)S(1)} %bitcast.43, bf16[1024,3072]{1,0:T(8,128)(2,1)} %param.13), kind=kOutput, calls=%fused_computation.20 | convolution fusion | flops 604274688 | bytes 5079040 | tf_op jit(solution)/shard_map/dot_general | solution.py:420
  28.4 2.8 %fusion.27.q_ref = bf16[144,1024]{1,0:T(8,128)(2,1)} fusion(bf16[144,1024]{1,0:T(8,128)(2,1)S(1)} %bitcast.44, bf16[1024,3072]{1,0:T(8,128)(2,1)} %param.13), kind=kOutput, calls=%fused_computation.28 | convolution fusion | flops 302137344 | bytes 2686976 | tf_op jit(solution)/shard_map/dot_general | solution.py:418
  31.4 0.2 pad_maximum_fusion.5
  31.6 0.2 convert_reduce_fusion
  31.9 0.3 fusion.30
  32.2 3.8 %fusion.15 = bf16[288,2048]{1,0:T(8,128)(2,1)S(1)} fusion(bf16[1024,3072]{1,0:T(8,128)(2,1)} %param.13, f32[1024]{0:T(1024)S(1)} %copy-done, f32[288]{0:T(512)S(1)} %add_rsqrt_fusion.1, f32[288]{0:T(512)S(1)} %broadcast_multiply_fusion.1, bf16[36,1024]{1,0:T(8,128)(2,1)S(1)} %reshape.167, bf16[36,1024]{1,0:T(8,128)(2,1)S(1)} %reshape.166, ...), kind=kOutput, calls=%fused_computation.19 | convolution fusion | flops 1212088320 | bytes 5970176 | tf_op jit(solution)/shard_map/dot_general | solution.py:432
  36.0 1.4 pad_maximum_fusion.kv_ref
  37.4 10.0 %shard_map.130.x_ref = bf16[144,1024]{1,0:T(8,128)(2,1)} custom-call(bf16[144,1024]{1,0:T(8,128)(2,1)} %fusion.27.q_ref, bf16[432,2048]{1,0:T(8,128)(2,1)} %pad_maximum_fusion.kv_ref, s32[144,1]{1,0:T(8,128)} %reshape.182.qw_ref, s32[1,432]{1,0:T(1,128)} %bitcast.45, bf16[144,1024]{1,0:T(8,128)(2,1)} %bitcast.35, bf16[1024,1024]{1,0:T(8,128)(2,1)} %w_ref.1), custom_call_target="tpu_custom_call" | custom-call | tf_op jit(solution)/shard_map/pallas_call | solution.py:111
  47.4 17.5 %shard_map.131 = bf16[8,144,1024]{2,1,0:T(8,128)(2,1)} custom-call(bf16[144,1024]{1,0:T(8,128)(2,1)} %shard_map.130.x_ref), custom_call_target="tpu_custom_call" | custom-call | tf_op jit(solution)/shard_map/pallas_call | solution.py:307
  64.9 4.3 %copy.22 = f32[8,6,24,1024]{3,2,0,1:T(8,128)} copy(bf16[8,6,24,1024]{3,2,1,0:T(8,128)(2,1)} %bitcast.36) | data formatting | bytes 7077888 | tf_op jit(solution)/shard_map/convert_element_type | solution.py:380
  69.3 10.6 %multiply_convert_fusion = bf16[5,6,192,320]{3,2,1,0:T(8,128)(2,1)S(1)} fusion(bf16[5,6,192,320]{3,2,1,0:T(8,128)(2,1)} %param.18, f32[5,192]{1,0:T(8,128)S(1)} %fusion.42, bf16[5,1024,320]{2,1,0:T(8,128)(2,1)} %all-gather.2.cloned.1.call-done, f32[5,1024]{1,0:T(8,128)S(1)} %copy-done.3, f32[5,1024]{1,0:T(8,128)S(1)} %copy-done.2, f32[6,192,1024]{2,1,0:T(8,128)} %bitcast.38), kind=kOutput, calls=%fused_computation.10 | convolution fusion | flops 3799941120 | bytes 15412992 | tf_op jit(solution)/shard_map/krnd,kdo->krno/dot_general | solution.py:384
  79.9 7.2 %multiply_reduce_fusion = bf16[6,192,1024]{2,1,0:T(8,128)(2,1)S(1)} fusion(f32[5,1024]{1,0:T(8,128)S(1)} %copy-done.2, bf16[5,6,192,320]{3,2,1,0:T(8,128)(2,1)S(1)} %multiply_convert_fusion, bf16[5,1024,320]{2,1,0:T(8,128)(2,1)S(1)} %copy-done.1), kind=kOutput, calls=%fused_computation | convolution fusion | flops 3785490432 | bytes 9342976 | tf_op jit(solution)/shard_map/krno,kdo->krnd/dot_general | solution.py:388
  87.1 1.7 %copy.28 = bf16[24,8,6,1024]{3,1,2,0:T(8,128)(2,1)} copy(bf16[24,8,6,1024]{3,1,0,2:T(8,128)(2,1)S(1)} %bitcast.40) | data formatting | bytes 4718592
  88.8 8.0 %fusion.8 = bf16[5,1024,320]{1,2,0:T(8,128)(2,1)S(1)} fusion(bf16[5,6,192,320]{3,2,1,0:T(8,128)(2,1)} %copy-done.4, f32[5,1024]{1,0:T(8,128)S(1)} %copy-done.3, f32[5,1024]{1,0:T(8,128)S(1)} %copy-done.2, f32[6,192,1024]{2,1,0:T(8,128)} %bitcast.39), kind=kOutput, calls=%fused_computation.12 | convolution fusion | flops 3795845120 | bytes 11722752 | tf_op jit(solution)/shard_map/krnd,krno->kdo/dot_general | solution.py:390
  96.8 3.6 %copy.23 = bf16[5,1024,320]{2,1,0:T(8,128)(2,1)} copy(bf16[5,1024,320]{1,2,0:T(8,128)(2,1)S(1)} %fusion.8) | data formatting | bytes 6553600 | tf_op jit(solution)/shard_map/convert_element_type | solution.py:482
  100.5 41.4 %shard_map.132 = f32[5,64,320]{2,1,0:T(8,128)} custom-call(bf16[5,4,4,64,320]{4,3,2,1,0:T(8,128)(2,1)} %bitcast.34), custom_call_target="tpu_custom_call" | custom-call | tf_op jit(solution)/shard_map/pallas_call | solution.py:242
  141.9 1.3 reshape.184
  143.2 0.9 copy.27
  144.1 1.8 %copy.31 = f32[5,64,320]{2,1,0:T(8,128)} copy(f32[5,64,320]{2,1,0:T(8,128)} %shard_map.132) | data formatting | bytes 819200
  (44 shorter events, 1.1 us)
Async XLA Ops:
  7.2 62.1 %all-gather.2.cloned.1.call-start = ((), (), s32[]{:S(2)}) async-start(), calls=%async_computation.1 | async-start | bytes 4177920 | tf_op jit(solution)/shard_map/all_gather | solution.py:457
  7.9 134.0 %reduce-scatter.4.cloned.1.call-start = ((), (), s32[]{:S(2)}) async-start(), calls=%async_computation.2 | async-start | bytes 2654208
  9.0 12.1 %collective-permute-start = (bf16[3,24,1024]{2,1,0:T(8,128)(2,1)S(1)}, bf16[3,24,1024]{2,1,0:T(8,128)(2,1)S(1)}, u32[]{:S(2)}, u32[]{:S(2)}) collective-permute-start(bf16[3,24,1024]{2,1,0:T(8,128)(2,1)S(1)} %get-tuple-element.11), channel_id=1, source_target_pairs={{0,8},{8,16},{16,24},{24,32},{32,40},{40,48},{48,56},{56,64},{64,7... | collective-permute-start | bytes 442376 | tf_op jit(solution)/shard_map/ppermute | solution.py:331
  12.5 8.6 %collective-permute-start.1 = (bf16[3,24,1024]{2,1,0:T(8,128)(2,1)S(1)}, bf16[3,24,1024]{2,1,0:T(8,128)(2,1)S(1)}, u32[]{:S(2)}, u32[]{:S(2)}) collective-permute-start(bf16[3,24,1024]{2,1,0:T(8,128)(2,1)S(1)} %get-tuple-element.12), channel_id=1, source_target_pairs={{8,0},{16,8},{24,16},{32,24},{40,32},{48,40},{56,48},{64,56},{72,6... | collective-permute-start | bytes 442376 | tf_op jit(solution)/shard_map/ppermute | solution.py:332
  22.2 9.0 %collective-permute-start.2 = (bf16[12,6,1024]{2,1,0:T(8,128)(2,1)S(1)}, bf16[12,6,1024]{2,1,0:T(8,128)(2,1)S(1)}, u32[]{:S(2)}, u32[]{:S(2)}) collective-permute-start(bf16[12,6,1024]{2,1,0:T(8,128)(2,1)S(1)} %get-tuple-element.9), channel_id=1, source_target_pairs={{0,1},{1,2},{2,3},{3,4},{4,5},{5,6},{6,7},{7,0},{8,9},{9,10},{10,1... | collective-permute-start | bytes 442376 | tf_op jit(solution)/shard_map/ppermute | solution.py:331
  22.2 9.1 %collective-permute-start.3 = (bf16[12,6,1024]{2,1,0:T(8,128)(2,1)S(1)}, bf16[12,6,1024]{2,1,0:T(8,128)(2,1)S(1)}, u32[]{:S(2)}, u32[]{:S(2)}) collective-permute-start(bf16[12,6,1024]{2,1,0:T(8,128)(2,1)S(1)} %get-tuple-element.10), channel_id=1, source_target_pairs={{1,0},{2,1},{3,2},{4,3},{5,4},{6,5},{7,6},{0,7},{9,8},{10,9},{11,1... | collective-permute-start | bytes 442376 | tf_op jit(solution)/shard_map/ppermute | solution.py:332
  28.4 3.8 %copy-start = (f32[1024]{0:T(1024)S(1)}, f32[1024]{0:T(1024)}, u32[]{:S(2)}) copy-start(f32[1024]{0:T(1024)} %param.12) | copy-start | bytes 12292
  64.9 4.4 %copy-start.2 = (f32[5,1024]{1,0:T(8,128)S(1)}, f32[5,1024]{1,0:T(8,128)}, u32[]{:S(2)}) copy-start(f32[5,1024]{1,0:T(8,128)} %param.15) | copy-start | bytes 61444
  64.9 4.3 %copy-start.3 = (f32[5,1024]{1,0:T(8,128)S(1)}, f32[5,1024]{1,0:T(8,128)}, u32[]{:S(2)}) copy-start(f32[5,1024]{1,0:T(8,128)} %param.16) | copy-start | bytes 61444
  69.3 10.6 %copy-start.1 = (bf16[5,1024,320]{2,1,0:T(8,128)(2,1)S(1)}, bf16[5,1024,320]{2,1,0:T(8,128)(2,1)}, u32[]{:S(2)}) copy-start(bf16[5,1024,320]{2,1,0:T(8,128)(2,1)} %all-gather.2.cloned.1.call-done) | copy-start | bytes 9830404
  79.9 7.2 %copy-start.4 = (bf16[5,6,192,320]{3,2,1,0:T(8,128)(2,1)}, bf16[5,6,192,320]{3,2,1,0:T(8,128)(2,1)S(1)}, u32[]{:S(2)}) copy-start(bf16[5,6,192,320]{3,2,1,0:T(8,128)(2,1)S(1)} %multiply_convert_fusion) | copy-start | bytes 11059204
Sparse Core Ops, SparseCore 0:
  10.1 52.8 all-gather.1
  88.9 38.0 reduce-scatter.3

commit v19 on v18

--- a/solution.py
+++ b/solution.py
@@ -87,12 +87,16 @@
     )(parts)
 
 
-def masked_window_attention(queries, keyval, query_win, key_win, heads, patches, output_proj):
+def masked_window_attention(queries, own_kv, halo_kv, query_win, key_win, heads, patches, output_proj):
     nq, width = queries.shape
     head_size = width // heads
     scale = 1.0 / float(head_size) ** 0.5
 
-    def kernel(q_ref, kv_ref, qw_ref, kw_ref, p_ref, w_ref, out_ref, attn_ref):
+    n_own = own_kv.shape[0]
+
+    def kernel(q_ref, own_ref, halo_ref, qw_ref, kw_ref, p_ref, w_ref, out_ref, attn_ref, kv_ref):
+        kv_ref[pl.ds(0, n_own), :] = own_ref[...]
+        kv_ref[pl.ds(n_own, halo_ref.shape[0]), :] = halo_ref[...]
         mask = qw_ref[...] == kw_ref[...]
         for h in range(heads):
             cols = slice(h * head_size, (h + 1) * head_size)
@@ -111,10 +115,13 @@
     return pl.pallas_call(
         kernel,
         out_shape=jax.ShapeDtypeStruct((nq, width), patches.dtype),
-        in_specs=[pl.BlockSpec(memory_space=pltpu.VMEM)] * 6,
+        in_specs=[pl.BlockSpec(memory_space=pltpu.VMEM)] * 7,
         out_specs=pl.BlockSpec(memory_space=pltpu.VMEM),
-        scratch_shapes=[pltpu.VMEM((nq, width), jnp.bfloat16)],
-    )(queries, keyval, query_win, key_win, patches, output_proj)
+        scratch_shapes=[
+            pltpu.VMEM((nq, width), jnp.bfloat16),
+            pltpu.VMEM((n_own + halo_kv.shape[0], own_kv.shape[1]), own_kv.dtype),
+        ],
+    )(queries, own_kv, halo_kv, query_win, key_win, patches, output_proj)
 
 
 def chip_pair_gather(block, axis, n, cid):
@@ -430,7 +437,6 @@
 
     halo_normed = layer_norm(ring(extended), norm_gain)
     halo_keyval = jnp.dot(halo_normed, input_proj[:, width:], preferred_element_type=jnp.float32)
-    keyval = jnp.concatenate([own_keyval, halo_keyval]).astype(jnp.bfloat16)
     global_row = lat_place * band_rows - half_rows + jnp.arange(ext_rows, dtype=jnp.int32)
     row_valid = (global_row >= 0) & (global_row < lat_count * band_rows)
     win_cols = ext_cols // WW
@@ -441,7 +447,8 @@
     key_win = jnp.concatenate([query_win.reshape(-1), ring(key_grid)])
     latent = masked_window_attention(
         queries,
-        keyval,
+        own_keyval.astype(jnp.bfloat16),
+        halo_keyval.astype(jnp.bfloat16),
         query_win.reshape(-1, 1),
         key_win.reshape(1, -1),
         HEADS,

time: 153 us -> 154 us (level)
  matrix products: 36.3 us -> 38.1 us
  transfers between devices with their start and end apart: 6 -> 6, of which waited for: 0 -> 0; matrix products, arithmetic and copies ran while one was open for 24% -> 25% of each run, Pallas kernels for 45% -> 45%
where the time goes in v19:
time: 154 us; the launch traced here: 153 us
  Pallas kernels  69 us (45%)
  matrix products  38.1 us (25%)
  local copies, waits for them, and re-layouts  16.9 us (11%)
  between operations  14.3 us (9%)
  starting transfers between devices  8.17 us (5%)
  other arithmetic  6.14 us (4%)
    pallas_call x1, Pallas kernels, grid_reduce_scatter(): pl.pallas_call(kernel, out_shape=jax.ShapeDtypeStruct((slots, rows, outs)...  41.4 us
    pallas_call x1, Pallas kernels, chip_ring_gather(): pl.pallas_call(kernel, out_shape=jax.ShapeDtypeStruct((n,) + block.shape,...  17.5 us
    dot_general x1, matrix products, slot_terms(): jnp.einsum('krnd,kdo->krno', rows, heads_full, preferred_element_type=jnp...  10.6 us
    pallas_call x1, Pallas kernels, masked_window_attention(): pl.pallas_call(kernel, out_shape=jax.ShapeDtypeStruct((nq, width), patche...  10.1 us
    dot_general x1, matrix products, slot_terms(): jnp.einsum('krnd,krno->kdo', rows, errors, preferred_element_type=jnp.flo...  8.03 us
    dot_general x1, matrix products, slot_terms(): jnp.einsum('krno,kdo->krnd', errors, heads_full, preferred_element_type=j...  7.22 us
    unnamed x14, local copies, waits for them, and re-layouts  5.76 us
    dot_general x1, matrix products, local(): jnp.dot(halo_normed, input_proj[:, width:], preferred_element_type=jnp.fl...  4.79 us
  transfers between devices with their start and end apart: 6, of which 0 were waited for; matrix products, arithmetic and copies ran while one was open for 25% of the time, Pallas kernels for 45%

profile of v19, /device:TPU:0, one launch (start us, length us, event | category | flops | bytes accessed | tf_op | source)
XLA Modules:
  0.0 153.3 jit_solution(10375138744814617208)
XLA Ops:
  7.2 0.7 all-gather.2.cloned.1.call-update
  7.9 1.0 fusion.48
  9.0 3.6 %collective-permute-start = (bf16[3,24,1024]{2,1,0:T(8,128)(2,1)S(1)}, bf16[3,24,1024]{2,1,0:T(8,128)(2,1)S(1)}, u32[]{:S(2)}, u32[]{:S(2)}) collective-permute-start(bf16[3,24,1024]{2,1,0:T(8,128)(2,1)S(1)} %get-tuple-element.11), channel_id=1, source_target_pairs={{0,8},{8,16},{16,24},{24,32},{32,40},{40,48},{48,56},{56,64},{64,7... | collective-permute-start | bytes 442376 | tf_op jit(solution)/shard_map/ppermute | solution.py:338
  12.5 1.3 collective-permute-start.1
  14.1 0.7 reshape.182.qw_ref
  14.8 0.1 reshape.171
  15.3 0.7 concatenate.15
  15.9 0.8 select_reduce_fusion
  16.7 1.1 convert_reduce_fusion.1
  17.8 1.2 fusion.35
  19.0 1.2 fusion.37
  20.2 0.9 fusion.42
  21.1 1.1 pad_maximum_fusion
  22.2 3.2 %collective-permute-start.3 = (bf16[12,6,1024]{2,1,0:T(8,128)(2,1)S(1)}, bf16[12,6,1024]{2,1,0:T(8,128)(2,1)S(1)}, u32[]{:S(2)}, u32[]{:S(2)}) collective-permute-start(bf16[12,6,1024]{2,1,0:T(8,128)(2,1)S(1)} %get-tuple-element.10), channel_id=1, source_target_pairs={{1,0},{2,1},{3,2},{4,3},{5,4},{6,5},{7,6},{0,7},{9,8},{10,9},{11,1... | collective-permute-start | bytes 442376 | tf_op jit(solution)/shard_map/ppermute | solution.py:339
  25.4 3.8 %fusion.18.own_ref = bf16[144,2048]{1,0:T(8,128)(2,1)} fusion(bf16[144,1024]{1,0:T(8,128)(2,1)S(1)} %bitcast.43, bf16[1024,3072]{1,0:T(8,128)(2,1)} %param.13), kind=kOutput, calls=%fused_computation.20 | convolution fusion | flops 604274688 | bytes 5079040 | tf_op jit(solution)/shard_map/dot_general | solution.py:427
  29.3 2.8 %fusion.27.q_ref = bf16[144,1024]{1,0:T(8,128)(2,1)} fusion(bf16[144,1024]{1,0:T(8,128)(2,1)S(1)} %bitcast.44, bf16[1024,3072]{1,0:T(8,128)(2,1)} %param.13), kind=kOutput, calls=%fused_computation.27 | convolution fusion | flops 302137344 | bytes 2686976 | tf_op jit(solution)/shard_map/dot_general | solution.py:425
  32.2 0.2 pad_maximum_fusion.4
  32.5 0.2 convert_reduce_fusion
  32.7 0.3 fusion.30
  33.0 4.8 %fusion.15.halo_ref = bf16[288,2048]{1,0:T(8,128)(2,1)} fusion(bf16[1024,3072]{1,0:T(8,128)(2,1)} %param.13, f32[1024]{0:T(1024)S(1)} %copy-done, f32[288]{0:T(512)S(1)} %add_rsqrt_fusion.1, f32[288]{0:T(512)S(1)} %broadcast_multiply_fusion.1, bf16[36,1024]{1,0:T(8,128)(2,1)S(1)} %reshape.167, bf16[36,1024]{1,0:T(8,128)(2,1)S(1)} %reshape.166, ...), kind=kOutput, calls=%fused_computation.19 | convolution fusion | flops 1212088320 | bytes 5970176 | tf_op jit(solution)/shard_map/dot_general | solution.py:439
  37.8 10.1 %shard_map.130.x_ref = bf16[144,1024]{1,0:T(8,128)(2,1)} custom-call(bf16[144,1024]{1,0:T(8,128)(2,1)} %fusion.27.q_ref, bf16[144,2048]{1,0:T(8,128)(2,1)} %fusion.18.own_ref, bf16[288,2048]{1,0:T(8,128)(2,1)} %fusion.15.halo_ref, s32[144,1]{1,0:T(8,128)} %reshape.182.qw_ref, s32[1,432]{1,0:T(1,128)} %bitcast.45, bf16[144,1024]{1,0:T(8,128)(2,1)} %bitcast.35, ...), custom_call_target="tpu_custom_call" | custom-call | tf_op jit(solution)/shard_map/pallas_call | solution.py:115
  47.9 17.5 %shard_map.131 = bf16[8,144,1024]{2,1,0:T(8,128)(2,1)} custom-call(bf16[144,1024]{1,0:T(8,128)(2,1)} %shard_map.130.x_ref), custom_call_target="tpu_custom_call" | custom-call | tf_op jit(solution)/shard_map/pallas_call | solution.py:314
  65.5 4.3 %copy.22 = f32[8,6,24,1024]{3,2,0,1:T(8,128)} copy(bf16[8,6,24,1024]{3,2,1,0:T(8,128)(2,1)} %bitcast.36) | data formatting | bytes 7077888 | tf_op jit(solution)/shard_map/convert_element_type | solution.py:387
  69.8 10.6 %multiply_convert_fusion = bf16[5,6,192,320]{3,2,1,0:T(8,128)(2,1)S(1)} fusion(bf16[5,6,192,320]{3,2,1,0:T(8,128)(2,1)} %param.18, f32[5,192]{1,0:T(8,128)S(1)} %fusion.42, bf16[5,1024,320]{2,1,0:T(8,128)(2,1)} %all-gather.2.cloned.1.call-done, f32[5,1024]{1,0:T(8,128)S(1)} %copy-done.3, f32[5,1024]{1,0:T(8,128)S(1)} %copy-done.2, f32[6,192,1024]{2,1,0:T(8,128)} %bitcast.38), kind=kOutput, calls=%fused_computation.10 | convolution fusion | flops 3799941120 | bytes 15412992 | tf_op jit(solution)/shard_map/krnd,kdo->krno/dot_general | solution.py:391
  80.4 7.2 %multiply_reduce_fusion = bf16[6,192,1024]{2,1,0:T(8,128)(2,1)S(1)} fusion(f32[5,1024]{1,0:T(8,128)S(1)} %copy-done.2, bf16[5,6,192,320]{3,2,1,0:T(8,128)(2,1)S(1)} %multiply_convert_fusion, bf16[5,1024,320]{2,1,0:T(8,128)(2,1)S(1)} %copy-done.1), kind=kOutput, calls=%fused_computation | convolution fusion | flops 3785490432 | bytes 9342976 | tf_op jit(solution)/shard_map/krno,kdo->krnd/dot_general | solution.py:395
  87.6 1.7 %copy.28 = bf16[24,8,6,1024]{3,1,2,0:T(8,128)(2,1)} copy(bf16[24,8,6,1024]{3,1,0,2:T(8,128)(2,1)S(1)} %bitcast.40) | data formatting | bytes 4718592
  89.3 8.0 %fusion.8 = bf16[5,1024,320]{1,2,0:T(8,128)(2,1)S(1)} fusion(bf16[5,6,192,320]{3,2,1,0:T(8,128)(2,1)} %copy-done.4, f32[5,1024]{1,0:T(8,128)S(1)} %copy-done.3, f32[5,1024]{1,0:T(8,128)S(1)} %copy-done.2, f32[6,192,1024]{2,1,0:T(8,128)} %bitcast.39), kind=kOutput, calls=%fused_computation.12 | convolution fusion | flops 3795845120 | bytes 11722752 | tf_op jit(solution)/shard_map/krnd,krno->kdo/dot_general | solution.py:397
  97.4 3.6 %copy.23 = bf16[5,1024,320]{2,1,0:T(8,128)(2,1)} copy(bf16[5,1024,320]{1,2,0:T(8,128)(2,1)S(1)} %fusion.8) | data formatting | bytes 6553600 | tf_op jit(solution)/shard_map/convert_element_type | solution.py:489
  101.0 41.4 %shard_map.132 = f32[5,64,320]{2,1,0:T(8,128)} custom-call(bf16[5,4,4,64,320]{4,3,2,1,0:T(8,128)(2,1)} %bitcast.34), custom_call_target="tpu_custom_call" | custom-call | tf_op jit(solution)/shard_map/pallas_call | solution.py:249
  142.4 1.3 reshape.184
  143.8 0.9 copy.27
  144.6 1.8 %copy.31 = f32[5,64,320]{2,1,0:T(8,128)} copy(f32[5,64,320]{2,1,0:T(8,128)} %shard_map.132) | data formatting | bytes 819200
  (43 shorter events, 1.0 us)
Async XLA Ops:
  7.2 62.6 %all-gather.2.cloned.1.call-start = ((), (), s32[]{:S(2)}) async-start(), calls=%async_computation.1 | async-start | bytes 4177920 | tf_op jit(solution)/shard_map/all_gather | solution.py:464
  7.9 134.5 %reduce-scatter.4.cloned.1.call-start = ((), (), s32[]{:S(2)}) async-start(), calls=%async_computation.2 | async-start | bytes 2654208
  9.0 12.1 %collective-permute-start = (bf16[3,24,1024]{2,1,0:T(8,128)(2,1)S(1)}, bf16[3,24,1024]{2,1,0:T(8,128)(2,1)S(1)}, u32[]{:S(2)}, u32[]{:S(2)}) collective-permute-start(bf16[3,24,1024]{2,1,0:T(8,128)(2,1)S(1)} %get-tuple-element.11), channel_id=1, source_target_pairs={{0,8},{8,16},{16,24},{24,32},{32,40},{40,48},{48,56},{56,64},{64,7... | collective-permute-start | bytes 442376 | tf_op jit(solution)/shard_map/ppermute | solution.py:338
  12.5 8.6 %collective-permute-start.1 = (bf16[3,24,1024]{2,1,0:T(8,128)(2,1)S(1)}, bf16[3,24,1024]{2,1,0:T(8,128)(2,1)S(1)}, u32[]{:S(2)}, u32[]{:S(2)}) collective-permute-start(bf16[3,24,1024]{2,1,0:T(8,128)(2,1)S(1)} %get-tuple-element.12), channel_id=1, source_target_pairs={{8,0},{16,8},{24,16},{32,24},{40,32},{48,40},{56,48},{64,56},{72,6... | collective-permute-start | bytes 442376 | tf_op jit(solution)/shard_map/ppermute | solution.py:339
  22.2 9.9 %collective-permute-start.2 = (bf16[12,6,1024]{2,1,0:T(8,128)(2,1)S(1)}, bf16[12,6,1024]{2,1,0:T(8,128)(2,1)S(1)}, u32[]{:S(2)}, u32[]{:S(2)}) collective-permute-start(bf16[12,6,1024]{2,1,0:T(8,128)(2,1)S(1)} %get-tuple-element.9), channel_id=1, source_target_pairs={{0,1},{1,2},{2,3},{3,4},{4,5},{5,6},{6,7},{7,0},{8,9},{9,10},{10,1... | collective-permute-start | bytes 442376 | tf_op jit(solution)/shard_map/ppermute | solution.py:338
  22.2 9.9 %collective-permute-start.3 = (bf16[12,6,1024]{2,1,0:T(8,128)(2,1)S(1)}, bf16[12,6,1024]{2,1,0:T(8,128)(2,1)S(1)}, u32[]{:S(2)}, u32[]{:S(2)}) collective-permute-start(bf16[12,6,1024]{2,1,0:T(8,128)(2,1)S(1)} %get-tuple-element.10), channel_id=1, source_target_pairs={{1,0},{2,1},{3,2},{4,3},{5,4},{6,5},{7,6},{0,7},{9,8},{10,9},{11,1... | collective-permute-start | bytes 442376 | tf_op jit(solution)/shard_map/ppermute | solution.py:339
  29.3 3.8 %copy-start = (f32[1024]{0:T(1024)S(1)}, f32[1024]{0:T(1024)}, u32[]{:S(2)}) copy-start(f32[1024]{0:T(1024)} %param.12) | copy-start | bytes 12292
  65.4 4.4 %copy-start.2 = (f32[5,1024]{1,0:T(8,128)S(1)}, f32[5,1024]{1,0:T(8,128)}, u32[]{:S(2)}) copy-start(f32[5,1024]{1,0:T(8,128)} %param.15) | copy-start | bytes 61444
  65.4 4.3 %copy-start.3 = (f32[5,1024]{1,0:T(8,128)S(1)}, f32[5,1024]{1,0:T(8,128)}, u32[]{:S(2)}) copy-start(f32[5,1024]{1,0:T(8,128)} %param.16) | copy-start | bytes 61444
  69.8 10.6 %copy-start.1 = (bf16[5,1024,320]{2,1,0:T(8,128)(2,1)S(1)}, bf16[5,1024,320]{2,1,0:T(8,128)(2,1)}, u32[]{:S(2)}) copy-start(bf16[5,1024,320]{2,1,0:T(8,128)(2,1)} %all-gather.2.cloned.1.call-done) | copy-start | bytes 9830404
  80.4 7.2 %copy-start.4 = (bf16[5,6,192,320]{3,2,1,0:T(8,128)(2,1)}, bf16[5,6,192,320]{3,2,1,0:T(8,128)(2,1)S(1)}, u32[]{:S(2)}) copy-start(bf16[5,6,192,320]{3,2,1,0:T(8,128)(2,1)S(1)} %multiply_convert_fusion) | copy-start | bytes 11059204
Sparse Core Ops, SparseCore 0:
  10.1 52.8 all-gather.1
  89.4 37.9 reduce-scatter.3

commit v20 on v19

--- a/solution.py
+++ b/solution.py
@@ -87,16 +87,22 @@
     )(parts)
 
 
-def masked_window_attention(queries, own_kv, halo_kv, query_win, key_win, heads, patches, output_proj):
+def masked_window_attention(queries, own_kv, halo, gain, kv_proj, query_win, key_win, heads, patches, output_proj):
     nq, width = queries.shape
     head_size = width // heads
     scale = 1.0 / float(head_size) ** 0.5
 
     n_own = own_kv.shape[0]
 
-    def kernel(q_ref, own_ref, halo_ref, qw_ref, kw_ref, p_ref, w_ref, out_ref, attn_ref, kv_ref):
+    def kernel(q_ref, own_ref, halo_ref, g_ref, kvw_ref, qw_ref, kw_ref, p_ref, w_ref, out_ref,
+               attn_ref, kv_ref):
+        wide = halo_ref[...].astype(jnp.float32)
+        centred = wide - jnp.mean(wide, axis=1, keepdims=True)
+        variance = jnp.mean(centred * centred, axis=1, keepdims=True)
+        normed = (centred * lax.rsqrt(variance + EPS) * g_ref[...]).astype(jnp.bfloat16)
+        kv_ref[pl.ds(n_own, halo_ref.shape[0]), :] = jnp.dot(
+            normed, kvw_ref[...], preferred_element_type=jnp.float32).astype(kv_ref.dtype)
         kv_ref[pl.ds(0, n_own), :] = own_ref[...]
-        kv_ref[pl.ds(n_own, halo_ref.shape[0]), :] = halo_ref[...]
         mask = qw_ref[...] == kw_ref[...]
         for h in range(heads):
             cols = slice(h * head_size, (h + 1) * head_size)
@@ -115,13 +121,13 @@
     return pl.pallas_call(
         kernel,
         out_shape=jax.ShapeDtypeStruct((nq, width), patches.dtype),
-        in_specs=[pl.BlockSpec(memory_space=pltpu.VMEM)] * 7,
+        in_specs=[pl.BlockSpec(memory_space=pltpu.VMEM)] * 9,
         out_specs=pl.BlockSpec(memory_space=pltpu.VMEM),
         scratch_shapes=[
             pltpu.VMEM((nq, width), jnp.bfloat16),
-            pltpu.VMEM((n_own + halo_kv.shape[0], own_kv.shape[1]), own_kv.dtype),
+            pltpu.VMEM((n_own + halo.shape[0], own_kv.shape[1]), own_kv.dtype),
         ],
-    )(queries, own_kv, halo_kv, query_win, key_win, patches, output_proj)
+    )(queries, own_kv, halo, gain, kv_proj, query_win, key_win, patches, output_proj)
 
 
 def chip_pair_gather(block, axis, n, cid):
@@ -435,8 +441,6 @@
             [part.reshape((-1,) + grid.shape[2:]) for part in (top, bottom, left, right)]
         )
 
-    halo_normed = layer_norm(ring(extended), norm_gain)
-    halo_keyval = jnp.dot(halo_normed, input_proj[:, width:], preferred_element_type=jnp.float32)
     global_row = lat_place * band_rows - half_rows + jnp.arange(ext_rows, dtype=jnp.int32)
     row_valid = (global_row >= 0) & (global_row < lat_count * band_rows)
     win_cols = ext_cols // WW
@@ -448,7 +452,9 @@
     latent = masked_window_attention(
         queries,
         own_keyval.astype(jnp.bfloat16),
-        halo_keyval.astype(jnp.bfloat16),
+        ring(extended),
+        norm_gain.reshape(1, width),
+        input_proj[:, width:],
         query_win.reshape(-1, 1),
         key_win.reshape(1, -1),
         HEADS,

time: 154 us -> 152 us (0.987)
  matrix products: 38.1 us -> 32.8 us
  local copies, waits for them, and re-layouts: 16.9 us -> 21.6 us
  other arithmetic: 6.14 us -> 1.94 us
  Pallas kernels: 69 us -> 71.4 us
    dot_general x1 -> x0, matrix products: 4.79 us -> none  [local(): jnp.dot(halo_normed, input_proj[:, width:], preferred_element_type=jnp.fl...]
    slice x0 -> x1, local copies, waits for them, and re-layouts: none -> 4.75 us  [local(): input_proj[:, width:]]
    pallas_call x1, Pallas kernels: 10.1 us -> 12.6 us  [masked_window_attention(): pl.pallas_call(kernel, out_shape=jax.ShapeDtypeStruct((nq, width), patche...]
    unnamed x14 -> x22, local copies, waits for them, and re-layouts: 5.76 us -> 5.75 us
  transfers between devices with their start and end apart: 6 -> 6, of which waited for: 0 -> 0; matrix products, arithmetic and copies ran while one was open for 25% -> 22% of each run, Pallas kernels for 45% -> 47%
where the time goes in v20:
time: 152 us; the launch traced here: 151 us
  Pallas kernels  71.4 us (47%)
  matrix products  32.8 us (22%)
  local copies, waits for them, and re-layouts  21.6 us (14%)
  between operations  14.3 us (9%)
  starting transfers between devices  8.3 us (5%)
  other arithmetic  1.94 us (1%)
    pallas_call x1, Pallas kernels, grid_reduce_scatter(): pl.pallas_call(kernel, out_shape=jax.ShapeDtypeStruct((slots, rows, outs)...  41.3 us
    pallas_call x1, Pallas kernels, chip_ring_gather(): pl.pallas_call(kernel, out_shape=jax.ShapeDtypeStruct((n,) + block.shape,...  17.5 us
    pallas_call x1, Pallas kernels, masked_window_attention(): pl.pallas_call(kernel, out_shape=jax.ShapeDtypeStruct((nq, width), patche...  12.6 us
    dot_general x1, matrix products, slot_terms(): jnp.einsum('krnd,kdo->krno', rows, heads_full, preferred_element_type=jnp...  10.6 us
    dot_general x1, matrix products, slot_terms(): jnp.einsum('krnd,krno->kdo', rows, errors, preferred_element_type=jnp.flo...  8.05 us
    dot_general x1, matrix products, slot_terms(): jnp.einsum('krno,kdo->krnd', errors, heads_full, preferred_element_type=j...  7.22 us
    unnamed x22, local copies, waits for them, and re-layouts  5.75 us
    slice x1, local copies, waits for them, and re-layouts, local(): input_proj[:, width:]  4.75 us
  transfers between devices with their start and end apart: 6, of which 0 were waited for; matrix products, arithmetic and copies ran while one was open for 22% of the time, Pallas kernels for 47%

profile of v20, /device:TPU:0, one launch (start us, length us, event | category | flops | bytes accessed | tf_op | source)
XLA Modules:
  0.0 151.2 jit_solution(4245473793061818041)
XLA Ops:
  7.2 0.7 all-gather.2.cloned.1.call-update
  7.9 1.0 fusion.30
  9.0 3.7 %collective-permute-start = (bf16[3,24,1024]{2,1,0:T(8,128)(2,1)S(1)}, bf16[3,24,1024]{2,1,0:T(8,128)(2,1)S(1)}, u32[]{:S(2)}, u32[]{:S(2)}) collective-permute-start(bf16[3,24,1024]{2,1,0:T(8,128)(2,1)S(1)} %get-tuple-element.11), channel_id=1, source_target_pairs={{0,8},{8,16},{16,24},{24,32},{32,40},{40,48},{48,56},{56,64},{64,7... | collective-permute-start | bytes 442376 | tf_op jit(solution)/shard_map/ppermute | solution.py:344
  12.7 1.3 collective-permute-start.1
  14.3 0.7 reshape.173.qw_ref
  15.0 0.1 reshape.162
  15.3 0.1 reshape.161
  15.4 4.7 %slice.57.kvw_ref = bf16[1024,2048]{1,0:T(8,128)(2,1)} slice(bf16[1024,3072]{1,0:T(8,128)(2,1)} %param.13), slice={[0:1024], [1024:3072]} | slice | bytes 8388608 | tf_op jit(solution)/shard_map/slice | solution.py:433
  20.2 0.7 concatenate.15
  20.9 0.1 select_reduce_fusion
  21.0 0.1 convert_reduce_fusion
  21.1 0.2 fusion.20
  21.3 0.2 fusion.22
  21.6 0.2 fusion.23
  21.9 0.1 pad_maximum_fusion
  22.0 3.2 %collective-permute-start.3 = (bf16[12,6,1024]{2,1,0:T(8,128)(2,1)S(1)}, bf16[12,6,1024]{2,1,0:T(8,128)(2,1)S(1)}, u32[]{:S(2)}, u32[]{:S(2)}) collective-permute-start(bf16[12,6,1024]{2,1,0:T(8,128)(2,1)S(1)} %get-tuple-element.10), channel_id=1, source_target_pairs={{1,0},{2,1},{3,2},{4,3},{5,4},{6,5},{7,6},{0,7},{9,8},{10,9},{11,1... | collective-permute-start | bytes 442376 | tf_op jit(solution)/shard_map/ppermute | solution.py:345
  25.2 3.9 %convolution_convert_fusion.own_ref = bf16[144,2048]{1,0:T(8,128)(2,1)} fusion(bf16[144,1024]{1,0:T(8,128)(2,1)S(1)} %bitcast.44, bf16[1024,3072]{1,0:T(8,128)(2,1)} %param.13), kind=kOutput, calls=%fused_computation.15 | convolution fusion | flops 604274688 | bytes 5079040 | tf_op jit(solution)/shard_map/dot_general | solution.py:433
  29.1 2.8 %fusion.15.q_ref = bf16[144,1024]{1,0:T(8,128)(2,1)} fusion(bf16[144,1024]{1,0:T(8,128)(2,1)S(1)} %bitcast.45, bf16[1024,3072]{1,0:T(8,128)(2,1)} %param.13), kind=kOutput, calls=%fused_computation.18 | convolution fusion | flops 302137344 | bytes 2686976 | tf_op jit(solution)/shard_map/dot_general | solution.py:431
  32.0 0.2 pad_maximum_fusion.4
  32.3 0.9 pad_maximum_fusion.1.halo_ref
  33.2 12.6 %shard_map.130.x_ref = bf16[144,1024]{1,0:T(8,128)(2,1)} custom-call(bf16[144,1024]{1,0:T(8,128)(2,1)} %fusion.15.q_ref, bf16[144,2048]{1,0:T(8,128)(2,1)} %convolution_convert_fusion.own_ref, bf16[288,1024]{1,0:T(8,128)(2,1)} %pad_maximum_fusion.1.halo_ref, f32[1,1024]{1,0:T(1,128)} %bitcast.46, bf16[1024,2048]{1,0:T(8,128)(2,1)} %slice.57.kvw_ref, ...), custom_call_target="tpu_custom_call" | custom-call | tf_op jit(solution)/shard_map/pallas_call | solution.py:121
  45.8 17.5 %shard_map.131 = bf16[8,144,1024]{2,1,0:T(8,128)(2,1)} custom-call(bf16[144,1024]{1,0:T(8,128)(2,1)} %shard_map.130.x_ref), custom_call_target="tpu_custom_call" | custom-call | tf_op jit(solution)/shard_map/pallas_call | solution.py:320
  63.3 4.3 %copy.22 = f32[8,6,24,1024]{3,2,0,1:T(8,128)} copy(bf16[8,6,24,1024]{3,2,1,0:T(8,128)(2,1)} %bitcast.37) | data formatting | bytes 7077888 | tf_op jit(solution)/shard_map/convert_element_type | solution.py:393
  67.7 10.6 %multiply_convert_fusion = bf16[5,6,192,320]{3,2,1,0:T(8,128)(2,1)S(1)} fusion(bf16[5,6,192,320]{3,2,1,0:T(8,128)(2,1)} %param.18, f32[5,192]{1,0:T(8,128)S(1)} %fusion.23, bf16[5,1024,320]{2,1,0:T(8,128)(2,1)} %all-gather.2.cloned.1.call-done, f32[5,1024]{1,0:T(8,128)S(1)} %copy-done.4, f32[5,1024]{1,0:T(8,128)S(1)} %copy-done.3, f32[6,192,1024]{2,1,0:T(8,128)} %bitcast.39), kind=kOutput, calls=%fused_computation.10 | convolution fusion | flops 3799941120 | bytes 15412992 | tf_op jit(solution)/shard_map/krnd,kdo->krno/dot_general | solution.py:397
  78.3 7.2 %multiply_reduce_fusion = bf16[6,192,1024]{2,1,0:T(8,128)(2,1)S(1)} fusion(f32[5,1024]{1,0:T(8,128)S(1)} %copy-done.3, bf16[5,6,192,320]{3,2,1,0:T(8,128)(2,1)S(1)} %multiply_convert_fusion, bf16[5,1024,320]{2,1,0:T(8,128)(2,1)S(1)} %copy-done.2), kind=kOutput, calls=%fused_computation | convolution fusion | flops 3785490432 | bytes 9342976 | tf_op jit(solution)/shard_map/krno,kdo->krnd/dot_general | solution.py:401
  85.6 1.6 %copy.28 = bf16[24,8,6,1024]{3,1,2,0:T(8,128)(2,1)} copy(bf16[24,8,6,1024]{3,1,0,2:T(8,128)(2,1)S(1)} %bitcast.41) | data formatting | bytes 4718592
  87.2 8.1 %fusion.8 = bf16[5,1024,320]{1,2,0:T(8,128)(2,1)S(1)} fusion(bf16[5,6,192,320]{3,2,1,0:T(8,128)(2,1)} %copy-done.8, f32[5,1024]{1,0:T(8,128)S(1)} %copy-done.4, f32[5,1024]{1,0:T(8,128)S(1)} %copy-done.3, f32[6,192,1024]{2,1,0:T(8,128)} %bitcast.40), kind=kOutput, calls=%fused_computation.12 | convolution fusion | flops 3795845120 | bytes 11722752 | tf_op jit(solution)/shard_map/krnd,krno->kdo/dot_general | solution.py:403
  95.3 3.6 %copy.23 = bf16[5,1024,320]{2,1,0:T(8,128)(2,1)} copy(bf16[5,1024,320]{1,2,0:T(8,128)(2,1)S(1)} %fusion.8) | data formatting | bytes 6553600 | tf_op jit(solution)/shard_map/convert_element_type | solution.py:495
  98.9 41.3 %shard_map.132 = f32[5,64,320]{2,1,0:T(8,128)} custom-call(bf16[5,4,4,64,320]{4,3,2,1,0:T(8,128)(2,1)} %bitcast.35), custom_call_target="tpu_custom_call" | custom-call | tf_op jit(solution)/shard_map/pallas_call | solution.py:255
  140.3 1.3 reshape.175
  141.6 0.9 copy.27
  142.5 1.8 %copy.31 = f32[5,64,320]{2,1,0:T(8,128)} copy(f32[5,64,320]{2,1,0:T(8,128)} %shard_map.132) | data formatting | bytes 819200
  (48 shorter events, 0.9 us)
Async XLA Ops:
  7.2 60.5 %all-gather.2.cloned.1.call-start = ((), (), s32[]{:S(2)}) async-start(), calls=%async_computation.1 | async-start | bytes 4177920 | tf_op jit(solution)/shard_map/all_gather | solution.py:470
  7.9 132.4 %reduce-scatter.4.cloned.1.call-start = ((), (), s32[]{:S(2)}) async-start(), calls=%async_computation.2 | async-start | bytes 2654208
  9.0 11.9 %copy-start.5 = (s32[4]{0:T(128)S(1)}, s32[4]{0:T(128)}, u32[]{:S(2)}) copy-start(s32[4]{0:T(128)} %param.19) | copy-start | bytes 52
  9.0 11.9 %copy-start.6 = (s32[1,8]{1,0:T(1,128)S(1)}, s32[1,8]{1,0:T(1,128)}, u32[]{:S(2)}) copy-start(s32[1,8]{1,0:T(1,128)} %param.20) | copy-start | bytes 100
  9.0 12.0 %copy-start = (bf16[6,24,1024]{2,1,0:T(8,128)(2,1)S(1)}, bf16[6,24,1024]{2,1,0:T(8,128)(2,1)}, u32[]{:S(2)}) copy-start(bf16[6,24,1024]{2,1,0:T(8,128)(2,1)} %param.11) | copy-start | bytes 884740
  9.0 12.9 %collective-permute-start = (bf16[3,24,1024]{2,1,0:T(8,128)(2,1)S(1)}, bf16[3,24,1024]{2,1,0:T(8,128)(2,1)S(1)}, u32[]{:S(2)}, u32[]{:S(2)}) collective-permute-start(bf16[3,24,1024]{2,1,0:T(8,128)(2,1)S(1)} %get-tuple-element.11), channel_id=1, source_target_pairs={{0,8},{8,16},{16,24},{24,32},{32,40},{40,48},{48,56},{56,64},{64,7... | collective-permute-start | bytes 442376 | tf_op jit(solution)/shard_map/ppermute | solution.py:344
  12.7 9.1 %collective-permute-start.1 = (bf16[3,24,1024]{2,1,0:T(8,128)(2,1)S(1)}, bf16[3,24,1024]{2,1,0:T(8,128)(2,1)S(1)}, u32[]{:S(2)}, u32[]{:S(2)}) collective-permute-start(bf16[3,24,1024]{2,1,0:T(8,128)(2,1)S(1)} %get-tuple-element.12), channel_id=1, source_target_pairs={{8,0},{16,8},{24,16},{32,24},{40,32},{48,40},{56,48},{64,56},{72,6... | collective-permute-start | bytes 442376 | tf_op jit(solution)/shard_map/ppermute | solution.py:345
  15.4 5.9 %copy-start.1 = (f32[1024]{0:T(1024)S(1)}, f32[1024]{0:T(1024)}, u32[]{:S(2)}) copy-start(f32[1024]{0:T(1024)} %param.12) | copy-start | bytes 12292
  15.4 6.2 %copy-start.7 = (s32[5]{0:T(128)S(1)}, s32[5]{0:T(128)}, u32[]{:S(2)}) copy-start(s32[5]{0:T(128)} %param.21) | copy-start | bytes 64
  22.0 9.9 %collective-permute-start.2 = (bf16[12,6,1024]{2,1,0:T(8,128)(2,1)S(1)}, bf16[12,6,1024]{2,1,0:T(8,128)(2,1)S(1)}, u32[]{:S(2)}, u32[]{:S(2)}) collective-permute-start(bf16[12,6,1024]{2,1,0:T(8,128)(2,1)S(1)} %get-tuple-element.9), channel_id=1, source_target_pairs={{0,1},{1,2},{2,3},{3,4},{4,5},{5,6},{6,7},{7,0},{8,9},{9,10},{10,1... | collective-permute-start | bytes 442376 | tf_op jit(solution)/shard_map/ppermute | solution.py:344
  22.0 9.9 %collective-permute-start.3 = (bf16[12,6,1024]{2,1,0:T(8,128)(2,1)S(1)}, bf16[12,6,1024]{2,1,0:T(8,128)(2,1)S(1)}, u32[]{:S(2)}, u32[]{:S(2)}) collective-permute-start(bf16[12,6,1024]{2,1,0:T(8,128)(2,1)S(1)} %get-tuple-element.10), channel_id=1, source_target_pairs={{1,0},{2,1},{3,2},{4,3},{5,4},{6,5},{7,6},{0,7},{9,8},{10,9},{11,1... | collective-permute-start | bytes 442376 | tf_op jit(solution)/shard_map/ppermute | solution.py:345
  45.8 21.9 %copy-start.3 = (f32[5,1024]{1,0:T(8,128)S(1)}, f32[5,1024]{1,0:T(8,128)}, u32[]{:S(2)}) copy-start(f32[5,1024]{1,0:T(8,128)} %param.15) | copy-start | bytes 61444
  45.8 21.9 %copy-start.4 = (f32[5,1024]{1,0:T(8,128)S(1)}, f32[5,1024]{1,0:T(8,128)}, u32[]{:S(2)}) copy-start(f32[5,1024]{1,0:T(8,128)} %param.16) | copy-start | bytes 61444
  67.7 10.6 %copy-start.2 = (bf16[5,1024,320]{2,1,0:T(8,128)(2,1)S(1)}, bf16[5,1024,320]{2,1,0:T(8,128)(2,1)}, u32[]{:S(2)}) copy-start(bf16[5,1024,320]{2,1,0:T(8,128)(2,1)} %all-gather.2.cloned.1.call-done) | copy-start | bytes 9830404
  78.3 7.2 %copy-start.8 = (bf16[5,6,192,320]{3,2,1,0:T(8,128)(2,1)}, bf16[5,6,192,320]{3,2,1,0:T(8,128)(2,1)S(1)}, u32[]{:S(2)}) copy-start(bf16[5,6,192,320]{3,2,1,0:T(8,128)(2,1)S(1)} %multiply_convert_fusion) | copy-start | bytes 11059204
Sparse Core Ops, SparseCore 0:
  10.1 52.9 all-gather.1
  87.4 37.9 reduce-scatter.3
